TPU v7x, 512 devices: a whole 4x8x8 slice. The times are simulated.
512 devices in a mesh: interval: 8 (over y), seq: 8 (over x, core), head: 8 (over z).
Axes of the slice: x: 4, y: 8, z: 8, core: 2. Of those that a mesh axis runs over, the one named last changes fastest.
Arguments:
- hidden_in: bfloat16 [8, 2048, 1536], P('interval', 'seq'), may hold values from -6 to 6
- ctx_grad: bfloat16 [8, 2048, 1536], P('interval', 'seq', 'head'), may hold values from -6 to 6
- w_query: bfloat16 [1536, 1536], P('head'), may hold values from -0.15625 to 0.15625
- w_key: bfloat16 [1536, 1536], P('head'), may hold values from -0.15625 to 0.15625
- w_value: bfloat16 [1536, 1536], P('head'), may hold values from -0.15625 to 0.15625
- w_junction: bfloat16 [1536, 128], replicated, may hold values from -0.15625 to 0.15625
- donor_pos: int32 [8, 8, 8, 64], P('interval', 'seq', None, 'head'), may hold values from 0 to 255
- acceptor_pos: int32 [8, 8, 8, 64], P('interval', 'seq', None, 'head'), may hold values from 0 to 255
- junction_counts: int32 [8, 8, 8], P('interval', 'seq'), may hold values from 16 to 64, as said below
- pred_grad: float32 [8, 8, 8, 64], P('interval', 'seq', None, 'head'), may hold values from -6 to 6
Outputs:
- grad_input: bfloat16 [8, 2048, 1536], P('interval', 'seq', 'head')
- grad_query: bfloat16 [1536, 1536], P('head')
- grad_key: bfloat16 [1536, 1536], P('head')
- grad_value: bfloat16 [1536, 1536], P('head')
Inputs may be any that keep to these rules, and one draw needn't show every extreme that they name: `junction_counts`: slots at or past a bucket's count are empty. In each interval one acceptor shard, drawn from the seed, has 64 live slots from every donor shard; every other bucket has 16 to 32.
All inputs are finite; a program needn't handle non-finite values.
Results may differ from a plain program's by a relative error of at most 0.022.
Values may be sent and summed in bfloat16 or wider, within the bound.
No kernel may reach another device: no remote copies, remote signals or barrier semaphores. Data moves between devices by JAX's collectives and lax.ppermute only.
A program may use at most 64 MiB of HBM per device.

v0:
```python
import jax
import jax.numpy as jnp
from jax import lax
from jax.sharding import PartitionSpec as P

HD = 192
PJ = 128


def on_device(
    hidden_in,
    ctx_grad,
    w_query,
    w_key,
    w_value,
    w_junction,
    donor_pos,
    acceptor_pos,
    junction_counts,
    pred_grad,
):
    hidden = hidden_in[0]
    local_len = hidden.shape[0]
    shard_count = lax.axis_size("seq")
    total_len = local_len * shard_count
    heads_dev = w_query.shape[0] // HD
    softmax_scale = HD ** (-0.5)
    pair_scale = PJ ** (-0.5)
    queries = jnp.einsum("td,cd->tc", hidden, w_query, preferred_element_type=jnp.float32).astype(
        jnp.bfloat16
    )
    key_rows = jnp.einsum("td,cd->tc", hidden, w_key, preferred_element_type=jnp.float32).astype(
        jnp.bfloat16
    )
    value_rows = jnp.einsum(
        "td,cd->tc", hidden, w_value, preferred_element_type=jnp.float32
    ).astype(jnp.bfloat16)
    features = jnp.dot(hidden, w_junction, preferred_element_type=jnp.float32).astype(jnp.bfloat16)
    all_keys, all_values, all_features = (
        lax.all_gather(key_rows, "seq", axis=0, tiled=True),
        lax.all_gather(value_rows, "seq", axis=0, tiled=True),
        lax.all_gather(features, "seq", axis=0, tiled=True),
    )
    query_heads = queries.reshape(local_len, heads_dev, HD)
    grad_heads = ctx_grad[0].reshape(local_len, heads_dev, HD)
    key_heads = all_keys.reshape(total_len, heads_dev, HD)
    value_heads = all_values.reshape(total_len, heads_dev, HD)
    scores = (
        jnp.einsum("qhd,khd->hqk", query_heads, key_heads, preferred_element_type=jnp.float32)
        * softmax_scale
    )
    row_max = jnp.max(scores, axis=-1, keepdims=True)
    expd = jnp.exp(scores - row_max)
    probs = expd / jnp.sum(expd, axis=-1, keepdims=True)
    dprobs = jnp.einsum("qhd,khd->hqk", grad_heads, value_heads, preferred_element_type=jnp.float32)
    row_delta = jnp.sum(probs * dprobs, axis=-1, keepdims=True)
    dscores = probs * (dprobs - row_delta)
    probs_b = probs.astype(jnp.bfloat16)
    dscores_b = dscores.astype(jnp.bfloat16)
    query_grad = (
        (
            jnp.einsum("hqk,khd->qhd", dscores_b, key_heads, preferred_element_type=jnp.float32)
            * softmax_scale
        )
        .astype(jnp.bfloat16)
        .reshape(local_len, heads_dev * HD)
    )
    key_term = (
        jnp.einsum("hqk,qhd->khd", dscores_b, query_heads, preferred_element_type=jnp.float32)
        * softmax_scale
    ).reshape(total_len, heads_dev * HD)
    value_term = jnp.einsum(
        "hqk,qhd->khd", probs_b, grad_heads, preferred_element_type=jnp.float32
    ).reshape(total_len, heads_dev * HD)
    key_sum, value_sum = (
        lax.psum_scatter(
            key_term.astype(jnp.bfloat16), "seq", scatter_dimension=0, tiled=True
        ).astype(jnp.float32),
        lax.psum_scatter(
            value_term.astype(jnp.bfloat16), "seq", scatter_dimension=0, tiled=True
        ).astype(jnp.float32),
    )
    key_grad = key_sum.astype(jnp.bfloat16)
    value_grad = value_sum.astype(jnp.bfloat16)
    donor_idx = donor_pos[0, 0]
    accept_idx = acceptor_pos[0, 0]
    slot_dev = donor_idx.shape[1]
    slot_ids = lax.axis_index("head") * slot_dev + jnp.arange(slot_dev, dtype=jnp.int32)
    live_slots = slot_ids[None, :] < junction_counts[0, 0][:, None]
    donor_feat = features[donor_idx].astype(jnp.float32)
    accept_glob = jnp.arange(shard_count, dtype=jnp.int32)[:, None] * local_len + accept_idx
    accept_rows = all_features[accept_glob]
    accept_feat = accept_rows.astype(jnp.float32)
    pair_score = jnp.sum(donor_feat * accept_feat, axis=-1) * pair_scale
    slot_grad = (
        jnp.where(live_slots, pred_grad[0, 0] * jax.nn.sigmoid(pair_score), 0.0) * pair_scale
    )
    donor_term = slot_grad[..., None] * accept_feat
    accept_term = slot_grad[..., None] * donor_feat
    pair_width = features.shape[1]
    grad_feat = (
        jnp.zeros((local_len, pair_width), jnp.float32)
        .at[donor_idx.reshape(-1)]
        .add(donor_term.reshape(-1, pair_width))
    )
    spread_term = (
        jnp.zeros((total_len, pair_width), jnp.float32)
        .at[accept_glob.reshape(-1)]
        .add(accept_term.reshape(-1, pair_width))
    )
    grad_feat = grad_feat + lax.psum_scatter(
        spread_term.astype(jnp.bfloat16), "seq", scatter_dimension=0, tiled=True
    ).astype(jnp.float32)
    grad_feat_b = grad_feat.astype(jnp.bfloat16)
    input_term = jnp.einsum("tc,cd->td", query_grad, w_query, preferred_element_type=jnp.float32)
    input_term = input_term + jnp.einsum(
        "tc,cd->td", key_grad, w_key, preferred_element_type=jnp.float32
    )
    input_term = input_term + jnp.einsum(
        "tc,cd->td", value_grad, w_value, preferred_element_type=jnp.float32
    )
    input_term = input_term + jnp.einsum(
        "tp,dp->td", grad_feat_b, w_junction, preferred_element_type=jnp.float32
    )
    grad_input = lax.psum_scatter(
        input_term.astype(jnp.bfloat16), "head", scatter_dimension=1, tiled=True
    )
    key_wterm = jnp.einsum("tc,td->cd", key_grad, hidden, preferred_element_type=jnp.float32)
    value_wterm = jnp.einsum("tc,td->cd", value_grad, hidden, preferred_element_type=jnp.float32)
    query_wterm = jnp.einsum("tc,td->cd", query_grad, hidden, preferred_element_type=jnp.float32)
    query_wsum, key_wsum, value_wsum = lax.psum(
        (query_wterm, key_wterm, value_wterm), ("interval", "seq")
    )
    return (
        grad_input[None],
        query_wsum.astype(jnp.bfloat16),
        key_wsum.astype(jnp.bfloat16),
        value_wsum.astype(jnp.bfloat16),
    )


def solution(mesh):
    placed = (
        P("interval", "seq", None),
        P("interval", "seq", "head"),
        P("head", None),
        P("head", None),
        P("head", None),
        P(),
        P("interval", "seq", None, "head"),
        P("interval", "seq", None, "head"),
        P("interval", "seq", None),
        P("interval", "seq", None, "head"),
    )
    return jax.shard_map(
        on_device,
        mesh=mesh,
        in_specs=placed,
        out_specs=(P("interval", "seq", "head"), P("head", None), P("head", None), P("head", None)),
        check_vma=False,
    )
```

profile of v0, /device:TPU:1, one launch (start us, length us, event | category | flops | bytes accessed | tf_op | source)
XLA Modules:
  0.0 443.7 jit_solution(17675293737374444175)
XLA Ops:
  7.2 0.0 copy-start
  7.2 0.0 reduce-scatter.9.cloned.1.call-start
  7.2 0.8 squeeze.15
  8.1 0.8 compare_select_fusion
  8.8 0.1 add.132
  8.9 0.1 add.133
  9.0 0.7 compare_select_fusion.1
  9.7 0.1 reshape.274
  9.8 0.0 copy-done
  9.8 1.4 convolution_convert_fusion.4
  11.1 0.0 copy-start.4
  11.1 20.0 %all_gather.11 = bf16[2048,128]{1,0:T(8,128)(2,1)S(1)} all-gather(bf16[256,128]{1,0:T(8,128)(2,1)S(1)} %convolution_convert_fusion.4), channel_id=1, replica_groups=mesh['interval'=8,'seq'=8,'head'=8] {'seq'}, dimensions={0}, use_global_device_ids=true | all-gather | bytes 589824 | tf_op jit(solution)/shard_map/all_gather | solution.py:42
  31.1 0.6 gather_fusion
  31.7 0.8 squeeze.16
  32.5 0.1 reshape.282
  32.6 0.1 lt.65
  32.7 0.7 lt.67
  33.4 0.1 lt.68
  33.5 0.6 gather_fusion.1
  34.1 0.1 fusion.23
  34.3 1.1 scatter_custom_fusion
  35.4 0.0 copy-start.3
  35.4 0.8 convert_element_type.105
  36.3 0.0 reduce-scatter.9.cloned.1.call-update
  36.3 0.0 reduce-scatter.5.cloned.1.call-start
  36.4 0.4 convolution_convert_fusion.3
  36.8 13.5 %all_gather.9 = bf16[2048,192]{0,1:T(8,128)(2,1)S(1)} all-gather(bf16[256,192]{0,1:T(8,128)(2,1)S(1)} %convolution_convert_fusion.3), channel_id=1, replica_groups=mesh['interval'=8,'seq'=8,'head'=8] {'seq'}, dimensions={0}, use_global_device_ids=true | all-gather | bytes 884736 | tf_op jit(solution)/shard_map/all_gather | solution.py:40
  50.3 0.4 convolution_convert_fusion.2
  50.7 0.4 convolution_convert_fusion.1
  51.1 14.4 %all_gather.10 = bf16[2048,192]{1,0:T(8,128)(2,1)S(1)} all-gather(bf16[256,192]{1,0:T(8,128)(2,1)S(1)} %convolution_convert_fusion.1), channel_id=1, replica_groups=mesh['interval'=8,'seq'=8,'head'=8] {'seq'}, dimensions={0}, use_global_device_ids=true | all-gather | bytes 884736 | tf_op jit(solution)/shard_map/all_gather | solution.py:41
  65.4 0.5 fusion.31
  66.0 0.4 fusion.4
  66.4 0.7 multiply_reduce_fusion
  67.2 0.6 multiply_convert_fusion
  67.8 0.0 copy-start.1
  67.8 1.0 copy-done.1
  68.8 1.3 fusion.2
  70.1 0.0 reduce-scatter.5.cloned.1.call-update
  70.1 0.0 copy-start.10
  70.1 0.0 reduce-scatter.7.cloned.1.call-start
  70.2 2.4 convolution_convert_fusion
  72.6 0.0 reduce-scatter.7.cloned.1.call-update
  72.6 0.0 reduce-scatter.11.cloned.1.call-start
  72.7 0.0 copy-done.10
  72.7 0.1 reshape_squeeze.4
  72.8 2.0 fusion.6
  74.8 0.4 fusion.32
  75.2 0.0 copy-start.7
  75.2 0.0 reduce-scatter.9.cloned.1.call-done
  75.3 0.9 convert_element_type.106
  76.2 1.1 scatter_custom_fusion.1
  77.2 31.9 %reduce-scatter.5.cloned.1.call-done = bf16[256,192]{0,1:T(8,128)(2,1)} async-done(((bf16[2048,192]{0,1:T(8,128)(2,1)}), bf16[256,192]{0,1:T(8,128)(2,1)}) %reduce-scatter.5.cloned.1.call-update) | async-done | bytes 98320 | tf_op jit(solution)/shard_map/reduce_scatter | solution.py:76
  109.1 2.7 convolution_add_fusion.2
  111.8 35.8 %reduce-scatter.7.cloned.1.call-done = bf16[256,192]{0,1:T(8,128)(2,1)} async-done(((bf16[2048,192]{0,1:T(8,128)(2,1)}), bf16[256,192]{0,1:T(8,128)(2,1)}) %reduce-scatter.7.cloned.1.call-update) | async-done | bytes 98320 | tf_op jit(solution)/shard_map/reduce_scatter | solution.py:79
  147.6 0.0 copy-done.7
  147.6 1.9 convolution_add_fusion.1
  149.5 0.0 copy-done.5
  149.5 1.3 fusion
  150.8 0.0 reduce-scatter.11.cloned.1.call-update
  150.8 0.3 fusion.12
  151.2 0.5 copy-done.8
  151.7 0.3 fusion.10
  152.0 1.3 fusion.8
  153.4 283.8 %all-reduce.2 = (bf16[192,1536]{1,0:T(8,128)(2,1)}, bf16[192,1536]{1,0:T(8,128)(2,1)}, bf16[192,1536]{1,0:T(8,128)(2,1)}) all-reduce(f32[192,1536]{1,0:T(8,128)S(1)} %fusion.12, f32[192,1536]{1,0:T(8,128)S(1)} %fusion.10, f32[192,1536]{1,0:T(8,128)} %fusion.8), channel_id=1, replica_groups=mesh['interval'=8,'seq'=8,'head'=8] {'interval','seq'}, use_global_device_ids=true, to_apply=%region_10.11 | all-reduce | flops 884736 | bytes 5308416 | tf_op jit(solution)/shard_map/psum | solution.py:131
  (21 shorter events, 0.1 us)
Async XLA Ops:
  7.2 2.6 copy-start
  7.2 68.1 %reduce-scatter.9.cloned.1.call-start = ((), (), s32[]{:S(2)}) async-start(), calls=%async_computation.6 | async-start | bytes 589824 | tf_op jit(solution)/shard_map/reduce_scatter | solution.py:111
  11.1 25.2 %copy-start.4 = (bf16[192,1536]{1,0:T(8,128)(2,1)S(1)}, bf16[192,1536]{1,0:T(8,128)(2,1)}, u32[]{:S(2)}) copy-start(bf16[192,1536]{1,0:T(8,128)(2,1)} %param.13) | copy-start | bytes 1769476
  35.4 14.8 %copy-start.3 = (bf16[192,1536]{1,0:T(8,128)(2,1)S(1)}, bf16[192,1536]{1,0:T(8,128)(2,1)}, u32[]{:S(2)}) copy-start(bf16[192,1536]{1,0:T(8,128)(2,1)} %param.12) | copy-start | bytes 1769476
  36.3 14.4 %copy-start.6 = (bf16[192,1536]{1,0:T(8,128)(2,1)S(1)}, bf16[192,1536]{1,0:T(8,128)(2,1)}, u32[]{:S(2)}) copy-start(bf16[192,1536]{1,0:T(8,128)(2,1)} %param.14) | copy-start | bytes 1769476
  36.3 72.8 %reduce-scatter.5.cloned.1.call-start = ((), (), s32[]{:S(2)}) async-start(), calls=%async_computation.4 | async-start | bytes 884736 | tf_op jit(solution)/shard_map/reduce_scatter | solution.py:76
  50.3 15.2 %copy-start.2 = (bf16[2048,192]{0,1:T(8,128)(2,1)}, bf16[2048,192]{0,1:T(8,128)(2,1)S(1)}, u32[]{:S(2)}) copy-start(bf16[2048,192]{0,1:T(8,128)(2,1)S(1)} %all_gather.9) | copy-start | bytes 2359300
  65.4 1.0 copy-start.11
  67.8 1.0 copy-start.1
  70.1 2.6 copy-start.10
  70.1 77.5 %reduce-scatter.7.cloned.1.call-start = ((), (), s32[]{:S(2)}) async-start(), calls=%async_computation.5 | async-start | bytes 884736 | tf_op jit(solution)/shard_map/reduce_scatter | solution.py:79
  72.6 364.6 %reduce-scatter.11.cloned.1.call-start = ((), (), s32[]{:S(2)}) async-start(), calls=%async_computation.7 | async-start | bytes 884736 | tf_op jit(solution)/shard_map/reduce_scatter | solution.py:125
  75.2 72.4 %copy-start.7 = (bf16[192,1536]{1,0:T(8,128)(2,1)S(1)}, bf16[192,1536]{1,0:T(8,128)(2,1)}, u32[]{:S(2)}) copy-start(bf16[192,1536]{1,0:T(8,128)(2,1)} %param.14) | copy-start | bytes 1769476
  111.8 37.7 %copy-start.5 = (bf16[1536,128]{1,0:T(8,128)(2,1)S(1)}, bf16[1536,128]{1,0:T(8,128)(2,1)}, u32[]{:S(2)}) copy-start(bf16[1536,128]{1,0:T(8,128)(2,1)} %param.15) | copy-start | bytes 1179652
  150.8 0.9 copy-start.8
  150.8 1.2 copy-start.9
Sparse Core Ops, SparseCore 0:
  36.4 33.3 reduce-scatter.8
  72.9 36.1 reduce-scatter.4
  111.9 35.6 reduce-scatter.6
  151.1 37.2 reduce-scatter.10
where the time goes:
time: 448 us; the launch traced here: 444 us
  blocking collectives  332 us (74%)
  waiting for transfers between devices  67.7 us (15%)
  matrix products  17.9 us (4%)
  between operations  14 us (3%)
  other arithmetic  6.61 us (1%)
  local copies, waits for them, and re-layouts  5.72 us (1%)
    psum x1, blocking collectives, on_device(): lax.psum((query_wterm, key_wterm, value_wterm), ('interval', 'seq'))  284 us
    reduce_scatter x1, waiting for transfers between devices, on_device(): lax.psum_scatter(value_term.astype(jnp.bfloat16), 'seq', scatter_dimensio...  35.8 us
    reduce_scatter x1, waiting for transfers between devices, on_device(): lax.psum_scatter(key_term.astype(jnp.bfloat16), 'seq', scatter_dimension=...  31.9 us
    all_gather x1, blocking collectives, on_device(): lax.all_gather(features, 'seq', axis=0, tiled=True)  20 us
    all_gather x1, blocking collectives, on_device(): lax.all_gather(value_rows, 'seq', axis=0, tiled=True)  14.4 us
    all_gather x1, blocking collectives, on_device(): lax.all_gather(key_rows, 'seq', axis=0, tiled=True)  13.5 us
  transfers between devices with their start and end apart: 4, of which 2 were waited for; matrix products, arithmetic and copies ran while one was open for 4% of the time, Pallas kernels for 0%

commit v1 on v0

v1 whole, which is shorter than its diff:
```python
import jax
import jax.numpy as jnp
from jax import lax
from jax.sharding import Mesh
from jax.sharding import PartitionSpec as P

HD = 192
PJ = 128
CORES = 2
F32 = jnp.float32
BF16 = jnp.bfloat16


def swap_cores(value):
    return lax.ppermute(value, "core", [(0, 1), (1, 0)])


def on_device(
    hidden_in,
    ctx_grad,
    w_query,
    w_key,
    w_value,
    w_junction,
    donor_pos,
    acceptor_pos,
    junction_counts,
    pred_grad,
):
    hidden = hidden_in[0]
    ctx = ctx_grad[0]
    tokens, width = hidden.shape
    chips = lax.axis_size("x")
    intervals = lax.axis_size("interval")
    core = lax.axis_index("core")
    half = chips * tokens
    softmax_scale = HD ** (-0.5)
    pair_scale = PJ ** (-0.5)

    def project(weight):
        return jnp.einsum("td,cd->tc", hidden, weight, preferred_element_type=F32).astype(BF16)

    queries, key_rows, value_rows = project(w_query), project(w_key), project(w_value)
    features = jnp.dot(hidden, w_junction, preferred_element_type=F32).astype(BF16)
    sent = jnp.concatenate([key_rows, value_rows, features], axis=1)
    copies = jnp.broadcast_to(sent[None], (chips,) + sent.shape).reshape(half, -1)
    mine = lax.all_to_all(copies, "x", 0, 0, tiled=True)
    theirs = swap_cores(mine)
    both = jnp.concatenate([mine, theirs], axis=0)
    keys, values, all_features = both[:, :HD], both[:, HD : 2 * HD], both[:, 2 * HD :]

    scores = jnp.einsum("qd,kd->qk", queries, keys, preferred_element_type=F32) * softmax_scale
    row_max = jnp.max(scores, axis=-1, keepdims=True)
    expd = jnp.exp(scores - row_max)
    probs = expd / jnp.sum(expd, axis=-1, keepdims=True)
    dprobs = jnp.einsum("qd,kd->qk", ctx, values, preferred_element_type=F32)
    row_delta = jnp.sum(probs * dprobs, axis=-1, keepdims=True)
    dscores_b = (probs * (dprobs - row_delta)).astype(BF16)
    probs_b = probs.astype(BF16)
    query_grad = (
        jnp.einsum("qk,kd->qd", dscores_b, keys, preferred_element_type=F32) * softmax_scale
    ).astype(BF16)
    key_term = (
        jnp.einsum("qk,qd->kd", dscores_b, queries, preferred_element_type=F32) * softmax_scale
    )
    value_term = jnp.einsum("qk,qd->kd", probs_b, ctx, preferred_element_type=F32)

    donor_idx = donor_pos[0, 0]
    buckets, slot_dev = donor_idx.shape
    slot_ids = lax.axis_index("head") * slot_dev + jnp.arange(slot_dev, dtype=jnp.int32)
    live_slots = slot_ids[None, :] < junction_counts[0, 0][:, None]
    shard = jnp.arange(buckets, dtype=jnp.int32)
    base = jnp.where(shard % CORES == core, 0, half) + (shard // CORES) * tokens
    accept_idx = base[:, None] + acceptor_pos[0, 0]
    donor_feat = features[donor_idx].astype(F32)
    accept_feat = all_features[accept_idx].astype(F32)
    pair_score = jnp.sum(donor_feat * accept_feat, axis=-1) * pair_scale
    slot_grad = (
        jnp.where(live_slots, pred_grad[0, 0] * jax.nn.sigmoid(pair_score), 0.0) * pair_scale
    )
    donor_term = slot_grad[..., None] * accept_feat
    accept_term = slot_grad[..., None] * donor_feat
    donor_sum = (
        jnp.zeros((tokens, PJ), F32).at[donor_idx.reshape(-1)].add(donor_term.reshape(-1, PJ))
    )
    spread = (
        jnp.zeros((CORES * half, PJ), F32)
        .at[accept_idx.reshape(-1)]
        .add(accept_term.reshape(-1, PJ))
    )

    terms = jnp.concatenate([key_term, value_term, spread], axis=1).astype(BF16)
    pair_sum = terms[:half].astype(F32) + swap_cores(terms[half:]).astype(F32)
    parts = lax.all_to_all(pair_sum.astype(BF16), "x", 0, 0, tiled=True)
    total = jnp.sum(parts.reshape(chips, tokens, -1).astype(F32), axis=0)
    key_grad = total[:, :HD].astype(BF16)
    value_grad = total[:, HD : 2 * HD].astype(BF16)
    feature_grad = (donor_sum + total[:, 2 * HD :]).astype(BF16)

    grads = jnp.concatenate([query_grad, key_grad, value_grad], axis=1)
    weights = jnp.concatenate([w_query, w_key, w_value], axis=0)
    input_term = jnp.dot(grads, weights, preferred_element_type=F32)
    input_term = input_term + jnp.einsum(
        "tp,dp->td", feature_grad, w_junction, preferred_element_type=F32
    )
    grad_input = lax.psum_scatter(
        input_term.astype(BF16), "head", scatter_dimension=1, tiled=True
    )

    rows = grads.shape[1]
    half_width = width // CORES
    weight_term = jnp.einsum("tc,td->cd", grads, hidden, preferred_element_type=F32).astype(BF16)

    def sum_parts(value, axis, count):
        got = lax.all_to_all(value, axis, 0, 0, tiled=True)
        return jnp.sum(got.reshape(count, -1, got.shape[-1]).astype(F32), axis=0).astype(BF16)

    term = weight_term.reshape(rows, CORES, half_width).transpose(1, 0, 2)
    term = sum_parts(term.reshape(CORES * rows, half_width), "core", CORES)
    term = sum_parts(term, "x", chips)
    part_rows = rows // chips
    cut = (2, part_rows // 2, intervals // 2, half_width // (intervals // 2))
    term = term.reshape(cut).transpose(0, 2, 1, 3).reshape(-1, cut[3])
    term = sum_parts(term, "interval", intervals)
    term = jnp.broadcast_to(term[None], (intervals,) + term.shape).reshape(-1, cut[3])
    term = lax.all_to_all(term, "interval", 0, 0, tiled=True)
    term = term.reshape(cut[0], cut[2], cut[1], cut[3]).transpose(0, 2, 1, 3)
    term = lax.all_gather(term.reshape(part_rows, half_width), "x", axis=0, tiled=True)
    other = swap_cores(term)
    left = jnp.where(core == 0, term, other)
    right = jnp.where(core == 0, other, term)
    whole = jnp.concatenate([left, right], axis=1)
    return grad_input[None], whole[:HD], whole[HD : 2 * HD], whole[2 * HD :]


def solution(mesh):
    axes = (mesh.shape["interval"], mesh.shape["seq"] // CORES, CORES, mesh.shape["head"])
    split = Mesh(mesh.devices.reshape(axes), ("interval", "x", "core", "head"))
    seq = ("x", "core")
    placed = (
        P("interval", seq, None),
        P("interval", seq, "head"),
        P("head", None),
        P("head", None),
        P("head", None),
        P(),
        P("interval", seq, None, "head"),
        P("interval", seq, None, "head"),
        P("interval", seq, None),
        P("interval", seq, None, "head"),
    )
    return jax.shard_map(
        on_device,
        mesh=split,
        in_specs=placed,
        out_specs=(P("interval", seq, "head"), P("head", None), P("head", None), P("head", None)),
        check_vma=False,
    )
```

time: 448 us -> 190 us (0.42)
  the two profiles are of different devices: /device:TPU:1 before, /device:TPU:2 now
where the time goes in v1:
time: 190 us; the launch traced here: 189 us
  waiting for transfers between devices  64 us (34%)
  blocking collectives  35 us (18%)
  starting transfers between devices  31.5 us (17%)
  local copies, waits for them, and re-layouts  17.2 us (9%)
  between operations  14.5 us (8%)
  matrix products  13.7 us (7%)
  other arithmetic  13.2 us (7%)
    all_to_all x2, blocking collectives, sum_parts(): got = lax.all_to_all(value, axis, 0, 0, tiled=True)  21.6 us
    reduce_scatter x1, waiting for transfers between devices, on_device(): lax.psum_scatter(input_term.astype(BF16), 'head', scatter_dimension=1, ti...  19 us
    all_gather x1, blocking collectives, on_device(): lax.all_gather(term.reshape(part_rows, half_width), 'x', axis=0, tiled=True)  13.4 us
    all_to_all x1, waiting for transfers between devices, on_device(): parts = lax.all_to_all(pair_sum.astype(BF16), 'x', 0, 0, tiled=True)  12.8 us
    all_to_all x1, waiting for transfers between devices, sum_parts(): got = lax.all_to_all(value, axis, 0, 0, tiled=True)  10.8 us
    all_to_all x1, waiting for transfers between devices, on_device(): mine = lax.all_to_all(copies, 'x', 0, 0, tiled=True)  9.43 us
    all_to_all x1, starting transfers between devices, on_device(): mine = lax.all_to_all(copies, 'x', 0, 0, tiled=True)  9.39 us
    all_to_all x1, waiting for transfers between devices, on_device(): term = lax.all_to_all(term, 'interval', 0, 0, tiled=True)  7.33 us
  transfers between devices with their start and end apart: 8, of which 7 were waited for; matrix products, arithmetic and copies ran while one was open for 10% of the time, Pallas kernels for 0%

profile of v1, /device:TPU:2, one launch (start us, length us, event | category | flops | bytes accessed | tf_op | source)
XLA Modules:
  0.0 189.2 jit_solution(3122860435319958120)
XLA Ops:
  7.2 1.1 copy-done
  8.3 1.4 convolution_convert_fusion.5
  9.7 1.5 convolution_convert_fusion.2
  11.2 0.4 convolution_convert_fusion.3
  11.7 0.1 copy.42
  11.9 1.1 broadcast_in_dim.17
  12.9 9.4 %all-to-all-start = ((bf16[4,256,512]{2,1,0:T(8,128)(2,1)}), bf16[4,256,512]{2,1,0:T(8,128)(2,1)S(1)}, u32[]{:S(2)}, u32[]{:S(2)}) async-start(bf16[4,256,512]{2,1,0:T(8,128)(2,1)} %broadcast_in_dim.17), calls=%async_computation | async-start | bytes 2097152 | tf_op jit(solution)/shard_map/all_to_all | solution.py:47
  22.3 9.4 %all-to-all-done = bf16[4,256,512]{2,1,0:T(8,128)(2,1)S(1)} async-done(((bf16[4,256,512]{2,1,0:T(8,128)(2,1)}), bf16[4,256,512]{2,1,0:T(8,128)(2,1)S(1)}, u32[]{:S(2)}, u32[]{:S(2)}) %all-to-all-start) | async-done | bytes 1048608 | tf_op jit(solution)/shard_map/all_to_all | solution.py:47
  31.7 1.9 %collective-permute-start = (bf16[1024,512]{1,0:T(8,128)(2,1)S(1)}, bf16[1024,512]{1,0:T(8,128)(2,1)S(1)}, u32[]{:S(2)}, u32[]{:S(2)}) collective-permute-start(bf16[1024,512]{1,0:T(8,128)(2,1)S(1)} %bitcast.71), channel_id=1, source_target_pairs={{0,8},{8,0},{1,9},{9,1},{2,10},{10,2},{3,11},{11,3},{4,12},{12,4},... | collective-permute-start | bytes 3145736 | tf_op jit(solution)/shard_map/ppermute | solution.py:15
  33.8 0.9 copy.44
  34.7 0.6 squeeze.19
  35.3 0.6 reshape.283
  36.0 0.6 lt.72
  36.6 0.7 lt.74
  37.3 0.7 lt.75
  38.0 0.6 squeeze.20
  38.6 0.7 add.139
  39.3 0.6 add.140
  39.9 0.6 pad_clamp_fusion.1
  40.5 0.8 gather_fusion
  41.3 1.3 pad_clamp_fusion
  42.5 1.2 fusion.33
  43.7 0.4 convolution_convert_fusion.4
  44.1 0.6 fusion.42
  44.7 0.4 fusion.3
  45.1 0.5 copy-done.22
  45.6 1.5 convolution_convert_fusion.1
  47.1 1.0 multiply_reduce_fusion
  48.1 0.6 multiply_convert_fusion
  48.7 1.0 copy-done.1
  49.7 1.3 fusion.1
  51.1 0.6 gather_fusion.1
  51.9 2.0 %scatter_custom_fusion = f32[2048,128]{1,0:T(8,128)} fusion(s32[64]{0:T(128)} %fusion.33, f32[]{:T(128)} %constant.30.clone.1, bf16[64,128]{1,0:T(8,128)(2,1)S(1)} %gather_fusion, f32[64]{0:T(128)S(1)} %fusion.35), kind=kCustom, calls=%fused_computation.56 | custom fusion | flops 24576 | bytes 1065728 | tf_op jit(solution)/shard_map/scatter-add | solution.py:89
  53.9 1.4 copy.45
  55.3 1.5 pad_maximum_fusion
  57.0 2.4 %collective-permute-start.1 = (bf16[1024,512]{0,1:T(8,128)(2,1)S(1)}, bf16[1024,512]{0,1:T(8,128)(2,1)S(1)}, u32[]{:S(2)}, u32[]{:S(2)}) collective-permute-start(bf16[1024,512]{0,1:T(8,128)(2,1)S(1)} %slice.56), channel_id=1, source_target_pairs={{0,8},{8,0},{1,9},{9,1},{2,10},{10,2},{3,11},{11,3},{4,12},{12,4},... | collective-permute-start | bytes 3145736 | tf_op jit(solution)/shard_map/ppermute | solution.py:15
  59.4 2.3 %collective-permute-done.1 = bf16[1024,512]{0,1:T(8,128)(2,1)S(1)} collective-permute-done((bf16[1024,512]{0,1:T(8,128)(2,1)S(1)}, bf16[1024,512]{0,1:T(8,128)(2,1)S(1)}, u32[]{:S(2)}, u32[]{:S(2)}) %collective-permute-start.1) | collective-permute-done | bytes 1048608 | tf_op jit(solution)/shard_map/ppermute | solution.py:15
  61.6 0.4 add_convert_fusion
  62.0 1.1 copy.60
  63.1 5.7 %all-to-all-start.1 = ((bf16[4,256,512]{1,2,0:T(8,128)(2,1)}), bf16[4,256,512]{1,2,0:T(8,128)(2,1)}, u32[]{:S(2)}, u32[]{:S(2)}) async-start(bf16[4,256,512]{1,2,0:T(8,128)(2,1)} %bitcast.79), calls=%async_computation.1 | async-start | bytes 2097152 | tf_op jit(solution)/shard_map/all_to_all | solution.py:94
  68.8 1.8 fusion.10
  70.6 12.8 %all-to-all-done.1 = bf16[4,256,512]{1,2,0:T(8,128)(2,1)} async-done(((bf16[4,256,512]{1,2,0:T(8,128)(2,1)}), bf16[4,256,512]{1,2,0:T(8,128)(2,1)}, u32[]{:S(2)}, u32[]{:S(2)}) %all-to-all-start.1) | async-done | bytes 1048608 | tf_op jit(solution)/shard_map/all_to_all | solution.py:94
  83.3 1.4 convert_reduce_fusion
  84.8 0.8 copy-done.3
  85.6 0.6 convolution_convert_fusion
  86.4 5.2 %all_to_all.48 = bf16[2,576,768]{2,1,0:T(8,128)(2,1)S(1)} all-to-all(bf16[2,576,768]{2,1,0:T(8,128)(2,1)S(1)} %bitcast.76), channel_id=1, replica_groups=mesh['interval'=8,'x'=4,'core'=2,'head'=8] {'core'}, dimensions={0} | all-to-all | bytes 3538944 | tf_op jit(solution)/shard_map/all_to_all | solution.py:115
  91.5 0.9 reduce_sum.76
  92.4 16.5 %all_to_all.49 = bf16[4,144,768]{2,1,0:T(8,128)(2,1)S(1)} all-to-all(bf16[4,144,768]{2,1,0:T(8,128)(2,1)S(1)} %bitcast.80), channel_id=1, replica_groups=mesh['interval'=8,'x'=4,'core'=2,'head'=8] {'x'}, dimensions={0} | all-to-all | bytes 1769472 | tf_op jit(solution)/shard_map/all_to_all | solution.py:115
  109.1 0.3 reshape.266
  109.3 0.7 copy.50
  110.1 6.7 %all-to-all-start.4 = ((bf16[8,72,192]{2,1,0:T(8,128)(2,1)}), bf16[8,72,192]{2,1,0:T(8,128)(2,1)S(1)}, u32[]{:S(2)}, u32[]{:S(2)}) async-start(bf16[8,72,192]{2,1,0:T(8,128)(2,1)} %bitcast.13), calls=%async_computation.5 | async-start | bytes 589824 | tf_op jit(solution)/shard_map/all_to_all | solution.py:115
  117.0 1.1 scatter_custom_fusion.1
  118.1 10.8 %all-to-all-done.4 = bf16[8,72,192]{2,1,0:T(8,128)(2,1)S(1)} async-done(((bf16[8,72,192]{2,1,0:T(8,128)(2,1)}), bf16[8,72,192]{2,1,0:T(8,128)(2,1)S(1)}, u32[]{:S(2)}, u32[]{:S(2)}) %all-to-all-start.4) | async-done | bytes 221216 | tf_op jit(solution)/shard_map/all_to_all | solution.py:115
  128.9 0.7 broadcast_in_dim.23
  129.7 3.4 %all-to-all-start.5 = ((bf16[8,72,192]{2,1,0:T(8,128)(2,1)}), bf16[8,72,192]{2,1,0:T(8,128)(2,1)S(1)}, u32[]{:S(2)}, u32[]{:S(2)}) async-start(bf16[8,72,192]{2,1,0:T(8,128)(2,1)} %broadcast_in_dim.23), calls=%async_computation.6 | async-start | bytes 589824 | tf_op jit(solution)/shard_map/all_to_all | solution.py:126
  133.2 2.0 %fusion.4 = f32[256,1536]{0,1:T(8,128)S(1)} fusion(bf16[192,1536]{1,0:T(8,128)(2,1)S(1)} %copy-done.6, bf16[192,1536]{1,0:T(8,128)(2,1)S(1)} %copy-done.8, bf16[192,1536]{1,0:T(8,128)(2,1)} %param.12, bf16[256,384]{0,1:T(8,128)(2,1)S(1)} %copy-done.5, bf16[256,192]{0,1:T(8,128)(2,1)S(1)} %fusion.10), kind=kOutput, calls=%fused_computation.29 | convolution fusion | flops 458883072 | bytes 3637248 | tf_op jit(solution)/shard_map/dot_general | solution.py:102
  135.3 1.2 fusion
  136.5 7.3 %all-to-all-done.5 = bf16[8,72,192]{2,1,0:T(8,128)(2,1)S(1)} async-done(((bf16[8,72,192]{2,1,0:T(8,128)(2,1)}), bf16[8,72,192]{2,1,0:T(8,128)(2,1)S(1)}, u32[]{:S(2)}, u32[]{:S(2)}) %all-to-all-start.5) | async-done | bytes 221216 | tf_op jit(solution)/shard_map/all_to_all | solution.py:126
  144.0 0.3 reshape.268
  144.2 13.4 %all_gather.3 = bf16[576,768]{1,0:T(8,128)(2,1)S(1)} all-gather(bf16[144,768]{1,0:T(8,128)(2,1)S(1)} %reshape.268), channel_id=1, replica_groups=mesh['interval'=8,'x'=4,'core'=2,'head'=8] {'x'}, dimensions={0}, use_global_device_ids=true | all-gather | bytes 1105920 | tf_op jit(solution)/shard_map/all_gather | solution.py:128
  157.6 1.9 %collective-permute-start.2 = (bf16[576,768]{1,0:T(8,128)(2,1)S(1)}, bf16[576,768]{1,0:T(8,128)(2,1)S(1)}, u32[]{:S(2)}, u32[]{:S(2)}) collective-permute-start(bf16[576,768]{1,0:T(8,128)(2,1)S(1)} %all_gather.3), channel_id=1, source_target_pairs={{0,8},{8,0},{1,9},{9,1},{2,10},{10,2},{3,11},{11,3},{4,12},{12,4},... | collective-permute-start | bytes 2654216 | tf_op jit(solution)/shard_map/ppermute | solution.py:15
  159.6 2.4 %collective-permute-done.2 = bf16[576,768]{1,0:T(8,128)(2,1)S(1)} collective-permute-done((bf16[576,768]{1,0:T(8,128)(2,1)S(1)}, bf16[576,768]{1,0:T(8,128)(2,1)S(1)}, u32[]{:S(2)}, u32[]{:S(2)}) %collective-permute-start.2) | collective-permute-done | bytes 884768 | tf_op jit(solution)/shard_map/ppermute | solution.py:15
  162.1 1.2 pad_maximum_fusion.1
  163.3 19.0 %reduce-scatter.2.cloned.1.call-done = bf16[256,192]{0,1:T(8,128)(2,1)} async-done(((bf16[256,1536]{0,1:T(8,128)(2,1)}), bf16[256,192]{0,1:T(8,128)(2,1)}) %reduce-scatter.2.cloned.1.call-update) | async-done | bytes 98320 | tf_op jit(solution)/shard_map/reduce_scatter | solution.py:106
  (67 shorter events, 1.4 us)
Async XLA Ops:
  7.2 1.1 copy-start
  7.2 4.0 %copy-start.7 = (bf16[192,1536]{1,0:T(8,128)(2,1)S(1)}, bf16[192,1536]{1,0:T(8,128)(2,1)}, u32[]{:S(2)}) copy-start(bf16[192,1536]{1,0:T(8,128)(2,1)} %param.13) | copy-start | bytes 1769476
  9.7 1.9 %copy-start.10 = (bf16[256,128]{0,1:T(8,128)(2,1)}, bf16[256,128]{0,1:T(8,128)(2,1)S(1)}, u32[]{:S(2)}) copy-start(bf16[256,128]{0,1:T(8,128)(2,1)S(1)} %convolution_convert_fusion.5) | copy-start | bytes 196612
  11.7 22.0 %copy-start.12 = (s32[1,1,8,8]{3,2,1,0:T(8,128)S(1)}, s32[1,1,8,8]{3,2,1,0:T(8,128)}, u32[]{:S(2)}) copy-start(s32[1,1,8,8]{3,2,1,0:T(8,128)} %param.17) | copy-start | bytes 772
  11.7 24.2 %copy-start.13 = (s32[1,1,8,8]{3,2,1,0:T(8,128)S(1)}, s32[1,1,8,8]{3,2,1,0:T(8,128)}, u32[]{:S(2)}) copy-start(s32[1,1,8,8]{3,2,1,0:T(8,128)} %param.16) | copy-start | bytes 772
  11.7 26.3 %copy-start.17 = (f32[1,1,8,8]{3,2,1,0:T(8,128)S(1)}, f32[1,1,8,8]{3,2,1,0:T(8,128)}, u32[]{:S(2)}) copy-start(f32[1,1,8,8]{3,2,1,0:T(8,128)} %param.19) | copy-start | bytes 772
  11.7 32.0 %copy-start.9 = (bf16[192,1536]{1,0:T(8,128)(2,1)S(1)}, bf16[192,1536]{1,0:T(8,128)(2,1)}, u32[]{:S(2)}) copy-start(bf16[192,1536]{1,0:T(8,128)(2,1)} %param.12) | copy-start | bytes 1769476
  12.9 18.8 %all-to-all-start = ((bf16[4,256,512]{2,1,0:T(8,128)(2,1)}), bf16[4,256,512]{2,1,0:T(8,128)(2,1)S(1)}, u32[]{:S(2)}, u32[]{:S(2)}) async-start(bf16[4,256,512]{2,1,0:T(8,128)(2,1)} %broadcast_in_dim.17), calls=%async_computation | async-start | bytes 2097152 | tf_op jit(solution)/shard_map/all_to_all | solution.py:47
  22.3 11.4 %copy-start.21 = (s32[8]{0:T(128)}, s32[8]{0:T(128)S(1)}, u32[]{:S(2)}) copy-start(s32[8]{0:T(128)S(1)} %fusion.31) | copy-start | bytes 100
  31.7 12.4 %collective-permute-start = (bf16[1024,512]{1,0:T(8,128)(2,1)S(1)}, bf16[1024,512]{1,0:T(8,128)(2,1)S(1)}, u32[]{:S(2)}, u32[]{:S(2)}) collective-permute-start(bf16[1024,512]{1,0:T(8,128)(2,1)S(1)} %bitcast.71), channel_id=1, source_target_pairs={{0,8},{8,0},{1,9},{9,1},{2,10},{10,2},{3,11},{11,3},{4,12},{12,4},... | collective-permute-start | bytes 3145736 | tf_op jit(solution)/shard_map/ppermute | solution.py:15
  44.7 0.9 copy-start.22
  48.7 1.0 copy-start.1
  49.7 1.4 copy-start.11
  49.7 2.1 %copy-start.18 = (s32[64]{0:T(128)S(1)}, s32[64]{0:T(128)}, u32[]{:S(2)}) copy-start(s32[64]{0:T(128)} %lt.72) | copy-start | bytes 772
  49.7 2.1 %copy-start.19 = (s32[64]{0:T(128)S(1)}, s32[64]{0:T(128)}, u32[]{:S(2)}) copy-start(s32[64]{0:T(128)} %lt.75) | copy-start | bytes 772
  49.7 2.1 %copy-start.20 = (f32[64]{0:T(128)S(1)}, f32[64]{0:T(128)}, u32[]{:S(2)}) copy-start(f32[64]{0:T(128)} %squeeze.20) | copy-start | bytes 772
  51.9 5.0 %copy-start.15 = (f32[64]{0:T(128)}, f32[64]{0:T(128)S(1)}, u32[]{:S(2)}) copy-start(f32[64]{0:T(128)S(1)} %fusion.35) | copy-start | bytes 772
  57.0 4.7 %collective-permute-start.1 = (bf16[1024,512]{0,1:T(8,128)(2,1)S(1)}, bf16[1024,512]{0,1:T(8,128)(2,1)S(1)}, u32[]{:S(2)}, u32[]{:S(2)}) collective-permute-start(bf16[1024,512]{0,1:T(8,128)(2,1)S(1)} %slice.56), channel_id=1, source_target_pairs={{0,8},{8,0},{1,9},{9,1},{2,10},{10,2},{3,11},{11,3},{4,12},{12,4},... | collective-permute-start | bytes 3145736 | tf_op jit(solution)/shard_map/ppermute | solution.py:15
  63.1 20.2 %all-to-all-start.1 = ((bf16[4,256,512]{1,2,0:T(8,128)(2,1)}), bf16[4,256,512]{1,2,0:T(8,128)(2,1)}, u32[]{:S(2)}, u32[]{:S(2)}) async-start(bf16[4,256,512]{1,2,0:T(8,128)(2,1)} %bitcast.79), calls=%async_computation.1 | async-start | bytes 2097152 | tf_op jit(solution)/shard_map/all_to_all | solution.py:94
  84.8 0.8 copy-start.3
  85.6 0.7 copy-start.4
  92.4 24.4 %copy-start.14 = (s32[1,1,8,8]{3,2,1,0:T(8,128)S(1)}, s32[1,1,8,8]{3,2,1,0:T(8,128)}, u32[]{:S(2)}) copy-start(s32[1,1,8,8]{3,2,1,0:T(8,128)} %param.16) | copy-start | bytes 772
  92.4 24.5 %slice-start = ((f32[256,512]{0,1:T(8,128)}), f32[256,128]{0,1:T(8,128)S(1)}, s32[]{:S(2)}) async-start(f32[256,512]{0,1:T(8,128)} %copy-done.3), calls=%async_computation.8 | async-start | bytes 262144 | tf_op jit(solution)/shard_map/slice | solution.py:98
  108.9 8.1 %copy-start.16 = (f32[64]{0:T(128)S(1)}, f32[64]{0:T(128)}, u32[]{:S(2)}) copy-start(f32[64]{0:T(128)} %copy-done.15) | copy-start | bytes 772
  108.9 24.3 %copy-start.5 = (bf16[256,384]{0,1:T(8,128)(2,1)S(1)}, bf16[256,384]{0,1:T(8,128)(2,1)}, u32[]{:S(2)}) copy-start(bf16[256,384]{0,1:T(8,128)(2,1)} %copy-done.4) | copy-start | bytes 589828
  108.9 24.3 %copy-start.6 = (bf16[192,1536]{1,0:T(8,128)(2,1)S(1)}, bf16[192,1536]{1,0:T(8,128)(2,1)}, u32[]{:S(2)}) copy-start(bf16[192,1536]{1,0:T(8,128)(2,1)} %param.14) | copy-start | bytes 1769476
  109.0 24.1 %copy-start.8 = (bf16[192,1536]{1,0:T(8,128)(2,1)S(1)}, bf16[192,1536]{1,0:T(8,128)(2,1)}, u32[]{:S(2)}) copy-start(bf16[192,1536]{1,0:T(8,128)(2,1)} %param.13) | copy-start | bytes 1769476
  110.1 18.8 %all-to-all-start.4 = ((bf16[8,72,192]{2,1,0:T(8,128)(2,1)}), bf16[8,72,192]{2,1,0:T(8,128)(2,1)S(1)}, u32[]{:S(2)}, u32[]{:S(2)}) async-start(bf16[8,72,192]{2,1,0:T(8,128)(2,1)} %bitcast.13), calls=%async_computation.5 | async-start | bytes 589824 | tf_op jit(solution)/shard_map/all_to_all | solution.py:115
  129.7 14.2 %all-to-all-start.5 = ((bf16[8,72,192]{2,1,0:T(8,128)(2,1)}), bf16[8,72,192]{2,1,0:T(8,128)(2,1)S(1)}, u32[]{:S(2)}, u32[]{:S(2)}) async-start(bf16[8,72,192]{2,1,0:T(8,128)(2,1)} %broadcast_in_dim.23), calls=%async_computation.6 | async-start | bytes 589824 | tf_op jit(solution)/shard_map/all_to_all | solution.py:126
  133.1 2.1 %copy-start.2 = (bf16[1536,128]{1,0:T(8,128)(2,1)S(1)}, bf16[1536,128]{1,0:T(8,128)(2,1)}, u32[]{:S(2)}) copy-start(bf16[1536,128]{1,0:T(8,128)(2,1)} %param.15) | copy-start | bytes 1179652
  133.1 49.2 %reduce-scatter.2.cloned.1.call-start = ((), (), s32[]{:S(2)}) async-start(), calls=%async_computation.7 | async-start | bytes 884736 | tf_op jit(solution)/shard_map/reduce_scatter | solution.py:106
  157.6 4.3 %collective-permute-start.2 = (bf16[576,768]{1,0:T(8,128)(2,1)S(1)}, bf16[576,768]{1,0:T(8,128)(2,1)S(1)}, u32[]{:S(2)}, u32[]{:S(2)}) collective-permute-start(bf16[576,768]{1,0:T(8,128)(2,1)S(1)} %all_gather.3), channel_id=1, source_target_pairs={{0,8},{8,0},{1,9},{9,1},{2,10},{10,2},{3,11},{11,3},{4,12},{12,4},... | collective-permute-start | bytes 2654216 | tf_op jit(solution)/shard_map/ppermute | solution.py:15
Sparse Core Ops, SparseCore 0:
  137.4 44.9 reduce-scatter.1

commit v2 on v1

v2 whole, which is shorter than its diff:
```python
import jax
import jax.numpy as jnp
from jax import lax
from jax.experimental import pallas as pl
from jax.experimental.pallas import tpu as pltpu
from jax.sharding import Mesh
from jax.sharding import PartitionSpec as P

HD = 192
PJ = 128
CORES = 2
LANES = 256
LOW = PJ // 2
F32 = jnp.float32
BF16 = jnp.bfloat16
VMEM_BYTES = 48 * 1024 * 1024


def contract(a, b, dim_a, dim_b):
    return lax.dot_general(a, b, (((dim_a,), (dim_b,)), ((), ())), preferred_element_type=F32)


def local_call(body, outs, scratch=(), scalars=0, operands=0):
    specs = [pl.BlockSpec(memory_space=pltpu.SMEM)] * scalars
    specs += [pl.BlockSpec(memory_space=pltpu.VMEM)] * operands
    return pl.pallas_call(
        body,
        out_shape=tuple(jax.ShapeDtypeStruct(shape, kind) for shape, kind in outs),
        in_specs=specs,
        out_specs=tuple(pl.BlockSpec(memory_space=pltpu.VMEM) for _ in outs),
        scratch_shapes=list(scratch),
        compiler_params=pltpu.CompilerParams(vmem_limit_bytes=VMEM_BYTES),
    )


def project_body(hidden, w_key, w_value, w_junction, copies):
    x = hidden[...]
    feats = contract(x, w_junction[...], 1, 0).astype(BF16)
    row = jnp.concatenate(
        [
            contract(x, w_key[...], 1, 1).astype(BF16),
            feats[:, :LOW],
            contract(x, w_value[...], 1, 1).astype(BF16),
            feats[:, LOW:],
        ],
        axis=1,
    )
    for chip in range(copies.shape[0]):
        copies[chip] = row


def split_terms(term):
    high = term.astype(BF16)
    return high, (term - high.astype(F32)).astype(BF16)


def attend_body(
    place,
    hidden,
    w_query,
    ctx_grad,
    own,
    mine,
    theirs,
    donor_pos,
    acceptor_pos,
    counts,
    pred_grad,
    terms_mine,
    terms_theirs,
    query_grad,
    donor_sum,
    queries,
    ctx,
    probs_b,
    dscores_b,
):
    tokens = hidden.shape[0]
    half = mine.shape[0]
    scale = HD ** (-0.5)
    queries[...] = jnp.zeros_like(queries)
    ctx[...] = jnp.zeros_like(ctx)
    queries[:, :HD] = contract(hidden[...], w_query[...], 1, 1).astype(BF16)
    ctx[:, :HD] = ctx_grad[...]
    sides = (mine, theirs)
    rows = 64
    for start in range(0, tokens, rows):
        band = pl.ds(start, rows)
        q, g = queries[band, :], ctx[band, :]
        scores = [contract(q, side[:, :LANES], 1, 1) * scale for side in sides]
        row_max = jnp.maximum(
            jnp.max(scores[0], axis=-1, keepdims=True), jnp.max(scores[1], axis=-1, keepdims=True)
        )
        expd = [jnp.exp(score - row_max) for score in scores]
        inverse = 1.0 / (
            jnp.sum(expd[0], axis=-1, keepdims=True) + jnp.sum(expd[1], axis=-1, keepdims=True)
        )
        probs = [value * inverse for value in expd]
        dprobs = [contract(g, side[:, LANES:], 1, 1) for side in sides]
        row_delta = jnp.sum(probs[0] * dprobs[0], axis=-1, keepdims=True) + jnp.sum(
            probs[1] * dprobs[1], axis=-1, keepdims=True
        )
        for i in range(2):
            probs_b[i, band, :] = probs[i].astype(BF16)
            dscores_b[i, band, :] = (probs[i] * (dprobs[i] - row_delta)).astype(BF16)

    buckets, per = donor_pos.shape
    slots = buckets * per
    core, first = place[0], place[1] * per
    shard_of = lax.broadcasted_iota(jnp.int32, (1, slots), 1) // per
    spread_out = (
        lax.broadcasted_iota(jnp.int32, (per, slots), 1) % per
        == lax.broadcasted_iota(jnp.int32, (per, slots), 0)
    ).astype(F32)
    own_row = lax.broadcasted_iota(jnp.int32, (buckets, slots), 0) == (
        lax.broadcasted_iota(jnp.int32, (buckets, slots), 1) // per
    )

    def to_lanes(value):
        wide = lax.dot_general(
            value.astype(F32),
            spread_out,
            (((1,), (0,)), ((), ())),
            precision=lax.Precision.HIGHEST,
            preferred_element_type=F32,
        )
        return jnp.sum(jnp.where(own_row, wide, 0.0), axis=0, keepdims=True)

    donor_idx = to_lanes(donor_pos[...]).astype(jnp.int32)
    local_idx = to_lanes(acceptor_pos[...]).astype(jnp.int32)
    accept_idx = (
        jnp.where(shard_of % CORES == core, 0, half) + (shard_of // CORES) * tokens + local_idx
    )
    slot_row = first + lax.broadcasted_iota(jnp.int32, (buckets, per), 1)
    live_grad = to_lanes(jnp.where(slot_row < counts[...], pred_grad[...], 0.0))
    on_diagonal = lax.broadcasted_iota(jnp.int32, (slots, slots), 0) == (
        lax.broadcasted_iota(jnp.int32, (slots, slots), 1)
    )
    live_column = jnp.sum(jnp.where(on_diagonal, live_grad, 0.0), axis=1, keepdims=True)

    def pick(rows_at, count, offset):
        at = lax.broadcasted_iota(jnp.int32, (count, slots), 0) + offset
        return jnp.where(at == rows_at, 1.0, 0.0).astype(BF16)

    donor_hot = pick(donor_idx, tokens, 0)
    accept_hot = (pick(accept_idx, half, 0), pick(accept_idx, half, half))
    donor_feat = contract(donor_hot, own[...], 0, 0)
    accept_feat = contract(accept_hot[0], mine[...], 0, 0) + contract(
        accept_hot[1], theirs[...], 0, 0
    )
    lane = lax.broadcasted_iota(jnp.int32, (1, 2 * LANES), 1) % LANES
    donor_feat = jnp.where(lane >= HD, donor_feat, 0.0)
    accept_feat = jnp.where(lane >= HD, accept_feat, 0.0)
    pair_scale = PJ ** (-0.5)
    pair_score = jnp.sum(donor_feat * accept_feat, axis=-1, keepdims=True) * pair_scale
    slot_grad = live_column * jax.nn.sigmoid(pair_score) * pair_scale
    donor_terms = split_terms(slot_grad * accept_feat)
    accept_terms = split_terms(slot_grad * donor_feat)
    donor_sum[...] = contract(donor_hot, donor_terms[0], 1, 0) + contract(
        donor_hot, donor_terms[1], 1, 0
    )

    terms = (terms_mine, terms_theirs)
    for i in (1, 0):
        for part, (grad, rows_in) in enumerate(((dscores_b, queries), (probs_b, ctx))):
            lanes = pl.ds(part * LANES, LANES)
            total = contract(grad[i], rows_in[...], 0, 0)
            if part == 0:
                total = total * scale
            for piece in accept_terms:
                total = total + contract(
                    accept_hot[i], piece[:, part * LANES : (part + 1) * LANES], 1, 0
                )
            terms[i][:, lanes] = total.astype(terms[i].dtype)
    query_grad[...] = (
        (
            contract(dscores_b[0], mine[:, :LANES], 1, 0)
            + contract(dscores_b[1], theirs[:, :LANES], 1, 0)
        )[:, :HD]
        * scale
    ).astype(BF16)


def pair_body(mine, theirs, total):
    total[...] = (mine[...].astype(F32) + theirs[...].astype(F32)).astype(BF16)


def input_body(parts, donor_sum, query_grad, w_query, w_key, w_value, w_junction, grads, term):
    total = donor_sum[...]
    for chip in range(parts.shape[0]):
        total = total + parts[chip].astype(F32)
    total = total.astype(BF16)
    key_grad, value_grad = total[:, :HD], total[:, LANES : LANES + HD]
    feature_grad = jnp.concatenate([total[:, HD:LANES], total[:, LANES + HD :]], axis=1)
    grads[...] = total
    value = contract(w_query[...], query_grad[...], 0, 1)
    value = value + contract(w_key[...], key_grad, 0, 1)
    value = value + contract(w_value[...], value_grad, 0, 1)
    value = value + contract(w_junction[...], feature_grad, 1, 1)
    term[...] = value.astype(BF16)


def weight_body(hidden, query_grad, grads, term):
    cut = hidden.shape[1] // CORES
    for part, grad in enumerate(
        (query_grad[...], grads[:, :HD], grads[:, LANES : LANES + HD])
    ):
        value = contract(grad, hidden[...], 0, 0).astype(BF16)
        for core in range(CORES):
            term[core, part * HD : (part + 1) * HD, :] = value[:, core * cut : (core + 1) * cut]


def swap_cores(value):
    return lax.ppermute(value, "core", [(0, 1), (1, 0)])


def on_device(
    hidden_in,
    ctx_grad,
    w_query,
    w_key,
    w_value,
    w_junction,
    donor_pos,
    acceptor_pos,
    junction_counts,
    pred_grad,
):
    hidden = hidden_in[0]
    tokens, width = hidden.shape
    chips = lax.axis_size("x")
    intervals = lax.axis_size("interval")
    core = lax.axis_index("core")
    half = chips * tokens
    row = 2 * LANES

    (copies,) = local_call(project_body, [((chips, tokens, row), BF16)], operands=4)(
        hidden, w_key, w_value, w_junction
    )
    mine = lax.all_to_all(copies, "x", 0, 0, tiled=True).reshape(half, row)
    theirs = swap_cores(mine)
    place = jnp.stack([core, lax.axis_index("head")]).astype(jnp.int32)
    terms_mine, terms_theirs, query_grad, donor_sum = local_call(
        attend_body,
        [
            ((half, row), BF16),
            ((half, row), BF16),
            ((tokens, HD), BF16),
            ((tokens, row), F32),
        ],
        scratch=[pltpu.VMEM((tokens, LANES), BF16)] * 2
        + [pltpu.VMEM((CORES, tokens, half), BF16)] * 2,
        scalars=1,
        operands=10,
    )(
        place,
        hidden,
        w_query,
        ctx_grad[0],
        copies[0],
        mine,
        theirs,
        donor_pos[0, 0],
        acceptor_pos[0, 0],
        junction_counts[0, 0][:, None],
        pred_grad[0, 0],
    )
    (pair_sum,) = local_call(pair_body, [((half, row), BF16)], operands=2)(
        terms_mine, swap_cores(terms_theirs)
    )
    parts = lax.all_to_all(pair_sum.reshape(chips, tokens, row), "x", 0, 0, tiled=True)
    grads, input_term = local_call(
        input_body, [((tokens, row), BF16), ((width, tokens), BF16)], operands=7
    )(parts, donor_sum, query_grad, w_query, w_key, w_value, w_junction)
    grad_input = lax.psum_scatter(input_term, "head", scatter_dimension=0, tiled=True)

    rows = 3 * HD
    half_width = width // CORES
    (term,) = local_call(weight_body, [((CORES, rows, half_width), BF16)], operands=3)(
        hidden, query_grad, grads
    )

    def sum_parts(value, axis, count):
        got = lax.all_to_all(value, axis, 0, 0, tiled=True)
        return jnp.sum(got.reshape(count, -1, got.shape[-1]).astype(F32), axis=0).astype(BF16)

    term = sum_parts(term, "core", CORES)
    term = sum_parts(term, "x", chips)
    part_rows = rows // chips
    cut = (2, part_rows // 2, intervals // 2, half_width // (intervals // 2))
    term = term.reshape(cut).transpose(0, 2, 1, 3).reshape(-1, cut[3])
    term = sum_parts(term, "interval", intervals)
    term = jnp.broadcast_to(term[None], (intervals,) + term.shape).reshape(-1, cut[3])
    term = lax.all_to_all(term, "interval", 0, 0, tiled=True)
    term = term.reshape(cut[0], cut[2], cut[1], cut[3]).transpose(0, 2, 1, 3)
    term, grad_input = lax.optimization_barrier((term, grad_input))
    term = lax.all_gather(term.reshape(part_rows, half_width), "x", axis=0, tiled=True)
    other = swap_cores(term)
    left = jnp.where(core == 0, term, other)
    right = jnp.where(core == 0, other, term)
    whole = jnp.concatenate([left, right], axis=1)
    return grad_input.T[None], whole[:HD], whole[HD : 2 * HD], whole[2 * HD :]


def solution(mesh):
    axes = (mesh.shape["interval"], mesh.shape["seq"] // CORES, CORES, mesh.shape["head"])
    split = Mesh(mesh.devices.reshape(axes), ("interval", "x", "core", "head"))
    seq = ("x", "core")
    placed = (
        P("interval", seq, None),
        P("interval", seq, "head"),
        P("head", None),
        P("head", None),
        P("head", None),
        P(),
        P("interval", seq, None, "head"),
        P("interval", seq, None, "head"),
        P("interval", seq, None),
        P("interval", seq, None, "head"),
    )
    return jax.shard_map(
        on_device,
        mesh=split,
        in_specs=placed,
        out_specs=(P("interval", seq, "head"), P("head", None), P("head", None), P("head", None)),
        check_vma=False,
    )
```

time: 190 us -> 155 us (0.82)
  the two profiles are of different devices: /device:TPU:2 before, /device:TPU:1 now
where the time goes in v2:
time: 155 us
  blocking collectives  94.7 us (61%)
  starting transfers between devices  18.4 us (12%)
  between operations  14.3 us (9%)
  Pallas kernels  11.3 us (7%)
  local copies, waits for them, and re-layouts  8.57 us (6%)
  waiting for transfers between devices  4.86 us (3%)
  other arithmetic  2.5 us (2%)
    all_to_all x3, blocking collectives, sum_parts(): got = lax.all_to_all(value, axis, 0, 0, tiled=True)  38.5 us
    ppermute x3, starting transfers between devices, swap_cores(): return lax.ppermute(value, 'core', [(0, 1), (1, 0)])  18.4 us
    all_to_all x1, blocking collectives, on_device(): lax.all_to_all(pair_sum.reshape(chips, tokens, row), 'x', 0, 0, tiled=True)  17.4 us
    all_to_all x1, blocking collectives, on_device(): mine = lax.all_to_all(copies, 'x', 0, 0, tiled=True).reshape(half, row)  15.3 us
    all_to_all x1, blocking collectives, on_device(): term = lax.all_to_all(term, 'interval', 0, 0, tiled=True)  12.7 us
    all_gather x1, blocking collectives, on_device(): lax.all_gather(term.reshape(part_rows, half_width), 'x', axis=0, tiled=True)  10.9 us
    unnamed x33, local copies, waits for them, and re-layouts  7.76 us
    pallas_call x1, Pallas kernels, on_device(): local_call(attend_body, [((half, row), BF16), ((half, row), BF16), ((toke...  7.57 us
  transfers between devices with their start and end apart: 4, of which 3 were waited for; matrix products, arithmetic and copies ran while one was open for 2% of the time, Pallas kernels for 0%

profile of v2, /device:TPU:1, one launch (start us, length us, event | category | flops | bytes accessed | tf_op | source)
XLA Modules:
  0.0 154.7 jit_solution(6236280888183816747)
XLA Ops:
  7.2 0.0 reduce-scatter.2.cloned.1.call-start
  7.2 0.0 copy-start
  7.2 1.1 copy-done
  8.3 0.0 copy-start.3
  8.3 1.1 copy-done.3
  9.4 0.0 copy-start.5
  9.4 1.1 copy-done.5
  10.5 0.0 copy-start.7
  10.5 1.0 copy-done.7
  11.5 0.8 shard_map.129
  12.2 0.0 copy-start.15
  12.3 0.0 copy-start.1
  12.3 0.0 copy-start.2
  12.3 0.0 copy-start.12
  12.3 0.0 copy-start.13
  12.3 0.0 copy-start.14
  12.3 15.3 %all_to_all.39 = bf16[4,256,512]{2,1,0:T(8,128)(2,1)S(1)} all-to-all(bf16[4,256,512]{2,1,0:T(8,128)(2,1)S(1)} %shard_map.129), channel_id=1, replica_groups=mesh['interval'=8,'x'=4,'core'=2,'head'=8] {'x'}, dimensions={0} | all-to-all | bytes 2097152 | tf_op jit(solution)/shard_map/all_to_all | solution.py:240
  27.6 7.5 %collective-permute-start = (bf16[1024,512]{1,0:T(8,128)(2,1)S(1)}, bf16[1024,512]{1,0:T(8,128)(2,1)}, u32[]{:S(2)}, u32[]{:S(2)}) collective-permute-start(bf16[1024,512]{1,0:T(8,128)(2,1)S(1)} %bitcast.25), channel_id=1, source_target_pairs={{0,8},{8,0},{1,9},{9,1},{2,10},{10,2},{3,11},{11,3},{4,12},{12,4},... | collective-permute-start | bytes 3145736 | tf_op jit(solution)/shard_map/ppermute | solution.py:214
  35.1 0.0 copy-done.15
  35.1 0.1 copy.23.counts
  35.1 1.7 %copy.22 = bf16[1,256,192]{2,1,0:T(8,128)(2,1)} copy(bf16[1,256,192]{1,2,0:T(8,128)(2,1)} %param.11) | data formatting | bytes 196608 | tf_op args[1]
  36.8 0.1 pad_add_fusion.place
  36.9 0.6 collective-permute-done.theirs
  37.4 0.0 copy-done.1
  37.4 0.0 copy-done.2
  37.4 0.0 copy-done.12
  37.5 0.0 copy-done.13
  37.5 0.0 copy-done.14
  37.5 0.0 copy-start.9
  37.5 0.9 copy-done.9
  38.4 7.6 %shard_map.130 = (bf16[1024,512]{1,0:T(8,128)(2,1)S(1)}, bf16[1024,512]{1,0:T(8,128)(2,1)S(1)}, bf16[256,192]{1,0:T(8,128)(2,1)S(1)}, f32[256,512]{1,0:T(8,128)S(1)}) custom-call(s32[2]{0:T(128)S(1)} %pad_add_fusion.place, bf16[256,1536]{1,0:T(8,128)(2,1)S(1)} %bitcast.22, bf16[192,1536]{1,0:T(8,128)(2,1)S(1)} %copy-done.2, bf16[256,192]{1,0:T(8,128)(2,1)S(1)} %bitcast.27, ...), custom_call_target="tpu_custom_call" | custom-call | tf_op jit(solution)/shard_map/pallas_call | solution.py:243
  46.0 0.0 copy-start.10
  46.0 2.3 %collective-permute-start.1 = (bf16[1024,512]{1,0:T(8,128)(2,1)S(1)}, bf16[1024,512]{1,0:T(8,128)(2,1)S(1)}, u32[]{:S(2)}, u32[]{:S(2)}) collective-permute-start(bf16[1024,512]{1,0:T(8,128)(2,1)S(1)} %get-tuple-element.14), channel_id=1, source_target_pairs={{0,8},{8,0},{1,9},{9,1},{2,10},{10,2},{3,11},{11,3},{4,12},{12,4},... | collective-permute-start | bytes 3145736 | tf_op jit(solution)/shard_map/ppermute | solution.py:214
  48.3 2.3 %collective-permute-done.1.theirs = bf16[1024,512]{1,0:T(8,128)(2,1)S(1)} collective-permute-done((bf16[1024,512]{1,0:T(8,128)(2,1)S(1)}, bf16[1024,512]{1,0:T(8,128)(2,1)S(1)}, u32[]{:S(2)}, u32[]{:S(2)}) %collective-permute-start.1) | collective-permute-done | bytes 1048608 | tf_op jit(solution)/shard_map/ppermute | solution.py:214
  50.5 0.2 shard_map.131
  50.8 0.0 copy-start.4
  50.8 0.0 copy-start.6
  50.8 0.0 copy-start.8
  50.8 17.4 %all_to_all.40.parts = bf16[4,256,512]{2,1,0:T(8,128)(2,1)S(1)} all-to-all(bf16[4,256,512]{2,1,0:T(8,128)(2,1)S(1)} %bitcast.24), channel_id=1, replica_groups=mesh['interval'=8,'x'=4,'core'=2,'head'=8] {'x'}, dimensions={0} | all-to-all | bytes 2097152 | tf_op jit(solution)/shard_map/all_to_all | solution.py:271
  68.2 0.0 copy-done.10
  68.2 0.0 copy-done.4
  68.2 0.0 copy-done.6
  68.2 0.0 copy-done.8
  68.2 2.1 %shard_map.132 = (bf16[256,512]{1,0:T(8,128)(2,1)S(1)}, bf16[1536,256]{1,0:T(8,128)(2,1)}) custom-call(bf16[4,256,512]{2,1,0:T(8,128)(2,1)S(1)} %all_to_all.40.parts, f32[256,512]{1,0:T(8,128)S(1)} %get-tuple-element.15.donor_sum, bf16[256,192]{1,0:T(8,128)(2,1)S(1)} %get-tuple-element.12.query_grad, bf16[192,1536]{1,0:T(8,128)(2,1)S(1)} %copy-done.2, ...), custom_call_target="tpu_custom_call" | custom-call | tf_op jit(solution)/shard_map/pallas_call | solution.py:272
  70.3 0.0 reduce-scatter.2.cloned.1.call-update
  70.3 0.0 copy-start.11
  70.3 0.9 copy-done.11
  71.2 0.6 shard_map.133
  71.9 6.0 %all_to_all.41 = bf16[2,576,768]{2,1,0:T(8,128)(2,1)S(1)} all-to-all(bf16[2,576,768]{2,1,0:T(8,128)(2,1)S(1)} %shard_map.133), channel_id=1, replica_groups=mesh['interval'=8,'x'=4,'core'=2,'head'=8] {'core'}, dimensions={0} | all-to-all | bytes 3538944 | tf_op jit(solution)/shard_map/all_to_all | solution.py:284
  77.9 0.9 reduce_sum.36
  78.8 15.5 %all_to_all.42 = bf16[4,144,768]{2,1,0:T(8,128)(2,1)S(1)} all-to-all(bf16[4,144,768]{2,1,0:T(8,128)(2,1)S(1)} %bitcast.31), channel_id=1, replica_groups=mesh['interval'=8,'x'=4,'core'=2,'head'=8] {'x'}, dimensions={0} | all-to-all | bytes 1769472 | tf_op jit(solution)/shard_map/all_to_all | solution.py:284
  94.2 0.1 reduce_sum.37
  94.4 0.3 reshape.41
  94.7 17.0 %all_to_all.43 = bf16[8,72,192]{2,1,0:T(8,128)(2,1)S(1)} all-to-all(bf16[8,72,192]{2,1,0:T(8,128)(2,1)S(1)} %bitcast.33), channel_id=1, replica_groups=mesh['interval'=8,'x'=4,'core'=2,'head'=8] {'interval'}, dimensions={0} | all-to-all | bytes 442368 | tf_op jit(solution)/shard_map/all_to_all | solution.py:284
  111.7 0.1 reduce_sum.38
  111.8 12.7 %all_to_all.44 = bf16[8,72,192]{2,1,0:T(8,128)(2,1)S(1)} all-to-all(bf16[8,72,192]{2,1,0:T(8,128)(2,1)S(1)} %broadcast_in_dim.4), channel_id=1, replica_groups=mesh['interval'=8,'x'=4,'core'=2,'head'=8] {'interval'}, dimensions={0} | all-to-all | bytes 442368 | tf_op jit(solution)/shard_map/all_to_all | solution.py:294
  124.5 0.0 reduce-scatter.2.cloned.1.call-done
  124.5 0.1 copy.25
  124.6 0.3 reshape.43
  124.9 10.9 %all_gather.3 = bf16[576,768]{1,0:T(8,128)(2,1)S(1)} all-gather(bf16[144,768]{1,0:T(8,128)(2,1)S(1)} %reshape.43), channel_id=1, replica_groups=mesh['interval'=8,'x'=4,'core'=2,'head'=8] {'x'}, dimensions={0}, use_global_device_ids=true | all-gather | bytes 1105920 | tf_op jit(solution)/shard_map/all_gather | solution.py:297
  135.8 8.6 %collective-permute-start.2 = (bf16[576,768]{1,0:T(8,128)(2,1)S(1)}, bf16[576,768]{1,0:T(8,128)(2,1)S(1)}, u32[]{:S(2)}, u32[]{:S(2)}) collective-permute-start(bf16[576,768]{1,0:T(8,128)(2,1)S(1)} %all_gather.3), channel_id=1, source_target_pairs={{0,8},{8,0},{1,9},{9,1},{2,10},{10,2},{3,11},{11,3},{4,12},{12,4},... | collective-permute-start | bytes 2654216 | tf_op jit(solution)/shard_map/ppermute | solution.py:214
  144.4 2.0 %collective-permute-done.2 = bf16[576,768]{1,0:T(8,128)(2,1)S(1)} collective-permute-done((bf16[576,768]{1,0:T(8,128)(2,1)S(1)}, bf16[576,768]{1,0:T(8,128)(2,1)S(1)}, u32[]{:S(2)}, u32[]{:S(2)}) %collective-permute-start.2) | collective-permute-done | bytes 884768 | tf_op jit(solution)/shard_map/ppermute | solution.py:214
  146.5 0.1 broadcast_select_fusion
  146.6 1.2 pad_maximum_fusion
  (3 shorter events, 0.1 us)
Async XLA Ops:
  7.2 117.3 %reduce-scatter.2.cloned.1.call-start = ((), (), s32[]{:S(2)}) async-start(), calls=%async_computation.7 | async-start | bytes 884736 | tf_op jit(solution)/shard_map/reduce_scatter | solution.py:275
  7.2 1.1 copy-start
  8.3 1.1 copy-start.3
  9.4 1.1 copy-start.5
  10.5 1.0 copy-start.7
  12.2 22.8 %copy-start.15 = (s32[1,1,8]{2,1,0:T(1,128)S(1)}, s32[1,1,8]{2,1,0:T(1,128)}, u32[]{:S(2)}) copy-start(s32[1,1,8]{2,1,0:T(1,128)} %param.18) | copy-start | bytes 100
  12.3 25.2 %copy-start.1 = (bf16[1,256,1536]{2,1,0:T(8,128)(2,1)S(1)}, bf16[1,256,1536]{2,1,0:T(8,128)(2,1)}, u32[]{:S(2)}) copy-start(bf16[1,256,1536]{2,1,0:T(8,128)(2,1)} %param.10) | copy-start | bytes 2359300
  12.3 25.2 %copy-start.2 = (bf16[192,1536]{1,0:T(8,128)(2,1)S(1)}, bf16[192,1536]{1,0:T(8,128)(2,1)}, u32[]{:S(2)}) copy-start(bf16[192,1536]{1,0:T(8,128)(2,1)} %w_query.3) | copy-start | bytes 1769476
  12.3 25.2 %copy-start.12 = (s32[1,1,8,8]{3,2,1,0:T(8,128)S(1)}, s32[1,1,8,8]{3,2,1,0:T(8,128)}, u32[]{:S(2)}) copy-start(s32[1,1,8,8]{3,2,1,0:T(8,128)} %param.16) | copy-start | bytes 772
  12.3 25.2 %copy-start.13 = (s32[1,1,8,8]{3,2,1,0:T(8,128)S(1)}, s32[1,1,8,8]{3,2,1,0:T(8,128)}, u32[]{:S(2)}) copy-start(s32[1,1,8,8]{3,2,1,0:T(8,128)} %param.17) | copy-start | bytes 772
  12.3 25.2 %copy-start.14 = (f32[1,1,8,8]{3,2,1,0:T(8,128)S(1)}, f32[1,1,8,8]{3,2,1,0:T(8,128)}, u32[]{:S(2)}) copy-start(f32[1,1,8,8]{3,2,1,0:T(8,128)} %param.19) | copy-start | bytes 772
  27.6 9.9 %collective-permute-start = (bf16[1024,512]{1,0:T(8,128)(2,1)S(1)}, bf16[1024,512]{1,0:T(8,128)(2,1)}, u32[]{:S(2)}, u32[]{:S(2)}) collective-permute-start(bf16[1024,512]{1,0:T(8,128)(2,1)S(1)} %bitcast.25), channel_id=1, source_target_pairs={{0,8},{8,0},{1,9},{9,1},{2,10},{10,2},{3,11},{11,3},{4,12},{12,4},... | collective-permute-start | bytes 3145736 | tf_op jit(solution)/shard_map/ppermute | solution.py:214
  37.5 0.9 copy-start.9
  46.0 22.3 %copy-start.10 = (bf16[256,192]{1,0:T(8,128)(2,1)}, bf16[256,192]{1,0:T(8,128)(2,1)S(1)}, u32[]{:S(2)}) copy-start(bf16[256,192]{1,0:T(8,128)(2,1)S(1)} %get-tuple-element.12.query_grad) | copy-start | bytes 294916
  46.0 4.6 %collective-permute-start.1 = (bf16[1024,512]{1,0:T(8,128)(2,1)S(1)}, bf16[1024,512]{1,0:T(8,128)(2,1)S(1)}, u32[]{:S(2)}, u32[]{:S(2)}) collective-permute-start(bf16[1024,512]{1,0:T(8,128)(2,1)S(1)} %get-tuple-element.14), channel_id=1, source_target_pairs={{0,8},{8,0},{1,9},{9,1},{2,10},{10,2},{3,11},{11,3},{4,12},{12,4},... | collective-permute-start | bytes 3145736 | tf_op jit(solution)/shard_map/ppermute | solution.py:214
  50.8 17.4 %copy-start.4 = (bf16[192,1536]{1,0:T(8,128)(2,1)S(1)}, bf16[192,1536]{1,0:T(8,128)(2,1)}, u32[]{:S(2)}) copy-start(bf16[192,1536]{1,0:T(8,128)(2,1)} %w_key.3) | copy-start | bytes 1769476
  50.8 17.4 %copy-start.6 = (bf16[192,1536]{1,0:T(8,128)(2,1)S(1)}, bf16[192,1536]{1,0:T(8,128)(2,1)}, u32[]{:S(2)}) copy-start(bf16[192,1536]{1,0:T(8,128)(2,1)} %w_value.3) | copy-start | bytes 1769476
  50.8 17.4 %copy-start.8 = (bf16[1536,128]{1,0:T(8,128)(2,1)S(1)}, bf16[1536,128]{1,0:T(8,128)(2,1)}, u32[]{:S(2)}) copy-start(bf16[1536,128]{1,0:T(8,128)(2,1)} %w_junction.3) | copy-start | bytes 1179652
  70.3 0.9 copy-start.11
  135.8 10.7 %collective-permute-start.2 = (bf16[576,768]{1,0:T(8,128)(2,1)S(1)}, bf16[576,768]{1,0:T(8,128)(2,1)S(1)}, u32[]{:S(2)}, u32[]{:S(2)}) collective-permute-start(bf16[576,768]{1,0:T(8,128)(2,1)S(1)} %all_gather.3), channel_id=1, source_target_pairs={{0,8},{8,0},{1,9},{9,1},{2,10},{10,2},{3,11},{11,3},{4,12},{12,4},... | collective-permute-start | bytes 2654216 | tf_op jit(solution)/shard_map/ppermute | solution.py:214
Sparse Core Ops, SparseCore 0:
  70.4 40.3 reduce-scatter.1

commit v3 on v1

v3 whole, which is shorter than its diff:
```python
import jax
import jax.numpy as jnp
from jax import lax
from jax.experimental import pallas as pl
from jax.experimental.pallas import tpu as pltpu
from jax.sharding import Mesh
from jax.sharding import PartitionSpec as P

HD = 192
PJ = 128
CORES = 2
LANES = 256
KV = 2 * HD
SHIFT = KV - LANES
F32 = jnp.float32
BF16 = jnp.bfloat16
VMEM_BYTES = 48 * 1024 * 1024


def contract(a, b, dim_a, dim_b, precision=None):
    return lax.dot_general(
        a, b, (((dim_a,), (dim_b,)), ((), ())), precision=precision, preferred_element_type=F32
    )


def iota(shape, axis):
    return lax.broadcasted_iota(jnp.int32, shape, axis)


def local_call(body, outs, operands, scratch=(), fetched=0):
    specs = [pl.BlockSpec(memory_space=pltpu.HBM)] * fetched
    specs += [pl.BlockSpec(memory_space=pltpu.VMEM)] * (operands - fetched)
    return pl.pallas_call(
        body,
        out_shape=tuple(jax.ShapeDtypeStruct(shape, kind) for shape, kind in outs),
        in_specs=specs,
        out_specs=tuple(pl.BlockSpec(memory_space=pltpu.VMEM) for _ in outs),
        scratch_shapes=list(scratch),
        compiler_params=pltpu.CompilerParams(vmem_limit_bytes=VMEM_BYTES),
    )


def split_terms(term, count=2):
    pieces = []
    for _ in range(count):
        piece = term.astype(BF16)
        pieces.append(piece)
        term = term - piece.astype(F32)
    return pieces


def project_body(
    hidden_hbm,
    w_key_hbm,
    w_value_hbm,
    w_junction_hbm,
    donor_hbm,
    acceptor_hbm,
    counts_hbm,
    pred_hbm,
    message,
    features,
    donor_hot,
    hidden,
    weights,
    w_junction,
    donor_pos,
    acceptor_pos,
    counts,
    pred_grad,
    sems,
):
    targets = (
        hidden,
        weights.at[pl.ds(0, HD)],
        weights.at[pl.ds(HD, HD)],
        w_junction,
        donor_pos,
        acceptor_pos,
        counts,
        pred_grad,
    )
    sources = (
        hidden_hbm,
        w_key_hbm,
        w_value_hbm,
        w_junction_hbm,
        donor_hbm,
        acceptor_hbm,
        counts_hbm,
        pred_hbm,
    )
    copies = [
        pltpu.make_async_copy(source, target, sems.at[i])
        for i, (source, target) in enumerate(zip(sources, targets))
    ]
    for copy in copies:
        copy.start()
    for copy in copies:
        copy.wait()
    chips = message.shape[0]
    tokens = hidden.shape[0]
    x = hidden[...]
    feats = contract(x, w_junction[...], 1, 0).astype(BF16)
    features[...] = feats
    rows = contract(x, weights[...], 1, 1).astype(BF16)

    buckets, per = donor_pos.shape
    slots = buckets * per
    square = iota((buckets, buckets), 0) == iota((buckets, buckets), 1)
    limit = jnp.sum(
        jnp.where(square, counts[...].astype(F32), 0.0), axis=1, keepdims=True
    )
    slot_ids = lax.axis_index("head") * per + iota((buckets, per), 1)
    live_grad = jnp.where(slot_ids.astype(F32) < limit, pred_grad[...], 0.0)
    pick_bucket = (iota((slots, buckets), 0) // per == iota((slots, buckets), 1)).astype(F32)
    own_slot = iota((slots, per), 0) % per == iota((slots, per), 1)

    def to_column(value):
        wide = contract(pick_bucket, value.astype(F32), 1, 0, lax.Precision.HIGHEST)
        return jnp.sum(jnp.where(own_slot, wide, 0.0), axis=1, keepdims=True)

    donor = to_column(donor_pos[...])
    hot = jnp.where(iota((slots, tokens), 1).astype(F32) == donor, 1.0, 0.0).astype(BF16)
    donor_hot[...] = hot
    lane = iota((slots, PJ), 1)
    scalars = [to_column(acceptor_pos[...])]
    scalars += [piece.astype(F32) for piece in split_terms(to_column(live_grad), 3)]
    extra = jnp.zeros((slots, PJ), F32)
    for i, column in enumerate(scalars):
        extra = jnp.where(lane == i, column, extra)
    slot_rows = jnp.concatenate(
        [
            contract(hot, feats, 1, 0).astype(BF16),
            extra.astype(BF16),
            jnp.zeros((slots, KV - 2 * PJ), BF16),
        ],
        axis=1,
    )
    part = slots // chips
    for chip in range(chips):
        message[chip, :tokens, :] = rows
        message[chip, tokens:, :] = slot_rows[chip * part : (chip + 1) * part, :]


def query_body(hidden, w_query, ctx_t, queries, ctx):
    tokens = hidden.shape[0]
    pad = jnp.zeros((tokens, LANES - HD), BF16)
    value = contract(hidden[...], w_query[...], 1, 1).astype(BF16)
    queries[...] = jnp.concatenate([value, pad], axis=1)
    ctx[...] = jnp.concatenate([pad, jnp.transpose(ctx_t[...].astype(F32)).astype(BF16)], axis=1)


def attend_body(
    queries,
    ctx,
    features,
    mine,
    theirs,
    terms_mine,
    terms_theirs,
    query_grad,
    accept_sum,
    probs_b,
    dscores_b,
):
    tokens = queries.shape[0]
    chips, height, _ = mine.shape
    half = chips * tokens
    scale = HD ** (-0.5)
    sides = [ref[:, :tokens, :].reshape(half, KV) for ref in (mine, theirs)]
    rows = 64
    for start in range(0, tokens, rows):
        band = pl.ds(start, rows)
        q, g = queries[band, :], ctx[band, :]
        scores = [contract(q, side[:, :LANES], 1, 1) * scale for side in sides]
        row_max = jnp.maximum(
            jnp.max(scores[0], axis=-1, keepdims=True), jnp.max(scores[1], axis=-1, keepdims=True)
        )
        expd = [jnp.exp(score - row_max) for score in scores]
        inverse = 1.0 / (
            jnp.sum(expd[0], axis=-1, keepdims=True) + jnp.sum(expd[1], axis=-1, keepdims=True)
        )
        probs = [value * inverse for value in expd]
        dprobs = [contract(g, side[:, SHIFT:], 1, 1) for side in sides]
        row_delta = jnp.sum(probs[0] * dprobs[0], axis=-1, keepdims=True) + jnp.sum(
            probs[1] * dprobs[1], axis=-1, keepdims=True
        )
        for i in range(2):
            probs_b[i, band, :] = probs[i].astype(BF16)
            dscores_b[i, band, :] = (probs[i] * (dprobs[i] - row_delta)).astype(BF16)

    core = lax.axis_index("core")
    part = height - tokens
    per = part // CORES

    def own_rows(ref):
        block = ref[:, tokens:, :].astype(F32)
        return jnp.where(core == 0, block[:, :per, :], block[:, per:, :]).reshape(chips * per, KV)

    slot_rows = jnp.concatenate([own_rows(mine), own_rows(theirs)], axis=0)
    slots = slot_rows.shape[0]
    donor_feat = slot_rows[:, :PJ]
    extra = slot_rows[:, PJ : 2 * PJ]
    acceptor = extra[:, 0:1]
    slot_scale = extra[:, 1:2] + extra[:, 2:3] + extra[:, 3:4]
    hot = jnp.where(iota((slots, tokens), 1).astype(F32) == acceptor, 1.0, 0.0).astype(BF16)
    accept_feat = contract(hot, features[...], 1, 0)
    pair_scale = PJ ** (-0.5)
    pair_score = jnp.sum(donor_feat * accept_feat, axis=-1, keepdims=True) * pair_scale
    slot_grad = slot_scale * jax.nn.sigmoid(pair_score) * pair_scale
    total = jnp.zeros((tokens, PJ), F32)
    for piece in split_terms(slot_grad * donor_feat):
        total = total + contract(hot, piece, 0, 0)
    accept_sum[...] = total
    back = (slot_grad * accept_feat).reshape(2, chips, per, PJ)
    blank = jnp.zeros((chips, per, PJ), F32)

    for i, terms in ((1, terms_theirs), (0, terms_mine)):
        key_term = contract(dscores_b[i], queries[...], 0, 0) * scale
        value_term = contract(probs_b[i], ctx[...], 0, 0)
        middle = key_term[:, SHIFT:] + value_term[:, :SHIFT]
        for first, value in (
            (0, key_term[:, :SHIFT]),
            (SHIFT, middle),
            (LANES, value_term[:, SHIFT:]),
        ):
            terms[:, :tokens, first : first + SHIFT] = value.astype(BF16).reshape(
                chips, tokens, SHIFT
            )
        upper = jnp.where(core == 0, back[i], blank)
        lower = jnp.where(core == 0, blank, back[i])
        terms[:, tokens:, :PJ] = jnp.concatenate([upper, lower], axis=1).astype(BF16)
        terms[:, tokens:, PJ:] = jnp.zeros((chips, part, KV - PJ), BF16)
    query_grad[...] = (
        (
            contract(dscores_b[0], sides[0][:, :LANES], 1, 0)
            + contract(dscores_b[1], sides[1][:, :LANES], 1, 0)
        )[:, :HD]
        * scale
    ).astype(BF16)


def pair_body(mine, theirs, total):
    total[...] = (mine[...].astype(F32) + theirs[...].astype(F32)).astype(BF16)


def grads_body(
    parts,
    accept_sum,
    donor_hot,
    query_grad,
    hidden,
    w_query,
    w_key,
    w_value,
    w_junction,
    weight_term,
    input_term,
):
    tokens, width = hidden.shape
    chips = parts.shape[0]
    total = jnp.zeros((tokens, KV), F32)
    for chip in range(chips):
        total = total + parts[chip, :tokens, :].astype(F32)
    grads = total.astype(BF16)
    part = parts.shape[1] - tokens
    slot_rows = parts[:, tokens:, :PJ].reshape(chips * part, PJ)
    feature_grad = (accept_sum[...] + contract(donor_hot[...], slot_rows, 0, 0)).astype(BF16)
    value = contract(w_query[...], query_grad[...], 0, 1)
    value = value + contract(w_key[...], grads[:, :HD], 0, 1)
    value = value + contract(w_value[...], grads[:, HD:], 0, 1)
    value = value + contract(w_junction[...], feature_grad, 1, 1)
    input_term[...] = value.astype(BF16).reshape(input_term.shape)
    cut = width // CORES
    first = 0
    for grad in (query_grad[...], grads):
        value = contract(grad, hidden[...], 0, 0).astype(BF16)
        for core in range(CORES):
            weight_term[core, first : first + value.shape[0], :] = value[
                :, core * cut : (core + 1) * cut
            ]
        first += value.shape[0]


def tiles_of(rows, columns, count):
    high, wide = rows * 2 // count, columns // 2
    return [(i, pl.ds(i // 2 * high, high), pl.ds(i % 2 * wide, wide)) for i in range(count)]


def sum_body(parts, total):
    value = parts[0].astype(F32)
    for i in range(1, parts.shape[0]):
        value = value + parts[i].astype(F32)
    total[...] = value.astype(total.dtype)


def cut_body(parts, tiles, whole):
    value = parts[0].astype(F32)
    for i in range(1, parts.shape[0]):
        value = value + parts[i].astype(F32)
    whole[...] = value
    for i, rows, columns in tiles_of(*whole.shape, tiles.shape[0]):
        tiles[i] = whole[rows, columns].astype(BF16)


def spread_body(parts, copies):
    value = parts[0].astype(F32)
    for i in range(1, parts.shape[0]):
        value = value + parts[i].astype(F32)
    value = value.astype(BF16)
    for i in range(copies.shape[0]):
        copies[i] = value


def join_body(tiles, joined, whole):
    for i, rows, columns in tiles_of(*whole.shape, tiles.shape[0]):
        whole[rows, columns] = tiles[i].astype(F32)
    joined[...] = whole[...].astype(BF16)


def place_body(mine, theirs, *outs):
    core = lax.axis_index("core")
    cut = mine.shape[1]
    for i, out in enumerate(outs):
        a, b = mine[i * HD : (i + 1) * HD, :], theirs[i * HD : (i + 1) * HD, :]
        out[:, :cut] = jnp.where(core == 0, a, b)
        out[:, cut:] = jnp.where(core == 0, b, a)


def swap_cores(value):
    return lax.ppermute(value, "core", [(0, 1), (1, 0)])


def exchange(value, axis):
    return lax.all_to_all(value, axis, 0, 0, tiled=True)


def on_device(
    hidden_in,
    ctx_grad,
    w_query,
    w_key,
    w_value,
    w_junction,
    donor_pos,
    acceptor_pos,
    junction_counts,
    pred_grad,
):
    hidden = hidden_in[0]
    tokens, width = hidden.shape
    chips = lax.axis_size("x")
    intervals = lax.axis_size("interval")
    heads = lax.axis_size("head")
    half = chips * tokens
    buckets, per = donor_pos.shape[2:]
    slots = buckets * per
    height = tokens + slots // chips

    message, features, donor_hot = local_call(
        project_body,
        [((chips, height, KV), BF16), ((tokens, PJ), BF16), ((slots, tokens), BF16)],
        operands=8,
        fetched=8,
        scratch=[
            pltpu.VMEM((tokens, width), BF16),
            pltpu.VMEM((KV, width), BF16),
            pltpu.VMEM((width, PJ), BF16),
            pltpu.VMEM((buckets, per), jnp.int32),
            pltpu.VMEM((buckets, per), jnp.int32),
            pltpu.VMEM((1, buckets), jnp.int32),
            pltpu.VMEM((buckets, per), F32),
            pltpu.SemaphoreType.DMA((8,)),
        ],
    )(
        hidden,
        w_key,
        w_value,
        w_junction,
        donor_pos[0, 0],
        acceptor_pos[0, 0],
        junction_counts[0],
        pred_grad[0, 0],
    )
    mine = exchange(message, "x")
    theirs = swap_cores(mine)
    queries, ctx = local_call(query_body, [((tokens, LANES), BF16)] * 2, operands=3)(
        hidden, w_query, ctx_grad[0].T
    )
    terms_mine, terms_theirs, query_grad, accept_sum = local_call(
        attend_body,
        [
            ((chips, height, KV), BF16),
            ((chips, height, KV), BF16),
            ((tokens, HD), BF16),
            ((tokens, PJ), F32),
        ],
        operands=5,
        scratch=[pltpu.VMEM((CORES, tokens, half), BF16)] * 2,
    )(queries, ctx, features, mine, theirs)
    (pair_sum,) = local_call(pair_body, [((chips, height, KV), BF16)], operands=2)(
        terms_mine, swap_cores(terms_theirs)
    )
    parts = exchange(pair_sum, "x")
    rows = 3 * HD
    cut = width // CORES
    weight_term, input_term = local_call(
        grads_body,
        [((CORES, rows, cut), BF16), ((heads, width // heads, tokens), BF16)],
        operands=9,
    )(
        parts,
        accept_sum,
        donor_hot,
        query_grad,
        hidden,
        w_query,
        w_key,
        w_value,
        w_junction,
    )
    input_parts = exchange(input_term, "head")

    (term,) = local_call(sum_body, [((rows, cut), BF16)], operands=1)(
        exchange(weight_term, "core")
    )
    part = rows // chips
    tile = (part * 2 // intervals, cut // 2)
    (tiles,) = local_call(
        cut_body, [((intervals,) + tile, BF16)], operands=1, scratch=[pltpu.VMEM((part, cut), F32)]
    )(exchange(term.reshape(chips, part, cut), "x"))
    (copies,) = local_call(spread_body, [((intervals,) + tile, BF16)], operands=1)(
        exchange(tiles, "interval")
    )
    (term,) = local_call(
        join_body, [((part, cut), BF16)], operands=1, scratch=[pltpu.VMEM((part, cut), F32)]
    )(exchange(copies, "interval"))
    term, input_parts = lax.optimization_barrier((term, input_parts))
    term = lax.all_gather(term, "x", axis=0, tiled=True)
    (grad_input,) = local_call(sum_body, [((width // heads, tokens), BF16)], operands=1)(
        input_parts
    )
    grads = local_call(place_body, [((HD, width), BF16)] * 3, operands=2)(term, swap_cores(term))
    return (grad_input.T[None],) + tuple(grads)


def solution(mesh):
    axes = (mesh.shape["interval"], mesh.shape["seq"] // CORES, CORES, mesh.shape["head"])
    split = Mesh(mesh.devices.reshape(axes), ("interval", "x", "core", "head"))
    seq = ("x", "core")
    placed = (
        P("interval", seq, None),
        P("interval", seq, "head"),
        P("head", None),
        P("head", None),
        P("head", None),
        P(),
        P("interval", seq, None, "head"),
        P("interval", seq, None, "head"),
        P("interval", seq, None),
        P("interval", seq, None, "head"),
    )
    return jax.shard_map(
        on_device,
        mesh=split,
        in_specs=placed,
        out_specs=(P("interval", seq, "head"), P("head", None), P("head", None), P("head", None)),
        check_vma=False,
    )
```

time: 190 us -> 164 us (0.86)
  the two profiles are of different devices: /device:TPU:2 before, /device:TPU:1 now
where the time goes in v3:
time: 164 us; the launch traced here: 163 us
  blocking collectives  89.8 us (55%)
  starting transfers between devices  29 us (18%)
  waiting for transfers between devices  24.7 us (15%)
  Pallas kernels  11.7 us (7%)
  local copies, waits for them, and re-layouts  6.99 us (4%)
    all_to_all x6, blocking collectives, exchange(): return lax.all_to_all(value, axis, 0, 0, tiled=True)  78.5 us
    all_to_all x1, waiting for transfers between devices, exchange(): return lax.all_to_all(value, axis, 0, 0, tiled=True)  19.9 us
    ppermute x3, starting transfers between devices, swap_cores(): return lax.ppermute(value, 'core', [(0, 1), (1, 0)])  19 us
    all_gather x1, blocking collectives, on_device(): term = lax.all_gather(term, 'x', axis=0, tiled=True)  11.2 us
    all_to_all x1, starting transfers between devices, exchange(): return lax.all_to_all(value, axis, 0, 0, tiled=True)  10 us
    unnamed x28, local copies, waits for them, and re-layouts  6.99 us
    ppermute x3, waiting for transfers between devices, swap_cores(): return lax.ppermute(value, 'core', [(0, 1), (1, 0)])  4.8 us
    pallas_call x1, Pallas kernels, on_device(): local_call(attend_body, [((chips, height, KV), BF16), ((chips, height, KV...  3.99 us
  transfers between devices with their start and end apart: 4, of which 4 were waited for; matrix products, arithmetic and copies ran while one was open for 0% of the time, Pallas kernels for 1%

profile of v3, /device:TPU:1, one launch (start us, length us, event | category | flops | bytes accessed | tf_op | source)
XLA Modules:
  0.0 162.9 jit_solution(13179031859749910782)
XLA Ops:
  0.6 0.0 copy-start
  0.6 1.1 copy-done
  1.8 0.0 copy-start.3
  1.8 1.1 copy-done.3
  2.8 0.0 copy-start.5
  2.8 1.1 copy-done.5
  3.9 0.0 copy-start.7
  3.9 1.0 copy-done.7
  4.9 0.0 copy-start.10
  4.9 0.7 copy-done.10
  5.6 0.0 copy-start.11
  5.6 0.7 copy-done.11
  6.3 0.0 copy-start.12
  6.3 0.7 copy-done.12
  7.0 0.0 copy-start.13
  7.0 0.7 copy-done.13
  7.6 0.0 copy-start.2
  7.6 0.0 copy-start.9
  7.6 1.6 shard_map.130
  9.2 13.2 %all_to_all.35.mine = bf16[4,272,384]{2,1,0:T(8,128)(2,1)S(1)} all-to-all(bf16[4,272,384]{2,1,0:T(8,128)(2,1)S(1)} %get-tuple-element.23), channel_id=1, replica_groups=mesh['interval'=8,'x'=4,'core'=2,'head'=8] {'x'}, dimensions={0} | all-to-all | bytes 1671168 | tf_op jit(solution)/shard_map/all_to_all | solution.py:336
  22.4 7.7 %collective-permute-start = (bf16[4,272,384]{2,1,0:T(8,128)(2,1)S(1)}, bf16[4,272,384]{2,1,0:T(8,128)(2,1)S(1)}, u32[]{:S(2)}, u32[]{:S(2)}) collective-permute-start(bf16[4,272,384]{2,1,0:T(8,128)(2,1)S(1)} %all_to_all.35.mine), channel_id=1, source_target_pairs={{0,8},{8,0},{1,9},{9,1},{2,10},{10,2},{3,11},{11,3},{4,12},{12,4},... | collective-permute-start | bytes 2506760 | tf_op jit(solution)/shard_map/ppermute | solution.py:332
  30.1 0.0 copy-done.2
  30.1 0.0 copy-done.9
  30.1 0.4 shard_map.129
  30.5 1.6 collective-permute-done.theirs
  32.1 4.0 %shard_map.131 = (bf16[4,272,384]{2,1,0:T(8,128)(2,1)S(1)}, bf16[4,272,384]{2,1,0:T(8,128)(2,1)S(1)}, bf16[256,192]{1,0:T(8,128)(2,1)S(1)}, f32[256,128]{1,0:T(8,128)S(1)}) custom-call(bf16[256,256]{1,0:T(8,128)(2,1)S(1)} %get-tuple-element.20.queries, bf16[256,256]{1,0:T(8,128)(2,1)S(1)} %get-tuple-element.21.ctx, ...), custom_call_target="tpu_custom_call" | custom-call | tf_op jit(solution)/shard_map/pallas_call | solution.py:391
  36.1 2.3 %collective-permute-start.1 = (bf16[4,272,384]{2,1,0:T(8,128)(2,1)S(1)}, bf16[4,272,384]{2,1,0:T(8,128)(2,1)S(1)}, u32[]{:S(2)}, u32[]{:S(2)}) collective-permute-start(bf16[4,272,384]{2,1,0:T(8,128)(2,1)S(1)} %get-tuple-element.25), channel_id=1, source_target_pairs={{0,8},{8,0},{1,9},{9,1},{2,10},{10,2},{3,11},{11,3},{4,12},{12,4},... | collective-permute-start | bytes 2506760 | tf_op jit(solution)/shard_map/ppermute | solution.py:332
  38.4 2.0 %collective-permute-done.1.theirs = bf16[4,272,384]{2,1,0:T(8,128)(2,1)S(1)} collective-permute-done((bf16[4,272,384]{2,1,0:T(8,128)(2,1)S(1)}, bf16[4,272,384]{2,1,0:T(8,128)(2,1)S(1)}, u32[]{:S(2)}, u32[]{:S(2)}) %collective-permute-start.1) | collective-permute-done | bytes 835616 | tf_op jit(solution)/shard_map/ppermute | solution.py:332
  40.3 0.0 copy-start.1
  40.3 0.0 copy-start.4
  40.3 0.0 copy-start.6
  40.3 0.0 copy-start.8
  40.3 0.2 shard_map.132
  40.6 14.8 %all_to_all.36.parts = bf16[4,272,384]{2,1,0:T(8,128)(2,1)S(1)} all-to-all(bf16[4,272,384]{2,1,0:T(8,128)(2,1)S(1)} %shard_map.132), channel_id=1, replica_groups=mesh['interval'=8,'x'=4,'core'=2,'head'=8] {'x'}, dimensions={0} | all-to-all | bytes 1671168 | tf_op jit(solution)/shard_map/all_to_all | solution.py:336
  55.4 0.0 copy-done.1
  55.4 0.0 copy-done.4
  55.4 0.0 copy-done.6
  55.4 0.0 copy-done.8
  55.4 3.0 %shard_map.133 = (bf16[2,576,768]{2,1,0:T(8,128)(2,1)}, bf16[8,192,256]{2,1,0:T(8,128)(2,1)}) custom-call(bf16[4,272,384]{2,1,0:T(8,128)(2,1)S(1)} %all_to_all.36.parts, f32[256,128]{1,0:T(8,128)S(1)} %get-tuple-element.26.accept_sum, bf16[64,256]{1,0:T(8,128)(2,1)S(1)} %get-tuple-element.27.donor_hot, bf16[256,192]{1,0:T(8,128)(2,1)S(1)} %get-tuple-element.28.query_grad, ...), custom_call_target="tpu_custom_call" | custom-call | tf_op jit(solution)/shard_map/pallas_call | solution.py:408
  58.4 7.4 %all_to_all.37.parts = bf16[2,576,768]{2,1,0:T(8,128)(2,1)S(1)} all-to-all(bf16[2,576,768]{2,1,0:T(8,128)(2,1)} %get-tuple-element.29), channel_id=1, replica_groups=mesh['interval'=8,'x'=4,'core'=2,'head'=8] {'core'}, dimensions={0} | all-to-all | bytes 3538944 | tf_op jit(solution)/shard_map/all_to_all | solution.py:336
  65.8 0.2 shard_map.134
  66.0 15.5 %all_to_all.38.parts = bf16[4,144,768]{2,1,0:T(8,128)(2,1)S(1)} all-to-all(bf16[4,144,768]{2,1,0:T(8,128)(2,1)S(1)} %bitcast.15), channel_id=1, replica_groups=mesh['interval'=8,'x'=4,'core'=2,'head'=8] {'x'}, dimensions={0} | all-to-all | bytes 1769472 | tf_op jit(solution)/shard_map/all_to_all | solution.py:336
  81.5 0.2 shard_map.135
  81.7 15.6 %all_to_all.39.parts = bf16[8,36,384]{2,1,0:T(8,128)(2,1)S(1)} all-to-all(bf16[8,36,384]{2,1,0:T(8,128)(2,1)S(1)} %shard_map.135), channel_id=1, replica_groups=mesh['interval'=8,'x'=4,'core'=2,'head'=8] {'interval'}, dimensions={0} | all-to-all | bytes 442368 | tf_op jit(solution)/shard_map/all_to_all | solution.py:336
  97.3 12.0 %all_to_all.40.tiles = bf16[8,36,384]{2,1,0:T(8,128)(2,1)S(1)} all-to-all(bf16[8,36,384]{2,1,0:T(8,128)(2,1)S(1)} %shard_map.136), channel_id=1, replica_groups=mesh['interval'=8,'x'=4,'core'=2,'head'=8] {'interval'}, dimensions={0} | all-to-all | bytes 442368 | tf_op jit(solution)/shard_map/all_to_all | solution.py:336
  109.3 10.0 %all-to-all-start.6 = ((bf16[8,192,256]{2,1,0:T(8,128)(2,1)}), bf16[8,192,256]{2,1,0:T(8,128)(2,1)S(1)}, u32[]{:S(2)}, u32[]{:S(2)}) async-start(bf16[8,192,256]{2,1,0:T(8,128)(2,1)} %get-tuple-element.30), calls=%async_computation.6 | async-start | bytes 1572864 | tf_op jit(solution)/shard_map/all_to_all | solution.py:336
  119.4 19.9 %all-to-all-done.6.parts = bf16[8,192,256]{2,1,0:T(8,128)(2,1)S(1)} async-done(((bf16[8,192,256]{2,1,0:T(8,128)(2,1)}), bf16[8,192,256]{2,1,0:T(8,128)(2,1)S(1)}, u32[]{:S(2)}, u32[]{:S(2)}) %all-to-all-start.6) | async-done | bytes 786464 | tf_op jit(solution)/shard_map/all_to_all | solution.py:336
  139.3 11.2 %all_gather.3.mine = bf16[576,768]{1,0:T(8,128)(2,1)S(1)} all-gather(bf16[144,768]{1,0:T(8,128)(2,1)S(1)} %shard_map.137), channel_id=1, replica_groups=mesh['interval'=8,'x'=4,'core'=2,'head'=8] {'x'}, dimensions={0}, use_global_device_ids=true | all-gather | bytes 1105920 | tf_op jit(solution)/shard_map/all_gather | solution.py:440
  150.5 9.0 %collective-permute-start.2 = (bf16[576,768]{1,0:T(8,128)(2,1)S(1)}, bf16[576,768]{1,0:T(8,128)(2,1)S(1)}, u32[]{:S(2)}, u32[]{:S(2)}) collective-permute-start(bf16[576,768]{1,0:T(8,128)(2,1)S(1)} %all_gather.3.mine), channel_id=1, source_target_pairs={{0,8},{8,0},{1,9},{9,1},{2,10},{10,2},{3,11},{11,3},{4,12},{12,4},... | collective-permute-start | bytes 2654216 | tf_op jit(solution)/shard_map/ppermute | solution.py:332
  159.6 0.7 shard_map.138
  160.3 1.3 collective-permute-done.2.theirs
  161.6 1.3 shard_map.139
  (2 shorter events, 0.1 us)
Async XLA Ops:
  0.6 1.1 copy-start
  1.8 1.1 copy-start.3
  2.8 1.1 copy-start.5
  3.9 1.0 copy-start.7
  4.9 0.7 copy-start.10
  5.6 0.7 copy-start.11
  6.3 0.7 copy-start.12
  7.0 0.7 copy-start.13
  7.6 22.5 %copy-start.2 = (bf16[192,1536]{1,0:T(8,128)(2,1)S(1)}, bf16[192,1536]{1,0:T(8,128)(2,1)}, u32[]{:S(2)}) copy-start(bf16[192,1536]{1,0:T(8,128)(2,1)} %w_query.3) | copy-start | bytes 1769476
  7.6 22.5 %copy-start.9 = (bf16[1,256,192]{1,2,0:T(8,128)(2,1)S(1)}, bf16[1,256,192]{1,2,0:T(8,128)(2,1)}, u32[]{:S(2)}) copy-start(bf16[1,256,192]{1,2,0:T(8,128)(2,1)} %param.11) | copy-start | bytes 294916
  22.4 9.6 %collective-permute-start = (bf16[4,272,384]{2,1,0:T(8,128)(2,1)S(1)}, bf16[4,272,384]{2,1,0:T(8,128)(2,1)S(1)}, u32[]{:S(2)}, u32[]{:S(2)}) collective-permute-start(bf16[4,272,384]{2,1,0:T(8,128)(2,1)S(1)} %all_to_all.35.mine), channel_id=1, source_target_pairs={{0,8},{8,0},{1,9},{9,1},{2,10},{10,2},{3,11},{11,3},{4,12},{12,4},... | collective-permute-start | bytes 2506760 | tf_op jit(solution)/shard_map/ppermute | solution.py:332
  36.1 4.2 %collective-permute-start.1 = (bf16[4,272,384]{2,1,0:T(8,128)(2,1)S(1)}, bf16[4,272,384]{2,1,0:T(8,128)(2,1)S(1)}, u32[]{:S(2)}, u32[]{:S(2)}) collective-permute-start(bf16[4,272,384]{2,1,0:T(8,128)(2,1)S(1)} %get-tuple-element.25), channel_id=1, source_target_pairs={{0,8},{8,0},{1,9},{9,1},{2,10},{10,2},{3,11},{11,3},{4,12},{12,4},... | collective-permute-start | bytes 2506760 | tf_op jit(solution)/shard_map/ppermute | solution.py:332
  40.3 15.0 %copy-start.1 = (bf16[1,256,1536]{2,1,0:T(8,128)(2,1)S(1)}, bf16[1,256,1536]{2,1,0:T(8,128)(2,1)}, u32[]{:S(2)}) copy-start(bf16[1,256,1536]{2,1,0:T(8,128)(2,1)} %param.10) | copy-start | bytes 2359300
  40.3 15.0 %copy-start.4 = (bf16[192,1536]{1,0:T(8,128)(2,1)S(1)}, bf16[192,1536]{1,0:T(8,128)(2,1)}, u32[]{:S(2)}) copy-start(bf16[192,1536]{1,0:T(8,128)(2,1)} %w_key.1) | copy-start | bytes 1769476
  40.3 15.0 %copy-start.6 = (bf16[192,1536]{1,0:T(8,128)(2,1)S(1)}, bf16[192,1536]{1,0:T(8,128)(2,1)}, u32[]{:S(2)}) copy-start(bf16[192,1536]{1,0:T(8,128)(2,1)} %w_value.1) | copy-start | bytes 1769476
  40.3 15.0 %copy-start.8 = (bf16[1536,128]{1,0:T(8,128)(2,1)S(1)}, bf16[1536,128]{1,0:T(8,128)(2,1)}, u32[]{:S(2)}) copy-start(bf16[1536,128]{1,0:T(8,128)(2,1)} %w_junction.1) | copy-start | bytes 1179652
  109.3 30.0 %all-to-all-start.6 = ((bf16[8,192,256]{2,1,0:T(8,128)(2,1)}), bf16[8,192,256]{2,1,0:T(8,128)(2,1)S(1)}, u32[]{:S(2)}, u32[]{:S(2)}) async-start(bf16[8,192,256]{2,1,0:T(8,128)(2,1)} %get-tuple-element.30), calls=%async_computation.6 | async-start | bytes 1572864 | tf_op jit(solution)/shard_map/all_to_all | solution.py:336
  150.5 11.0 %collective-permute-start.2 = (bf16[576,768]{1,0:T(8,128)(2,1)S(1)}, bf16[576,768]{1,0:T(8,128)(2,1)S(1)}, u32[]{:S(2)}, u32[]{:S(2)}) collective-permute-start(bf16[576,768]{1,0:T(8,128)(2,1)S(1)} %all_gather.3.mine), channel_id=1, source_target_pairs={{0,8},{8,0},{1,9},{9,1},{2,10},{10,2},{3,11},{11,3},{4,12},{12,4},... | collective-permute-start | bytes 2654216 | tf_op jit(solution)/shard_map/ppermute | solution.py:332

commit v4 on v3

--- a/solution.py
+++ b/solution.py
@@ -1,3 +1,5 @@
+import functools
+
 import jax
 import jax.numpy as jnp
 from jax import lax
@@ -245,6 +247,22 @@
     total[...] = (mine[...].astype(F32) + theirs[...].astype(F32)).astype(BF16)
 
 
+def halve(value, kept, sent, index):
+    count = kept.shape[0]
+    blocks = value.reshape((count, 2) + kept.shape[1:])
+    odd = lax.rem(index, 2) == 1
+    kept[...] = jnp.where(odd, blocks[:, 1], blocks[:, 0])
+    sent[...] = jnp.where(odd, blocks[:, 0], blocks[:, 1]).astype(sent.dtype)
+
+
+def halve_body(level, held, got, kept, sent):
+    halve(held[...] + got[...].astype(F32), kept, sent, lax.axis_index("head") // 2**level)
+
+
+def last_body(held, got, total):
+    total[...] = (held[0] + got[0].astype(F32)).astype(total.dtype)
+
+
 def grads_body(
     parts,
     accept_sum,
@@ -256,7 +274,8 @@
     w_value,
     w_junction,
     weight_term,
-    input_term,
+    kept,
+    sent,
 ):
     tokens, width = hidden.shape
     chips = parts.shape[0]
@@ -271,7 +290,7 @@
     value = value + contract(w_key[...], grads[:, :HD], 0, 1)
     value = value + contract(w_value[...], grads[:, HD:], 0, 1)
     value = value + contract(w_junction[...], feature_grad, 1, 1)
-    input_term[...] = value.astype(BF16).reshape(input_term.shape)
+    halve(value, kept, sent, lax.axis_index("head"))
     cut = width // CORES
     first = 0
     for grad in (query_grad[...], grads):
@@ -374,14 +393,19 @@
             pltpu.SemaphoreType.DMA((8,)),
         ],
     )(
-        hidden,
-        w_key,
-        w_value,
-        w_junction,
-        donor_pos[0, 0],
-        acceptor_pos[0, 0],
-        junction_counts[0],
-        pred_grad[0, 0],
+        *(
+            pltpu.with_memory_space_constraint(value, pltpu.HBM)
+            for value in (
+                hidden,
+                w_key,
+                w_value,
+                w_junction,
+                donor_pos[0, 0],
+                acceptor_pos[0, 0],
+                junction_counts[0],
+                pred_grad[0, 0],
+            )
+        )
     )
     mine = exchange(message, "x")
     theirs = swap_cores(mine)
@@ -405,9 +429,14 @@
     parts = exchange(pair_sum, "x")
     rows = 3 * HD
     cut = width // CORES
-    weight_term, input_term = local_call(
+    block = (width // heads, tokens)
+    weight_term, held, sent = local_call(
         grads_body,
-        [((CORES, rows, cut), BF16), ((heads, width // heads, tokens), BF16)],
+        [
+            ((CORES, rows, cut), BF16),
+            ((heads // 2,) + block, F32),
+            ((heads // 2,) + block, BF16),
+        ],
         operands=9,
     )(
         parts,
@@ -420,7 +449,17 @@
         w_value,
         w_junction,
     )
-    input_parts = exchange(input_term, "head")
+
+    def flip(value, level):
+        return lax.ppermute(value, "head", [(i, i ^ 2**level) for i in range(heads)])
+
+    def fold(level, held, got):
+        count = heads // 2 ** (level + 1)
+        return local_call(
+            functools.partial(halve_body, level),
+            [((count,) + block, F32), ((count,) + block, BF16)],
+            operands=2,
+        )(held, got)
 
     (term,) = local_call(sum_body, [((rows, cut), BF16)], operands=1)(
         exchange(weight_term, "core")
@@ -430,17 +469,19 @@
     (tiles,) = local_call(
         cut_body, [((intervals,) + tile, BF16)], operands=1, scratch=[pltpu.VMEM((part, cut), F32)]
     )(exchange(term.reshape(chips, part, cut), "x"))
+    tiles, got = lax.optimization_barrier((tiles, flip(sent, 0)))
+    held, sent = fold(1, held, got)
     (copies,) = local_call(spread_body, [((intervals,) + tile, BF16)], operands=1)(
         exchange(tiles, "interval")
     )
+    copies, got = lax.optimization_barrier((copies, flip(sent, 1)))
+    held, sent = fold(2, held, got)
     (term,) = local_call(
         join_body, [((part, cut), BF16)], operands=1, scratch=[pltpu.VMEM((part, cut), F32)]
     )(exchange(copies, "interval"))
-    term, input_parts = lax.optimization_barrier((term, input_parts))
+    term, got = lax.optimization_barrier((term, flip(sent, 2)))
     term = lax.all_gather(term, "x", axis=0, tiled=True)
-    (grad_input,) = local_call(sum_body, [((width // heads, tokens), BF16)], operands=1)(
-        input_parts
-    )
+    (grad_input,) = local_call(last_body, [(block, BF16)], operands=2)(held, got)
     grads = local_call(place_body, [((HD, width), BF16)] * 3, operands=2)(term, swap_cores(term))
     return (grad_input.T[None],) + tuple(grads)
 

time: 164 us -> 140 us (0.85)
  blocking collectives: 89.8 us -> 46.8 us
  starting transfers between devices: 29 us -> 52.8 us
  local copies, waits for them, and re-layouts: 6.99 us -> 0.02 us
  Pallas kernels: 11.7 us -> 15.2 us
    all_to_all x6 -> x3, blocking collectives: 78.5 us -> 35.5 us  [exchange(): return lax.all_to_all(value, axis, 0, 0, tiled=True)]
    ppermute x0 -> x3, starting transfers between devices: none -> 19.2 us  [flip(): lax.ppermute(value, 'head', [(i, i ^ 2 ** level) for i in range(heads)])]
    unnamed x28 -> x12, local copies, waits for them, and re-layouts: 6.99 us -> 0.02 us
    all_to_all x1 -> x3, waiting for transfers between devices: 19.9 us -> 13.3 us  [exchange(): return lax.all_to_all(value, axis, 0, 0, tiled=True)]
    all_to_all x1 -> x3, starting transfers between devices: 10 us -> 16.1 us  [exchange(): return lax.all_to_all(value, axis, 0, 0, tiled=True)]
    ppermute x0 -> x3, waiting for transfers between devices: none -> 5.79 us  [flip(): lax.ppermute(value, 'head', [(i, i ^ 2 ** level) for i in range(heads)])]
    pallas_call x2 -> x4, Pallas kernels: 3.74 us -> 3.72 us  [the longest x1 2.9 us: on_device(): local_call(grads_body, [((CORES, rows, cut), BF16), ((heads // 2,) + bloc...]
  transfers between devices with their start and end apart: 4 -> 9, of which waited for: 4 -> 7; matrix products, arithmetic and copies ran while one was open for 0% -> 0% of each run, Pallas kernels for 1% -> 2%
where the time goes in v4:
time: 140 us
  starting transfers between devices  52.8 us (38%)
  blocking collectives  46.8 us (33%)
  waiting for transfers between devices  24 us (17%)
  Pallas kernels  15.2 us (11%)
    all_to_all x3, blocking collectives, exchange(): return lax.all_to_all(value, axis, 0, 0, tiled=True)  35.5 us
    ppermute x3, starting transfers between devices, flip(): lax.ppermute(value, 'head', [(i, i ^ 2 ** level) for i in range(heads)])  19.2 us
    ppermute x3, starting transfers between devices, swap_cores(): return lax.ppermute(value, 'core', [(0, 1), (1, 0)])  17.4 us
    all_to_all x3, starting transfers between devices, exchange(): return lax.all_to_all(value, axis, 0, 0, tiled=True)  16.1 us
    all_to_all x3, waiting for transfers between devices, exchange(): return lax.all_to_all(value, axis, 0, 0, tiled=True)  13.3 us
    all_gather x1, blocking collectives, on_device(): term = lax.all_gather(term, 'x', axis=0, tiled=True)  11.3 us
    ppermute x3, waiting for transfers between devices, flip(): lax.ppermute(value, 'head', [(i, i ^ 2 ** level) for i in range(heads)])  5.79 us
    ppermute x3, waiting for transfers between devices, swap_cores(): return lax.ppermute(value, 'core', [(0, 1), (1, 0)])  4.88 us
  transfers between devices with their start and end apart: 9, of which 7 were waited for; matrix products, arithmetic and copies ran while one was open for 0% of the time, Pallas kernels for 2%

profile of v4, /device:TPU:1, one launch (start us, length us, event | category | flops | bytes accessed | tf_op | source)
XLA Modules:
  0.0 139.5 jit_solution(17393060306776533077)
XLA Ops:
  0.6 0.0 copy-start
  0.6 0.0 copy-start.1
  0.7 0.0 copy-start.5
  0.7 2.8 %shard_map.130 = (bf16[4,272,384]{2,1,0:T(8,128)(2,1)S(1)}, bf16[256,128]{1,0:T(8,128)(2,1)S(1)}, bf16[64,256]{1,0:T(8,128)(2,1)S(1)}) custom-call(bf16[256,1536]{1,0:T(8,128)(2,1)} %bitcast.12, bf16[192,1536]{1,0:T(8,128)(2,1)} %w_key.1, bf16[192,1536]{1,0:T(8,128)(2,1)} %w_value.1, bf16[1536,128]{1,0:T(8,128)(2,1)} %w_junction.1, s32[8,8]{1,0:T(8,128)} %bitcast.17, ...), custom_call_target="tpu_custom_call" | custom-call | tf_op jit(solution)/shard_map/pallas_call | solution.py:380
  3.4 13.2 %all_to_all.30.mine = bf16[4,272,384]{2,1,0:T(8,128)(2,1)S(1)} all-to-all(bf16[4,272,384]{2,1,0:T(8,128)(2,1)S(1)} %get-tuple-element.32), channel_id=1, replica_groups=mesh['interval'=8,'x'=4,'core'=2,'head'=8] {'x'}, dimensions={0} | all-to-all | bytes 1671168 | tf_op jit(solution)/shard_map/all_to_all | solution.py:355
  16.7 7.7 %collective-permute-start = (bf16[4,272,384]{2,1,0:T(8,128)(2,1)S(1)}, bf16[4,272,384]{2,1,0:T(8,128)(2,1)S(1)}, u32[]{:S(2)}, u32[]{:S(2)}) collective-permute-start(bf16[4,272,384]{2,1,0:T(8,128)(2,1)S(1)} %all_to_all.30.mine), channel_id=1, source_target_pairs={{0,8},{8,0},{1,9},{9,1},{2,10},{10,2},{3,11},{11,3},{4,12},{12,4},... | collective-permute-start | bytes 2506760 | tf_op jit(solution)/shard_map/ppermute | solution.py:351
  24.4 0.0 copy-done
  24.4 0.0 copy-done.1
  24.4 0.0 copy-done.5
  24.4 0.4 shard_map.129
  24.8 1.5 %collective-permute-done.theirs = bf16[4,272,384]{2,1,0:T(8,128)(2,1)S(1)} collective-permute-done((bf16[4,272,384]{2,1,0:T(8,128)(2,1)S(1)}, bf16[4,272,384]{2,1,0:T(8,128)(2,1)S(1)}, u32[]{:S(2)}, u32[]{:S(2)}) %collective-permute-start) | collective-permute-done | bytes 835616 | tf_op jit(solution)/shard_map/ppermute | solution.py:351
  26.3 4.0 %shard_map.131 = (bf16[4,272,384]{2,1,0:T(8,128)(2,1)S(1)}, bf16[4,272,384]{2,1,0:T(8,128)(2,1)S(1)}, bf16[256,192]{1,0:T(8,128)(2,1)S(1)}, f32[256,128]{1,0:T(8,128)S(1)}) custom-call(bf16[256,256]{1,0:T(8,128)(2,1)S(1)} %get-tuple-element.29.queries, bf16[256,256]{1,0:T(8,128)(2,1)S(1)} %get-tuple-element.30.ctx, ...), custom_call_target="tpu_custom_call" | custom-call | tf_op jit(solution)/shard_map/pallas_call | solution.py:415
  30.3 2.3 %collective-permute-start.1 = (bf16[4,272,384]{2,1,0:T(8,128)(2,1)S(1)}, bf16[4,272,384]{2,1,0:T(8,128)(2,1)S(1)}, u32[]{:S(2)}, u32[]{:S(2)}) collective-permute-start(bf16[4,272,384]{2,1,0:T(8,128)(2,1)S(1)} %get-tuple-element.34), channel_id=1, source_target_pairs={{0,8},{8,0},{1,9},{9,1},{2,10},{10,2},{3,11},{11,3},{4,12},{12,4},... | collective-permute-start | bytes 2506760 | tf_op jit(solution)/shard_map/ppermute | solution.py:351
  32.6 2.0 %collective-permute-done.1.theirs = bf16[4,272,384]{2,1,0:T(8,128)(2,1)S(1)} collective-permute-done((bf16[4,272,384]{2,1,0:T(8,128)(2,1)S(1)}, bf16[4,272,384]{2,1,0:T(8,128)(2,1)S(1)}, u32[]{:S(2)}, u32[]{:S(2)}) %collective-permute-start.1) | collective-permute-done | bytes 835616 | tf_op jit(solution)/shard_map/ppermute | solution.py:351
  34.6 0.0 copy-start.2
  34.6 0.0 copy-start.3
  34.6 0.0 copy-start.4
  34.6 0.2 shard_map.132
  34.8 14.8 %all_to_all.31.parts = bf16[4,272,384]{2,1,0:T(8,128)(2,1)S(1)} all-to-all(bf16[4,272,384]{2,1,0:T(8,128)(2,1)S(1)} %shard_map.132), channel_id=1, replica_groups=mesh['interval'=8,'x'=4,'core'=2,'head'=8] {'x'}, dimensions={0} | all-to-all | bytes 1671168 | tf_op jit(solution)/shard_map/all_to_all | solution.py:355
  49.6 0.0 copy-done.2
  49.6 0.0 copy-done.3
  49.6 0.0 copy-done.4
  49.6 2.9 %shard_map.133 = (bf16[2,576,768]{2,1,0:T(8,128)(2,1)}, f32[4,192,256]{2,1,0:T(8,128)S(1)}, bf16[4,192,256]{2,1,0:T(8,128)(2,1)S(1)}) custom-call(bf16[4,272,384]{2,1,0:T(8,128)(2,1)S(1)} %all_to_all.31.parts, f32[256,128]{1,0:T(8,128)S(1)} %get-tuple-element.35.accept_sum, bf16[64,256]{1,0:T(8,128)(2,1)S(1)} %get-tuple-element.36.donor_hot, ...), custom_call_target="tpu_custom_call" | custom-call | tf_op jit(solution)/shard_map/pallas_call | solution.py:433
  52.5 7.4 %all_to_all.32.parts = bf16[2,576,768]{2,1,0:T(8,128)(2,1)S(1)} all-to-all(bf16[2,576,768]{2,1,0:T(8,128)(2,1)} %get-tuple-element.39), channel_id=1, replica_groups=mesh['interval'=8,'x'=4,'core'=2,'head'=8] {'core'}, dimensions={0} | all-to-all | bytes 3538944 | tf_op jit(solution)/shard_map/all_to_all | solution.py:355
  59.9 1.1 shard_map.134
  61.1 3.5 %all-to-all-start.3 = ((bf16[4,144,768]{2,1,0:T(8,128)(2,1)}), bf16[4,144,768]{2,1,0:T(8,128)(2,1)S(1)}, u32[]{:S(2)}, u32[]{:S(2)}) async-start(bf16[4,144,768]{2,1,0:T(8,128)(2,1)} %bitcast.7), calls=%async_computation.3 | async-start | bytes 1769472 | tf_op jit(solution)/shard_map/all_to_all | solution.py:355
  64.6 3.4 %collective-permute-start.2 = (bf16[4,192,256]{2,1,0:T(8,128)(2,1)S(1)}, bf16[4,192,256]{2,1,0:T(8,128)(2,1)S(1)}, u32[]{:S(2)}, u32[]{:S(2)}) collective-permute-start(bf16[4,192,256]{2,1,0:T(8,128)(2,1)S(1)} %get-tuple-element.40), channel_id=1, source_target_pairs={{0,1},{1,0},{2,3},{3,2},{4,5},{5,4},{6,7},{7,6},{8,9},{9,8},{10,11... | collective-permute-start | bytes 1179656 | tf_op jit(solution)/shard_map/ppermute | solution.py:454
  68.0 9.7 %all-to-all-done.3.parts = bf16[4,144,768]{2,1,0:T(8,128)(2,1)S(1)} async-done(((bf16[4,144,768]{2,1,0:T(8,128)(2,1)}), bf16[4,144,768]{2,1,0:T(8,128)(2,1)S(1)}, u32[]{:S(2)}, u32[]{:S(2)}) %all-to-all-start.3) | async-done | bytes 884768 | tf_op jit(solution)/shard_map/all_to_all | solution.py:355
  77.6 0.9 shard_map.135
  78.5 0.0 collective-permute-done.2.got
  78.5 6.2 %all-to-all-start.4 = ((bf16[8,36,384]{2,1,0:T(8,128)(2,1)}), bf16[8,36,384]{2,1,0:T(8,128)(2,1)S(1)}, u32[]{:S(2)}, u32[]{:S(2)}) async-start(bf16[8,36,384]{2,1,0:T(8,128)(2,1)} %shard_map.135), calls=%async_computation.4 | async-start | bytes 491520 | tf_op jit(solution)/shard_map/all_to_all | solution.py:355
  84.8 0.1 shard_map.136
  84.9 5.8 %collective-permute-start.3 = (bf16[2,192,256]{2,1,0:T(8,128)(2,1)S(1)}, bf16[2,192,256]{2,1,0:T(8,128)(2,1)S(1)}, u32[]{:S(2)}, u32[]{:S(2)}) collective-permute-start(bf16[2,192,256]{2,1,0:T(8,128)(2,1)S(1)} %get-tuple-element.44), channel_id=1, source_target_pairs={{0,2},{1,3},{2,0},{3,1},{4,6},{5,7},{6,4},{7,5},{8,10},{9,11},{10,... | collective-permute-start | bytes 589832 | tf_op jit(solution)/shard_map/ppermute | solution.py:454
  90.7 3.6 %all-to-all-done.4.parts = bf16[8,36,384]{2,1,0:T(8,128)(2,1)S(1)} async-done(((bf16[8,36,384]{2,1,0:T(8,128)(2,1)}), bf16[8,36,384]{2,1,0:T(8,128)(2,1)S(1)}, u32[]{:S(2)}, u32[]{:S(2)}) %all-to-all-start.4) | async-done | bytes 221216 | tf_op jit(solution)/shard_map/all_to_all | solution.py:355
  94.3 0.7 shard_map.137
  95.1 3.6 %collective-permute-done.3.got = bf16[2,192,256]{2,1,0:T(8,128)(2,1)S(1)} collective-permute-done((bf16[2,192,256]{2,1,0:T(8,128)(2,1)S(1)}, bf16[2,192,256]{2,1,0:T(8,128)(2,1)S(1)}, u32[]{:S(2)}, u32[]{:S(2)}) %collective-permute-start.3) | collective-permute-done | bytes 196640 | tf_op jit(solution)/shard_map/ppermute | solution.py:454
  98.6 6.4 %all-to-all-start.5 = ((bf16[8,36,384]{2,1,0:T(8,128)(2,1)}), bf16[8,36,384]{2,1,0:T(8,128)(2,1)S(1)}, u32[]{:S(2)}, u32[]{:S(2)}) async-start(bf16[8,36,384]{2,1,0:T(8,128)(2,1)} %shard_map.137), calls=%async_computation.5 | async-start | bytes 491520 | tf_op jit(solution)/shard_map/all_to_all | solution.py:355
  105.0 0.1 shard_map.138
  105.1 10.0 %collective-permute-start.4 = (bf16[1,192,256]{2,1,0:T(8,128)(2,1)S(1)}, bf16[1,192,256]{2,1,0:T(8,128)(2,1)S(1)}, u32[]{:S(2)}, u32[]{:S(2)}) collective-permute-start(bf16[1,192,256]{2,1,0:T(8,128)(2,1)S(1)} %get-tuple-element.48), channel_id=1, source_target_pairs={{0,4},{1,5},{2,6},{3,7},{4,0},{5,1},{6,2},{7,3},{8,12},{9,13},{10,... | collective-permute-start | bytes 294920 | tf_op jit(solution)/shard_map/ppermute | solution.py:454
  115.1 0.0 all-to-all-done.5.tiles
  115.1 2.2 %collective-permute-done.4.got = bf16[1,192,256]{2,1,0:T(8,128)(2,1)S(1)} collective-permute-done((bf16[1,192,256]{2,1,0:T(8,128)(2,1)S(1)}, bf16[1,192,256]{2,1,0:T(8,128)(2,1)S(1)}, u32[]{:S(2)}, u32[]{:S(2)}) %collective-permute-start.4) | collective-permute-done | bytes 98336 | tf_op jit(solution)/shard_map/ppermute | solution.py:454
  117.4 11.3 %all_gather.3.mine = bf16[576,768]{1,0:T(8,128)(2,1)S(1)} all-gather(bf16[144,768]{1,0:T(8,128)(2,1)S(1)} %shard_map.139), channel_id=1, replica_groups=mesh['interval'=8,'x'=4,'core'=2,'head'=8] {'x'}, dimensions={0}, use_global_device_ids=true | all-gather | bytes 1105920 | tf_op jit(solution)/shard_map/all_gather | solution.py:483
  128.6 7.5 %collective-permute-start.5 = (bf16[576,768]{1,0:T(8,128)(2,1)S(1)}, bf16[576,768]{1,0:T(8,128)(2,1)S(1)}, u32[]{:S(2)}, u32[]{:S(2)}) collective-permute-start(bf16[576,768]{1,0:T(8,128)(2,1)S(1)} %all_gather.3.mine), channel_id=1, source_target_pairs={{0,8},{8,0},{1,9},{9,1},{2,10},{10,2},{3,11},{11,3},{4,12},{12,4},... | collective-permute-start | bytes 2654216 | tf_op jit(solution)/shard_map/ppermute | solution.py:351
  136.1 0.7 shard_map.140
  136.8 1.4 collective-permute-done.5.theirs
  138.2 1.3 shard_map.141
  (1 shorter events, 0.0 us)
Async XLA Ops:
  0.6 23.7 %copy-start = (bf16[1,256,1536]{2,1,0:T(8,128)(2,1)S(1)}, bf16[1,256,1536]{2,1,0:T(8,128)(2,1)}, u32[]{:S(2)}) copy-start(bf16[1,256,1536]{2,1,0:T(8,128)(2,1)} %param.10) | copy-start | bytes 2359300
  0.6 23.7 %copy-start.1 = (bf16[192,1536]{1,0:T(8,128)(2,1)S(1)}, bf16[192,1536]{1,0:T(8,128)(2,1)}, u32[]{:S(2)}) copy-start(bf16[192,1536]{1,0:T(8,128)(2,1)} %w_query.3) | copy-start | bytes 1769476
  0.7 23.7 %copy-start.5 = (bf16[1,256,192]{1,2,0:T(8,128)(2,1)S(1)}, bf16[1,256,192]{1,2,0:T(8,128)(2,1)}, u32[]{:S(2)}) copy-start(bf16[1,256,192]{1,2,0:T(8,128)(2,1)} %param.11) | copy-start | bytes 294916
  16.7 9.6 %collective-permute-start = (bf16[4,272,384]{2,1,0:T(8,128)(2,1)S(1)}, bf16[4,272,384]{2,1,0:T(8,128)(2,1)S(1)}, u32[]{:S(2)}, u32[]{:S(2)}) collective-permute-start(bf16[4,272,384]{2,1,0:T(8,128)(2,1)S(1)} %all_to_all.30.mine), channel_id=1, source_target_pairs={{0,8},{8,0},{1,9},{9,1},{2,10},{10,2},{3,11},{11,3},{4,12},{12,4},... | collective-permute-start | bytes 2506760 | tf_op jit(solution)/shard_map/ppermute | solution.py:351
  30.3 4.2 %collective-permute-start.1 = (bf16[4,272,384]{2,1,0:T(8,128)(2,1)S(1)}, bf16[4,272,384]{2,1,0:T(8,128)(2,1)S(1)}, u32[]{:S(2)}, u32[]{:S(2)}) collective-permute-start(bf16[4,272,384]{2,1,0:T(8,128)(2,1)S(1)} %get-tuple-element.34), channel_id=1, source_target_pairs={{0,8},{8,0},{1,9},{9,1},{2,10},{10,2},{3,11},{11,3},{4,12},{12,4},... | collective-permute-start | bytes 2506760 | tf_op jit(solution)/shard_map/ppermute | solution.py:351
  34.6 15.0 %copy-start.2 = (bf16[192,1536]{1,0:T(8,128)(2,1)S(1)}, bf16[192,1536]{1,0:T(8,128)(2,1)}, u32[]{:S(2)}) copy-start(bf16[192,1536]{1,0:T(8,128)(2,1)} %w_key.1) | copy-start | bytes 1769476
  34.6 15.0 %copy-start.3 = (bf16[192,1536]{1,0:T(8,128)(2,1)S(1)}, bf16[192,1536]{1,0:T(8,128)(2,1)}, u32[]{:S(2)}) copy-start(bf16[192,1536]{1,0:T(8,128)(2,1)} %w_value.1) | copy-start | bytes 1769476
  34.6 15.0 %copy-start.4 = (bf16[1536,128]{1,0:T(8,128)(2,1)S(1)}, bf16[1536,128]{1,0:T(8,128)(2,1)}, u32[]{:S(2)}) copy-start(bf16[1536,128]{1,0:T(8,128)(2,1)} %w_junction.1) | copy-start | bytes 1179652
  61.1 16.6 %all-to-all-start.3 = ((bf16[4,144,768]{2,1,0:T(8,128)(2,1)}), bf16[4,144,768]{2,1,0:T(8,128)(2,1)S(1)}, u32[]{:S(2)}, u32[]{:S(2)}) async-start(bf16[4,144,768]{2,1,0:T(8,128)(2,1)} %bitcast.7), calls=%async_computation.3 | async-start | bytes 1769472 | tf_op jit(solution)/shard_map/all_to_all | solution.py:355
  64.6 13.9 %collective-permute-start.2 = (bf16[4,192,256]{2,1,0:T(8,128)(2,1)S(1)}, bf16[4,192,256]{2,1,0:T(8,128)(2,1)S(1)}, u32[]{:S(2)}, u32[]{:S(2)}) collective-permute-start(bf16[4,192,256]{2,1,0:T(8,128)(2,1)S(1)} %get-tuple-element.40), channel_id=1, source_target_pairs={{0,1},{1,0},{2,3},{3,2},{4,5},{5,4},{6,7},{7,6},{8,9},{9,8},{10,11... | collective-permute-start | bytes 1179656 | tf_op jit(solution)/shard_map/ppermute | solution.py:454
  78.5 15.8 %all-to-all-start.4 = ((bf16[8,36,384]{2,1,0:T(8,128)(2,1)}), bf16[8,36,384]{2,1,0:T(8,128)(2,1)S(1)}, u32[]{:S(2)}, u32[]{:S(2)}) async-start(bf16[8,36,384]{2,1,0:T(8,128)(2,1)} %shard_map.135), calls=%async_computation.4 | async-start | bytes 491520 | tf_op jit(solution)/shard_map/all_to_all | solution.py:355
  84.9 13.7 %collective-permute-start.3 = (bf16[2,192,256]{2,1,0:T(8,128)(2,1)S(1)}, bf16[2,192,256]{2,1,0:T(8,128)(2,1)S(1)}, u32[]{:S(2)}, u32[]{:S(2)}) collective-permute-start(bf16[2,192,256]{2,1,0:T(8,128)(2,1)S(1)} %get-tuple-element.44), channel_id=1, source_target_pairs={{0,2},{1,3},{2,0},{3,1},{4,6},{5,7},{6,4},{7,5},{8,10},{9,11},{10,... | collective-permute-start | bytes 589832 | tf_op jit(solution)/shard_map/ppermute | solution.py:454
  98.6 16.5 %all-to-all-start.5 = ((bf16[8,36,384]{2,1,0:T(8,128)(2,1)}), bf16[8,36,384]{2,1,0:T(8,128)(2,1)S(1)}, u32[]{:S(2)}, u32[]{:S(2)}) async-start(bf16[8,36,384]{2,1,0:T(8,128)(2,1)} %shard_map.137), calls=%async_computation.5 | async-start | bytes 491520 | tf_op jit(solution)/shard_map/all_to_all | solution.py:355
  105.1 12.3 %collective-permute-start.4 = (bf16[1,192,256]{2,1,0:T(8,128)(2,1)S(1)}, bf16[1,192,256]{2,1,0:T(8,128)(2,1)S(1)}, u32[]{:S(2)}, u32[]{:S(2)}) collective-permute-start(bf16[1,192,256]{2,1,0:T(8,128)(2,1)S(1)} %get-tuple-element.48), channel_id=1, source_target_pairs={{0,4},{1,5},{2,6},{3,7},{4,0},{5,1},{6,2},{7,3},{8,12},{9,13},{10,... | collective-permute-start | bytes 294920 | tf_op jit(solution)/shard_map/ppermute | solution.py:454
  128.6 9.5 %collective-permute-start.5 = (bf16[576,768]{1,0:T(8,128)(2,1)S(1)}, bf16[576,768]{1,0:T(8,128)(2,1)S(1)}, u32[]{:S(2)}, u32[]{:S(2)}) collective-permute-start(bf16[576,768]{1,0:T(8,128)(2,1)S(1)} %all_gather.3.mine), channel_id=1, source_target_pairs={{0,8},{8,0},{1,9},{9,1},{2,10},{10,2},{3,11},{11,3},{4,12},{12,4},... | collective-permute-start | bytes 2654216 | tf_op jit(solution)/shard_map/ppermute | solution.py:351

commit v5 on v4

--- a/solution.py
+++ b/solution.py
@@ -98,14 +98,16 @@
     ]
     for copy in copies:
         copy.start()
-    for copy in copies:
+    for copy in copies[:3]:
         copy.wait()
     chips = message.shape[0]
     tokens = hidden.shape[0]
     x = hidden[...]
+    rows = contract(x, weights[...], 1, 1).astype(BF16)
+    for copy in copies[3:]:
+        copy.wait()
     feats = contract(x, w_junction[...], 1, 0).astype(BF16)
     features[...] = feats
-    rows = contract(x, weights[...], 1, 1).astype(BF16)
 
     buckets, per = donor_pos.shape
     slots = buckets * per
@@ -159,9 +161,8 @@
     features,
     mine,
     theirs,
-    terms_mine,
     terms_theirs,
-    query_grad,
+    back_mine,
     accept_sum,
     probs_b,
     dscores_b,
@@ -216,35 +217,43 @@
         total = total + contract(hot, piece, 0, 0)
     accept_sum[...] = total
     back = (slot_grad * accept_feat).reshape(2, chips, per, PJ)
-    blank = jnp.zeros((chips, per, PJ), F32)
-
-    for i, terms in ((1, terms_theirs), (0, terms_mine)):
-        key_term = contract(dscores_b[i], queries[...], 0, 0) * scale
-        value_term = contract(probs_b[i], ctx[...], 0, 0)
-        middle = key_term[:, SHIFT:] + value_term[:, :SHIFT]
-        for first, value in (
-            (0, key_term[:, :SHIFT]),
-            (SHIFT, middle),
-            (LANES, value_term[:, SHIFT:]),
-        ):
-            terms[:, :tokens, first : first + SHIFT] = value.astype(BF16).reshape(
-                chips, tokens, SHIFT
-            )
-        upper = jnp.where(core == 0, back[i], blank)
-        lower = jnp.where(core == 0, blank, back[i])
-        terms[:, tokens:, :PJ] = jnp.concatenate([upper, lower], axis=1).astype(BF16)
-        terms[:, tokens:, PJ:] = jnp.zeros((chips, part, KV - PJ), BF16)
-    query_grad[...] = (
-        (
-            contract(dscores_b[0], sides[0][:, :LANES], 1, 0)
-            + contract(dscores_b[1], sides[1][:, :LANES], 1, 0)
-        )[:, :HD]
-        * scale
-    ).astype(BF16)
-
-
-def pair_body(mine, theirs, total):
-    total[...] = (mine[...].astype(F32) + theirs[...].astype(F32)).astype(BF16)
+    blank = jnp.zeros((2, chips, per, PJ), F32)
+
+    upper = jnp.where(core == 0, back, blank)
+    lower = jnp.where(core == 0, blank, back)
+    back = jnp.concatenate([upper, lower], axis=2).astype(BF16)
+    back_mine[...] = back[0]
+    write_terms(terms_theirs, dscores_b[1], probs_b[1], queries[...], ctx[...], back[1])
+
+
+def write_terms(terms, dscores, probs, queries, ctx, back):
+    chips, height, _ = terms.shape
+    part = back.shape[1]
+    tokens = height - part
+    key_term = contract(dscores, queries, 0, 0) * HD ** (-0.5)
+    value_term = contract(probs, ctx, 0, 0)
+    middle = key_term[:, SHIFT:] + value_term[:, :SHIFT]
+    for first, value in (
+        (0, key_term[:, :SHIFT]),
+        (SHIFT, middle),
+        (LANES, value_term[:, SHIFT:]),
+    ):
+        terms[:, :tokens, first : first + SHIFT] = value.astype(BF16).reshape(
+            chips, tokens, SHIFT
+        )
+    terms[:, tokens:, :PJ] = back
+    terms[:, tokens:, PJ:] = jnp.zeros((chips, part, KV - PJ), BF16)
+
+
+def own_body(queries, ctx, mine, theirs, back, probs_b, dscores_b, terms_mine, query_grad):
+    write_terms(terms_mine, dscores_b[0], probs_b[0], queries[...], ctx[...], back[...])
+    chips, _, _ = mine.shape
+    tokens = queries.shape[0]
+    total = jnp.zeros((tokens, LANES), F32)
+    for i, side in enumerate((mine, theirs)):
+        keys = side[:, :tokens, :LANES].reshape(chips * tokens, LANES)
+        total = total + contract(dscores_b[i], keys, 1, 0)
+    query_grad[...] = (total[:, :HD] * HD ** (-0.5)).astype(BF16)
 
 
 def halve(value, kept, sent, index):
@@ -255,35 +264,57 @@
     sent[...] = jnp.where(odd, blocks[:, 0], blocks[:, 1]).astype(sent.dtype)
 
 
-def halve_body(level, held, got, kept, sent):
-    halve(held[...] + got[...].astype(F32), kept, sent, lax.axis_index("head") // 2**level)
-
-
-def last_body(held, got, total):
-    total[...] = (held[0] + got[0].astype(F32)).astype(total.dtype)
-
-
-def grads_body(
+def quarter_body(held, got, *outs):
+    place = lax.axis_index("head") // 2
+    value = held[...] + got[...].astype(F32)
+    for i, out in enumerate(outs):
+        block = value[i]
+        for other in range(1, len(outs)):
+            block = jnp.where(place == other, value[i ^ other], block)
+        out[...] = block.astype(out.dtype)
+
+
+def total_body(*refs):
+    value = refs[0][...].astype(F32)
+    for ref in refs[1:-1]:
+        value = value + ref[...].astype(F32)
+    refs[-1][...] = value.astype(refs[-1].dtype)
+
+
+def grads_body(parts, query_grad, hidden, grads, kept, sent):
+    tokens, width = hidden.shape
+    total = jnp.zeros((tokens, KV), F32)
+    for chip in range(parts.shape[0]):
+        total = total + parts[chip, :tokens, :].astype(F32)
+    grads[...] = total.astype(BF16)
+    core = lax.axis_index("core")
+    cut = width // CORES
+    first = 0
+    for grad in (query_grad[...], grads[...]):
+        value = contract(grad, hidden[...], 0, 0)
+        rows = pl.ds(first, value.shape[0])
+        left, right = value[:, :cut], value[:, cut:]
+        kept[rows, :] = jnp.where(core == 0, left, right)
+        sent[rows, :] = jnp.where(core == 0, right, left).astype(BF16)
+        first += value.shape[0]
+
+
+def input_body(
     parts,
     accept_sum,
     donor_hot,
+    grads,
     query_grad,
-    hidden,
     w_query,
     w_key,
     w_value,
     w_junction,
-    weight_term,
     kept,
     sent,
 ):
-    tokens, width = hidden.shape
-    chips = parts.shape[0]
-    total = jnp.zeros((tokens, KV), F32)
-    for chip in range(chips):
-        total = total + parts[chip, :tokens, :].astype(F32)
-    grads = total.astype(BF16)
-    part = parts.shape[1] - tokens
+    chips, height, _ = parts.shape
+    tokens = grads.shape[0]
+    part = height - tokens
     slot_rows = parts[:, tokens:, :PJ].reshape(chips * part, PJ)
     feature_grad = (accept_sum[...] + contract(donor_hot[...], slot_rows, 0, 0)).astype(BF16)
     value = contract(w_query[...], query_grad[...], 0, 1)
@@ -291,27 +322,11 @@
     value = value + contract(w_value[...], grads[:, HD:], 0, 1)
     value = value + contract(w_junction[...], feature_grad, 1, 1)
     halve(value, kept, sent, lax.axis_index("head"))
-    cut = width // CORES
-    first = 0
-    for grad in (query_grad[...], grads):
-        value = contract(grad, hidden[...], 0, 0).astype(BF16)
-        for core in range(CORES):
-            weight_term[core, first : first + value.shape[0], :] = value[
-                :, core * cut : (core + 1) * cut
-            ]
-        first += value.shape[0]
 
 
 def tiles_of(rows, columns, count):
     high, wide = rows * 2 // count, columns // 2
     return [(i, pl.ds(i // 2 * high, high), pl.ds(i % 2 * wide, wide)) for i in range(count)]
-
-
-def sum_body(parts, total):
-    value = parts[0].astype(F32)
-    for i in range(1, parts.shape[0]):
-        value = value + parts[i].astype(F32)
-    total[...] = value.astype(total.dtype)
 
 
 def cut_body(parts, tiles, whole):
@@ -412,76 +427,73 @@
     queries, ctx = local_call(query_body, [((tokens, LANES), BF16)] * 2, operands=3)(
         hidden, w_query, ctx_grad[0].T
     )
-    terms_mine, terms_theirs, query_grad, accept_sum = local_call(
+    terms_theirs, back_mine, accept_sum, probs_b, dscores_b = local_call(
         attend_body,
         [
             ((chips, height, KV), BF16),
-            ((chips, height, KV), BF16),
-            ((tokens, HD), BF16),
+            ((chips, height - tokens, PJ), BF16),
             ((tokens, PJ), F32),
+            ((CORES, tokens, half), BF16),
+            ((CORES, tokens, half), BF16),
         ],
         operands=5,
-        scratch=[pltpu.VMEM((CORES, tokens, half), BF16)] * 2,
     )(queries, ctx, features, mine, theirs)
-    (pair_sum,) = local_call(pair_body, [((chips, height, KV), BF16)], operands=2)(
-        terms_mine, swap_cores(terms_theirs)
+    terms_theirs = swap_cores(terms_theirs)
+    terms_mine, query_grad = local_call(
+        own_body, [((chips, height, KV), BF16), ((tokens, HD), BF16)], operands=7
+    )(queries, ctx, mine, theirs, back_mine, probs_b, dscores_b)
+    (pair_sum,) = local_call(total_body, [((chips, height, KV), BF16)], operands=2)(
+        terms_mine, terms_theirs
     )
     parts = exchange(pair_sum, "x")
     rows = 3 * HD
     cut = width // CORES
     block = (width // heads, tokens)
-    weight_term, held, sent = local_call(
+    grads, weight_held, weight_sent = local_call(
         grads_body,
-        [
-            ((CORES, rows, cut), BF16),
-            ((heads // 2,) + block, F32),
-            ((heads // 2,) + block, BF16),
-        ],
+        [((tokens, KV), BF16), ((rows, cut), F32), ((rows, cut), BF16)],
+        operands=3,
+    )(parts, query_grad, hidden)
+    weight_got = swap_cores(weight_sent)
+    held, sent = local_call(
+        input_body,
+        [((heads // 2,) + block, F32), ((heads // 2,) + block, BF16)],
         operands=9,
     )(
         parts,
         accept_sum,
         donor_hot,
+        grads,
         query_grad,
-        hidden,
         w_query,
         w_key,
         w_value,
         w_junction,
     )
 
-    def flip(value, level):
-        return lax.ppermute(value, "head", [(i, i ^ 2**level) for i in range(heads)])
-
-    def fold(level, held, got):
-        count = heads // 2 ** (level + 1)
-        return local_call(
-            functools.partial(halve_body, level),
-            [((count,) + block, F32), ((count,) + block, BF16)],
-            operands=2,
-        )(held, got)
-
-    (term,) = local_call(sum_body, [((rows, cut), BF16)], operands=1)(
-        exchange(weight_term, "core")
-    )
+    def flip(value, mask):
+        return lax.ppermute(value, "head", [(i, i ^ mask) for i in range(heads)])
+
+    (term,) = local_call(total_body, [((rows, cut), BF16)], operands=2)(weight_held, weight_got)
     part = rows // chips
     tile = (part * 2 // intervals, cut // 2)
     (tiles,) = local_call(
         cut_body, [((intervals,) + tile, BF16)], operands=1, scratch=[pltpu.VMEM((part, cut), F32)]
     )(exchange(term.reshape(chips, part, cut), "x"))
-    tiles, got = lax.optimization_barrier((tiles, flip(sent, 0)))
-    held, sent = fold(1, held, got)
+    tiles, got = lax.optimization_barrier((tiles, flip(sent, 1)))
+    held, *sent = local_call(
+        quarter_body, [(block, F32)] + [(block, BF16)] * (heads // 2 - 1), operands=2
+    )(held, got)
     (copies,) = local_call(spread_body, [((intervals,) + tile, BF16)], operands=1)(
         exchange(tiles, "interval")
     )
-    copies, got = lax.optimization_barrier((copies, flip(sent, 1)))
-    held, sent = fold(2, held, got)
     (term,) = local_call(
         join_body, [((part, cut), BF16)], operands=1, scratch=[pltpu.VMEM((part, cut), F32)]
     )(exchange(copies, "interval"))
-    term, got = lax.optimization_barrier((term, flip(sent, 2)))
+    got = [flip(value, 2 * (i + 1)) for i, value in enumerate(sent)]
+    term, *got = lax.optimization_barrier((term, *got))
     term = lax.all_gather(term, "x", axis=0, tiled=True)
-    (grad_input,) = local_call(last_body, [(block, BF16)], operands=2)(held, got)
+    (grad_input,) = local_call(total_body, [(block, BF16)], operands=heads // 2)(held, *got)
     grads = local_call(place_body, [((HD, width), BF16)] * 3, operands=2)(term, swap_cores(term))
     return (grad_input.T[None],) + tuple(grads)
 

time: 140 us -> 147 us (1.050)
  blocking collectives: 46.8 us -> 55.1 us
  local copies, waits for them, and re-layouts: 0.02 us -> 5.99 us
  starting transfers between devices: 52.8 us -> 47.4 us
  waiting for transfers between devices: 24 us -> 22.1 us
    all_to_all x3 -> x2, waiting for transfers between devices: 13.3 us -> 2.99 us  [exchange(): return lax.all_to_all(value, axis, 0, 0, tiled=True)]
    all_to_all x3 -> x2, starting transfers between devices: 16.1 us -> 7.04 us  [exchange(): return lax.all_to_all(value, axis, 0, 0, tiled=True)]
    all_to_all x3, blocking collectives: 35.5 us -> 44.5 us  [exchange(): return lax.all_to_all(value, axis, 0, 0, tiled=True)]
    ppermute x3 -> x4, waiting for transfers between devices: 5.79 us -> 13 us  [flip(): return lax.ppermute(value, 'head', [(i, i ^ mask) for i in range(heads)])]
    unnamed x12 -> x28, local copies, waits for them, and re-layouts: 0.02 us -> 5.99 us
    ppermute x3 -> x4, starting transfers between devices: 17.4 us -> 21.4 us  [swap_cores(): return lax.ppermute(value, 'core', [(0, 1), (1, 0)])]
    ppermute x3 -> x4, waiting for transfers between devices: 4.88 us -> 6.12 us  [swap_cores(): return lax.ppermute(value, 'core', [(0, 1), (1, 0)])]
    ppermute x3 -> x4, starting transfers between devices: 19.2 us -> 19 us  [flip(): return lax.ppermute(value, 'head', [(i, i ^ mask) for i in range(heads)])]
  transfers between devices with their start and end apart: 9 -> 10, of which waited for: 7 -> 8; matrix products, arithmetic and copies ran while one was open for 0% -> 0% of each run, Pallas kernels for 2% -> 3%
where the time goes in v5:
time: 147 us; the launch traced here: 146 us
  blocking collectives  55.1 us (37%)
  starting transfers between devices  47.4 us (32%)
  waiting for transfers between devices  22.1 us (15%)
  Pallas kernels  14.5 us (10%)
  local copies, waits for them, and re-layouts  5.99 us (4%)
    all_to_all x3, blocking collectives, exchange(): return lax.all_to_all(value, axis, 0, 0, tiled=True)  44.5 us
    ppermute x4, starting transfers between devices, swap_cores(): return lax.ppermute(value, 'core', [(0, 1), (1, 0)])  21.4 us
    ppermute x4, starting transfers between devices, flip(): return lax.ppermute(value, 'head', [(i, i ^ mask) for i in range(heads)])  19 us
    ppermute x4, waiting for transfers between devices, flip(): return lax.ppermute(value, 'head', [(i, i ^ mask) for i in range(heads)])  13 us
    all_gather x1, blocking collectives, on_device(): term = lax.all_gather(term, 'x', axis=0, tiled=True)  10.6 us
    all_to_all x2, starting transfers between devices, exchange(): return lax.all_to_all(value, axis, 0, 0, tiled=True)  7.04 us
    ppermute x4, waiting for transfers between devices, swap_cores(): return lax.ppermute(value, 'core', [(0, 1), (1, 0)])  6.12 us
    unnamed x28, local copies, waits for them, and re-layouts  5.99 us
  transfers between devices with their start and end apart: 10, of which 8 were waited for; matrix products, arithmetic and copies ran while one was open for 0% of the time, Pallas kernels for 3%

profile of v5, /device:TPU:1, one launch (start us, length us, event | category | flops | bytes accessed | tf_op | source)
XLA Modules:
  0.0 146.1 jit_solution(12663547291081587584)
XLA Ops:
  0.6 0.0 copy-start
  0.6 0.0 copy-start.1
  0.7 0.0 copy-start.13
  0.7 2.9 %shard_map.130 = (bf16[4,272,384]{2,1,0:T(8,128)(2,1)S(1)}, bf16[256,128]{1,0:T(8,128)(2,1)S(1)}, bf16[64,256]{1,0:T(8,128)(2,1)S(1)}) custom-call(bf16[256,1536]{1,0:T(8,128)(2,1)} %bitcast.12, bf16[192,1536]{1,0:T(8,128)(2,1)} %w_key.1, bf16[192,1536]{1,0:T(8,128)(2,1)} %w_value.1, bf16[1536,128]{1,0:T(8,128)(2,1)} %w_junction.1, s32[8,8]{1,0:T(8,128)} %bitcast.17, ...), custom_call_target="tpu_custom_call" | custom-call | tf_op jit(solution)/shard_map/pallas_call | solution.py:395
  3.6 13.2 %all_to_all.25.mine = bf16[4,272,384]{2,1,0:T(8,128)(2,1)S(1)} all-to-all(bf16[4,272,384]{2,1,0:T(8,128)(2,1)S(1)} %get-tuple-element.36), channel_id=1, replica_groups=mesh['interval'=8,'x'=4,'core'=2,'head'=8] {'x'}, dimensions={0} | all-to-all | bytes 1671168 | tf_op jit(solution)/shard_map/all_to_all | solution.py:370
  16.8 7.7 %collective-permute-start = (bf16[4,272,384]{2,1,0:T(8,128)(2,1)S(1)}, bf16[4,272,384]{2,1,0:T(8,128)(2,1)S(1)}, u32[]{:S(2)}, u32[]{:S(2)}) collective-permute-start(bf16[4,272,384]{2,1,0:T(8,128)(2,1)S(1)} %all_to_all.25.mine), channel_id=1, source_target_pairs={{0,8},{8,0},{1,9},{9,1},{2,10},{10,2},{3,11},{11,3},{4,12},{12,4},... | collective-permute-start | bytes 2506760 | tf_op jit(solution)/shard_map/ppermute | solution.py:366
  24.5 0.0 copy-done
  24.5 0.0 copy-done.1
  24.5 0.0 copy-done.13
  24.5 0.4 shard_map.129
  24.9 1.5 %collective-permute-done.theirs = bf16[4,272,384]{2,1,0:T(8,128)(2,1)S(1)} collective-permute-done((bf16[4,272,384]{2,1,0:T(8,128)(2,1)S(1)}, bf16[4,272,384]{2,1,0:T(8,128)(2,1)S(1)}, u32[]{:S(2)}, u32[]{:S(2)}) %collective-permute-start) | collective-permute-done | bytes 835616 | tf_op jit(solution)/shard_map/ppermute | solution.py:366
  26.5 3.5 %shard_map.131 = (bf16[4,272,384]{2,1,0:T(8,128)(2,1)S(1)}, bf16[4,16,128]{2,1,0:T(8,128)(2,1)S(1)}, f32[256,128]{1,0:T(8,128)S(1)}, bf16[2,256,1024]{2,1,0:T(8,128)(2,1)S(1)}, bf16[2,256,1024]{2,1,0:T(8,128)(2,1)S(1)}) custom-call(bf16[256,256]{1,0:T(8,128)(2,1)S(1)} %get-tuple-element.34.queries, bf16[256,256]{1,0:T(8,128)(2,1)S(1)} %get-tuple-element.35.ctx, ...), custom_call_target="tpu_custom_call" | custom-call | tf_op jit(solution)/shard_map/pallas_call | solution.py:430
  30.0 0.0 copy-start.11
  30.0 0.6 copy-done.11
  30.6 2.3 %collective-permute-start.1 = (bf16[4,272,384]{2,1,0:T(8,128)(2,1)S(1)}, bf16[4,272,384]{2,1,0:T(8,128)(2,1)S(1)}, u32[]{:S(2)}, u32[]{:S(2)}) collective-permute-start(bf16[4,272,384]{2,1,0:T(8,128)(2,1)S(1)} %get-tuple-element.42), channel_id=1, source_target_pairs={{0,8},{8,0},{1,9},{9,1},{2,10},{10,2},{3,11},{11,3},{4,12},{12,4},... | collective-permute-start | bytes 2506760 | tf_op jit(solution)/shard_map/ppermute | solution.py:366
  32.9 0.7 shard_map.132
  33.6 0.0 copy-start.7
  33.7 1.2 collective-permute-done.1.refs_1_
  34.9 0.2 shard_map.133
  35.1 14.7 %all_to_all.26.parts = bf16[4,272,384]{2,1,0:T(8,128)(2,1)S(1)} all-to-all(bf16[4,272,384]{2,1,0:T(8,128)(2,1)S(1)} %shard_map.133), channel_id=1, replica_groups=mesh['interval'=8,'x'=4,'core'=2,'head'=8] {'x'}, dimensions={0} | all-to-all | bytes 1671168 | tf_op jit(solution)/shard_map/all_to_all | solution.py:370
  49.7 0.0 copy-done.7
  49.7 0.7 shard_map.134
  50.4 0.0 copy-start.9
  50.4 0.7 copy-done.9
  51.1 3.4 %collective-permute-start.2 = (bf16[576,768]{1,0:T(8,128)(2,1)S(1)}, bf16[576,768]{1,0:T(8,128)(2,1)S(1)}, u32[]{:S(2)}, u32[]{:S(2)}) collective-permute-start(bf16[576,768]{1,0:T(8,128)(2,1)S(1)} %get-tuple-element.49), channel_id=1, source_target_pairs={{0,8},{8,0},{1,9},{9,1},{2,10},{10,2},{3,11},{11,3},{4,12},{12,4},... | collective-permute-start | bytes 2654216 | tf_op jit(solution)/shard_map/ppermute | solution.py:366
  54.5 2.0 %collective-permute-done.2.refs_1_ = bf16[576,768]{1,0:T(8,128)(2,1)S(1)} collective-permute-done((bf16[576,768]{1,0:T(8,128)(2,1)S(1)}, bf16[576,768]{1,0:T(8,128)(2,1)S(1)}, u32[]{:S(2)}, u32[]{:S(2)}) %collective-permute-start.2) | collective-permute-done | bytes 884768 | tf_op jit(solution)/shard_map/ppermute | solution.py:366
  56.5 1.1 shard_map.136
  57.6 0.0 copy-start.2
  57.6 0.0 copy-start.3
  57.6 3.6 %all-to-all-start.2 = ((bf16[4,144,768]{2,1,0:T(8,128)(2,1)}), bf16[4,144,768]{2,1,0:T(8,128)(2,1)S(1)}, u32[]{:S(2)}, u32[]{:S(2)}) async-start(bf16[4,144,768]{2,1,0:T(8,128)(2,1)} %bitcast.7), calls=%async_computation.2 | async-start | bytes 1769472 | tf_op jit(solution)/shard_map/all_to_all | solution.py:370
  61.2 0.0 copy-done.2
  61.2 0.0 copy-done.3
  61.2 0.0 copy-start.4
  61.2 1.0 copy-done.4
  62.2 0.0 copy-start.8
  62.2 0.9 copy-done.8
  63.1 0.0 copy-start.10
  63.1 0.9 copy-done.10
  64.1 0.9 copy-done.12
  65.0 1.9 %shard_map.135 = (f32[4,192,256]{2,1,0:T(8,128)S(1)}, bf16[4,192,256]{2,1,0:T(8,128)(2,1)}) custom-call(bf16[4,272,384]{2,1,0:T(8,128)(2,1)S(1)} %all_to_all.26.parts, f32[256,128]{1,0:T(8,128)S(1)} %copy-done.12, bf16[64,256]{1,0:T(8,128)(2,1)S(1)} %get-tuple-element.44.donor_hot, bf16[256,384]{1,0:T(8,128)(2,1)S(1)} %copy-done.10, ...), custom_call_target="tpu_custom_call" | custom-call | tf_op jit(solution)/shard_map/pallas_call | solution.py:458
  66.9 0.0 copy-start.5
  66.9 0.9 copy-done.5
  67.8 0.0 copy-start.6
  67.8 3.5 %collective-permute-start.3 = (bf16[4,192,256]{2,1,0:T(8,128)(2,1)}, bf16[4,192,256]{2,1,0:T(8,128)(2,1)S(1)}, u32[]{:S(2)}, u32[]{:S(2)}) collective-permute-start(bf16[4,192,256]{2,1,0:T(8,128)(2,1)} %get-tuple-element.50), channel_id=1, source_target_pairs={{0,1},{1,0},{2,3},{3,2},{4,5},{5,4},{6,7},{7,6},{8,9},{9,8},{10,11... | collective-permute-start | bytes 1179656 | tf_op jit(solution)/shard_map/ppermute | solution.py:475
  71.3 3.0 %all-to-all-done.2.parts = bf16[4,144,768]{2,1,0:T(8,128)(2,1)S(1)} async-done(((bf16[4,144,768]{2,1,0:T(8,128)(2,1)}), bf16[4,144,768]{2,1,0:T(8,128)(2,1)S(1)}, u32[]{:S(2)}, u32[]{:S(2)}) %all-to-all-start.2) | async-done | bytes 884768 | tf_op jit(solution)/shard_map/all_to_all | solution.py:370
  74.3 0.2 shard_map.137
  74.5 5.9 %collective-permute-done.3.got = bf16[4,192,256]{2,1,0:T(8,128)(2,1)S(1)} collective-permute-done((bf16[4,192,256]{2,1,0:T(8,128)(2,1)}, bf16[4,192,256]{2,1,0:T(8,128)(2,1)S(1)}, u32[]{:S(2)}, u32[]{:S(2)}) %collective-permute-start.3) | collective-permute-done | bytes 393248 | tf_op jit(solution)/shard_map/ppermute | solution.py:475
  80.4 16.6 %all_to_all.27.parts = bf16[8,36,384]{2,1,0:T(8,128)(2,1)S(1)} all-to-all(bf16[8,36,384]{2,1,0:T(8,128)(2,1)S(1)} %shard_map.137), channel_id=1, replica_groups=mesh['interval'=8,'x'=4,'core'=2,'head'=8] {'interval'}, dimensions={0} | all-to-all | bytes 442368 | tf_op jit(solution)/shard_map/all_to_all | solution.py:370
  97.0 0.7 shard_map.139
  97.7 3.4 %all-to-all-start.4 = ((bf16[8,36,384]{2,1,0:T(8,128)(2,1)}), bf16[8,36,384]{2,1,0:T(8,128)(2,1)S(1)}, u32[]{:S(2)}, u32[]{:S(2)}) async-start(bf16[8,36,384]{2,1,0:T(8,128)(2,1)} %shard_map.139), calls=%async_computation.4 | async-start | bytes 491520 | tf_op jit(solution)/shard_map/all_to_all | solution.py:370
  101.1 0.0 copy-done.6
  101.1 0.2 shard_map.138
  101.3 5.8 %collective-permute-start.4 = (bf16[192,256]{1,0:T(8,128)(2,1)S(1)}, bf16[192,256]{1,0:T(8,128)(2,1)S(1)}, u32[]{:S(2)}, u32[]{:S(2)}) collective-permute-start(bf16[192,256]{1,0:T(8,128)(2,1)S(1)} %get-tuple-element.54), channel_id=1, source_target_pairs={{0,2},{1,3},{2,0},{3,1},{4,6},{5,7},{6,4},{7,5},{8,10},{9,11},{10,... | collective-permute-start | bytes 294920 | tf_op jit(solution)/shard_map/ppermute | solution.py:475
  107.1 7.7 %collective-permute-start.5 = (bf16[192,256]{1,0:T(8,128)(2,1)S(1)}, bf16[192,256]{1,0:T(8,128)(2,1)S(1)}, u32[]{:S(2)}, u32[]{:S(2)}) collective-permute-start(bf16[192,256]{1,0:T(8,128)(2,1)S(1)} %get-tuple-element.55), channel_id=1, source_target_pairs={{0,4},{1,5},{2,6},{3,7},{4,0},{5,1},{6,2},{7,3},{8,12},{9,13},{10,... | collective-permute-start | bytes 294920 | tf_op jit(solution)/shard_map/ppermute | solution.py:475
  114.9 1.9 %collective-permute-start.6 = (bf16[192,256]{1,0:T(8,128)(2,1)S(1)}, bf16[192,256]{1,0:T(8,128)(2,1)S(1)}, u32[]{:S(2)}, u32[]{:S(2)}) collective-permute-start(bf16[192,256]{1,0:T(8,128)(2,1)S(1)} %get-tuple-element.56), channel_id=1, source_target_pairs={{0,6},{1,7},{2,4},{3,5},{4,2},{5,3},{6,0},{7,1},{8,14},{9,15},{10,... | collective-permute-start | bytes 294920 | tf_op jit(solution)/shard_map/ppermute | solution.py:475
  116.8 0.0 all-to-all-done.4.tiles
  116.9 0.0 collective-permute-done.4.refs_1_
  116.9 0.2 collective-permute-done.5.refs_2_
  117.1 6.9 %collective-permute-done.6.refs_3_ = bf16[192,256]{1,0:T(8,128)(2,1)S(1)} collective-permute-done((bf16[192,256]{1,0:T(8,128)(2,1)S(1)}, bf16[192,256]{1,0:T(8,128)(2,1)S(1)}, u32[]{:S(2)}, u32[]{:S(2)}) %collective-permute-start.6) | collective-permute-done | bytes 98336 | tf_op jit(solution)/shard_map/ppermute | solution.py:475
  124.0 10.6 %all_gather.3.mine = bf16[576,768]{1,0:T(8,128)(2,1)S(1)} all-gather(bf16[144,768]{1,0:T(8,128)(2,1)S(1)} %shard_map.140), channel_id=1, replica_groups=mesh['interval'=8,'x'=4,'core'=2,'head'=8] {'x'}, dimensions={0}, use_global_device_ids=true | all-gather | bytes 1105920 | tf_op jit(solution)/shard_map/all_gather | solution.py:495
  134.6 8.1 %collective-permute-start.7 = (bf16[576,768]{1,0:T(8,128)(2,1)S(1)}, bf16[576,768]{1,0:T(8,128)(2,1)S(1)}, u32[]{:S(2)}, u32[]{:S(2)}) collective-permute-start(bf16[576,768]{1,0:T(8,128)(2,1)S(1)} %all_gather.3.mine), channel_id=1, source_target_pairs={{0,8},{8,0},{1,9},{9,1},{2,10},{10,2},{3,11},{11,3},{4,12},{12,4},... | collective-permute-start | bytes 2654216 | tf_op jit(solution)/shard_map/ppermute | solution.py:366
  142.7 0.7 shard_map.141
  143.4 1.3 collective-permute-done.7.theirs
  144.7 1.3 shard_map.142
  (2 shorter events, 0.0 us)
Async XLA Ops:
  0.6 23.9 %copy-start = (bf16[1,256,1536]{2,1,0:T(8,128)(2,1)S(1)}, bf16[1,256,1536]{2,1,0:T(8,128)(2,1)}, u32[]{:S(2)}) copy-start(bf16[1,256,1536]{2,1,0:T(8,128)(2,1)} %param.10) | copy-start | bytes 2359300
  0.6 23.9 %copy-start.1 = (bf16[192,1536]{1,0:T(8,128)(2,1)S(1)}, bf16[192,1536]{1,0:T(8,128)(2,1)}, u32[]{:S(2)}) copy-start(bf16[192,1536]{1,0:T(8,128)(2,1)} %w_query.3) | copy-start | bytes 1769476
  0.7 23.9 %copy-start.13 = (bf16[1,256,192]{1,2,0:T(8,128)(2,1)S(1)}, bf16[1,256,192]{1,2,0:T(8,128)(2,1)}, u32[]{:S(2)}) copy-start(bf16[1,256,192]{1,2,0:T(8,128)(2,1)} %param.11) | copy-start | bytes 294916
  16.8 9.6 %collective-permute-start = (bf16[4,272,384]{2,1,0:T(8,128)(2,1)S(1)}, bf16[4,272,384]{2,1,0:T(8,128)(2,1)S(1)}, u32[]{:S(2)}, u32[]{:S(2)}) collective-permute-start(bf16[4,272,384]{2,1,0:T(8,128)(2,1)S(1)} %all_to_all.25.mine), channel_id=1, source_target_pairs={{0,8},{8,0},{1,9},{9,1},{2,10},{10,2},{3,11},{11,3},{4,12},{12,4},... | collective-permute-start | bytes 2506760 | tf_op jit(solution)/shard_map/ppermute | solution.py:366
  30.0 0.7 copy-start.11
  30.6 4.2 %collective-permute-start.1 = (bf16[4,272,384]{2,1,0:T(8,128)(2,1)S(1)}, bf16[4,272,384]{2,1,0:T(8,128)(2,1)S(1)}, u32[]{:S(2)}, u32[]{:S(2)}) collective-permute-start(bf16[4,272,384]{2,1,0:T(8,128)(2,1)S(1)} %get-tuple-element.42), channel_id=1, source_target_pairs={{0,8},{8,0},{1,9},{9,1},{2,10},{10,2},{3,11},{11,3},{4,12},{12,4},... | collective-permute-start | bytes 2506760 | tf_op jit(solution)/shard_map/ppermute | solution.py:366
  33.6 16.1 %copy-start.7 = (bf16[256,192]{1,0:T(8,128)(2,1)}, bf16[256,192]{1,0:T(8,128)(2,1)S(1)}, u32[]{:S(2)}) copy-start(bf16[256,192]{1,0:T(8,128)(2,1)S(1)} %get-tuple-element.45.query_grad) | copy-start | bytes 294916
  50.4 0.7 copy-start.9
  51.1 5.4 %collective-permute-start.2 = (bf16[576,768]{1,0:T(8,128)(2,1)S(1)}, bf16[576,768]{1,0:T(8,128)(2,1)S(1)}, u32[]{:S(2)}, u32[]{:S(2)}) collective-permute-start(bf16[576,768]{1,0:T(8,128)(2,1)S(1)} %get-tuple-element.49), channel_id=1, source_target_pairs={{0,8},{8,0},{1,9},{9,1},{2,10},{10,2},{3,11},{11,3},{4,12},{12,4},... | collective-permute-start | bytes 2654216 | tf_op jit(solution)/shard_map/ppermute | solution.py:366
  57.6 3.6 %copy-start.2 = (bf16[192,1536]{1,0:T(8,128)(2,1)S(1)}, bf16[192,1536]{1,0:T(8,128)(2,1)}, u32[]{:S(2)}) copy-start(bf16[192,1536]{1,0:T(8,128)(2,1)} %w_key.1) | copy-start | bytes 1769476
  57.6 3.7 %copy-start.3 = (bf16[192,1536]{1,0:T(8,128)(2,1)S(1)}, bf16[192,1536]{1,0:T(8,128)(2,1)}, u32[]{:S(2)}) copy-start(bf16[192,1536]{1,0:T(8,128)(2,1)} %w_value.1) | copy-start | bytes 1769476
  57.6 16.7 %all-to-all-start.2 = ((bf16[4,144,768]{2,1,0:T(8,128)(2,1)}), bf16[4,144,768]{2,1,0:T(8,128)(2,1)S(1)}, u32[]{:S(2)}, u32[]{:S(2)}) async-start(bf16[4,144,768]{2,1,0:T(8,128)(2,1)} %bitcast.7), calls=%async_computation.2 | async-start | bytes 1769472 | tf_op jit(solution)/shard_map/all_to_all | solution.py:370
  61.2 1.0 copy-start.4
  62.2 0.9 copy-start.8
  63.1 0.9 copy-start.10
  64.1 0.9 copy-start.12
  66.9 0.9 copy-start.5
  67.8 33.4 %copy-start.6 = (f32[4,192,256]{2,1,0:T(8,128)S(1)}, f32[4,192,256]{2,1,0:T(8,128)}, u32[]{:S(2)}) copy-start(f32[4,192,256]{2,1,0:T(8,128)} %copy-done.5) | copy-start | bytes 2359300
  67.8 12.6 %collective-permute-start.3 = (bf16[4,192,256]{2,1,0:T(8,128)(2,1)}, bf16[4,192,256]{2,1,0:T(8,128)(2,1)S(1)}, u32[]{:S(2)}, u32[]{:S(2)}) collective-permute-start(bf16[4,192,256]{2,1,0:T(8,128)(2,1)} %get-tuple-element.50), channel_id=1, source_target_pairs={{0,1},{1,0},{2,3},{3,2},{4,5},{5,4},{6,7},{7,6},{8,9},{9,8},{10,11... | collective-permute-start | bytes 1179656 | tf_op jit(solution)/shard_map/ppermute | solution.py:475
  97.7 19.1 %all-to-all-start.4 = ((bf16[8,36,384]{2,1,0:T(8,128)(2,1)}), bf16[8,36,384]{2,1,0:T(8,128)(2,1)S(1)}, u32[]{:S(2)}, u32[]{:S(2)}) async-start(bf16[8,36,384]{2,1,0:T(8,128)(2,1)} %shard_map.139), calls=%async_computation.4 | async-start | bytes 491520 | tf_op jit(solution)/shard_map/all_to_all | solution.py:370
  101.3 15.5 %collective-permute-start.4 = (bf16[192,256]{1,0:T(8,128)(2,1)S(1)}, bf16[192,256]{1,0:T(8,128)(2,1)S(1)}, u32[]{:S(2)}, u32[]{:S(2)}) collective-permute-start(bf16[192,256]{1,0:T(8,128)(2,1)S(1)} %get-tuple-element.54), channel_id=1, source_target_pairs={{0,2},{1,3},{2,0},{3,1},{4,6},{5,7},{6,4},{7,5},{8,10},{9,11},{10,... | collective-permute-start | bytes 294920 | tf_op jit(solution)/shard_map/ppermute | solution.py:475
  107.1 9.9 %collective-permute-start.5 = (bf16[192,256]{1,0:T(8,128)(2,1)S(1)}, bf16[192,256]{1,0:T(8,128)(2,1)S(1)}, u32[]{:S(2)}, u32[]{:S(2)}) collective-permute-start(bf16[192,256]{1,0:T(8,128)(2,1)S(1)} %get-tuple-element.55), channel_id=1, source_target_pairs={{0,4},{1,5},{2,6},{3,7},{4,0},{5,1},{6,2},{7,3},{8,12},{9,13},{10,... | collective-permute-start | bytes 294920 | tf_op jit(solution)/shard_map/ppermute | solution.py:475
  114.9 9.1 %collective-permute-start.6 = (bf16[192,256]{1,0:T(8,128)(2,1)S(1)}, bf16[192,256]{1,0:T(8,128)(2,1)S(1)}, u32[]{:S(2)}, u32[]{:S(2)}) collective-permute-start(bf16[192,256]{1,0:T(8,128)(2,1)S(1)} %get-tuple-element.56), channel_id=1, source_target_pairs={{0,6},{1,7},{2,4},{3,5},{4,2},{5,3},{6,0},{7,1},{8,14},{9,15},{10,... | collective-permute-start | bytes 294920 | tf_op jit(solution)/shard_map/ppermute | solution.py:475
  134.6 10.1 %collective-permute-start.7 = (bf16[576,768]{1,0:T(8,128)(2,1)S(1)}, bf16[576,768]{1,0:T(8,128)(2,1)S(1)}, u32[]{:S(2)}, u32[]{:S(2)}) collective-permute-start(bf16[576,768]{1,0:T(8,128)(2,1)S(1)} %all_gather.3.mine), channel_id=1, source_target_pairs={{0,8},{8,0},{1,9},{9,1},{2,10},{10,2},{3,11},{11,3},{4,12},{12,4},... | collective-permute-start | bytes 2654216 | tf_op jit(solution)/shard_map/ppermute | solution.py:366

commit v6 on v5

--- a/solution.py
+++ b/solution.py
@@ -16,7 +16,7 @@
 SHIFT = KV - LANES
 F32 = jnp.float32
 BF16 = jnp.bfloat16
-VMEM_BYTES = 48 * 1024 * 1024
+VMEM_BYTES = 20 * 1024 * 1024
 
 
 def contract(a, b, dim_a, dim_b, precision=None):
@@ -264,14 +264,8 @@
     sent[...] = jnp.where(odd, blocks[:, 0], blocks[:, 1]).astype(sent.dtype)
 
 
-def quarter_body(held, got, *outs):
-    place = lax.axis_index("head") // 2
-    value = held[...] + got[...].astype(F32)
-    for i, out in enumerate(outs):
-        block = value[i]
-        for other in range(1, len(outs)):
-            block = jnp.where(place == other, value[i ^ other], block)
-        out[...] = block.astype(out.dtype)
+def halve_body(level, held, got, kept, sent):
+    halve(held[...] + got[...].astype(F32), kept, sent, lax.axis_index("head") // 2**level)
 
 
 def total_body(*refs):
@@ -454,7 +448,6 @@
         [((tokens, KV), BF16), ((rows, cut), F32), ((rows, cut), BF16)],
         operands=3,
     )(parts, query_grad, hidden)
-    weight_got = swap_cores(weight_sent)
     held, sent = local_call(
         input_body,
         [((heads // 2,) + block, F32), ((heads // 2,) + block, BF16)],
@@ -471,29 +464,41 @@
         w_junction,
     )
 
-    def flip(value, mask):
-        return lax.ppermute(value, "head", [(i, i ^ mask) for i in range(heads)])
-
+    def flip(value, level):
+        return lax.ppermute(value, "head", [(i, i ^ 2**level) for i in range(heads)])
+
+    def fold(level, held, got):
+        count = heads // 2 ** (level + 1)
+        return local_call(
+            functools.partial(halve_body, level),
+            [((count,) + block, F32), ((count,) + block, BF16)],
+            operands=2,
+        )(held, got)
+
+    weight_got, sent = lax.optimization_barrier((swap_cores(weight_sent), sent))
     (term,) = local_call(total_body, [((rows, cut), BF16)], operands=2)(weight_held, weight_got)
     part = rows // chips
     tile = (part * 2 // intervals, cut // 2)
     (tiles,) = local_call(
         cut_body, [((intervals,) + tile, BF16)], operands=1, scratch=[pltpu.VMEM((part, cut), F32)]
     )(exchange(term.reshape(chips, part, cut), "x"))
-    tiles, got = lax.optimization_barrier((tiles, flip(sent, 1)))
-    held, *sent = local_call(
-        quarter_body, [(block, F32)] + [(block, BF16)] * (heads // 2 - 1), operands=2
-    )(held, got)
+    tiles, got = lax.optimization_barrier((tiles, flip(sent, 0)))
+    held, sent = fold(1, held, got)
+    got = flip(sent, 1)
     (copies,) = local_call(spread_body, [((intervals,) + tile, BF16)], operands=1)(
         exchange(tiles, "interval")
     )
     (term,) = local_call(
         join_body, [((part, cut), BF16)], operands=1, scratch=[pltpu.VMEM((part, cut), F32)]
     )(exchange(copies, "interval"))
-    got = [flip(value, 2 * (i + 1)) for i, value in enumerate(sent)]
-    term, *got = lax.optimization_barrier((term, *got))
+    term, got = lax.optimization_barrier((term, got))
+    held, sent = fold(2, held, got)
+    term, sent = lax.optimization_barrier((term, sent))
+    got = flip(sent, 2)
     term = lax.all_gather(term, "x", axis=0, tiled=True)
-    (grad_input,) = local_call(total_body, [(block, BF16)], operands=heads // 2)(held, *got)
+    term, got = lax.optimization_barrier((term, got))
+    (grad_input,) = local_call(total_body, [((1,) + block, BF16)], operands=2)(held, got)
+    grad_input = grad_input[0]
     grads = local_call(place_body, [((HD, width), BF16)] * 3, operands=2)(term, swap_cores(term))
     return (grad_input.T[None],) + tuple(grads)
 

time: 147 us -> 138 us (0.939)
  local copies, waits for them, and re-layouts: 5.99 us -> 0.03 us
  waiting for transfers between devices: 22.1 us -> 20.2 us
    ppermute x4 -> x3, waiting for transfers between devices: 13 us -> 2.35 us  [flip(): lax.ppermute(value, 'head', [(i, i ^ 2 ** level) for i in range(heads)])]
    all_to_all x2, waiting for transfers between devices: 2.99 us -> 12.8 us  [exchange(): return lax.all_to_all(value, axis, 0, 0, tiled=True)]
    unnamed x28 -> x12, local copies, waits for them, and re-layouts: 5.99 us -> 0.03 us
    ppermute x4, starting transfers between devices: 21.4 us -> 19.3 us  [swap_cores(): return lax.ppermute(value, 'core', [(0, 1), (1, 0)])]
    ppermute x4 -> x3, starting transfers between devices: 19 us -> 21 us  [flip(): lax.ppermute(value, 'head', [(i, i ^ 2 ** level) for i in range(heads)])]
  transfers between devices with their start and end apart: 10 -> 9, of which waited for: 8 -> 7; matrix products, arithmetic and copies ran while one was open for 0% -> 0% of each run, Pallas kernels for 3% -> 2%
where the time goes in v6:
time: 138 us
  blocking collectives  55.6 us (40%)
  starting transfers between devices  47.3 us (34%)
  waiting for transfers between devices  20.2 us (15%)
  Pallas kernels  13.7 us (10%)
    all_to_all x3, blocking collectives, exchange(): return lax.all_to_all(value, axis, 0, 0, tiled=True)  43.6 us
    ppermute x3, starting transfers between devices, flip(): lax.ppermute(value, 'head', [(i, i ^ 2 ** level) for i in range(heads)])  21 us
    ppermute x4, starting transfers between devices, swap_cores(): return lax.ppermute(value, 'core', [(0, 1), (1, 0)])  19.3 us
    all_to_all x2, waiting for transfers between devices, exchange(): return lax.all_to_all(value, axis, 0, 0, tiled=True)  12.8 us
    all_gather x1, blocking collectives, on_device(): term = lax.all_gather(term, 'x', axis=0, tiled=True)  11.9 us
    all_to_all x2, starting transfers between devices, exchange(): return lax.all_to_all(value, axis, 0, 0, tiled=True)  6.91 us
    ppermute x4, waiting for transfers between devices, swap_cores(): return lax.ppermute(value, 'core', [(0, 1), (1, 0)])  5 us
    pallas_call x1, Pallas kernels, on_device(): local_call(attend_body, [((chips, height, KV), BF16), ((chips, height - t...  3.5 us
  transfers between devices with their start and end apart: 9, of which 7 were waited for; matrix products, arithmetic and copies ran while one was open for 0% of the time, Pallas kernels for 2%

profile of v6, /device:TPU:1, one launch (start us, length us, event | category | flops | bytes accessed | tf_op | source)
XLA Modules:
  0.0 137.6 jit_solution(6695861426075828931)
XLA Ops:
  0.6 0.0 copy-start
  0.6 0.0 copy-start.1
  0.7 0.0 copy-start.5
  0.7 2.9 %shard_map.130 = (bf16[4,272,384]{2,1,0:T(8,128)(2,1)S(1)}, bf16[256,128]{1,0:T(8,128)(2,1)S(1)}, bf16[64,256]{1,0:T(8,128)(2,1)S(1)}) custom-call(bf16[256,1536]{1,0:T(8,128)(2,1)} %bitcast.14, bf16[192,1536]{1,0:T(8,128)(2,1)} %w_key.1, bf16[192,1536]{1,0:T(8,128)(2,1)} %w_value.1, bf16[1536,128]{1,0:T(8,128)(2,1)} %w_junction.1, s32[8,8]{1,0:T(8,128)} %bitcast.19, ...), custom_call_target="tpu_custom_call" | custom-call | tf_op jit(solution)/shard_map/pallas_call | solution.py:389
  3.6 13.2 %all_to_all.25.mine = bf16[4,272,384]{2,1,0:T(8,128)(2,1)S(1)} all-to-all(bf16[4,272,384]{2,1,0:T(8,128)(2,1)S(1)} %get-tuple-element.40), channel_id=1, replica_groups=mesh['interval'=8,'x'=4,'core'=2,'head'=8] {'x'}, dimensions={0} | all-to-all | bytes 1671168 | tf_op jit(solution)/shard_map/all_to_all | solution.py:364
  16.8 7.7 %collective-permute-start = (bf16[4,272,384]{2,1,0:T(8,128)(2,1)S(1)}, bf16[4,272,384]{2,1,0:T(8,128)(2,1)S(1)}, u32[]{:S(2)}, u32[]{:S(2)}) collective-permute-start(bf16[4,272,384]{2,1,0:T(8,128)(2,1)S(1)} %all_to_all.25.mine), channel_id=1, source_target_pairs={{0,8},{8,0},{1,9},{9,1},{2,10},{10,2},{3,11},{11,3},{4,12},{12,4},... | collective-permute-start | bytes 2506760 | tf_op jit(solution)/shard_map/ppermute | solution.py:360
  24.5 0.0 copy-done
  24.5 0.0 copy-done.1
  24.5 0.0 copy-done.5
  24.5 0.4 shard_map.129
  24.9 1.5 %collective-permute-done.theirs = bf16[4,272,384]{2,1,0:T(8,128)(2,1)S(1)} collective-permute-done((bf16[4,272,384]{2,1,0:T(8,128)(2,1)S(1)}, bf16[4,272,384]{2,1,0:T(8,128)(2,1)S(1)}, u32[]{:S(2)}, u32[]{:S(2)}) %collective-permute-start) | collective-permute-done | bytes 835616 | tf_op jit(solution)/shard_map/ppermute | solution.py:360
  26.5 3.5 %shard_map.131 = (bf16[4,272,384]{2,1,0:T(8,128)(2,1)S(1)}, bf16[4,16,128]{2,1,0:T(8,128)(2,1)S(1)}, f32[256,128]{1,0:T(8,128)S(1)}, bf16[2,256,1024]{2,1,0:T(8,128)(2,1)S(1)}, bf16[2,256,1024]{2,1,0:T(8,128)(2,1)S(1)}) custom-call(bf16[256,256]{1,0:T(8,128)(2,1)S(1)} %get-tuple-element.38.queries, bf16[256,256]{1,0:T(8,128)(2,1)S(1)} %get-tuple-element.39.ctx, ...), custom_call_target="tpu_custom_call" | custom-call | tf_op jit(solution)/shard_map/pallas_call | solution.py:424
  30.0 2.3 %collective-permute-start.1 = (bf16[4,272,384]{2,1,0:T(8,128)(2,1)S(1)}, bf16[4,272,384]{2,1,0:T(8,128)(2,1)S(1)}, u32[]{:S(2)}, u32[]{:S(2)}) collective-permute-start(bf16[4,272,384]{2,1,0:T(8,128)(2,1)S(1)} %get-tuple-element.46), channel_id=1, source_target_pairs={{0,8},{8,0},{1,9},{9,1},{2,10},{10,2},{3,11},{11,3},{4,12},{12,4},... | collective-permute-start | bytes 2506760 | tf_op jit(solution)/shard_map/ppermute | solution.py:360
  32.3 0.7 shard_map.132
  33.0 1.2 collective-permute-done.1.refs_1_
  34.2 0.2 shard_map.133
  34.4 0.0 copy-start.2
  34.4 0.0 copy-start.3
  34.4 0.0 copy-start.4
  34.5 14.8 %all_to_all.26.parts = bf16[4,272,384]{2,1,0:T(8,128)(2,1)S(1)} all-to-all(bf16[4,272,384]{2,1,0:T(8,128)(2,1)S(1)} %shard_map.133), channel_id=1, replica_groups=mesh['interval'=8,'x'=4,'core'=2,'head'=8] {'x'}, dimensions={0} | all-to-all | bytes 1671168 | tf_op jit(solution)/shard_map/all_to_all | solution.py:364
  49.3 0.7 shard_map.134
  49.9 3.4 %collective-permute-start.2 = (bf16[576,768]{1,0:T(8,128)(2,1)S(1)}, bf16[576,768]{1,0:T(8,128)(2,1)S(1)}, u32[]{:S(2)}, u32[]{:S(2)}) collective-permute-start(bf16[576,768]{1,0:T(8,128)(2,1)S(1)} %get-tuple-element.53), channel_id=1, source_target_pairs={{0,8},{8,0},{1,9},{9,1},{2,10},{10,2},{3,11},{11,3},{4,12},{12,4},... | collective-permute-start | bytes 2654216 | tf_op jit(solution)/shard_map/ppermute | solution.py:360
  53.3 0.0 copy-done.2
  53.3 0.0 copy-done.3
  53.4 0.0 copy-done.4
  53.4 1.1 shard_map.135
  54.5 0.9 collective-permute-done.2.refs_1_
  55.4 1.1 shard_map.136
  56.4 3.5 %all-to-all-start.2 = ((bf16[4,144,768]{2,1,0:T(8,128)(2,1)}), bf16[4,144,768]{2,1,0:T(8,128)(2,1)S(1)}, u32[]{:S(2)}, u32[]{:S(2)}) async-start(bf16[4,144,768]{2,1,0:T(8,128)(2,1)} %bitcast.7), calls=%async_computation.2 | async-start | bytes 1769472 | tf_op jit(solution)/shard_map/all_to_all | solution.py:364
  60.0 3.4 %collective-permute-start.3 = (bf16[4,192,256]{2,1,0:T(8,128)(2,1)S(1)}, bf16[4,192,256]{2,1,0:T(8,128)(2,1)S(1)}, u32[]{:S(2)}, u32[]{:S(2)}) collective-permute-start(bf16[4,192,256]{2,1,0:T(8,128)(2,1)S(1)} %get-tuple-element.56), channel_id=1, source_target_pairs={{0,1},{1,0},{2,3},{3,2},{4,5},{5,4},{6,7},{7,6},{8,9},{9,8},{10,11... | collective-permute-start | bytes 1179656 | tf_op jit(solution)/shard_map/ppermute | solution.py:468
  63.4 9.7 %all-to-all-done.2.parts = bf16[4,144,768]{2,1,0:T(8,128)(2,1)S(1)} async-done(((bf16[4,144,768]{2,1,0:T(8,128)(2,1)}), bf16[4,144,768]{2,1,0:T(8,128)(2,1)S(1)}, u32[]{:S(2)}, u32[]{:S(2)}) %all-to-all-start.2) | async-done | bytes 884768 | tf_op jit(solution)/shard_map/all_to_all | solution.py:364
  73.0 0.2 shard_map.137
  73.2 0.0 collective-permute-done.3.got
  73.2 15.6 %all_to_all.27.parts = bf16[8,36,384]{2,1,0:T(8,128)(2,1)S(1)} all-to-all(bf16[8,36,384]{2,1,0:T(8,128)(2,1)S(1)} %shard_map.137), channel_id=1, replica_groups=mesh['interval'=8,'x'=4,'core'=2,'head'=8] {'interval'}, dimensions={0} | all-to-all | bytes 442368 | tf_op jit(solution)/shard_map/all_to_all | solution.py:364
  88.8 0.7 shard_map.139
  89.5 3.4 %all-to-all-start.4 = ((bf16[8,36,384]{2,1,0:T(8,128)(2,1)}), bf16[8,36,384]{2,1,0:T(8,128)(2,1)S(1)}, u32[]{:S(2)}, u32[]{:S(2)}) async-start(bf16[8,36,384]{2,1,0:T(8,128)(2,1)} %shard_map.139), calls=%async_computation.4 | async-start | bytes 491520 | tf_op jit(solution)/shard_map/all_to_all | solution.py:364
  92.9 0.1 shard_map.138
  93.1 5.8 %collective-permute-start.4 = (bf16[2,192,256]{2,1,0:T(8,128)(2,1)S(1)}, bf16[2,192,256]{2,1,0:T(8,128)(2,1)S(1)}, u32[]{:S(2)}, u32[]{:S(2)}) collective-permute-start(bf16[2,192,256]{2,1,0:T(8,128)(2,1)S(1)} %get-tuple-element.60), channel_id=1, source_target_pairs={{0,2},{1,3},{2,0},{3,1},{4,6},{5,7},{6,4},{7,5},{8,10},{9,11},{10,... | collective-permute-start | bytes 589832 | tf_op jit(solution)/shard_map/ppermute | solution.py:468
  98.9 3.2 %all-to-all-done.4.tiles = bf16[8,36,384]{2,1,0:T(8,128)(2,1)S(1)} async-done(((bf16[8,36,384]{2,1,0:T(8,128)(2,1)}), bf16[8,36,384]{2,1,0:T(8,128)(2,1)S(1)}, u32[]{:S(2)}, u32[]{:S(2)}) %all-to-all-start.4) | async-done | bytes 221216 | tf_op jit(solution)/shard_map/all_to_all | solution.py:364
  102.1 2.3 %collective-permute-done.4.got = bf16[2,192,256]{2,1,0:T(8,128)(2,1)S(1)} collective-permute-done((bf16[2,192,256]{2,1,0:T(8,128)(2,1)S(1)}, bf16[2,192,256]{2,1,0:T(8,128)(2,1)S(1)}, u32[]{:S(2)}, u32[]{:S(2)}) %collective-permute-start.4) | collective-permute-done | bytes 196640 | tf_op jit(solution)/shard_map/ppermute | solution.py:468
  104.5 0.1 shard_map.141
  104.5 11.8 %collective-permute-start.5 = (bf16[1,192,256]{2,1,0:T(8,128)(2,1)S(1)}, bf16[1,192,256]{2,1,0:T(8,128)(2,1)S(1)}, u32[]{:S(2)}, u32[]{:S(2)}) collective-permute-start(bf16[1,192,256]{2,1,0:T(8,128)(2,1)S(1)} %get-tuple-element.66), channel_id=1, source_target_pairs={{0,4},{1,5},{2,6},{3,7},{4,0},{5,1},{6,2},{7,3},{8,12},{9,13},{10,... | collective-permute-start | bytes 294920 | tf_op jit(solution)/shard_map/ppermute | solution.py:468
  116.3 11.9 %all_gather.3.mine = bf16[576,768]{1,0:T(8,128)(2,1)S(1)} all-gather(bf16[144,768]{1,0:T(8,128)(2,1)S(1)} %shard_map.140), channel_id=1, replica_groups=mesh['interval'=8,'x'=4,'core'=2,'head'=8] {'x'}, dimensions={0}, use_global_device_ids=true | all-gather | bytes 1105920 | tf_op jit(solution)/shard_map/all_gather | solution.py:498
  128.3 0.0 collective-permute-done.5.refs_1_
  128.3 6.0 %collective-permute-start.6 = (bf16[576,768]{1,0:T(8,128)(2,1)S(1)}, bf16[576,768]{1,0:T(8,128)(2,1)S(1)}, u32[]{:S(2)}, u32[]{:S(2)}) collective-permute-start(bf16[576,768]{1,0:T(8,128)(2,1)S(1)} %all_gather.3.mine), channel_id=1, source_target_pairs={{0,8},{8,0},{1,9},{9,1},{2,10},{10,2},{3,11},{11,3},{4,12},{12,4},... | collective-permute-start | bytes 2654216 | tf_op jit(solution)/shard_map/ppermute | solution.py:360
  134.3 0.7 shard_map.142
  134.9 1.4 collective-permute-done.6.theirs
  136.3 1.3 shard_map.143
  (1 shorter events, 0.0 us)
Async XLA Ops:
  0.6 23.9 %copy-start = (bf16[1,256,1536]{2,1,0:T(8,128)(2,1)S(1)}, bf16[1,256,1536]{2,1,0:T(8,128)(2,1)}, u32[]{:S(2)}) copy-start(bf16[1,256,1536]{2,1,0:T(8,128)(2,1)} %param.10) | copy-start | bytes 2359300
  0.6 23.9 %copy-start.1 = (bf16[192,1536]{1,0:T(8,128)(2,1)S(1)}, bf16[192,1536]{1,0:T(8,128)(2,1)}, u32[]{:S(2)}) copy-start(bf16[192,1536]{1,0:T(8,128)(2,1)} %w_query.3) | copy-start | bytes 1769476
  0.7 23.9 %copy-start.5 = (bf16[1,256,192]{1,2,0:T(8,128)(2,1)S(1)}, bf16[1,256,192]{1,2,0:T(8,128)(2,1)}, u32[]{:S(2)}) copy-start(bf16[1,256,192]{1,2,0:T(8,128)(2,1)} %param.11) | copy-start | bytes 294916
  16.8 9.6 %collective-permute-start = (bf16[4,272,384]{2,1,0:T(8,128)(2,1)S(1)}, bf16[4,272,384]{2,1,0:T(8,128)(2,1)S(1)}, u32[]{:S(2)}, u32[]{:S(2)}) collective-permute-start(bf16[4,272,384]{2,1,0:T(8,128)(2,1)S(1)} %all_to_all.25.mine), channel_id=1, source_target_pairs={{0,8},{8,0},{1,9},{9,1},{2,10},{10,2},{3,11},{11,3},{4,12},{12,4},... | collective-permute-start | bytes 2506760 | tf_op jit(solution)/shard_map/ppermute | solution.py:360
  30.0 4.2 %collective-permute-start.1 = (bf16[4,272,384]{2,1,0:T(8,128)(2,1)S(1)}, bf16[4,272,384]{2,1,0:T(8,128)(2,1)S(1)}, u32[]{:S(2)}, u32[]{:S(2)}) collective-permute-start(bf16[4,272,384]{2,1,0:T(8,128)(2,1)S(1)} %get-tuple-element.46), channel_id=1, source_target_pairs={{0,8},{8,0},{1,9},{9,1},{2,10},{10,2},{3,11},{11,3},{4,12},{12,4},... | collective-permute-start | bytes 2506760 | tf_op jit(solution)/shard_map/ppermute | solution.py:360
  34.4 18.9 %copy-start.2 = (bf16[192,1536]{1,0:T(8,128)(2,1)S(1)}, bf16[192,1536]{1,0:T(8,128)(2,1)}, u32[]{:S(2)}) copy-start(bf16[192,1536]{1,0:T(8,128)(2,1)} %w_key.1) | copy-start | bytes 1769476
  34.4 18.9 %copy-start.3 = (bf16[192,1536]{1,0:T(8,128)(2,1)S(1)}, bf16[192,1536]{1,0:T(8,128)(2,1)}, u32[]{:S(2)}) copy-start(bf16[192,1536]{1,0:T(8,128)(2,1)} %w_value.1) | copy-start | bytes 1769476
  34.4 18.9 %copy-start.4 = (bf16[1536,128]{1,0:T(8,128)(2,1)S(1)}, bf16[1536,128]{1,0:T(8,128)(2,1)}, u32[]{:S(2)}) copy-start(bf16[1536,128]{1,0:T(8,128)(2,1)} %w_junction.1) | copy-start | bytes 1179652
  49.9 5.4 %collective-permute-start.2 = (bf16[576,768]{1,0:T(8,128)(2,1)S(1)}, bf16[576,768]{1,0:T(8,128)(2,1)S(1)}, u32[]{:S(2)}, u32[]{:S(2)}) collective-permute-start(bf16[576,768]{1,0:T(8,128)(2,1)S(1)} %get-tuple-element.53), channel_id=1, source_target_pairs={{0,8},{8,0},{1,9},{9,1},{2,10},{10,2},{3,11},{11,3},{4,12},{12,4},... | collective-permute-start | bytes 2654216 | tf_op jit(solution)/shard_map/ppermute | solution.py:360
  56.4 16.6 %all-to-all-start.2 = ((bf16[4,144,768]{2,1,0:T(8,128)(2,1)}), bf16[4,144,768]{2,1,0:T(8,128)(2,1)S(1)}, u32[]{:S(2)}, u32[]{:S(2)}) async-start(bf16[4,144,768]{2,1,0:T(8,128)(2,1)} %bitcast.7), calls=%async_computation.2 | async-start | bytes 1769472 | tf_op jit(solution)/shard_map/all_to_all | solution.py:364
  60.0 13.3 %collective-permute-start.3 = (bf16[4,192,256]{2,1,0:T(8,128)(2,1)S(1)}, bf16[4,192,256]{2,1,0:T(8,128)(2,1)S(1)}, u32[]{:S(2)}, u32[]{:S(2)}) collective-permute-start(bf16[4,192,256]{2,1,0:T(8,128)(2,1)S(1)} %get-tuple-element.56), channel_id=1, source_target_pairs={{0,1},{1,0},{2,3},{3,2},{4,5},{5,4},{6,7},{7,6},{8,9},{9,8},{10,11... | collective-permute-start | bytes 1179656 | tf_op jit(solution)/shard_map/ppermute | solution.py:468
  89.5 12.5 %all-to-all-start.4 = ((bf16[8,36,384]{2,1,0:T(8,128)(2,1)}), bf16[8,36,384]{2,1,0:T(8,128)(2,1)S(1)}, u32[]{:S(2)}, u32[]{:S(2)}) async-start(bf16[8,36,384]{2,1,0:T(8,128)(2,1)} %shard_map.139), calls=%async_computation.4 | async-start | bytes 491520 | tf_op jit(solution)/shard_map/all_to_all | solution.py:364
  93.1 11.4 %collective-permute-start.4 = (bf16[2,192,256]{2,1,0:T(8,128)(2,1)S(1)}, bf16[2,192,256]{2,1,0:T(8,128)(2,1)S(1)}, u32[]{:S(2)}, u32[]{:S(2)}) collective-permute-start(bf16[2,192,256]{2,1,0:T(8,128)(2,1)S(1)} %get-tuple-element.60), channel_id=1, source_target_pairs={{0,2},{1,3},{2,0},{3,1},{4,6},{5,7},{6,4},{7,5},{8,10},{9,11},{10,... | collective-permute-start | bytes 589832 | tf_op jit(solution)/shard_map/ppermute | solution.py:468
  104.5 23.8 %collective-permute-start.5 = (bf16[1,192,256]{2,1,0:T(8,128)(2,1)S(1)}, bf16[1,192,256]{2,1,0:T(8,128)(2,1)S(1)}, u32[]{:S(2)}, u32[]{:S(2)}) collective-permute-start(bf16[1,192,256]{2,1,0:T(8,128)(2,1)S(1)} %get-tuple-element.66), channel_id=1, source_target_pairs={{0,4},{1,5},{2,6},{3,7},{4,0},{5,1},{6,2},{7,3},{8,12},{9,13},{10,... | collective-permute-start | bytes 294920 | tf_op jit(solution)/shard_map/ppermute | solution.py:468
  128.3 8.0 %collective-permute-start.6 = (bf16[576,768]{1,0:T(8,128)(2,1)S(1)}, bf16[576,768]{1,0:T(8,128)(2,1)S(1)}, u32[]{:S(2)}, u32[]{:S(2)}) collective-permute-start(bf16[576,768]{1,0:T(8,128)(2,1)S(1)} %all_gather.3.mine), channel_id=1, source_target_pairs={{0,8},{8,0},{1,9},{9,1},{2,10},{10,2},{3,11},{11,3},{4,12},{12,4},... | collective-permute-start | bytes 2654216 | tf_op jit(solution)/shard_map/ppermute | solution.py:360

commit v7 on v5

--- a/solution.py
+++ b/solution.py
@@ -1,5 +1,3 @@
-import functools
-
 import jax
 import jax.numpy as jnp
 from jax import lax
@@ -16,7 +14,7 @@
 SHIFT = KV - LANES
 F32 = jnp.float32
 BF16 = jnp.bfloat16
-VMEM_BYTES = 48 * 1024 * 1024
+VMEM_BYTES = 20 * 1024 * 1024
 
 
 def contract(a, b, dim_a, dim_b, precision=None):
@@ -29,14 +27,14 @@
     return lax.broadcasted_iota(jnp.int32, shape, axis)
 
 
-def local_call(body, outs, operands, scratch=(), fetched=0):
+def local_call(body, outs, operands, scratch=(), fetched=0, space=pltpu.VMEM):
     specs = [pl.BlockSpec(memory_space=pltpu.HBM)] * fetched
-    specs += [pl.BlockSpec(memory_space=pltpu.VMEM)] * (operands - fetched)
+    specs += [pl.BlockSpec(memory_space=space)] * (operands - fetched)
     return pl.pallas_call(
         body,
         out_shape=tuple(jax.ShapeDtypeStruct(shape, kind) for shape, kind in outs),
         in_specs=specs,
-        out_specs=tuple(pl.BlockSpec(memory_space=pltpu.VMEM) for _ in outs),
+        out_specs=tuple(pl.BlockSpec(memory_space=space) for _ in outs),
         scratch_shapes=list(scratch),
         compiler_params=pltpu.CompilerParams(vmem_limit_bytes=VMEM_BYTES),
     )
@@ -73,24 +71,24 @@
     sems,
 ):
     targets = (
+        donor_pos,
+        acceptor_pos,
+        counts,
+        pred_grad,
         hidden,
         weights.at[pl.ds(0, HD)],
         weights.at[pl.ds(HD, HD)],
         w_junction,
-        donor_pos,
-        acceptor_pos,
-        counts,
-        pred_grad,
     )
     sources = (
+        donor_hbm,
+        acceptor_hbm,
+        counts_hbm,
+        pred_hbm,
         hidden_hbm,
         w_key_hbm,
         w_value_hbm,
         w_junction_hbm,
-        donor_hbm,
-        acceptor_hbm,
-        counts_hbm,
-        pred_hbm,
     )
     copies = [
         pltpu.make_async_copy(source, target, sems.at[i])
@@ -98,17 +96,10 @@
     ]
     for copy in copies:
         copy.start()
-    for copy in copies[:3]:
+    for copy in copies[:4]:
         copy.wait()
     chips = message.shape[0]
     tokens = hidden.shape[0]
-    x = hidden[...]
-    rows = contract(x, weights[...], 1, 1).astype(BF16)
-    for copy in copies[3:]:
-        copy.wait()
-    feats = contract(x, w_junction[...], 1, 0).astype(BF16)
-    features[...] = feats
-
     buckets, per = donor_pos.shape
     slots = buckets * per
     square = iota((buckets, buckets), 0) == iota((buckets, buckets), 1)
@@ -133,6 +124,12 @@
     extra = jnp.zeros((slots, PJ), F32)
     for i, column in enumerate(scalars):
         extra = jnp.where(lane == i, column, extra)
+    for copy in copies[4:]:
+        copy.wait()
+    x = hidden[...]
+    rows = contract(x, weights[...], 1, 1).astype(BF16)
+    feats = contract(x, w_junction[...], 1, 0).astype(BF16)
+    features[...] = feats
     slot_rows = jnp.concatenate(
         [
             contract(hot, feats, 1, 0).astype(BF16),
@@ -256,22 +253,27 @@
     query_grad[...] = (total[:, :HD] * HD ** (-0.5)).astype(BF16)
 
 
-def halve(value, kept, sent, index):
-    count = kept.shape[0]
-    blocks = value.reshape((count, 2) + kept.shape[1:])
+def halve(value, index):
+    blocks = value.reshape((value.shape[0] // 2, 2) + value.shape[1:])
     odd = lax.rem(index, 2) == 1
-    kept[...] = jnp.where(odd, blocks[:, 1], blocks[:, 0])
-    sent[...] = jnp.where(odd, blocks[:, 0], blocks[:, 1]).astype(sent.dtype)
-
-
-def quarter_body(held, got, *outs):
-    place = lax.axis_index("head") // 2
-    value = held[...] + got[...].astype(F32)
-    for i, out in enumerate(outs):
-        block = value[i]
-        for other in range(1, len(outs)):
-            block = jnp.where(place == other, value[i ^ other], block)
-        out[...] = block.astype(out.dtype)
+    kept = jnp.where(odd, blocks[:, 1], blocks[:, 0])
+    sent = jnp.where(odd, blocks[:, 0], blocks[:, 1])
+    return kept, sent.astype(BF16)
+
+
+def second_body(held, got, kept, near, far):
+    value, sent = halve(held[...] + got[...].astype(F32), lax.axis_index("head") // 2)
+    kept[...] = value
+    side = near.shape[-1]
+    near[...] = sent[:, :, :side]
+    far[...] = sent[:, :, side:]
+
+
+def third_body(held, near, far, kept, sent):
+    got = jnp.concatenate([near[...], far[...]], axis=2).astype(F32)
+    value, leaving = halve(held[...] + got, lax.axis_index("head") // 4)
+    kept[...] = value[0]
+    sent[...] = leaving[0]
 
 
 def total_body(*refs):
@@ -321,7 +323,8 @@
     value = value + contract(w_key[...], grads[:, :HD], 0, 1)
     value = value + contract(w_value[...], grads[:, HD:], 0, 1)
     value = value + contract(w_junction[...], feature_grad, 1, 1)
-    halve(value, kept, sent, lax.axis_index("head"))
+    blocks = value.reshape((2 * kept.shape[0],) + kept.shape[1:])
+    kept[...], sent[...] = halve(blocks, lax.axis_index("head"))
 
 
 def tiles_of(rows, columns, count):
@@ -353,13 +356,23 @@
     joined[...] = whole[...].astype(BF16)
 
 
-def place_body(mine, theirs, *outs):
+def place_body(mine, theirs, *refs):
+    outs, sems = refs[:-1], refs[-1]
     core = lax.axis_index("core")
     cut = mine.shape[1]
+    copies = []
     for i, out in enumerate(outs):
-        a, b = mine[i * HD : (i + 1) * HD, :], theirs[i * HD : (i + 1) * HD, :]
-        out[:, :cut] = jnp.where(core == 0, a, b)
-        out[:, cut:] = jnp.where(core == 0, b, a)
+        for j, (source, place) in enumerate(((mine, core), (theirs, 1 - core))):
+            columns = pl.ds(pl.multiple_of(place * cut, cut), cut)
+            copies.append(
+                pltpu.make_async_copy(
+                    source.at[pl.ds(i * HD, HD)], out.at[:, columns], sems.at[2 * i + j]
+                )
+            )
+    for copy in copies:
+        copy.start()
+    for copy in copies:
+        copy.wait()
 
 
 def swap_cores(value):
@@ -454,7 +467,6 @@
         [((tokens, KV), BF16), ((rows, cut), F32), ((rows, cut), BF16)],
         operands=3,
     )(parts, query_grad, hidden)
-    weight_got = swap_cores(weight_sent)
     held, sent = local_call(
         input_body,
         [((heads // 2,) + block, F32), ((heads // 2,) + block, BF16)],
@@ -474,6 +486,7 @@
     def flip(value, mask):
         return lax.ppermute(value, "head", [(i, i ^ mask) for i in range(heads)])
 
+    weight_got, sent = lax.optimization_barrier((swap_cores(weight_sent), sent))
     (term,) = local_call(total_body, [((rows, cut), BF16)], operands=2)(weight_held, weight_got)
     part = rows // chips
     tile = (part * 2 // intervals, cut // 2)
@@ -481,20 +494,33 @@
         cut_body, [((intervals,) + tile, BF16)], operands=1, scratch=[pltpu.VMEM((part, cut), F32)]
     )(exchange(term.reshape(chips, part, cut), "x"))
     tiles, got = lax.optimization_barrier((tiles, flip(sent, 1)))
-    held, *sent = local_call(
-        quarter_body, [(block, F32)] + [(block, BF16)] * (heads // 2 - 1), operands=2
+    side = tokens // 2
+    held, near, far = local_call(
+        second_body,
+        [((heads // 4,) + block, F32)] + [((heads // 4, block[0], side), BF16)] * 2,
+        operands=2,
     )(held, got)
+    got = (flip(near, 2), flip(far, 6))
     (copies,) = local_call(spread_body, [((intervals,) + tile, BF16)], operands=1)(
         exchange(tiles, "interval")
     )
     (term,) = local_call(
         join_body, [((part, cut), BF16)], operands=1, scratch=[pltpu.VMEM((part, cut), F32)]
     )(exchange(copies, "interval"))
-    got = [flip(value, 2 * (i + 1)) for i, value in enumerate(sent)]
     term, *got = lax.optimization_barrier((term, *got))
+    held, sent = local_call(third_body, [(block, F32), (block, BF16)], operands=3)(held, *got)
+    term, sent = lax.optimization_barrier((term, sent))
+    got = flip(sent, 4)
     term = lax.all_gather(term, "x", axis=0, tiled=True)
-    (grad_input,) = local_call(total_body, [(block, BF16)], operands=heads // 2)(held, *got)
-    grads = local_call(place_body, [((HD, width), BF16)] * 3, operands=2)(term, swap_cores(term))
+    term, got = lax.optimization_barrier((term, got))
+    (grad_input,) = local_call(total_body, [(block, BF16)], operands=2)(held, got)
+    grads = local_call(
+        place_body,
+        [((HD, width), BF16)] * 3,
+        operands=2,
+        scratch=[pltpu.SemaphoreType.DMA((2 * 3,))],
+        space=pl.ANY,
+    )(term, swap_cores(term))
     return (grad_input.T[None],) + tuple(grads)
 
 

time: 147 us -> 140 us (0.952)
  local copies, waits for them, and re-layouts: 5.99 us -> 0.03 us
  starting transfers between devices: 47.4 us -> 52 us
  waiting for transfers between devices: 22.1 us -> 17.6 us
    ppermute x4, waiting for transfers between devices: 13 us -> 2.98 us  [flip(): return lax.ppermute(value, 'head', [(i, i ^ mask) for i in range(heads)])]
    all_to_all x2, waiting for transfers between devices: 2.99 us -> 9.66 us  [exchange(): return lax.all_to_all(value, axis, 0, 0, tiled=True)]
    unnamed x28 -> x12, local copies, waits for them, and re-layouts: 5.99 us -> 0.03 us
    ppermute x4, starting transfers between devices: 19 us -> 22.8 us  [flip(): return lax.ppermute(value, 'head', [(i, i ^ mask) for i in range(heads)])]
  transfers between devices with their start and end apart: 10 -> 10, of which waited for: 8 -> 6; matrix products, arithmetic and copies ran while one was open for 0% -> 0% of each run, Pallas kernels for 3% -> 2%
where the time goes in v7:
time: 140 us; the launch traced here: 139 us
  blocking collectives  55.1 us (39%)
  starting transfers between devices  52 us (37%)
  waiting for transfers between devices  17.6 us (13%)
  Pallas kernels  13.5 us (10%)
    all_to_all x3, blocking collectives, exchange(): return lax.all_to_all(value, axis, 0, 0, tiled=True)  43.6 us
    ppermute x4, starting transfers between devices, flip(): return lax.ppermute(value, 'head', [(i, i ^ mask) for i in range(heads)])  22.8 us
    ppermute x4, starting transfers between devices, swap_cores(): return lax.ppermute(value, 'core', [(0, 1), (1, 0)])  22.3 us
    all_gather x1, blocking collectives, on_device(): term = lax.all_gather(term, 'x', axis=0, tiled=True)  11.5 us
    all_to_all x2, waiting for transfers between devices, exchange(): return lax.all_to_all(value, axis, 0, 0, tiled=True)  9.66 us
    all_to_all x2, starting transfers between devices, exchange(): return lax.all_to_all(value, axis, 0, 0, tiled=True)  6.91 us
    ppermute x4, waiting for transfers between devices, swap_cores(): return lax.ppermute(value, 'core', [(0, 1), (1, 0)])  5 us
    pallas_call x1, Pallas kernels, on_device(): local_call(attend_body, [((chips, height, KV), BF16), ((chips, height - t...  3.5 us
  transfers between devices with their start and end apart: 10, of which 6 were waited for; matrix products, arithmetic and copies ran while one was open for 0% of the time, Pallas kernels for 2%

profile of v7, /device:TPU:1, one launch (start us, length us, event | category | flops | bytes accessed | tf_op | source)
XLA Modules:
  0.0 139.2 jit_solution(446532737201313374)
XLA Ops:
  0.6 0.0 copy-start
  0.6 0.0 copy-start.1
  0.7 0.0 copy-start.5
  0.7 2.8 %shard_map.130 = (bf16[4,272,384]{2,1,0:T(8,128)(2,1)S(1)}, bf16[256,128]{1,0:T(8,128)(2,1)S(1)}, bf16[64,256]{1,0:T(8,128)(2,1)S(1)}) custom-call(bf16[256,1536]{1,0:T(8,128)(2,1)} %bitcast.12, bf16[192,1536]{1,0:T(8,128)(2,1)} %w_key.1, bf16[192,1536]{1,0:T(8,128)(2,1)} %w_value.1, bf16[1536,128]{1,0:T(8,128)(2,1)} %w_junction.1, s32[8,8]{1,0:T(8,128)} %bitcast.17, ...), custom_call_target="tpu_custom_call" | custom-call | tf_op jit(solution)/shard_map/pallas_call | solution.py:408
  3.4 13.2 %all_to_all.25.mine = bf16[4,272,384]{2,1,0:T(8,128)(2,1)S(1)} all-to-all(bf16[4,272,384]{2,1,0:T(8,128)(2,1)S(1)} %get-tuple-element.42), channel_id=1, replica_groups=mesh['interval'=8,'x'=4,'core'=2,'head'=8] {'x'}, dimensions={0} | all-to-all | bytes 1671168 | tf_op jit(solution)/shard_map/all_to_all | solution.py:383
  16.7 7.7 %collective-permute-start = (bf16[4,272,384]{2,1,0:T(8,128)(2,1)S(1)}, bf16[4,272,384]{2,1,0:T(8,128)(2,1)S(1)}, u32[]{:S(2)}, u32[]{:S(2)}) collective-permute-start(bf16[4,272,384]{2,1,0:T(8,128)(2,1)S(1)} %all_to_all.25.mine), channel_id=1, source_target_pairs={{0,8},{8,0},{1,9},{9,1},{2,10},{10,2},{3,11},{11,3},{4,12},{12,4},... | collective-permute-start | bytes 2506760 | tf_op jit(solution)/shard_map/ppermute | solution.py:379
  24.4 0.0 copy-done
  24.4 0.0 copy-done.1
  24.4 0.0 copy-done.5
  24.4 0.4 shard_map.129
  24.8 1.5 %collective-permute-done.theirs = bf16[4,272,384]{2,1,0:T(8,128)(2,1)S(1)} collective-permute-done((bf16[4,272,384]{2,1,0:T(8,128)(2,1)S(1)}, bf16[4,272,384]{2,1,0:T(8,128)(2,1)S(1)}, u32[]{:S(2)}, u32[]{:S(2)}) %collective-permute-start) | collective-permute-done | bytes 835616 | tf_op jit(solution)/shard_map/ppermute | solution.py:379
  26.3 3.5 %shard_map.131 = (bf16[4,272,384]{2,1,0:T(8,128)(2,1)S(1)}, bf16[4,16,128]{2,1,0:T(8,128)(2,1)S(1)}, f32[256,128]{1,0:T(8,128)S(1)}, bf16[2,256,1024]{2,1,0:T(8,128)(2,1)S(1)}, bf16[2,256,1024]{2,1,0:T(8,128)(2,1)S(1)}) custom-call(bf16[256,256]{1,0:T(8,128)(2,1)S(1)} %get-tuple-element.40.queries, bf16[256,256]{1,0:T(8,128)(2,1)S(1)} %get-tuple-element.41.ctx, ...), custom_call_target="tpu_custom_call" | custom-call | tf_op jit(solution)/shard_map/pallas_call | solution.py:443
  29.8 2.3 %collective-permute-start.1 = (bf16[4,272,384]{2,1,0:T(8,128)(2,1)S(1)}, bf16[4,272,384]{2,1,0:T(8,128)(2,1)S(1)}, u32[]{:S(2)}, u32[]{:S(2)}) collective-permute-start(bf16[4,272,384]{2,1,0:T(8,128)(2,1)S(1)} %get-tuple-element.48), channel_id=1, source_target_pairs={{0,8},{8,0},{1,9},{9,1},{2,10},{10,2},{3,11},{11,3},{4,12},{12,4},... | collective-permute-start | bytes 2506760 | tf_op jit(solution)/shard_map/ppermute | solution.py:379
  32.1 0.7 shard_map.132
  32.9 1.2 collective-permute-done.1.refs_1_
  34.1 0.2 shard_map.133
  34.3 0.0 copy-start.2
  34.3 0.0 copy-start.3
  34.3 0.0 copy-start.4
  34.3 14.8 %all_to_all.26.parts = bf16[4,272,384]{2,1,0:T(8,128)(2,1)S(1)} all-to-all(bf16[4,272,384]{2,1,0:T(8,128)(2,1)S(1)} %shard_map.133), channel_id=1, replica_groups=mesh['interval'=8,'x'=4,'core'=2,'head'=8] {'x'}, dimensions={0} | all-to-all | bytes 1671168 | tf_op jit(solution)/shard_map/all_to_all | solution.py:383
  49.1 0.7 shard_map.134
  49.8 3.4 %collective-permute-start.2 = (bf16[576,768]{1,0:T(8,128)(2,1)S(1)}, bf16[576,768]{1,0:T(8,128)(2,1)S(1)}, u32[]{:S(2)}, u32[]{:S(2)}) collective-permute-start(bf16[576,768]{1,0:T(8,128)(2,1)S(1)} %get-tuple-element.55), channel_id=1, source_target_pairs={{0,8},{8,0},{1,9},{9,1},{2,10},{10,2},{3,11},{11,3},{4,12},{12,4},... | collective-permute-start | bytes 2654216 | tf_op jit(solution)/shard_map/ppermute | solution.py:379
  53.2 0.0 copy-done.2
  53.2 0.0 copy-done.3
  53.2 0.0 copy-done.4
  53.2 1.1 shard_map.135
  54.4 0.9 collective-permute-done.2.refs_1_
  55.2 1.1 shard_map.136
  56.3 3.5 %all-to-all-start.2 = ((bf16[4,144,768]{2,1,0:T(8,128)(2,1)}), bf16[4,144,768]{2,1,0:T(8,128)(2,1)S(1)}, u32[]{:S(2)}, u32[]{:S(2)}) async-start(bf16[4,144,768]{2,1,0:T(8,128)(2,1)} %bitcast.7), calls=%async_computation.2 | async-start | bytes 1769472 | tf_op jit(solution)/shard_map/all_to_all | solution.py:383
  59.8 3.4 %collective-permute-start.3 = (bf16[4,192,256]{2,1,0:T(8,128)(2,1)S(1)}, bf16[4,192,256]{2,1,0:T(8,128)(2,1)S(1)}, u32[]{:S(2)}, u32[]{:S(2)}) collective-permute-start(bf16[4,192,256]{2,1,0:T(8,128)(2,1)S(1)} %get-tuple-element.58), channel_id=1, source_target_pairs={{0,1},{1,0},{2,3},{3,2},{4,5},{5,4},{6,7},{7,6},{8,9},{9,8},{10,11... | collective-permute-start | bytes 1179656 | tf_op jit(solution)/shard_map/ppermute | solution.py:487
  63.2 9.7 %all-to-all-done.2.parts = bf16[4,144,768]{2,1,0:T(8,128)(2,1)S(1)} async-done(((bf16[4,144,768]{2,1,0:T(8,128)(2,1)}), bf16[4,144,768]{2,1,0:T(8,128)(2,1)S(1)}, u32[]{:S(2)}, u32[]{:S(2)}) %all-to-all-start.2) | async-done | bytes 884768 | tf_op jit(solution)/shard_map/all_to_all | solution.py:383
  72.9 0.2 shard_map.137
  73.1 0.0 collective-permute-done.3.got
  73.1 15.6 %all_to_all.27.parts = bf16[8,36,384]{2,1,0:T(8,128)(2,1)S(1)} all-to-all(bf16[8,36,384]{2,1,0:T(8,128)(2,1)S(1)} %shard_map.137), channel_id=1, replica_groups=mesh['interval'=8,'x'=4,'core'=2,'head'=8] {'interval'}, dimensions={0} | all-to-all | bytes 442368 | tf_op jit(solution)/shard_map/all_to_all | solution.py:383
  88.6 0.7 shard_map.139
  89.4 3.4 %all-to-all-start.4 = ((bf16[8,36,384]{2,1,0:T(8,128)(2,1)}), bf16[8,36,384]{2,1,0:T(8,128)(2,1)S(1)}, u32[]{:S(2)}, u32[]{:S(2)}) async-start(bf16[8,36,384]{2,1,0:T(8,128)(2,1)} %shard_map.139), calls=%async_computation.4 | async-start | bytes 491520 | tf_op jit(solution)/shard_map/all_to_all | solution.py:383
  92.8 0.1 shard_map.138
  92.9 5.8 %collective-permute-start.4 = (bf16[2,192,128]{2,1,0:T(8,128)(2,1)S(1)}, bf16[2,192,128]{2,1,0:T(8,128)(2,1)S(1)}, u32[]{:S(2)}, u32[]{:S(2)}) collective-permute-start(bf16[2,192,128]{2,1,0:T(8,128)(2,1)S(1)} %get-tuple-element.62), channel_id=1, source_target_pairs={{0,2},{1,3},{2,0},{3,1},{4,6},{5,7},{6,4},{7,5},{8,10},{9,11},{10,... | collective-permute-start | bytes 294920 | tf_op jit(solution)/shard_map/ppermute | solution.py:487
  98.7 7.0 %collective-permute-start.5 = (bf16[2,192,128]{2,1,0:T(8,128)(2,1)S(1)}, bf16[2,192,128]{2,1,0:T(8,128)(2,1)S(1)}, u32[]{:S(2)}, u32[]{:S(2)}) collective-permute-start(bf16[2,192,128]{2,1,0:T(8,128)(2,1)S(1)} %get-tuple-element.63), channel_id=1, source_target_pairs={{0,6},{1,7},{2,4},{3,5},{4,2},{5,3},{6,0},{7,1},{8,14},{9,15},{10,... | collective-permute-start | bytes 294920 | tf_op jit(solution)/shard_map/ppermute | solution.py:487
  105.8 0.0 all-to-all-done.4.tiles
  105.8 0.0 collective-permute-done.4.near
  105.8 3.0 %collective-permute-done.5.far = bf16[2,192,128]{2,1,0:T(8,128)(2,1)S(1)} collective-permute-done((bf16[2,192,128]{2,1,0:T(8,128)(2,1)S(1)}, bf16[2,192,128]{2,1,0:T(8,128)(2,1)S(1)}, u32[]{:S(2)}, u32[]{:S(2)}) %collective-permute-start.5) | collective-permute-done | bytes 98336 | tf_op jit(solution)/shard_map/ppermute | solution.py:487
  108.9 6.5 %collective-permute-start.6 = (bf16[192,256]{1,0:T(8,128)(2,1)S(1)}, bf16[192,256]{1,0:T(8,128)(2,1)S(1)}, u32[]{:S(2)}, u32[]{:S(2)}) collective-permute-start(bf16[192,256]{1,0:T(8,128)(2,1)S(1)} %get-tuple-element.70), channel_id=1, source_target_pairs={{0,4},{1,5},{2,6},{3,7},{4,0},{5,1},{6,2},{7,3},{8,12},{9,13},{10,... | collective-permute-start | bytes 294920 | tf_op jit(solution)/shard_map/ppermute | solution.py:487
  115.4 11.5 %all_gather.3.mine = bf16[576,768]{1,0:T(8,128)(2,1)S(1)} all-gather(bf16[144,768]{1,0:T(8,128)(2,1)S(1)} %shard_map.140), channel_id=1, replica_groups=mesh['interval'=8,'x'=4,'core'=2,'head'=8] {'x'}, dimensions={0}, use_global_device_ids=true | all-gather | bytes 1105920 | tf_op jit(solution)/shard_map/all_gather | solution.py:514
  126.9 0.0 collective-permute-done.6.refs_1_
  126.9 9.0 %collective-permute-start.7 = (bf16[576,768]{1,0:T(8,128)(2,1)S(1)}, bf16[576,768]{1,0:T(8,128)(2,1)S(1)}, u32[]{:S(2)}, u32[]{:S(2)}) collective-permute-start(bf16[576,768]{1,0:T(8,128)(2,1)S(1)} %all_gather.3.mine), channel_id=1, source_target_pairs={{0,8},{8,0},{1,9},{9,1},{2,10},{10,2},{3,11},{11,3},{4,12},{12,4},... | collective-permute-start | bytes 2654216 | tf_op jit(solution)/shard_map/ppermute | solution.py:379
  135.9 0.7 shard_map.142
  136.6 1.4 collective-permute-done.7.theirs
  138.0 1.2 shard_map.143
  (2 shorter events, 0.1 us)
Async XLA Ops:
  0.6 23.7 %copy-start = (bf16[1,256,1536]{2,1,0:T(8,128)(2,1)S(1)}, bf16[1,256,1536]{2,1,0:T(8,128)(2,1)}, u32[]{:S(2)}) copy-start(bf16[1,256,1536]{2,1,0:T(8,128)(2,1)} %param.10) | copy-start | bytes 2359300
  0.6 23.7 %copy-start.1 = (bf16[192,1536]{1,0:T(8,128)(2,1)S(1)}, bf16[192,1536]{1,0:T(8,128)(2,1)}, u32[]{:S(2)}) copy-start(bf16[192,1536]{1,0:T(8,128)(2,1)} %w_query.3) | copy-start | bytes 1769476
  0.7 23.7 %copy-start.5 = (bf16[1,256,192]{1,2,0:T(8,128)(2,1)S(1)}, bf16[1,256,192]{1,2,0:T(8,128)(2,1)}, u32[]{:S(2)}) copy-start(bf16[1,256,192]{1,2,0:T(8,128)(2,1)} %param.11) | copy-start | bytes 294916
  16.7 9.6 %collective-permute-start = (bf16[4,272,384]{2,1,0:T(8,128)(2,1)S(1)}, bf16[4,272,384]{2,1,0:T(8,128)(2,1)S(1)}, u32[]{:S(2)}, u32[]{:S(2)}) collective-permute-start(bf16[4,272,384]{2,1,0:T(8,128)(2,1)S(1)} %all_to_all.25.mine), channel_id=1, source_target_pairs={{0,8},{8,0},{1,9},{9,1},{2,10},{10,2},{3,11},{11,3},{4,12},{12,4},... | collective-permute-start | bytes 2506760 | tf_op jit(solution)/shard_map/ppermute | solution.py:379
  29.8 4.2 %collective-permute-start.1 = (bf16[4,272,384]{2,1,0:T(8,128)(2,1)S(1)}, bf16[4,272,384]{2,1,0:T(8,128)(2,1)S(1)}, u32[]{:S(2)}, u32[]{:S(2)}) collective-permute-start(bf16[4,272,384]{2,1,0:T(8,128)(2,1)S(1)} %get-tuple-element.48), channel_id=1, source_target_pairs={{0,8},{8,0},{1,9},{9,1},{2,10},{10,2},{3,11},{11,3},{4,12},{12,4},... | collective-permute-start | bytes 2506760 | tf_op jit(solution)/shard_map/ppermute | solution.py:379
  34.3 18.9 %copy-start.2 = (bf16[192,1536]{1,0:T(8,128)(2,1)S(1)}, bf16[192,1536]{1,0:T(8,128)(2,1)}, u32[]{:S(2)}) copy-start(bf16[192,1536]{1,0:T(8,128)(2,1)} %w_key.1) | copy-start | bytes 1769476
  34.3 18.9 %copy-start.3 = (bf16[192,1536]{1,0:T(8,128)(2,1)S(1)}, bf16[192,1536]{1,0:T(8,128)(2,1)}, u32[]{:S(2)}) copy-start(bf16[192,1536]{1,0:T(8,128)(2,1)} %w_value.1) | copy-start | bytes 1769476
  34.3 18.9 %copy-start.4 = (bf16[1536,128]{1,0:T(8,128)(2,1)S(1)}, bf16[1536,128]{1,0:T(8,128)(2,1)}, u32[]{:S(2)}) copy-start(bf16[1536,128]{1,0:T(8,128)(2,1)} %w_junction.1) | copy-start | bytes 1179652
  49.8 5.4 %collective-permute-start.2 = (bf16[576,768]{1,0:T(8,128)(2,1)S(1)}, bf16[576,768]{1,0:T(8,128)(2,1)S(1)}, u32[]{:S(2)}, u32[]{:S(2)}) collective-permute-start(bf16[576,768]{1,0:T(8,128)(2,1)S(1)} %get-tuple-element.55), channel_id=1, source_target_pairs={{0,8},{8,0},{1,9},{9,1},{2,10},{10,2},{3,11},{11,3},{4,12},{12,4},... | collective-permute-start | bytes 2654216 | tf_op jit(solution)/shard_map/ppermute | solution.py:379
  56.3 16.6 %all-to-all-start.2 = ((bf16[4,144,768]{2,1,0:T(8,128)(2,1)}), bf16[4,144,768]{2,1,0:T(8,128)(2,1)S(1)}, u32[]{:S(2)}, u32[]{:S(2)}) async-start(bf16[4,144,768]{2,1,0:T(8,128)(2,1)} %bitcast.7), calls=%async_computation.2 | async-start | bytes 1769472 | tf_op jit(solution)/shard_map/all_to_all | solution.py:383
  59.8 13.3 %collective-permute-start.3 = (bf16[4,192,256]{2,1,0:T(8,128)(2,1)S(1)}, bf16[4,192,256]{2,1,0:T(8,128)(2,1)S(1)}, u32[]{:S(2)}, u32[]{:S(2)}) collective-permute-start(bf16[4,192,256]{2,1,0:T(8,128)(2,1)S(1)} %get-tuple-element.58), channel_id=1, source_target_pairs={{0,1},{1,0},{2,3},{3,2},{4,5},{5,4},{6,7},{7,6},{8,9},{9,8},{10,11... | collective-permute-start | bytes 1179656 | tf_op jit(solution)/shard_map/ppermute | solution.py:487
  89.4 16.4 %all-to-all-start.4 = ((bf16[8,36,384]{2,1,0:T(8,128)(2,1)}), bf16[8,36,384]{2,1,0:T(8,128)(2,1)S(1)}, u32[]{:S(2)}, u32[]{:S(2)}) async-start(bf16[8,36,384]{2,1,0:T(8,128)(2,1)} %shard_map.139), calls=%async_computation.4 | async-start | bytes 491520 | tf_op jit(solution)/shard_map/all_to_all | solution.py:383
  92.9 12.9 %collective-permute-start.4 = (bf16[2,192,128]{2,1,0:T(8,128)(2,1)S(1)}, bf16[2,192,128]{2,1,0:T(8,128)(2,1)S(1)}, u32[]{:S(2)}, u32[]{:S(2)}) collective-permute-start(bf16[2,192,128]{2,1,0:T(8,128)(2,1)S(1)} %get-tuple-element.62), channel_id=1, source_target_pairs={{0,2},{1,3},{2,0},{3,1},{4,6},{5,7},{6,4},{7,5},{8,10},{9,11},{10,... | collective-permute-start | bytes 294920 | tf_op jit(solution)/shard_map/ppermute | solution.py:487
  98.7 10.1 %collective-permute-start.5 = (bf16[2,192,128]{2,1,0:T(8,128)(2,1)S(1)}, bf16[2,192,128]{2,1,0:T(8,128)(2,1)S(1)}, u32[]{:S(2)}, u32[]{:S(2)}) collective-permute-start(bf16[2,192,128]{2,1,0:T(8,128)(2,1)S(1)} %get-tuple-element.63), channel_id=1, source_target_pairs={{0,6},{1,7},{2,4},{3,5},{4,2},{5,3},{6,0},{7,1},{8,14},{9,15},{10,... | collective-permute-start | bytes 294920 | tf_op jit(solution)/shard_map/ppermute | solution.py:487
  108.9 18.1 %collective-permute-start.6 = (bf16[192,256]{1,0:T(8,128)(2,1)S(1)}, bf16[192,256]{1,0:T(8,128)(2,1)S(1)}, u32[]{:S(2)}, u32[]{:S(2)}) collective-permute-start(bf16[192,256]{1,0:T(8,128)(2,1)S(1)} %get-tuple-element.70), channel_id=1, source_target_pairs={{0,4},{1,5},{2,6},{3,7},{4,0},{5,1},{6,2},{7,3},{8,12},{9,13},{10,... | collective-permute-start | bytes 294920 | tf_op jit(solution)/shard_map/ppermute | solution.py:487
  126.9 11.0 %collective-permute-start.7 = (bf16[576,768]{1,0:T(8,128)(2,1)S(1)}, bf16[576,768]{1,0:T(8,128)(2,1)S(1)}, u32[]{:S(2)}, u32[]{:S(2)}) collective-permute-start(bf16[576,768]{1,0:T(8,128)(2,1)S(1)} %all_gather.3.mine), channel_id=1, source_target_pairs={{0,8},{8,0},{1,9},{9,1},{2,10},{10,2},{3,11},{11,3},{4,12},{12,4},... | collective-permute-start | bytes 2654216 | tf_op jit(solution)/shard_map/ppermute | solution.py:379

commit v8 on v7

--- a/solution.py
+++ b/solution.py
@@ -9,6 +9,7 @@
 HD = 192
 PJ = 128
 CORES = 2
+SIDES = 2
 LANES = 256
 KV = 2 * HD
 SHIFT = KV - LANES
@@ -106,7 +107,8 @@
     limit = jnp.sum(
         jnp.where(square, counts[...].astype(F32), 0.0), axis=1, keepdims=True
     )
-    slot_ids = lax.axis_index("head") * per + iota((buckets, per), 1)
+    head = lax.axis_index("pair") * SIDES + lax.axis_index("side")
+    slot_ids = head * per + iota((buckets, per), 1)
     live_grad = jnp.where(slot_ids.astype(F32) < limit, pred_grad[...], 0.0)
     pick_bucket = (iota((slots, buckets), 0) // per == iota((slots, buckets), 1)).astype(F32)
     own_slot = iota((slots, per), 0) % per == iota((slots, per), 1)
@@ -253,27 +255,12 @@
     query_grad[...] = (total[:, :HD] * HD ** (-0.5)).astype(BF16)
 
 
-def halve(value, index):
+def halve(value, side):
     blocks = value.reshape((value.shape[0] // 2, 2) + value.shape[1:])
-    odd = lax.rem(index, 2) == 1
+    odd = side == 1
     kept = jnp.where(odd, blocks[:, 1], blocks[:, 0])
     sent = jnp.where(odd, blocks[:, 0], blocks[:, 1])
     return kept, sent.astype(BF16)
-
-
-def second_body(held, got, kept, near, far):
-    value, sent = halve(held[...] + got[...].astype(F32), lax.axis_index("head") // 2)
-    kept[...] = value
-    side = near.shape[-1]
-    near[...] = sent[:, :, :side]
-    far[...] = sent[:, :, side:]
-
-
-def third_body(held, near, far, kept, sent):
-    got = jnp.concatenate([near[...], far[...]], axis=2).astype(F32)
-    value, leaving = halve(held[...] + got, lax.axis_index("head") // 4)
-    kept[...] = value[0]
-    sent[...] = leaving[0]
 
 
 def total_body(*refs):
@@ -324,12 +311,19 @@
     value = value + contract(w_value[...], grads[:, HD:], 0, 1)
     value = value + contract(w_junction[...], feature_grad, 1, 1)
     blocks = value.reshape((2 * kept.shape[0],) + kept.shape[1:])
-    kept[...], sent[...] = halve(blocks, lax.axis_index("head"))
+    kept[...], sent[...] = halve(blocks, lax.axis_index("side"))
 
 
 def tiles_of(rows, columns, count):
     high, wide = rows * 2 // count, columns // 2
     return [(i, pl.ds(i // 2 * high, high), pl.ds(i % 2 * wide, wide)) for i in range(count)]
+
+
+def sum_body(parts, total):
+    value = parts[0].astype(F32)
+    for i in range(1, parts.shape[0]):
+        value = value + parts[i].astype(F32)
+    total[...] = value.astype(total.dtype)
 
 
 def cut_body(parts, tiles, whole):
@@ -375,8 +369,8 @@
         copy.wait()
 
 
-def swap_cores(value):
-    return lax.ppermute(value, "core", [(0, 1), (1, 0)])
+def swap(value, axis="core"):
+    return lax.ppermute(value, axis, [(0, 1), (1, 0)])
 
 
 def exchange(value, axis):
@@ -399,7 +393,7 @@
     tokens, width = hidden.shape
     chips = lax.axis_size("x")
     intervals = lax.axis_size("interval")
-    heads = lax.axis_size("head")
+    heads = lax.axis_size("pair") * SIDES
     half = chips * tokens
     buckets, per = donor_pos.shape[2:]
     slots = buckets * per
@@ -436,7 +430,7 @@
         )
     )
     mine = exchange(message, "x")
-    theirs = swap_cores(mine)
+    theirs = swap(mine)
     queries, ctx = local_call(query_body, [((tokens, LANES), BF16)] * 2, operands=3)(
         hidden, w_query, ctx_grad[0].T
     )
@@ -451,7 +445,7 @@
         ],
         operands=5,
     )(queries, ctx, features, mine, theirs)
-    terms_theirs = swap_cores(terms_theirs)
+    terms_theirs = swap(terms_theirs)
     terms_mine, query_grad = local_call(
         own_body, [((chips, height, KV), BF16), ((tokens, HD), BF16)], operands=7
     )(queries, ctx, mine, theirs, back_mine, probs_b, dscores_b)
@@ -483,67 +477,56 @@
         w_junction,
     )
 
-    def flip(value, mask):
-        return lax.ppermute(value, "head", [(i, i ^ mask) for i in range(heads)])
-
-    weight_got, sent = lax.optimization_barrier((swap_cores(weight_sent), sent))
+    weight_got, sent = lax.optimization_barrier((swap(weight_sent), sent))
     (term,) = local_call(total_body, [((rows, cut), BF16)], operands=2)(weight_held, weight_got)
     part = rows // chips
     tile = (part * 2 // intervals, cut // 2)
     (tiles,) = local_call(
         cut_body, [((intervals,) + tile, BF16)], operands=1, scratch=[pltpu.VMEM((part, cut), F32)]
     )(exchange(term.reshape(chips, part, cut), "x"))
-    tiles, got = lax.optimization_barrier((tiles, flip(sent, 1)))
-    side = tokens // 2
-    held, near, far = local_call(
-        second_body,
-        [((heads // 4,) + block, F32)] + [((heads // 4, block[0], side), BF16)] * 2,
-        operands=2,
-    )(held, got)
-    got = (flip(near, 2), flip(far, 6))
+    tiles, got = lax.optimization_barrier((tiles, swap(sent, "side")))
+    (blocks,) = local_call(total_body, [((heads // SIDES,) + block, BF16)], operands=2)(held, got)
     (copies,) = local_call(spread_body, [((intervals,) + tile, BF16)], operands=1)(
         exchange(tiles, "interval")
     )
     (term,) = local_call(
         join_body, [((part, cut), BF16)], operands=1, scratch=[pltpu.VMEM((part, cut), F32)]
     )(exchange(copies, "interval"))
-    term, *got = lax.optimization_barrier((term, *got))
-    held, sent = local_call(third_body, [(block, F32), (block, BF16)], operands=3)(held, *got)
-    term, sent = lax.optimization_barrier((term, sent))
-    got = flip(sent, 4)
+    blocks = exchange(blocks, "pair")
     term = lax.all_gather(term, "x", axis=0, tiled=True)
-    term, got = lax.optimization_barrier((term, got))
-    (grad_input,) = local_call(total_body, [(block, BF16)], operands=2)(held, got)
+    term, blocks = lax.optimization_barrier((term, blocks))
+    (grad_input,) = local_call(sum_body, [(block, BF16)], operands=1)(blocks)
     grads = local_call(
         place_body,
         [((HD, width), BF16)] * 3,
         operands=2,
         scratch=[pltpu.SemaphoreType.DMA((2 * 3,))],
         space=pl.ANY,
-    )(term, swap_cores(term))
+    )(term, swap(term))
     return (grad_input.T[None],) + tuple(grads)
 
 
 def solution(mesh):
-    axes = (mesh.shape["interval"], mesh.shape["seq"] // CORES, CORES, mesh.shape["head"])
-    split = Mesh(mesh.devices.reshape(axes), ("interval", "x", "core", "head"))
-    seq = ("x", "core")
+    axes = (mesh.shape["interval"], mesh.shape["seq"] // CORES, CORES)
+    axes += (mesh.shape["head"] // SIDES, SIDES)
+    split = Mesh(mesh.devices.reshape(axes), ("interval", "x", "core", "pair", "side"))
+    seq, head = ("x", "core"), ("pair", "side")
     placed = (
         P("interval", seq, None),
-        P("interval", seq, "head"),
-        P("head", None),
-        P("head", None),
-        P("head", None),
+        P("interval", seq, head),
+        P(head, None),
+        P(head, None),
+        P(head, None),
         P(),
-        P("interval", seq, None, "head"),
-        P("interval", seq, None, "head"),
+        P("interval", seq, None, head),
+        P("interval", seq, None, head),
         P("interval", seq, None),
-        P("interval", seq, None, "head"),
+        P("interval", seq, None, head),
     )
     return jax.shard_map(
         on_device,
         mesh=split,
         in_specs=placed,
-        out_specs=(P("interval", seq, "head"), P("head", None), P("head", None), P("head", None)),
+        out_specs=(P("interval", seq, head), P(head, None), P(head, None), P(head, None)),
         check_vma=False,
     )

time: 140 us -> 136 us (0.971)
  starting transfers between devices: 52 us -> 42.7 us
  waiting for transfers between devices: 17.6 us -> 23 us
    ppermute x8 -> x5, starting transfers between devices: 45.1 us -> 25.8 us  [swap(): return lax.ppermute(value, axis, [(0, 1), (1, 0)])]
    all_to_all x2 -> x3, starting transfers between devices: 6.91 us -> 16.9 us  [exchange(): return lax.all_to_all(value, axis, 0, 0, tiled=True)]
    all_to_all x2 -> x3, waiting for transfers between devices: 9.66 us -> 18 us  [exchange(): return lax.all_to_all(value, axis, 0, 0, tiled=True)]
    ppermute x8 -> x5, waiting for transfers between devices: 7.98 us -> 4.97 us  [swap(): return lax.ppermute(value, axis, [(0, 1), (1, 0)])]
  transfers between devices with their start and end apart: 10 -> 8, of which waited for: 6 -> 6; matrix products, arithmetic and copies ran while one was open for 0% -> 0% of each run, Pallas kernels for 2% -> 3%
where the time goes in v8:
time: 136 us
  blocking collectives  55.1 us (41%)
  starting transfers between devices  42.7 us (31%)
  waiting for transfers between devices  23 us (17%)
  Pallas kernels  14.2 us (10%)
    all_to_all x3, blocking collectives, exchange(): return lax.all_to_all(value, axis, 0, 0, tiled=True)  43.6 us
    ppermute x5, starting transfers between devices, swap(): return lax.ppermute(value, axis, [(0, 1), (1, 0)])  25.8 us
    all_to_all x3, waiting for transfers between devices, exchange(): return lax.all_to_all(value, axis, 0, 0, tiled=True)  18 us
    all_to_all x3, starting transfers between devices, exchange(): return lax.all_to_all(value, axis, 0, 0, tiled=True)  16.9 us
    all_gather x1, blocking collectives, on_device(): term = lax.all_gather(term, 'x', axis=0, tiled=True)  11.5 us
    ppermute x5, waiting for transfers between devices, swap(): return lax.ppermute(value, axis, [(0, 1), (1, 0)])  4.97 us
    pallas_call x1, Pallas kernels, on_device(): local_call(attend_body, [((chips, height, KV), BF16), ((chips, height - t...  3.5 us
    pallas_call x1, Pallas kernels, on_device(): local_call(project_body, [((chips, height, KV), BF16), ((tokens, PJ), BF1...  2.76 us
  transfers between devices with their start and end apart: 8, of which 6 were waited for; matrix products, arithmetic and copies ran while one was open for 0% of the time, Pallas kernels for 3%

profile of v8, /device:TPU:1, one launch (start us, length us, event | category | flops | bytes accessed | tf_op | source)
XLA Modules:
  0.0 135.8 jit_solution(1475643477816766151)
XLA Ops:
  0.6 0.0 copy-start
  0.6 0.0 copy-start.1
  0.7 0.0 copy-start.5
  0.7 2.8 %shard_map.130 = (bf16[4,272,384]{2,1,0:T(8,128)(2,1)S(1)}, bf16[256,128]{1,0:T(8,128)(2,1)S(1)}, bf16[64,256]{1,0:T(8,128)(2,1)S(1)}) custom-call(bf16[256,1536]{1,0:T(8,128)(2,1)} %bitcast.12, bf16[192,1536]{1,0:T(8,128)(2,1)} %w_key.1, bf16[192,1536]{1,0:T(8,128)(2,1)} %w_value.1, bf16[1536,128]{1,0:T(8,128)(2,1)} %w_junction.1, s32[8,8]{1,0:T(8,128)} %bitcast.17, ...), custom_call_target="tpu_custom_call" | custom-call | tf_op jit(solution)/shard_map/pallas_call | solution.py:402
  3.4 13.2 %all_to_all.30.mine = bf16[4,272,384]{2,1,0:T(8,128)(2,1)S(1)} all-to-all(bf16[4,272,384]{2,1,0:T(8,128)(2,1)S(1)} %get-tuple-element.32), channel_id=1, replica_groups=mesh['interval'=8,'x'=4,'core'=2,'pair'=4,'side'=2] {'x'}, dimensions={0} | all-to-all | bytes 1671168 | tf_op jit(solution)/shard_map/all_to_all | solution.py:377
  16.7 7.7 %collective-permute-start = (bf16[4,272,384]{2,1,0:T(8,128)(2,1)S(1)}, bf16[4,272,384]{2,1,0:T(8,128)(2,1)S(1)}, u32[]{:S(2)}, u32[]{:S(2)}) collective-permute-start(bf16[4,272,384]{2,1,0:T(8,128)(2,1)S(1)} %all_to_all.30.mine), channel_id=1, source_target_pairs={{0,8},{8,0},{1,9},{9,1},{2,10},{10,2},{3,11},{11,3},{4,12},{12,4},... | collective-permute-start | bytes 2506760 | tf_op jit(solution)/shard_map/ppermute | solution.py:373
  24.4 0.0 copy-done
  24.4 0.0 copy-done.1
  24.4 0.0 copy-done.5
  24.4 0.4 shard_map.129
  24.8 1.5 %collective-permute-done.theirs = bf16[4,272,384]{2,1,0:T(8,128)(2,1)S(1)} collective-permute-done((bf16[4,272,384]{2,1,0:T(8,128)(2,1)S(1)}, bf16[4,272,384]{2,1,0:T(8,128)(2,1)S(1)}, u32[]{:S(2)}, u32[]{:S(2)}) %collective-permute-start) | collective-permute-done | bytes 835616 | tf_op jit(solution)/shard_map/ppermute | solution.py:373
  26.3 3.5 %shard_map.131 = (bf16[4,272,384]{2,1,0:T(8,128)(2,1)S(1)}, bf16[4,16,128]{2,1,0:T(8,128)(2,1)S(1)}, f32[256,128]{1,0:T(8,128)S(1)}, bf16[2,256,1024]{2,1,0:T(8,128)(2,1)S(1)}, bf16[2,256,1024]{2,1,0:T(8,128)(2,1)S(1)}) custom-call(bf16[256,256]{1,0:T(8,128)(2,1)S(1)} %get-tuple-element.30.queries, bf16[256,256]{1,0:T(8,128)(2,1)S(1)} %get-tuple-element.31.ctx, ...), custom_call_target="tpu_custom_call" | custom-call | tf_op jit(solution)/shard_map/pallas_call | solution.py:437
  29.8 2.3 %collective-permute-start.1 = (bf16[4,272,384]{2,1,0:T(8,128)(2,1)S(1)}, bf16[4,272,384]{2,1,0:T(8,128)(2,1)S(1)}, u32[]{:S(2)}, u32[]{:S(2)}) collective-permute-start(bf16[4,272,384]{2,1,0:T(8,128)(2,1)S(1)} %get-tuple-element.38), channel_id=1, source_target_pairs={{0,8},{8,0},{1,9},{9,1},{2,10},{10,2},{3,11},{11,3},{4,12},{12,4},... | collective-permute-start | bytes 2506760 | tf_op jit(solution)/shard_map/ppermute | solution.py:373
  32.1 0.7 shard_map.132
  32.9 1.2 collective-permute-done.1.refs_1_
  34.1 0.2 shard_map.133
  34.3 0.0 copy-start.2
  34.3 0.0 copy-start.3
  34.3 0.0 copy-start.4
  34.3 14.8 %all_to_all.31.parts = bf16[4,272,384]{2,1,0:T(8,128)(2,1)S(1)} all-to-all(bf16[4,272,384]{2,1,0:T(8,128)(2,1)S(1)} %shard_map.133), channel_id=1, replica_groups=mesh['interval'=8,'x'=4,'core'=2,'pair'=4,'side'=2] {'x'}, dimensions={0} | all-to-all | bytes 1671168 | tf_op jit(solution)/shard_map/all_to_all | solution.py:377
  49.1 0.7 shard_map.134
  49.8 3.4 %collective-permute-start.2 = (bf16[576,768]{1,0:T(8,128)(2,1)S(1)}, bf16[576,768]{1,0:T(8,128)(2,1)S(1)}, u32[]{:S(2)}, u32[]{:S(2)}) collective-permute-start(bf16[576,768]{1,0:T(8,128)(2,1)S(1)} %get-tuple-element.41), channel_id=1, source_target_pairs={{0,8},{8,0},{1,9},{9,1},{2,10},{10,2},{3,11},{11,3},{4,12},{12,4},... | collective-permute-start | bytes 2654216 | tf_op jit(solution)/shard_map/ppermute | solution.py:373
  53.2 0.0 copy-done.2
  53.2 0.0 copy-done.3
  53.2 0.0 copy-done.4
  53.2 1.1 shard_map.135
  54.4 0.9 collective-permute-done.2.refs_1_
  55.2 1.1 shard_map.136
  56.3 3.5 %all-to-all-start.2 = ((bf16[4,144,768]{2,1,0:T(8,128)(2,1)}), bf16[4,144,768]{2,1,0:T(8,128)(2,1)S(1)}, u32[]{:S(2)}, u32[]{:S(2)}) async-start(bf16[4,144,768]{2,1,0:T(8,128)(2,1)} %bitcast.7), calls=%async_computation.2 | async-start | bytes 1769472 | tf_op jit(solution)/shard_map/all_to_all | solution.py:377
  59.8 3.4 %collective-permute-start.3 = (bf16[4,192,256]{2,1,0:T(8,128)(2,1)S(1)}, bf16[4,192,256]{2,1,0:T(8,128)(2,1)S(1)}, u32[]{:S(2)}, u32[]{:S(2)}) collective-permute-start(bf16[4,192,256]{2,1,0:T(8,128)(2,1)S(1)} %get-tuple-element.47), channel_id=1, source_target_pairs={{0,1},{1,0},{2,3},{3,2},{4,5},{5,4},{6,7},{7,6},{8,9},{9,8},{10,11... | collective-permute-start | bytes 1179656 | tf_op jit(solution)/shard_map/ppermute | solution.py:373
  63.2 9.7 %all-to-all-done.2.parts = bf16[4,144,768]{2,1,0:T(8,128)(2,1)S(1)} async-done(((bf16[4,144,768]{2,1,0:T(8,128)(2,1)}), bf16[4,144,768]{2,1,0:T(8,128)(2,1)S(1)}, u32[]{:S(2)}, u32[]{:S(2)}) %all-to-all-start.2) | async-done | bytes 884768 | tf_op jit(solution)/shard_map/all_to_all | solution.py:377
  72.9 0.2 shard_map.137
  73.1 0.0 collective-permute-done.3.refs_1_
  73.1 15.6 %all_to_all.32.parts = bf16[8,36,384]{2,1,0:T(8,128)(2,1)S(1)} all-to-all(bf16[8,36,384]{2,1,0:T(8,128)(2,1)S(1)} %shard_map.137), channel_id=1, replica_groups=mesh['interval'=8,'x'=4,'core'=2,'pair'=4,'side'=2] {'interval'}, dimensions={0} | all-to-all | bytes 442368 | tf_op jit(solution)/shard_map/all_to_all | solution.py:377
  88.6 0.7 shard_map.138
  89.4 3.4 %all-to-all-start.4 = ((bf16[8,36,384]{2,1,0:T(8,128)(2,1)}), bf16[8,36,384]{2,1,0:T(8,128)(2,1)S(1)}, u32[]{:S(2)}, u32[]{:S(2)}) async-start(bf16[8,36,384]{2,1,0:T(8,128)(2,1)} %shard_map.138), calls=%async_computation.4 | async-start | bytes 491520 | tf_op jit(solution)/shard_map/all_to_all | solution.py:377
  92.8 0.8 shard_map.140
  93.6 8.3 %all-to-all-done.4.tiles = bf16[8,36,384]{2,1,0:T(8,128)(2,1)S(1)} async-done(((bf16[8,36,384]{2,1,0:T(8,128)(2,1)}), bf16[8,36,384]{2,1,0:T(8,128)(2,1)S(1)}, u32[]{:S(2)}, u32[]{:S(2)}) %all-to-all-start.4) | async-done | bytes 221216 | tf_op jit(solution)/shard_map/all_to_all | solution.py:377
  101.9 10.0 %all-to-all-start.5 = ((bf16[4,192,256]{2,1,0:T(8,128)(2,1)}), bf16[4,192,256]{2,1,0:T(8,128)(2,1)S(1)}, u32[]{:S(2)}, u32[]{:S(2)}) async-start(bf16[4,192,256]{2,1,0:T(8,128)(2,1)} %shard_map.140), calls=%async_computation.5 | async-start | bytes 786432 | tf_op jit(solution)/shard_map/all_to_all | solution.py:377
  112.0 11.5 %all_gather.3.mine = bf16[576,768]{1,0:T(8,128)(2,1)S(1)} all-gather(bf16[144,768]{1,0:T(8,128)(2,1)S(1)} %shard_map.139), channel_id=1, replica_groups=mesh['interval'=8,'x'=4,'core'=2,'pair'=4,'side'=2] {'x'}, dimensions={0}, use_global_device_ids=true | all-gather | bytes 1105920 | tf_op jit(solution)/shard_map/all_gather | solution.py:496
  123.5 0.0 all-to-all-done.5.parts
  123.5 9.0 %collective-permute-start.4 = (bf16[576,768]{1,0:T(8,128)(2,1)S(1)}, bf16[576,768]{1,0:T(8,128)(2,1)S(1)}, u32[]{:S(2)}, u32[]{:S(2)}) collective-permute-start(bf16[576,768]{1,0:T(8,128)(2,1)S(1)} %all_gather.3.mine), channel_id=1, source_target_pairs={{0,8},{8,0},{1,9},{9,1},{2,10},{10,2},{3,11},{11,3},{4,12},{12,4},... | collective-permute-start | bytes 2654216 | tf_op jit(solution)/shard_map/ppermute | solution.py:373
  132.6 0.7 shard_map.141
  133.2 1.3 collective-permute-done.4.theirs
  134.6 1.2 shard_map.142
  (1 shorter events, 0.0 us)
Async XLA Ops:
  0.6 23.7 %copy-start = (bf16[1,256,1536]{2,1,0:T(8,128)(2,1)S(1)}, bf16[1,256,1536]{2,1,0:T(8,128)(2,1)}, u32[]{:S(2)}) copy-start(bf16[1,256,1536]{2,1,0:T(8,128)(2,1)} %param.10) | copy-start | bytes 2359300
  0.6 23.7 %copy-start.1 = (bf16[192,1536]{1,0:T(8,128)(2,1)S(1)}, bf16[192,1536]{1,0:T(8,128)(2,1)}, u32[]{:S(2)}) copy-start(bf16[192,1536]{1,0:T(8,128)(2,1)} %w_query.3) | copy-start | bytes 1769476
  0.7 23.7 %copy-start.5 = (bf16[1,256,192]{1,2,0:T(8,128)(2,1)S(1)}, bf16[1,256,192]{1,2,0:T(8,128)(2,1)}, u32[]{:S(2)}) copy-start(bf16[1,256,192]{1,2,0:T(8,128)(2,1)} %param.11) | copy-start | bytes 294916
  16.7 9.6 %collective-permute-start = (bf16[4,272,384]{2,1,0:T(8,128)(2,1)S(1)}, bf16[4,272,384]{2,1,0:T(8,128)(2,1)S(1)}, u32[]{:S(2)}, u32[]{:S(2)}) collective-permute-start(bf16[4,272,384]{2,1,0:T(8,128)(2,1)S(1)} %all_to_all.30.mine), channel_id=1, source_target_pairs={{0,8},{8,0},{1,9},{9,1},{2,10},{10,2},{3,11},{11,3},{4,12},{12,4},... | collective-permute-start | bytes 2506760 | tf_op jit(solution)/shard_map/ppermute | solution.py:373
  29.8 4.2 %collective-permute-start.1 = (bf16[4,272,384]{2,1,0:T(8,128)(2,1)S(1)}, bf16[4,272,384]{2,1,0:T(8,128)(2,1)S(1)}, u32[]{:S(2)}, u32[]{:S(2)}) collective-permute-start(bf16[4,272,384]{2,1,0:T(8,128)(2,1)S(1)} %get-tuple-element.38), channel_id=1, source_target_pairs={{0,8},{8,0},{1,9},{9,1},{2,10},{10,2},{3,11},{11,3},{4,12},{12,4},... | collective-permute-start | bytes 2506760 | tf_op jit(solution)/shard_map/ppermute | solution.py:373
  34.3 18.9 %copy-start.2 = (bf16[192,1536]{1,0:T(8,128)(2,1)S(1)}, bf16[192,1536]{1,0:T(8,128)(2,1)}, u32[]{:S(2)}) copy-start(bf16[192,1536]{1,0:T(8,128)(2,1)} %w_key.1) | copy-start | bytes 1769476
  34.3 18.9 %copy-start.3 = (bf16[192,1536]{1,0:T(8,128)(2,1)S(1)}, bf16[192,1536]{1,0:T(8,128)(2,1)}, u32[]{:S(2)}) copy-start(bf16[192,1536]{1,0:T(8,128)(2,1)} %w_value.1) | copy-start | bytes 1769476
  34.3 18.9 %copy-start.4 = (bf16[1536,128]{1,0:T(8,128)(2,1)S(1)}, bf16[1536,128]{1,0:T(8,128)(2,1)}, u32[]{:S(2)}) copy-start(bf16[1536,128]{1,0:T(8,128)(2,1)} %w_junction.1) | copy-start | bytes 1179652
  49.8 5.4 %collective-permute-start.2 = (bf16[576,768]{1,0:T(8,128)(2,1)S(1)}, bf16[576,768]{1,0:T(8,128)(2,1)S(1)}, u32[]{:S(2)}, u32[]{:S(2)}) collective-permute-start(bf16[576,768]{1,0:T(8,128)(2,1)S(1)} %get-tuple-element.41), channel_id=1, source_target_pairs={{0,8},{8,0},{1,9},{9,1},{2,10},{10,2},{3,11},{11,3},{4,12},{12,4},... | collective-permute-start | bytes 2654216 | tf_op jit(solution)/shard_map/ppermute | solution.py:373
  56.3 16.6 %all-to-all-start.2 = ((bf16[4,144,768]{2,1,0:T(8,128)(2,1)}), bf16[4,144,768]{2,1,0:T(8,128)(2,1)S(1)}, u32[]{:S(2)}, u32[]{:S(2)}) async-start(bf16[4,144,768]{2,1,0:T(8,128)(2,1)} %bitcast.7), calls=%async_computation.2 | async-start | bytes 1769472 | tf_op jit(solution)/shard_map/all_to_all | solution.py:377
  59.8 13.3 %collective-permute-start.3 = (bf16[4,192,256]{2,1,0:T(8,128)(2,1)S(1)}, bf16[4,192,256]{2,1,0:T(8,128)(2,1)S(1)}, u32[]{:S(2)}, u32[]{:S(2)}) collective-permute-start(bf16[4,192,256]{2,1,0:T(8,128)(2,1)S(1)} %get-tuple-element.47), channel_id=1, source_target_pairs={{0,1},{1,0},{2,3},{3,2},{4,5},{5,4},{6,7},{7,6},{8,9},{9,8},{10,11... | collective-permute-start | bytes 1179656 | tf_op jit(solution)/shard_map/ppermute | solution.py:373
  89.4 12.5 %all-to-all-start.4 = ((bf16[8,36,384]{2,1,0:T(8,128)(2,1)}), bf16[8,36,384]{2,1,0:T(8,128)(2,1)S(1)}, u32[]{:S(2)}, u32[]{:S(2)}) async-start(bf16[8,36,384]{2,1,0:T(8,128)(2,1)} %shard_map.138), calls=%async_computation.4 | async-start | bytes 491520 | tf_op jit(solution)/shard_map/all_to_all | solution.py:377
  101.9 21.6 %all-to-all-start.5 = ((bf16[4,192,256]{2,1,0:T(8,128)(2,1)}), bf16[4,192,256]{2,1,0:T(8,128)(2,1)S(1)}, u32[]{:S(2)}, u32[]{:S(2)}) async-start(bf16[4,192,256]{2,1,0:T(8,128)(2,1)} %shard_map.140), calls=%async_computation.5 | async-start | bytes 786432 | tf_op jit(solution)/shard_map/all_to_all | solution.py:377
  123.5 11.1 %collective-permute-start.4 = (bf16[576,768]{1,0:T(8,128)(2,1)S(1)}, bf16[576,768]{1,0:T(8,128)(2,1)S(1)}, u32[]{:S(2)}, u32[]{:S(2)}) collective-permute-start(bf16[576,768]{1,0:T(8,128)(2,1)S(1)} %all_gather.3.mine), channel_id=1, source_target_pairs={{0,8},{8,0},{1,9},{9,1},{2,10},{10,2},{3,11},{11,3},{4,12},{12,4},... | collective-permute-start | bytes 2654216 | tf_op jit(solution)/shard_map/ppermute | solution.py:373

commit v9 on v8

--- a/solution.py
+++ b/solution.py
@@ -11,6 +11,7 @@
 CORES = 2
 SIDES = 2
 LANES = 256
+BAND = 128
 KV = 2 * HD
 SHIFT = KV - LANES
 F32 = jnp.float32
@@ -60,7 +61,6 @@
     counts_hbm,
     pred_hbm,
     message,
-    features,
     donor_hot,
     hidden,
     weights,
@@ -131,7 +131,6 @@
     x = hidden[...]
     rows = contract(x, weights[...], 1, 1).astype(BF16)
     feats = contract(x, w_junction[...], 1, 0).astype(BF16)
-    features[...] = feats
     slot_rows = jnp.concatenate(
         [
             contract(hot, feats, 1, 0).astype(BF16),
@@ -146,91 +145,104 @@
         message[chip, tokens:, :] = slot_rows[chip * part : (chip + 1) * part, :]
 
 
-def query_body(hidden, w_query, ctx_t, queries, ctx):
+def query_body(hidden, w_query, w_junction, ctx_t, rows):
     tokens = hidden.shape[0]
     pad = jnp.zeros((tokens, LANES - HD), BF16)
     value = contract(hidden[...], w_query[...], 1, 1).astype(BF16)
-    queries[...] = jnp.concatenate([value, pad], axis=1)
-    ctx[...] = jnp.concatenate([pad, jnp.transpose(ctx_t[...].astype(F32)).astype(BF16)], axis=1)
-
-
-def attend_body(
-    queries,
-    ctx,
-    features,
-    mine,
-    theirs,
-    terms_theirs,
-    back_mine,
-    accept_sum,
-    probs_b,
-    dscores_b,
-):
-    tokens = queries.shape[0]
+    rows[:, :LANES] = jnp.concatenate([value, pad], axis=1)
+    ctx = jnp.transpose(ctx_t[...].astype(F32)).astype(BF16)
+    rows[:, LANES : 2 * LANES] = jnp.concatenate([pad, ctx], axis=1)
+    rows[:, 2 * LANES :] = contract(hidden[...], w_junction[...], 1, 0).astype(BF16)
+
+
+def diagonal(size):
+    return iota((size, size), 0) == iota((size, size), 1)
+
+
+def score_body(own, other, mine, expd, dprobs, stats):
+    tokens = own.shape[0]
+    half = mine.shape[0] * tokens
+    keys = mine[:, :tokens, :].reshape(half, KV)
+    square = diagonal(BAND)
+    blank = jnp.zeros((8 - 3, BAND), F32)
+    for i, rows in enumerate((own, other)):
+        for start in range(0, tokens, BAND):
+            band = pl.ds(start, BAND)
+            score = contract(rows[band, :LANES], keys[:, :LANES], 1, 1) * HD ** (-0.5)
+            row_max = jnp.max(score, axis=-1, keepdims=True)
+            value = jnp.exp(score - row_max)
+            dprob = contract(rows[band, LANES : 2 * LANES], keys[:, SHIFT:], 1, 1)
+            expd[i, band, :] = value
+            dprobs[i, band, :] = dprob
+            columns = (
+                row_max,
+                jnp.sum(value, axis=-1, keepdims=True),
+                jnp.sum(value * dprob, axis=-1, keepdims=True),
+            )
+            lines = [
+                jnp.sum(jnp.where(square, column, 0.0), axis=0, keepdims=True)
+                for column in columns
+            ]
+            stats[i, :, band] = jnp.concatenate(lines + [blank], axis=0)
+
+
+def slot_body(own, other, mine, back, kept_sum, sent_sum):
+    tokens = own.shape[0]
     chips, height, _ = mine.shape
-    half = chips * tokens
-    scale = HD ** (-0.5)
-    sides = [ref[:, :tokens, :].reshape(half, KV) for ref in (mine, theirs)]
-    rows = 64
-    for start in range(0, tokens, rows):
-        band = pl.ds(start, rows)
-        q, g = queries[band, :], ctx[band, :]
-        scores = [contract(q, side[:, :LANES], 1, 1) * scale for side in sides]
-        row_max = jnp.maximum(
-            jnp.max(scores[0], axis=-1, keepdims=True), jnp.max(scores[1], axis=-1, keepdims=True)
-        )
-        expd = [jnp.exp(score - row_max) for score in scores]
-        inverse = 1.0 / (
-            jnp.sum(expd[0], axis=-1, keepdims=True) + jnp.sum(expd[1], axis=-1, keepdims=True)
-        )
-        probs = [value * inverse for value in expd]
-        dprobs = [contract(g, side[:, SHIFT:], 1, 1) for side in sides]
-        row_delta = jnp.sum(probs[0] * dprobs[0], axis=-1, keepdims=True) + jnp.sum(
-            probs[1] * dprobs[1], axis=-1, keepdims=True
-        )
-        for i in range(2):
-            probs_b[i, band, :] = probs[i].astype(BF16)
-            dscores_b[i, band, :] = (probs[i] * (dprobs[i] - row_delta)).astype(BF16)
-
-    core = lax.axis_index("core")
     part = height - tokens
-    per = part // CORES
-
-    def own_rows(ref):
-        block = ref[:, tokens:, :].astype(F32)
-        return jnp.where(core == 0, block[:, :per, :], block[:, per:, :]).reshape(chips * per, KV)
-
-    slot_rows = jnp.concatenate([own_rows(mine), own_rows(theirs)], axis=0)
-    slots = slot_rows.shape[0]
+    slots = chips * part
+    slot_rows = mine[:, tokens:, :].astype(F32).reshape(slots, KV)
     donor_feat = slot_rows[:, :PJ]
     extra = slot_rows[:, PJ : 2 * PJ]
     acceptor = extra[:, 0:1]
     slot_scale = extra[:, 1:2] + extra[:, 2:3] + extra[:, 3:4]
-    hot = jnp.where(iota((slots, tokens), 1).astype(F32) == acceptor, 1.0, 0.0).astype(BF16)
-    accept_feat = contract(hot, features[...], 1, 0)
+    shard = iota((slots, 1), 0) % part // (part // CORES)
+    here = shard == lax.axis_index("core")
+    place = iota((slots, tokens), 1).astype(F32) == acceptor
+    hots = [
+        jnp.where(place, jnp.where(chosen, 1.0, 0.0), 0.0).astype(BF16)
+        for chosen in (here, jnp.logical_not(here))
+    ]
+    accept_feat = contract(hots[0], own[:, 2 * LANES :], 1, 0) + contract(
+        hots[1], other[:, 2 * LANES :], 1, 0
+    )
     pair_scale = PJ ** (-0.5)
     pair_score = jnp.sum(donor_feat * accept_feat, axis=-1, keepdims=True) * pair_scale
     slot_grad = slot_scale * jax.nn.sigmoid(pair_score) * pair_scale
-    total = jnp.zeros((tokens, PJ), F32)
-    for piece in split_terms(slot_grad * donor_feat):
-        total = total + contract(hot, piece, 0, 0)
-    accept_sum[...] = total
-    back = (slot_grad * accept_feat).reshape(2, chips, per, PJ)
-    blank = jnp.zeros((2, chips, per, PJ), F32)
-
-    upper = jnp.where(core == 0, back, blank)
-    lower = jnp.where(core == 0, blank, back)
-    back = jnp.concatenate([upper, lower], axis=2).astype(BF16)
-    back_mine[...] = back[0]
-    write_terms(terms_theirs, dscores_b[1], probs_b[1], queries[...], ctx[...], back[1])
-
-
-def write_terms(terms, dscores, probs, queries, ctx, back):
-    chips, height, _ = terms.shape
-    part = back.shape[1]
-    tokens = height - part
-    key_term = contract(dscores, queries, 0, 0) * HD ** (-0.5)
-    value_term = contract(probs, ctx, 0, 0)
+    pieces = split_terms(slot_grad * donor_feat)
+    for hot, total in zip(hots, (kept_sum, sent_sum)):
+        total[...] = contract(hot, pieces[0], 0, 0) + contract(hot, pieces[1], 0, 0)
+    back[...] = (slot_grad * accept_feat).astype(BF16).reshape(chips, part, PJ)
+
+
+def grad_body(
+    own, other, mine, expd, dprobs, stats, got, back, sent_sum, terms, kept, sent, probs_b, dscores_b
+):
+    tokens = own.shape[0]
+    chips, height, _ = mine.shape
+    part = height - tokens
+    half = chips * tokens
+    scale = HD ** (-0.5)
+    square = diagonal(BAND)
+    for i in range(CORES):
+        for start in range(0, tokens, BAND):
+            band = pl.ds(start, BAND)
+            here, there = stats[i, :, band], got[1 - i, :, band]
+            top = jnp.maximum(here[0:1], there[0:1])
+            near, far = jnp.exp(here[0:1] - top), jnp.exp(there[0:1] - top)
+            inverse = 1.0 / (here[1:2] * near + there[1:2] * far)
+            delta = (here[2:3] * near + there[2:3] * far) * inverse
+            factor, delta = (
+                jnp.sum(jnp.where(square, line, 0.0), axis=1, keepdims=True)
+                for line in (near * inverse, delta)
+            )
+            probs = expd[i, band, :] * factor
+            rows = pl.ds(i * tokens + start, BAND)
+            probs_b[rows, :] = probs.astype(BF16)
+            dscores_b[rows, :] = (probs * (dprobs[i, band, :] - delta)).astype(BF16)
+    rows = jnp.concatenate([own[:, : 2 * LANES], other[:, : 2 * LANES]], axis=0)
+    key_term = contract(dscores_b[...], rows[:, :LANES], 0, 0) * scale
+    value_term = contract(probs_b[...], rows[:, LANES:], 0, 0)
     middle = key_term[:, SHIFT:] + value_term[:, :SHIFT]
     for first, value in (
         (0, key_term[:, :SHIFT]),
@@ -240,19 +252,13 @@
         terms[:, :tokens, first : first + SHIFT] = value.astype(BF16).reshape(
             chips, tokens, SHIFT
         )
-    terms[:, tokens:, :PJ] = back
+    terms[:, tokens:, :PJ] = back[...]
     terms[:, tokens:, PJ:] = jnp.zeros((chips, part, KV - PJ), BF16)
-
-
-def own_body(queries, ctx, mine, theirs, back, probs_b, dscores_b, terms_mine, query_grad):
-    write_terms(terms_mine, dscores_b[0], probs_b[0], queries[...], ctx[...], back[...])
-    chips, _, _ = mine.shape
-    tokens = queries.shape[0]
-    total = jnp.zeros((tokens, LANES), F32)
-    for i, side in enumerate((mine, theirs)):
-        keys = side[:, :tokens, :LANES].reshape(chips * tokens, LANES)
-        total = total + contract(dscores_b[i], keys, 1, 0)
-    query_grad[...] = (total[:, :HD] * HD ** (-0.5)).astype(BF16)
+    keys = mine[:, :tokens, :LANES].reshape(half, LANES)
+    query_term = contract(dscores_b[...], keys, 1, 0) * scale
+    kept[...] = query_term[:tokens, :]
+    sent[:, :LANES] = query_term[tokens:, :].astype(BF16)
+    sent[:, LANES:] = sent_sum[...].astype(BF16)
 
 
 def halve(value, side):
@@ -270,8 +276,10 @@
     refs[-1][...] = value.astype(refs[-1].dtype)
 
 
-def grads_body(parts, query_grad, hidden, grads, kept, sent):
+def grads_body(parts, query_held, query_got, hidden, grads, query_grad, kept, sent):
     tokens, width = hidden.shape
+    query = query_held[:, :HD] + query_got[:, :HD].astype(F32)
+    query_grad[...] = query.astype(BF16)
     total = jnp.zeros((tokens, KV), F32)
     for chip in range(parts.shape[0]):
         total = total + parts[chip, :tokens, :].astype(F32)
@@ -290,7 +298,8 @@
 
 def input_body(
     parts,
-    accept_sum,
+    kept_sum,
+    query_got,
     donor_hot,
     grads,
     query_grad,
@@ -305,7 +314,8 @@
     tokens = grads.shape[0]
     part = height - tokens
     slot_rows = parts[:, tokens:, :PJ].reshape(chips * part, PJ)
-    feature_grad = (accept_sum[...] + contract(donor_hot[...], slot_rows, 0, 0)).astype(BF16)
+    feature_grad = kept_sum[...] + query_got[:, LANES:].astype(F32)
+    feature_grad = (feature_grad + contract(donor_hot[...], slot_rows, 0, 0)).astype(BF16)
     value = contract(w_query[...], query_grad[...], 0, 1)
     value = value + contract(w_key[...], grads[:, :HD], 0, 1)
     value = value + contract(w_value[...], grads[:, HD:], 0, 1)
@@ -399,9 +409,9 @@
     slots = buckets * per
     height = tokens + slots // chips
 
-    message, features, donor_hot = local_call(
+    message, donor_hot = local_call(
         project_body,
-        [((chips, height, KV), BF16), ((tokens, PJ), BF16), ((slots, tokens), BF16)],
+        [((chips, height, KV), BF16), ((slots, tokens), BF16)],
         operands=8,
         fetched=8,
         scratch=[
@@ -430,44 +440,50 @@
         )
     )
     mine = exchange(message, "x")
-    theirs = swap(mine)
-    queries, ctx = local_call(query_body, [((tokens, LANES), BF16)] * 2, operands=3)(
-        hidden, w_query, ctx_grad[0].T
-    )
-    terms_theirs, back_mine, accept_sum, probs_b, dscores_b = local_call(
-        attend_body,
+    (own,) = local_call(query_body, [((tokens, 2 * LANES + PJ), BF16)], operands=4)(
+        hidden, w_query, w_junction, ctx_grad[0].T
+    )
+    other = swap(own)
+    expd, dprobs, stats = local_call(
+        score_body,
+        [((CORES, tokens, half), F32), ((CORES, tokens, half), F32), ((CORES, 8, tokens), F32)],
+        operands=3,
+    )(own, other, mine)
+    got = swap(stats)
+    back, kept_sum, sent_sum = local_call(
+        slot_body,
+        [((chips, height - tokens, PJ), BF16), ((tokens, PJ), F32), ((tokens, PJ), F32)],
+        operands=3,
+    )(own, other, mine)
+    terms, query_held, query_sent = local_call(
+        grad_body,
         [
             ((chips, height, KV), BF16),
-            ((chips, height - tokens, PJ), BF16),
-            ((tokens, PJ), F32),
-            ((CORES, tokens, half), BF16),
-            ((CORES, tokens, half), BF16),
+            ((tokens, LANES), F32),
+            ((tokens, LANES + PJ), BF16),
         ],
-        operands=5,
-    )(queries, ctx, features, mine, theirs)
-    terms_theirs = swap(terms_theirs)
-    terms_mine, query_grad = local_call(
-        own_body, [((chips, height, KV), BF16), ((tokens, HD), BF16)], operands=7
-    )(queries, ctx, mine, theirs, back_mine, probs_b, dscores_b)
-    (pair_sum,) = local_call(total_body, [((chips, height, KV), BF16)], operands=2)(
-        terms_mine, terms_theirs
-    )
-    parts = exchange(pair_sum, "x")
+        operands=9,
+        scratch=[pltpu.VMEM((CORES * tokens, half), BF16)] * 2,
+    )(own, other, mine, expd, dprobs, stats, got, back, sent_sum)
+    query_got = swap(query_sent)
+    parts = exchange(terms, "x")
+    parts, query_got = lax.optimization_barrier((parts, query_got))
     rows = 3 * HD
     cut = width // CORES
     block = (width // heads, tokens)
-    grads, weight_held, weight_sent = local_call(
+    grads, query_grad, weight_held, weight_sent = local_call(
         grads_body,
-        [((tokens, KV), BF16), ((rows, cut), F32), ((rows, cut), BF16)],
-        operands=3,
-    )(parts, query_grad, hidden)
+        [((tokens, KV), BF16), ((tokens, HD), BF16), ((rows, cut), F32), ((rows, cut), BF16)],
+        operands=4,
+    )(parts, query_held, query_got, hidden)
     held, sent = local_call(
         input_body,
         [((heads // 2,) + block, F32), ((heads // 2,) + block, BF16)],
-        operands=9,
+        operands=10,
     )(
         parts,
-        accept_sum,
+        kept_sum,
+        query_got,
         donor_hot,
         grads,
         query_grad,

time: 136 us -> 136 us (level)
  blocking collectives: 55.1 us -> 26.2 us
  starting transfers between devices: 42.7 us -> 56.5 us
  waiting for transfers between devices: 23 us -> 32.9 us
  local copies, waits for them, and re-layouts: 0.03 us -> 4.38 us
    all_to_all x3 -> x1, blocking collectives: 43.6 us -> 15 us  [exchange(): return lax.all_to_all(value, axis, 0, 0, tiled=True)]
    all_to_all x3 -> x5, waiting for transfers between devices: 18 us -> 28.7 us  [exchange(): return lax.all_to_all(value, axis, 0, 0, tiled=True)]
    all_to_all x3 -> x5, starting transfers between devices: 16.9 us -> 25.4 us  [exchange(): return lax.all_to_all(value, axis, 0, 0, tiled=True)]
    ppermute x5 -> x6, starting transfers between devices: 25.8 us -> 31.1 us  [swap(): return lax.ppermute(value, axis, [(0, 1), (1, 0)])]
    unnamed x12 -> x20, local copies, waits for them, and re-layouts: 0.03 us -> 4.38 us
    ppermute x5 -> x6, waiting for transfers between devices: 4.97 us -> 4.2 us  [swap(): return lax.ppermute(value, axis, [(0, 1), (1, 0)])]
  transfers between devices with their start and end apart: 8 -> 11, of which waited for: 6 -> 6; matrix products, arithmetic and copies ran while one was open for 0% -> 0% of each run, Pallas kernels for 3% -> 3%
where the time goes in v9:
time: 136 us
  starting transfers between devices  56.5 us (42%)
  waiting for transfers between devices  32.9 us (24%)
  blocking collectives  26.2 us (19%)
  Pallas kernels  14.7 us (11%)
  local copies, waits for them, and re-layouts  4.38 us (3%)
    ppermute x6, starting transfers between devices, swap(): return lax.ppermute(value, axis, [(0, 1), (1, 0)])  31.1 us
    all_to_all x5, waiting for transfers between devices, exchange(): return lax.all_to_all(value, axis, 0, 0, tiled=True)  28.7 us
    all_to_all x5, starting transfers between devices, exchange(): return lax.all_to_all(value, axis, 0, 0, tiled=True)  25.4 us
    all_to_all x1, blocking collectives, exchange(): return lax.all_to_all(value, axis, 0, 0, tiled=True)  15 us
    all_gather x1, blocking collectives, on_device(): term = lax.all_gather(term, 'x', axis=0, tiled=True)  11.2 us
    unnamed x20, local copies, waits for them, and re-layouts  4.38 us
    ppermute x6, waiting for transfers between devices, swap(): return lax.ppermute(value, axis, [(0, 1), (1, 0)])  4.2 us
    pallas_call x1, Pallas kernels, on_device(): local_call(project_body, [((chips, height, KV), BF16), ((slots, tokens),...  3.7 us
  transfers between devices with their start and end apart: 11, of which 6 were waited for; matrix products, arithmetic and copies ran while one was open for 0% of the time, Pallas kernels for 3%

profile of v9, /device:TPU:1, one launch (start us, length us, event | category | flops | bytes accessed | tf_op | source)
XLA Modules:
  0.0 135.6 jit_solution(12730870075113699509)
XLA Ops:
  0.6 0.0 copy-start.1
  0.6 0.0 copy-start
  0.7 0.0 copy-start.2
  0.7 0.0 copy-start.8
  0.7 3.7 %shard_map.130 = (bf16[4,272,384]{2,1,0:T(8,128)(2,1)}, bf16[64,256]{1,0:T(8,128)(2,1)S(1)}) custom-call(bf16[256,1536]{1,0:T(8,128)(2,1)} %bitcast.12, bf16[192,1536]{1,0:T(8,128)(2,1)} %w_key.1, bf16[192,1536]{1,0:T(8,128)(2,1)} %w_value.1, bf16[1536,128]{1,0:T(8,128)(2,1)} %w_junction.3, s32[8,8]{1,0:T(8,128)} %bitcast.17, s32[8,8]{1,0:T(8,128)} %bitcast.18, ...), custom_call_target="tpu_custom_call" | custom-call | tf_op jit(solution)/shard_map/pallas_call | solution.py:412
  4.4 4.9 %all-to-all-start = ((bf16[4,272,384]{2,1,0:T(8,128)(2,1)}), bf16[4,272,384]{2,1,0:T(8,128)(2,1)S(1)}, u32[]{:S(2)}, u32[]{:S(2)}) async-start(bf16[4,272,384]{2,1,0:T(8,128)(2,1)} %get-tuple-element.32), calls=%async_computation | async-start | bytes 1671168 | tf_op jit(solution)/shard_map/all_to_all | solution.py:387
  9.2 0.0 copy-done.1
  9.2 0.0 copy-done
  9.2 0.0 copy-done.2
  9.2 0.0 copy-done.8
  9.3 0.6 shard_map.129.own
  9.8 7.5 %collective-permute-start = (bf16[256,640]{1,0:T(8,128)(2,1)S(1)}, bf16[256,640]{1,0:T(8,128)(2,1)S(1)}, u32[]{:S(2)}, u32[]{:S(2)}) collective-permute-start(bf16[256,640]{1,0:T(8,128)(2,1)S(1)} %shard_map.129.own), channel_id=1, source_target_pairs={{0,8},{8,0},{1,9},{9,1},{2,10},{10,2},{3,11},{11,3},{4,12},{12,4},... | collective-permute-start | bytes 983048 | tf_op jit(solution)/shard_map/ppermute | solution.py:383
  17.3 1.2 collective-permute-done.other
  18.6 0.0 all-to-all-done.mine
  18.6 1.8 %shard_map.131 = (f32[2,256,1024]{2,1,0:T(8,128)S(1)}, f32[2,256,1024]{2,1,0:T(8,128)S(1)}, f32[2,8,256]{2,1,0:T(8,128)S(1)}) custom-call(bf16[256,640]{1,0:T(8,128)(2,1)S(1)} %shard_map.129.own, bf16[256,640]{1,0:T(8,128)(2,1)S(1)} %collective-permute-done.other, bf16[4,272,384]{2,1,0:T(8,128)(2,1)S(1)} %all-to-all-done.mine), custom_call_target="tpu_custom_call" | custom-call | tf_op jit(solution)/shard_map/pallas_call | solution.py:447
  20.3 7.8 %collective-permute-start.1 = (f32[2,8,256]{2,1,0:T(8,128)S(1)}, f32[2,8,256]{2,1,0:T(8,128)S(1)}, u32[]{:S(2)}, u32[]{:S(2)}) collective-permute-start(f32[2,8,256]{2,1,0:T(8,128)S(1)} %get-tuple-element.35.stats), channel_id=1, source_target_pairs={{0,8},{8,0},{1,9},{9,1},{2,10},{10,2},{3,11},{11,3},{4,12},{12,4},... | collective-permute-start | bytes 49160 | tf_op jit(solution)/shard_map/ppermute | solution.py:383
  28.2 0.6 shard_map.132
  28.8 0.0 copy-start.6
  28.8 0.6 copy-done.6
  29.4 0.0 collective-permute-done.1.got
  29.4 1.5 %shard_map.133 = (bf16[4,272,384]{2,1,0:T(8,128)(2,1)S(1)}, f32[256,256]{1,0:T(8,128)S(1)}, bf16[256,384]{1,0:T(8,128)(2,1)S(1)}) custom-call(bf16[256,640]{1,0:T(8,128)(2,1)S(1)} %shard_map.129.own, bf16[256,640]{1,0:T(8,128)(2,1)S(1)} %collective-permute-done.other, bf16[4,272,384]{2,1,0:T(8,128)(2,1)S(1)} %all-to-all-done.mine, ...), custom_call_target="tpu_custom_call" | custom-call | tf_op jit(solution)/shard_map/pallas_call | solution.py:458
  30.9 0.0 copy-start.5
  31.0 0.9 copy-done.5
  31.9 0.0 copy-start.9
  31.9 0.7 copy-done.9
  32.5 0.0 copy-start.7
  32.5 3.6 %all-to-all-start.1 = ((bf16[4,272,384]{2,1,0:T(8,128)(2,1)}), bf16[4,272,384]{2,1,0:T(8,128)(2,1)S(1)}, u32[]{:S(2)}, u32[]{:S(2)}) async-start(bf16[4,272,384]{2,1,0:T(8,128)(2,1)} %copy-done.5), calls=%async_computation.1 | async-start | bytes 1671168 | tf_op jit(solution)/shard_map/all_to_all | solution.py:387
  36.2 1.9 %collective-permute-start.2 = (bf16[256,384]{1,0:T(8,128)(2,1)}, bf16[256,384]{1,0:T(8,128)(2,1)S(1)}, u32[]{:S(2)}, u32[]{:S(2)}) collective-permute-start(bf16[256,384]{1,0:T(8,128)(2,1)} %copy-done.9), channel_id=1, source_target_pairs={{0,8},{8,0},{1,9},{9,1},{2,10},{10,2},{3,11},{11,3},{4,12},{12,4},... | collective-permute-start | bytes 589832 | tf_op jit(solution)/shard_map/ppermute | solution.py:383
  38.1 1.6 %collective-permute-done.2.query_got = bf16[256,384]{1,0:T(8,128)(2,1)S(1)} collective-permute-done((bf16[256,384]{1,0:T(8,128)(2,1)}, bf16[256,384]{1,0:T(8,128)(2,1)S(1)}, u32[]{:S(2)}, u32[]{:S(2)}) %collective-permute-start.2) | collective-permute-done | bytes 196640 | tf_op jit(solution)/shard_map/ppermute | solution.py:383
  39.7 9.4 %all-to-all-done.1.parts = bf16[4,272,384]{2,1,0:T(8,128)(2,1)S(1)} async-done(((bf16[4,272,384]{2,1,0:T(8,128)(2,1)}), bf16[4,272,384]{2,1,0:T(8,128)(2,1)S(1)}, u32[]{:S(2)}, u32[]{:S(2)}) %all-to-all-start.1) | async-done | bytes 835616 | tf_op jit(solution)/shard_map/all_to_all | solution.py:387
  49.1 0.7 shard_map.134
  49.8 2.7 %collective-permute-start.3 = (bf16[576,768]{1,0:T(8,128)(2,1)S(1)}, bf16[576,768]{1,0:T(8,128)(2,1)S(1)}, u32[]{:S(2)}, u32[]{:S(2)}) collective-permute-start(bf16[576,768]{1,0:T(8,128)(2,1)S(1)} %get-tuple-element.44), channel_id=1, source_target_pairs={{0,8},{8,0},{1,9},{9,1},{2,10},{10,2},{3,11},{11,3},{4,12},{12,4},... | collective-permute-start | bytes 2654216 | tf_op jit(solution)/shard_map/ppermute | solution.py:383
  52.5 0.0 copy-done.7
  52.5 0.0 copy-start.3
  52.5 1.1 copy-done.3
  53.6 0.0 copy-start.4
  53.6 1.1 copy-done.4
  54.7 1.1 shard_map.135
  55.8 0.0 collective-permute-done.3.refs_1_
  55.8 1.1 shard_map.136
  56.9 3.5 %all-to-all-start.2 = ((bf16[4,144,768]{2,1,0:T(8,128)(2,1)}), bf16[4,144,768]{2,1,0:T(8,128)(2,1)S(1)}, u32[]{:S(2)}, u32[]{:S(2)}) async-start(bf16[4,144,768]{2,1,0:T(8,128)(2,1)} %bitcast.7), calls=%async_computation.2 | async-start | bytes 1769472 | tf_op jit(solution)/shard_map/all_to_all | solution.py:387
  60.4 2.5 %collective-permute-start.4 = (bf16[4,192,256]{2,1,0:T(8,128)(2,1)S(1)}, bf16[4,192,256]{2,1,0:T(8,128)(2,1)S(1)}, u32[]{:S(2)}, u32[]{:S(2)}) collective-permute-start(bf16[4,192,256]{2,1,0:T(8,128)(2,1)S(1)} %get-tuple-element.51), channel_id=1, source_target_pairs={{0,1},{1,0},{2,3},{3,2},{4,5},{5,4},{6,7},{7,6},{8,9},{9,8},{10,11... | collective-permute-start | bytes 1179656 | tf_op jit(solution)/shard_map/ppermute | solution.py:383
  62.9 10.9 %all-to-all-done.2.parts = bf16[4,144,768]{2,1,0:T(8,128)(2,1)S(1)} async-done(((bf16[4,144,768]{2,1,0:T(8,128)(2,1)}), bf16[4,144,768]{2,1,0:T(8,128)(2,1)S(1)}, u32[]{:S(2)}, u32[]{:S(2)}) %all-to-all-start.2) | async-done | bytes 884768 | tf_op jit(solution)/shard_map/all_to_all | solution.py:387
  73.9 0.2 shard_map.137
  74.1 0.0 collective-permute-done.4.refs_1_
  74.1 15.0 %all_to_all.30.parts = bf16[8,36,384]{2,1,0:T(8,128)(2,1)S(1)} all-to-all(bf16[8,36,384]{2,1,0:T(8,128)(2,1)S(1)} %shard_map.137), channel_id=1, replica_groups=mesh['interval'=8,'x'=4,'core'=2,'pair'=4,'side'=2] {'interval'}, dimensions={0} | all-to-all | bytes 442368 | tf_op jit(solution)/shard_map/all_to_all | solution.py:387
  89.1 0.7 shard_map.138
  89.8 3.4 %all-to-all-start.4 = ((bf16[8,36,384]{2,1,0:T(8,128)(2,1)}), bf16[8,36,384]{2,1,0:T(8,128)(2,1)S(1)}, u32[]{:S(2)}, u32[]{:S(2)}) async-start(bf16[8,36,384]{2,1,0:T(8,128)(2,1)} %shard_map.138), calls=%async_computation.4 | async-start | bytes 491520 | tf_op jit(solution)/shard_map/all_to_all | solution.py:387
  93.2 0.8 shard_map.140
  94.1 8.3 %all-to-all-done.4.tiles = bf16[8,36,384]{2,1,0:T(8,128)(2,1)S(1)} async-done(((bf16[8,36,384]{2,1,0:T(8,128)(2,1)}), bf16[8,36,384]{2,1,0:T(8,128)(2,1)S(1)}, u32[]{:S(2)}, u32[]{:S(2)}) %all-to-all-start.4) | async-done | bytes 221216 | tf_op jit(solution)/shard_map/all_to_all | solution.py:387
  102.4 10.0 %all-to-all-start.5 = ((bf16[4,192,256]{2,1,0:T(8,128)(2,1)}), bf16[4,192,256]{2,1,0:T(8,128)(2,1)S(1)}, u32[]{:S(2)}, u32[]{:S(2)}) async-start(bf16[4,192,256]{2,1,0:T(8,128)(2,1)} %shard_map.140), calls=%async_computation.5 | async-start | bytes 786432 | tf_op jit(solution)/shard_map/all_to_all | solution.py:387
  112.4 11.2 %all_gather.3.mine = bf16[576,768]{1,0:T(8,128)(2,1)S(1)} all-gather(bf16[144,768]{1,0:T(8,128)(2,1)S(1)} %shard_map.139), channel_id=1, replica_groups=mesh['interval'=8,'x'=4,'core'=2,'pair'=4,'side'=2] {'x'}, dimensions={0}, use_global_device_ids=true | all-gather | bytes 1105920 | tf_op jit(solution)/shard_map/all_gather | solution.py:512
  123.6 0.0 all-to-all-done.5.parts
  123.6 8.6 %collective-permute-start.5 = (bf16[576,768]{1,0:T(8,128)(2,1)S(1)}, bf16[576,768]{1,0:T(8,128)(2,1)S(1)}, u32[]{:S(2)}, u32[]{:S(2)}) collective-permute-start(bf16[576,768]{1,0:T(8,128)(2,1)S(1)} %all_gather.3.mine), channel_id=1, source_target_pairs={{0,8},{8,0},{1,9},{9,1},{2,10},{10,2},{3,11},{11,3},{4,12},{12,4},... | collective-permute-start | bytes 2654216 | tf_op jit(solution)/shard_map/ppermute | solution.py:383
  132.3 0.7 shard_map.141
  133.0 1.3 collective-permute-done.5.theirs
  134.3 1.2 shard_map.142
  (1 shorter events, 0.0 us)
Async XLA Ops:
  0.6 8.6 %copy-start.1 = (bf16[1536,128]{1,0:T(8,128)(2,1)S(1)}, bf16[1536,128]{1,0:T(8,128)(2,1)}, u32[]{:S(2)}) copy-start(bf16[1536,128]{1,0:T(8,128)(2,1)} %w_junction.3) | copy-start | bytes 1179652
  0.6 8.6 %copy-start = (bf16[1,256,1536]{2,1,0:T(8,128)(2,1)S(1)}, bf16[1,256,1536]{2,1,0:T(8,128)(2,1)}, u32[]{:S(2)}) copy-start(bf16[1,256,1536]{2,1,0:T(8,128)(2,1)} %param.10) | copy-start | bytes 2359300
  0.7 8.6 %copy-start.2 = (bf16[192,1536]{1,0:T(8,128)(2,1)S(1)}, bf16[192,1536]{1,0:T(8,128)(2,1)}, u32[]{:S(2)}) copy-start(bf16[192,1536]{1,0:T(8,128)(2,1)} %w_query.3) | copy-start | bytes 1769476
  0.7 8.6 %copy-start.8 = (bf16[1,256,192]{1,2,0:T(8,128)(2,1)S(1)}, bf16[1,256,192]{1,2,0:T(8,128)(2,1)}, u32[]{:S(2)}) copy-start(bf16[1,256,192]{1,2,0:T(8,128)(2,1)} %param.11) | copy-start | bytes 294916
  4.4 14.2 %all-to-all-start = ((bf16[4,272,384]{2,1,0:T(8,128)(2,1)}), bf16[4,272,384]{2,1,0:T(8,128)(2,1)S(1)}, u32[]{:S(2)}, u32[]{:S(2)}) async-start(bf16[4,272,384]{2,1,0:T(8,128)(2,1)} %get-tuple-element.32), calls=%async_computation | async-start | bytes 1671168 | tf_op jit(solution)/shard_map/all_to_all | solution.py:387
  9.8 8.7 %collective-permute-start = (bf16[256,640]{1,0:T(8,128)(2,1)S(1)}, bf16[256,640]{1,0:T(8,128)(2,1)S(1)}, u32[]{:S(2)}, u32[]{:S(2)}) collective-permute-start(bf16[256,640]{1,0:T(8,128)(2,1)S(1)} %shard_map.129.own), channel_id=1, source_target_pairs={{0,8},{8,0},{1,9},{9,1},{2,10},{10,2},{3,11},{11,3},{4,12},{12,4},... | collective-permute-start | bytes 983048 | tf_op jit(solution)/shard_map/ppermute | solution.py:383
  20.3 9.1 %collective-permute-start.1 = (f32[2,8,256]{2,1,0:T(8,128)S(1)}, f32[2,8,256]{2,1,0:T(8,128)S(1)}, u32[]{:S(2)}, u32[]{:S(2)}) collective-permute-start(f32[2,8,256]{2,1,0:T(8,128)S(1)} %get-tuple-element.35.stats), channel_id=1, source_target_pairs={{0,8},{8,0},{1,9},{9,1},{2,10},{10,2},{3,11},{11,3},{4,12},{12,4},... | collective-permute-start | bytes 49160 | tf_op jit(solution)/shard_map/ppermute | solution.py:383
  28.8 0.7 copy-start.6
  30.9 0.9 copy-start.5
  31.9 0.7 copy-start.9
  32.5 20.0 %copy-start.7 = (f32[256,128]{1,0:T(8,128)S(1)}, f32[256,128]{1,0:T(8,128)}, u32[]{:S(2)}) copy-start(f32[256,128]{1,0:T(8,128)} %copy-done.6) | copy-start | bytes 393220
  32.5 16.6 %all-to-all-start.1 = ((bf16[4,272,384]{2,1,0:T(8,128)(2,1)}), bf16[4,272,384]{2,1,0:T(8,128)(2,1)S(1)}, u32[]{:S(2)}, u32[]{:S(2)}) async-start(bf16[4,272,384]{2,1,0:T(8,128)(2,1)} %copy-done.5), calls=%async_computation.1 | async-start | bytes 1671168 | tf_op jit(solution)/shard_map/all_to_all | solution.py:387
  36.2 3.5 %collective-permute-start.2 = (bf16[256,384]{1,0:T(8,128)(2,1)}, bf16[256,384]{1,0:T(8,128)(2,1)S(1)}, u32[]{:S(2)}, u32[]{:S(2)}) collective-permute-start(bf16[256,384]{1,0:T(8,128)(2,1)} %copy-done.9), channel_id=1, source_target_pairs={{0,8},{8,0},{1,9},{9,1},{2,10},{10,2},{3,11},{11,3},{4,12},{12,4},... | collective-permute-start | bytes 589832 | tf_op jit(solution)/shard_map/ppermute | solution.py:383
  49.8 6.0 %collective-permute-start.3 = (bf16[576,768]{1,0:T(8,128)(2,1)S(1)}, bf16[576,768]{1,0:T(8,128)(2,1)S(1)}, u32[]{:S(2)}, u32[]{:S(2)}) collective-permute-start(bf16[576,768]{1,0:T(8,128)(2,1)S(1)} %get-tuple-element.44), channel_id=1, source_target_pairs={{0,8},{8,0},{1,9},{9,1},{2,10},{10,2},{3,11},{11,3},{4,12},{12,4},... | collective-permute-start | bytes 2654216 | tf_op jit(solution)/shard_map/ppermute | solution.py:383
  52.5 1.1 copy-start.3
  53.6 1.1 copy-start.4
  56.9 17.0 %all-to-all-start.2 = ((bf16[4,144,768]{2,1,0:T(8,128)(2,1)}), bf16[4,144,768]{2,1,0:T(8,128)(2,1)S(1)}, u32[]{:S(2)}, u32[]{:S(2)}) async-start(bf16[4,144,768]{2,1,0:T(8,128)(2,1)} %bitcast.7), calls=%async_computation.2 | async-start | bytes 1769472 | tf_op jit(solution)/shard_map/all_to_all | solution.py:387
  60.4 13.7 %collective-permute-start.4 = (bf16[4,192,256]{2,1,0:T(8,128)(2,1)S(1)}, bf16[4,192,256]{2,1,0:T(8,128)(2,1)S(1)}, u32[]{:S(2)}, u32[]{:S(2)}) collective-permute-start(bf16[4,192,256]{2,1,0:T(8,128)(2,1)S(1)} %get-tuple-element.51), channel_id=1, source_target_pairs={{0,1},{1,0},{2,3},{3,2},{4,5},{5,4},{6,7},{7,6},{8,9},{9,8},{10,11... | collective-permute-start | bytes 1179656 | tf_op jit(solution)/shard_map/ppermute | solution.py:383
  89.8 12.5 %all-to-all-start.4 = ((bf16[8,36,384]{2,1,0:T(8,128)(2,1)}), bf16[8,36,384]{2,1,0:T(8,128)(2,1)S(1)}, u32[]{:S(2)}, u32[]{:S(2)}) async-start(bf16[8,36,384]{2,1,0:T(8,128)(2,1)} %shard_map.138), calls=%async_computation.4 | async-start | bytes 491520 | tf_op jit(solution)/shard_map/all_to_all | solution.py:387
  102.4 21.3 %all-to-all-start.5 = ((bf16[4,192,256]{2,1,0:T(8,128)(2,1)}), bf16[4,192,256]{2,1,0:T(8,128)(2,1)S(1)}, u32[]{:S(2)}, u32[]{:S(2)}) async-start(bf16[4,192,256]{2,1,0:T(8,128)(2,1)} %shard_map.140), calls=%async_computation.5 | async-start | bytes 786432 | tf_op jit(solution)/shard_map/all_to_all | solution.py:387
  123.6 10.7 %collective-permute-start.5 = (bf16[576,768]{1,0:T(8,128)(2,1)S(1)}, bf16[576,768]{1,0:T(8,128)(2,1)S(1)}, u32[]{:S(2)}, u32[]{:S(2)}) collective-permute-start(bf16[576,768]{1,0:T(8,128)(2,1)S(1)} %all_gather.3.mine), channel_id=1, source_target_pairs={{0,8},{8,0},{1,9},{9,1},{2,10},{10,2},{3,11},{11,3},{4,12},{12,4},... | collective-permute-start | bytes 2654216 | tf_op jit(solution)/shard_map/ppermute | solution.py:383

commit v10 on v9

--- a/solution.py
+++ b/solution.py
@@ -32,11 +32,16 @@
 def local_call(body, outs, operands, scratch=(), fetched=0, space=pltpu.VMEM):
     specs = [pl.BlockSpec(memory_space=pltpu.HBM)] * fetched
     specs += [pl.BlockSpec(memory_space=space)] * (operands - fetched)
+    shapes = [
+        (pltpu.HBM if len(out) > 2 else jax.ShapeDtypeStruct)(out[0], out[1]) for out in outs
+    ]
     return pl.pallas_call(
         body,
-        out_shape=tuple(jax.ShapeDtypeStruct(shape, kind) for shape, kind in outs),
+        out_shape=tuple(shapes),
         in_specs=specs,
-        out_specs=tuple(pl.BlockSpec(memory_space=space) for _ in outs),
+        out_specs=tuple(
+            pl.BlockSpec(memory_space=pltpu.HBM if len(out) > 2 else space) for out in outs
+        ),
         scratch_shapes=list(scratch),
         compiler_params=pltpu.CompilerParams(vmem_limit_bytes=VMEM_BYTES),
     )
@@ -62,6 +67,8 @@
     pred_hbm,
     message,
     donor_hot,
+    rows,
+    slot_rows,
     hidden,
     weights,
     w_junction,
@@ -70,6 +77,7 @@
     counts,
     pred_grad,
     sems,
+    row_sems,
 ):
     targets = (
         donor_pos,
@@ -129,9 +137,16 @@
     for copy in copies[4:]:
         copy.wait()
     x = hidden[...]
-    rows = contract(x, weights[...], 1, 1).astype(BF16)
+    rows[...] = contract(x, weights[...], 1, 1).astype(BF16)
+    part = slots // chips
+    leaving = [
+        pltpu.make_async_copy(rows, message.at[chip, pl.ds(0, tokens)], row_sems.at[chip])
+        for chip in range(chips)
+    ]
+    for copy in leaving:
+        copy.start()
     feats = contract(x, w_junction[...], 1, 0).astype(BF16)
-    slot_rows = jnp.concatenate(
+    slot_rows[...] = jnp.concatenate(
         [
             contract(hot, feats, 1, 0).astype(BF16),
             extra.astype(BF16),
@@ -139,10 +154,18 @@
         ],
         axis=1,
     )
-    part = slots // chips
-    for chip in range(chips):
-        message[chip, :tokens, :] = rows
-        message[chip, tokens:, :] = slot_rows[chip * part : (chip + 1) * part, :]
+    last = [
+        pltpu.make_async_copy(
+            slot_rows.at[pl.ds(chip * part, part)],
+            message.at[chip, pl.ds(tokens, part)],
+            row_sems.at[chips + chip],
+        )
+        for chip in range(chips)
+    ]
+    for copy in last:
+        copy.start()
+    for copy in leaving + last:
+        copy.wait()
 
 
 def query_body(hidden, w_query, w_junction, ctx_t, rows):
@@ -216,7 +239,23 @@
 
 
 def grad_body(
-    own, other, mine, expd, dprobs, stats, got, back, sent_sum, terms, kept, sent, probs_b, dscores_b
+    own,
+    other,
+    mine,
+    expd,
+    dprobs,
+    stats,
+    got,
+    back,
+    sent_sum,
+    terms_out,
+    sent_out,
+    kept,
+    terms,
+    sent,
+    probs_b,
+    dscores_b,
+    sems,
 ):
     tokens = own.shape[0]
     chips, height, _ = mine.shape
@@ -254,11 +293,17 @@
         )
     terms[:, tokens:, :PJ] = back[...]
     terms[:, tokens:, PJ:] = jnp.zeros((chips, part, KV - PJ), BF16)
+    first = pltpu.make_async_copy(terms, terms_out, sems.at[0])
+    first.start()
     keys = mine[:, :tokens, :LANES].reshape(half, LANES)
     query_term = contract(dscores_b[...], keys, 1, 0) * scale
     kept[...] = query_term[:tokens, :]
     sent[:, :LANES] = query_term[tokens:, :].astype(BF16)
     sent[:, LANES:] = sent_sum[...].astype(BF16)
+    second = pltpu.make_async_copy(sent, sent_out, sems.at[1])
+    second.start()
+    first.wait()
+    second.wait()
 
 
 def halve(value, side):
@@ -297,25 +342,40 @@
 
 
 def input_body(
+    w_query_hbm,
+    w_key_hbm,
+    w_value_hbm,
+    w_junction_hbm,
     parts,
     kept_sum,
     query_got,
     donor_hot,
     grads,
     query_grad,
+    kept,
+    sent,
     w_query,
     w_key,
     w_value,
     w_junction,
-    kept,
-    sent,
+    sems,
 ):
+    sources = (w_junction_hbm, w_query_hbm, w_key_hbm, w_value_hbm)
+    targets = (w_junction, w_query, w_key, w_value)
+    copies = [
+        pltpu.make_async_copy(source, target, sems.at[i])
+        for i, (source, target) in enumerate(zip(sources, targets))
+    ]
+    for copy in copies:
+        copy.start()
     chips, height, _ = parts.shape
     tokens = grads.shape[0]
     part = height - tokens
     slot_rows = parts[:, tokens:, :PJ].reshape(chips * part, PJ)
     feature_grad = kept_sum[...] + query_got[:, LANES:].astype(F32)
     feature_grad = (feature_grad + contract(donor_hot[...], slot_rows, 0, 0)).astype(BF16)
+    for copy in copies:
+        copy.wait()
     value = contract(w_query[...], query_grad[...], 0, 1)
     value = value + contract(w_key[...], grads[:, :HD], 0, 1)
     value = value + contract(w_value[...], grads[:, HD:], 0, 1)
@@ -381,6 +441,10 @@
 
 def swap(value, axis="core"):
     return lax.ppermute(value, axis, [(0, 1), (1, 0)])
+
+
+def in_hbm(*values):
+    return [pltpu.with_memory_space_constraint(value, pltpu.HBM) for value in values]
 
 
 def exchange(value, axis):
@@ -411,10 +475,12 @@
 
     message, donor_hot = local_call(
         project_body,
-        [((chips, height, KV), BF16), ((slots, tokens), BF16)],
+        [((chips, height, KV), BF16, True), ((slots, tokens), BF16)],
         operands=8,
         fetched=8,
         scratch=[
+            pltpu.VMEM((tokens, KV), BF16),
+            pltpu.VMEM((slots, KV), BF16),
             pltpu.VMEM((tokens, width), BF16),
             pltpu.VMEM((KV, width), BF16),
             pltpu.VMEM((width, PJ), BF16),
@@ -423,20 +489,18 @@
             pltpu.VMEM((1, buckets), jnp.int32),
             pltpu.VMEM((buckets, per), F32),
             pltpu.SemaphoreType.DMA((8,)),
+            pltpu.SemaphoreType.DMA((2 * chips,)),
         ],
     )(
-        *(
-            pltpu.with_memory_space_constraint(value, pltpu.HBM)
-            for value in (
-                hidden,
-                w_key,
-                w_value,
-                w_junction,
-                donor_pos[0, 0],
-                acceptor_pos[0, 0],
-                junction_counts[0],
-                pred_grad[0, 0],
-            )
+        *in_hbm(
+            hidden,
+            w_key,
+            w_value,
+            w_junction,
+            donor_pos[0, 0],
+            acceptor_pos[0, 0],
+            junction_counts[0],
+            pred_grad[0, 0],
         )
     )
     mine = exchange(message, "x")
@@ -455,15 +519,20 @@
         [((chips, height - tokens, PJ), BF16), ((tokens, PJ), F32), ((tokens, PJ), F32)],
         operands=3,
     )(own, other, mine)
-    terms, query_held, query_sent = local_call(
+    terms, query_sent, query_held = local_call(
         grad_body,
         [
-            ((chips, height, KV), BF16),
+            ((chips, height, KV), BF16, True),
+            ((tokens, LANES + PJ), BF16, True),
             ((tokens, LANES), F32),
-            ((tokens, LANES + PJ), BF16),
         ],
         operands=9,
-        scratch=[pltpu.VMEM((CORES * tokens, half), BF16)] * 2,
+        scratch=[
+            pltpu.VMEM((chips, height, KV), BF16),
+            pltpu.VMEM((tokens, LANES + PJ), BF16),
+        ]
+        + [pltpu.VMEM((CORES * tokens, half), BF16)] * 2
+        + [pltpu.SemaphoreType.DMA((2,))],
     )(own, other, mine, expd, dprobs, stats, got, back, sent_sum)
     query_got = swap(query_sent)
     parts = exchange(terms, "x")
@@ -480,17 +549,17 @@
         input_body,
         [((heads // 2,) + block, F32), ((heads // 2,) + block, BF16)],
         operands=10,
+        fetched=4,
+        scratch=[pltpu.VMEM((HD, width), BF16)] * 3
+        + [pltpu.VMEM((width, PJ), BF16), pltpu.SemaphoreType.DMA((4,))],
     )(
+        *in_hbm(w_query, w_key, w_value, w_junction),
         parts,
         kept_sum,
         query_got,
         donor_hot,
         grads,
         query_grad,
-        w_query,
-        w_key,
-        w_value,
-        w_junction,
     )
 
     weight_got, sent = lax.optimization_barrier((swap(weight_sent), sent))

time: 136 us -> 134 us (0.985)
  local copies, waits for them, and re-layouts: 4.38 us -> 0.02 us
  Pallas kernels: 14.7 us -> 17.1 us
    unnamed x20 -> x8, local copies, waits for them, and re-layouts: 4.38 us -> 0.02 us
    pallas_call x1, Pallas kernels: 1.12 us -> 2.68 us  [on_device(): local_call(input_body, [((heads // 2,) + block, F32), ((heads // 2,) + bl...]
  transfers between devices with their start and end apart: 11 -> 11, of which waited for: 6 -> 7; matrix products, arithmetic and copies ran while one was open for 0% -> 0% of each run, Pallas kernels for 3% -> 4%
where the time goes in v10:
time: 134 us
  starting transfers between devices  57.1 us (43%)
  waiting for transfers between devices  32.4 us (24%)
  blocking collectives  26.2 us (20%)
  Pallas kernels  17.1 us (13%)
    ppermute x6, starting transfers between devices, swap(): return lax.ppermute(value, axis, [(0, 1), (1, 0)])  31.8 us
    all_to_all x5, waiting for transfers between devices, exchange(): return lax.all_to_all(value, axis, 0, 0, tiled=True)  28.3 us
    all_to_all x5, starting transfers between devices, exchange(): return lax.all_to_all(value, axis, 0, 0, tiled=True)  25.3 us
    all_to_all x1, blocking collectives, exchange(): return lax.all_to_all(value, axis, 0, 0, tiled=True)  15 us
    all_gather x1, blocking collectives, on_device(): term = lax.all_gather(term, 'x', axis=0, tiled=True)  11.2 us
    ppermute x6, waiting for transfers between devices, swap(): return lax.ppermute(value, axis, [(0, 1), (1, 0)])  4.09 us
    pallas_call x1, Pallas kernels, on_device(): local_call(project_body, [((chips, height, KV), BF16, True), ((slots, tok...  3.48 us
  transfers between devices with their start and end apart: 11, of which 7 were waited for; matrix products, arithmetic and copies ran while one was open for 0% of the time, Pallas kernels for 4%

profile of v10, /device:TPU:1, one launch (start us, length us, event | category | flops | bytes accessed | tf_op | source)
XLA Modules:
  0.0 133.6 jit_solution(1044523797170799093)
XLA Ops:
  0.6 0.0 copy-start.1
  0.6 0.0 copy-start
  0.7 0.0 copy-start.2
  0.7 0.0 copy-start.3
  0.7 3.5 %shard_map.130 = (bf16[4,272,384]{2,1,0:T(8,128)(2,1)}, bf16[64,256]{1,0:T(8,128)(2,1)S(1)}) custom-call(bf16[256,1536]{1,0:T(8,128)(2,1)} %bitcast.12, bf16[192,1536]{1,0:T(8,128)(2,1)} %w_key_hbm.3, bf16[192,1536]{1,0:T(8,128)(2,1)} %w_value_hbm.3, bf16[1536,128]{1,0:T(8,128)(2,1)} %w_junction_hbm.3, s32[8,8]{1,0:T(8,128)} %bitcast.17, s32[8,8]{1,0:T(8,128)} %bitcast.18, ...), custom_call_target="tpu_custom_call" | custom-call | tf_op jit(solution)/shard_map/pallas_call | solution.py:476
  4.2 4.9 %all-to-all-start = ((bf16[4,272,384]{2,1,0:T(8,128)(2,1)}), bf16[4,272,384]{2,1,0:T(8,128)(2,1)S(1)}, u32[]{:S(2)}, u32[]{:S(2)}) async-start(bf16[4,272,384]{2,1,0:T(8,128)(2,1)} %get-tuple-element.32), calls=%async_computation | async-start | bytes 1671168 | tf_op jit(solution)/shard_map/all_to_all | solution.py:451
  9.0 0.0 copy-done.1
  9.0 0.0 copy-done
  9.0 0.0 copy-done.2
  9.0 0.0 copy-done.3
  9.0 0.6 shard_map.129.own
  9.6 7.5 %collective-permute-start = (bf16[256,640]{1,0:T(8,128)(2,1)S(1)}, bf16[256,640]{1,0:T(8,128)(2,1)S(1)}, u32[]{:S(2)}, u32[]{:S(2)}) collective-permute-start(bf16[256,640]{1,0:T(8,128)(2,1)S(1)} %shard_map.129.own), channel_id=1, source_target_pairs={{0,8},{8,0},{1,9},{9,1},{2,10},{10,2},{3,11},{11,3},{4,12},{12,4},... | collective-permute-start | bytes 983048 | tf_op jit(solution)/shard_map/ppermute | solution.py:443
  17.1 1.2 collective-permute-done.other
  18.3 0.0 all-to-all-done.mine
  18.3 1.8 %shard_map.131 = (f32[2,256,1024]{2,1,0:T(8,128)S(1)}, f32[2,256,1024]{2,1,0:T(8,128)S(1)}, f32[2,8,256]{2,1,0:T(8,128)S(1)}) custom-call(bf16[256,640]{1,0:T(8,128)(2,1)S(1)} %shard_map.129.own, bf16[256,640]{1,0:T(8,128)(2,1)S(1)} %collective-permute-done.other, bf16[4,272,384]{2,1,0:T(8,128)(2,1)S(1)} %all-to-all-done.mine), custom_call_target="tpu_custom_call" | custom-call | tf_op jit(solution)/shard_map/pallas_call | solution.py:511
  20.1 7.8 %collective-permute-start.1 = (f32[2,8,256]{2,1,0:T(8,128)S(1)}, f32[2,8,256]{2,1,0:T(8,128)S(1)}, u32[]{:S(2)}, u32[]{:S(2)}) collective-permute-start(f32[2,8,256]{2,1,0:T(8,128)S(1)} %get-tuple-element.35.stats), channel_id=1, source_target_pairs={{0,8},{8,0},{1,9},{9,1},{2,10},{10,2},{3,11},{11,3},{4,12},{12,4},... | collective-permute-start | bytes 49160 | tf_op jit(solution)/shard_map/ppermute | solution.py:443
  28.0 0.6 shard_map.132
  28.6 0.2 collective-permute-done.1.got
  28.8 2.5 %shard_map.133 = (bf16[4,272,384]{2,1,0:T(8,128)(2,1)}, bf16[256,384]{1,0:T(8,128)(2,1)}, f32[256,256]{1,0:T(8,128)S(1)}) custom-call(bf16[256,640]{1,0:T(8,128)(2,1)S(1)} %shard_map.129.own, bf16[256,640]{1,0:T(8,128)(2,1)S(1)} %collective-permute-done.other, bf16[4,272,384]{2,1,0:T(8,128)(2,1)S(1)} %all-to-all-done.mine, ...), custom_call_target="tpu_custom_call" | custom-call | tf_op jit(solution)/shard_map/pallas_call | solution.py:522
  31.3 3.5 %all-to-all-start.1 = ((bf16[4,272,384]{2,1,0:T(8,128)(2,1)}), bf16[4,272,384]{2,1,0:T(8,128)(2,1)S(1)}, u32[]{:S(2)}, u32[]{:S(2)}) async-start(bf16[4,272,384]{2,1,0:T(8,128)(2,1)} %get-tuple-element.38), calls=%async_computation.1 | async-start | bytes 1671168 | tf_op jit(solution)/shard_map/all_to_all | solution.py:451
  34.8 2.3 %collective-permute-start.2 = (bf16[256,384]{1,0:T(8,128)(2,1)}, bf16[256,384]{1,0:T(8,128)(2,1)S(1)}, u32[]{:S(2)}, u32[]{:S(2)}) collective-permute-start(bf16[256,384]{1,0:T(8,128)(2,1)} %get-tuple-element.39), channel_id=1, source_target_pairs={{0,8},{8,0},{1,9},{9,1},{2,10},{10,2},{3,11},{11,3},{4,12},{12,4},... | collective-permute-start | bytes 589832 | tf_op jit(solution)/shard_map/ppermute | solution.py:443
  37.1 1.3 collective-permute-done.2.query_got
  38.4 9.0 %all-to-all-done.1.parts = bf16[4,272,384]{2,1,0:T(8,128)(2,1)S(1)} async-done(((bf16[4,272,384]{2,1,0:T(8,128)(2,1)}), bf16[4,272,384]{2,1,0:T(8,128)(2,1)S(1)}, u32[]{:S(2)}, u32[]{:S(2)}) %all-to-all-start.1) | async-done | bytes 835616 | tf_op jit(solution)/shard_map/all_to_all | solution.py:451
  47.4 0.7 shard_map.134
  48.1 3.1 %collective-permute-start.3 = (bf16[576,768]{1,0:T(8,128)(2,1)S(1)}, bf16[576,768]{1,0:T(8,128)(2,1)S(1)}, u32[]{:S(2)}, u32[]{:S(2)}) collective-permute-start(bf16[576,768]{1,0:T(8,128)(2,1)S(1)} %get-tuple-element.44), channel_id=1, source_target_pairs={{0,8},{8,0},{1,9},{9,1},{2,10},{10,2},{3,11},{11,3},{4,12},{12,4},... | collective-permute-start | bytes 2654216 | tf_op jit(solution)/shard_map/ppermute | solution.py:443
  51.2 2.7 %shard_map.135 = (f32[4,192,256]{2,1,0:T(8,128)S(1)}, bf16[4,192,256]{2,1,0:T(8,128)(2,1)S(1)}) custom-call(bf16[192,1536]{1,0:T(8,128)(2,1)} %w_query_hbm.1, bf16[192,1536]{1,0:T(8,128)(2,1)} %w_key_hbm.3, bf16[192,1536]{1,0:T(8,128)(2,1)} %w_value_hbm.3, bf16[1536,128]{1,0:T(8,128)(2,1)} %w_junction_hbm.3, bf16[4,272,384]{2,1,0:T(8,128)(2,1)S(1)} %all-to-all-done.1.parts, ...), custom_call_target="tpu_custom_call" | custom-call | tf_op jit(solution)/shard_map/pallas_call | solution.py:548
  53.9 0.0 collective-permute-done.3.refs_1_
  53.9 1.1 shard_map.136
  54.9 3.5 %all-to-all-start.2 = ((bf16[4,144,768]{2,1,0:T(8,128)(2,1)}), bf16[4,144,768]{2,1,0:T(8,128)(2,1)S(1)}, u32[]{:S(2)}, u32[]{:S(2)}) async-start(bf16[4,144,768]{2,1,0:T(8,128)(2,1)} %bitcast.7), calls=%async_computation.2 | async-start | bytes 1769472 | tf_op jit(solution)/shard_map/all_to_all | solution.py:451
  58.4 2.5 %collective-permute-start.4 = (bf16[4,192,256]{2,1,0:T(8,128)(2,1)S(1)}, bf16[4,192,256]{2,1,0:T(8,128)(2,1)S(1)}, u32[]{:S(2)}, u32[]{:S(2)}) collective-permute-start(bf16[4,192,256]{2,1,0:T(8,128)(2,1)S(1)} %get-tuple-element.51), channel_id=1, source_target_pairs={{0,1},{1,0},{2,3},{3,2},{4,5},{5,4},{6,7},{7,6},{8,9},{9,8},{10,11... | collective-permute-start | bytes 1179656 | tf_op jit(solution)/shard_map/ppermute | solution.py:443
  61.0 10.9 %all-to-all-done.2.parts = bf16[4,144,768]{2,1,0:T(8,128)(2,1)S(1)} async-done(((bf16[4,144,768]{2,1,0:T(8,128)(2,1)}), bf16[4,144,768]{2,1,0:T(8,128)(2,1)S(1)}, u32[]{:S(2)}, u32[]{:S(2)}) %all-to-all-start.2) | async-done | bytes 884768 | tf_op jit(solution)/shard_map/all_to_all | solution.py:451
  71.9 0.2 shard_map.137
  72.1 0.0 collective-permute-done.4.refs_1_
  72.1 15.0 %all_to_all.30.parts = bf16[8,36,384]{2,1,0:T(8,128)(2,1)S(1)} all-to-all(bf16[8,36,384]{2,1,0:T(8,128)(2,1)S(1)} %shard_map.137), channel_id=1, replica_groups=mesh['interval'=8,'x'=4,'core'=2,'pair'=4,'side'=2] {'interval'}, dimensions={0} | all-to-all | bytes 442368 | tf_op jit(solution)/shard_map/all_to_all | solution.py:451
  87.1 0.7 shard_map.138
  87.9 3.4 %all-to-all-start.4 = ((bf16[8,36,384]{2,1,0:T(8,128)(2,1)}), bf16[8,36,384]{2,1,0:T(8,128)(2,1)S(1)}, u32[]{:S(2)}, u32[]{:S(2)}) async-start(bf16[8,36,384]{2,1,0:T(8,128)(2,1)} %shard_map.138), calls=%async_computation.4 | async-start | bytes 491520 | tf_op jit(solution)/shard_map/all_to_all | solution.py:451
  91.3 0.8 shard_map.140
  92.1 8.3 %all-to-all-done.4.tiles = bf16[8,36,384]{2,1,0:T(8,128)(2,1)S(1)} async-done(((bf16[8,36,384]{2,1,0:T(8,128)(2,1)}), bf16[8,36,384]{2,1,0:T(8,128)(2,1)S(1)}, u32[]{:S(2)}, u32[]{:S(2)}) %all-to-all-start.4) | async-done | bytes 221216 | tf_op jit(solution)/shard_map/all_to_all | solution.py:451
  100.4 10.0 %all-to-all-start.5 = ((bf16[4,192,256]{2,1,0:T(8,128)(2,1)}), bf16[4,192,256]{2,1,0:T(8,128)(2,1)S(1)}, u32[]{:S(2)}, u32[]{:S(2)}) async-start(bf16[4,192,256]{2,1,0:T(8,128)(2,1)} %shard_map.140), calls=%async_computation.5 | async-start | bytes 786432 | tf_op jit(solution)/shard_map/all_to_all | solution.py:451
  110.5 11.2 %all_gather.3.mine = bf16[576,768]{1,0:T(8,128)(2,1)S(1)} all-gather(bf16[144,768]{1,0:T(8,128)(2,1)S(1)} %shard_map.139), channel_id=1, replica_groups=mesh['interval'=8,'x'=4,'core'=2,'pair'=4,'side'=2] {'x'}, dimensions={0}, use_global_device_ids=true | all-gather | bytes 1105920 | tf_op jit(solution)/shard_map/all_gather | solution.py:581
  121.7 0.0 all-to-all-done.5.parts
  121.7 8.6 %collective-permute-start.5 = (bf16[576,768]{1,0:T(8,128)(2,1)S(1)}, bf16[576,768]{1,0:T(8,128)(2,1)S(1)}, u32[]{:S(2)}, u32[]{:S(2)}) collective-permute-start(bf16[576,768]{1,0:T(8,128)(2,1)S(1)} %all_gather.3.mine), channel_id=1, source_target_pairs={{0,8},{8,0},{1,9},{9,1},{2,10},{10,2},{3,11},{11,3},{4,12},{12,4},... | collective-permute-start | bytes 2654216 | tf_op jit(solution)/shard_map/ppermute | solution.py:443
  130.3 0.7 shard_map.141
  131.0 1.3 %collective-permute-done.5.theirs = bf16[576,768]{1,0:T(8,128)(2,1)S(1)} collective-permute-done((bf16[576,768]{1,0:T(8,128)(2,1)S(1)}, bf16[576,768]{1,0:T(8,128)(2,1)S(1)}, u32[]{:S(2)}, u32[]{:S(2)}) %collective-permute-start.5) | collective-permute-done | bytes 884768 | tf_op jit(solution)/shard_map/ppermute | solution.py:443
  132.4 1.2 shard_map.142
  (1 shorter events, 0.0 us)
Async XLA Ops:
  0.6 8.4 %copy-start.1 = (bf16[1536,128]{1,0:T(8,128)(2,1)S(1)}, bf16[1536,128]{1,0:T(8,128)(2,1)}, u32[]{:S(2)}) copy-start(bf16[1536,128]{1,0:T(8,128)(2,1)} %w_junction_hbm.3) | copy-start | bytes 1179652
  0.6 8.4 %copy-start = (bf16[1,256,1536]{2,1,0:T(8,128)(2,1)S(1)}, bf16[1,256,1536]{2,1,0:T(8,128)(2,1)}, u32[]{:S(2)}) copy-start(bf16[1,256,1536]{2,1,0:T(8,128)(2,1)} %param.10) | copy-start | bytes 2359300
  0.7 8.4 %copy-start.2 = (bf16[192,1536]{1,0:T(8,128)(2,1)S(1)}, bf16[192,1536]{1,0:T(8,128)(2,1)}, u32[]{:S(2)}) copy-start(bf16[192,1536]{1,0:T(8,128)(2,1)} %w_query_hbm.1) | copy-start | bytes 1769476
  0.7 8.4 %copy-start.3 = (bf16[1,256,192]{1,2,0:T(8,128)(2,1)S(1)}, bf16[1,256,192]{1,2,0:T(8,128)(2,1)}, u32[]{:S(2)}) copy-start(bf16[1,256,192]{1,2,0:T(8,128)(2,1)} %param.11) | copy-start | bytes 294916
  4.2 14.2 %all-to-all-start = ((bf16[4,272,384]{2,1,0:T(8,128)(2,1)}), bf16[4,272,384]{2,1,0:T(8,128)(2,1)S(1)}, u32[]{:S(2)}, u32[]{:S(2)}) async-start(bf16[4,272,384]{2,1,0:T(8,128)(2,1)} %get-tuple-element.32), calls=%async_computation | async-start | bytes 1671168 | tf_op jit(solution)/shard_map/all_to_all | solution.py:451
  9.6 8.7 %collective-permute-start = (bf16[256,640]{1,0:T(8,128)(2,1)S(1)}, bf16[256,640]{1,0:T(8,128)(2,1)S(1)}, u32[]{:S(2)}, u32[]{:S(2)}) collective-permute-start(bf16[256,640]{1,0:T(8,128)(2,1)S(1)} %shard_map.129.own), channel_id=1, source_target_pairs={{0,8},{8,0},{1,9},{9,1},{2,10},{10,2},{3,11},{11,3},{4,12},{12,4},... | collective-permute-start | bytes 983048 | tf_op jit(solution)/shard_map/ppermute | solution.py:443
  20.1 8.7 %collective-permute-start.1 = (f32[2,8,256]{2,1,0:T(8,128)S(1)}, f32[2,8,256]{2,1,0:T(8,128)S(1)}, u32[]{:S(2)}, u32[]{:S(2)}) collective-permute-start(f32[2,8,256]{2,1,0:T(8,128)S(1)} %get-tuple-element.35.stats), channel_id=1, source_target_pairs={{0,8},{8,0},{1,9},{9,1},{2,10},{10,2},{3,11},{11,3},{4,12},{12,4},... | collective-permute-start | bytes 49160 | tf_op jit(solution)/shard_map/ppermute | solution.py:443
  31.3 16.1 %all-to-all-start.1 = ((bf16[4,272,384]{2,1,0:T(8,128)(2,1)}), bf16[4,272,384]{2,1,0:T(8,128)(2,1)S(1)}, u32[]{:S(2)}, u32[]{:S(2)}) async-start(bf16[4,272,384]{2,1,0:T(8,128)(2,1)} %get-tuple-element.38), calls=%async_computation.1 | async-start | bytes 1671168 | tf_op jit(solution)/shard_map/all_to_all | solution.py:451
  34.8 3.5 %collective-permute-start.2 = (bf16[256,384]{1,0:T(8,128)(2,1)}, bf16[256,384]{1,0:T(8,128)(2,1)S(1)}, u32[]{:S(2)}, u32[]{:S(2)}) collective-permute-start(bf16[256,384]{1,0:T(8,128)(2,1)} %get-tuple-element.39), channel_id=1, source_target_pairs={{0,8},{8,0},{1,9},{9,1},{2,10},{10,2},{3,11},{11,3},{4,12},{12,4},... | collective-permute-start | bytes 589832 | tf_op jit(solution)/shard_map/ppermute | solution.py:443
  48.1 5.8 %collective-permute-start.3 = (bf16[576,768]{1,0:T(8,128)(2,1)S(1)}, bf16[576,768]{1,0:T(8,128)(2,1)S(1)}, u32[]{:S(2)}, u32[]{:S(2)}) collective-permute-start(bf16[576,768]{1,0:T(8,128)(2,1)S(1)} %get-tuple-element.44), channel_id=1, source_target_pairs={{0,8},{8,0},{1,9},{9,1},{2,10},{10,2},{3,11},{11,3},{4,12},{12,4},... | collective-permute-start | bytes 2654216 | tf_op jit(solution)/shard_map/ppermute | solution.py:443
  54.9 17.0 %all-to-all-start.2 = ((bf16[4,144,768]{2,1,0:T(8,128)(2,1)}), bf16[4,144,768]{2,1,0:T(8,128)(2,1)S(1)}, u32[]{:S(2)}, u32[]{:S(2)}) async-start(bf16[4,144,768]{2,1,0:T(8,128)(2,1)} %bitcast.7), calls=%async_computation.2 | async-start | bytes 1769472 | tf_op jit(solution)/shard_map/all_to_all | solution.py:451
  58.4 13.7 %collective-permute-start.4 = (bf16[4,192,256]{2,1,0:T(8,128)(2,1)S(1)}, bf16[4,192,256]{2,1,0:T(8,128)(2,1)S(1)}, u32[]{:S(2)}, u32[]{:S(2)}) collective-permute-start(bf16[4,192,256]{2,1,0:T(8,128)(2,1)S(1)} %get-tuple-element.51), channel_id=1, source_target_pairs={{0,1},{1,0},{2,3},{3,2},{4,5},{5,4},{6,7},{7,6},{8,9},{9,8},{10,11... | collective-permute-start | bytes 1179656 | tf_op jit(solution)/shard_map/ppermute | solution.py:443
  87.9 12.5 %all-to-all-start.4 = ((bf16[8,36,384]{2,1,0:T(8,128)(2,1)}), bf16[8,36,384]{2,1,0:T(8,128)(2,1)S(1)}, u32[]{:S(2)}, u32[]{:S(2)}) async-start(bf16[8,36,384]{2,1,0:T(8,128)(2,1)} %shard_map.138), calls=%async_computation.4 | async-start | bytes 491520 | tf_op jit(solution)/shard_map/all_to_all | solution.py:451
  100.4 21.3 %all-to-all-start.5 = ((bf16[4,192,256]{2,1,0:T(8,128)(2,1)}), bf16[4,192,256]{2,1,0:T(8,128)(2,1)S(1)}, u32[]{:S(2)}, u32[]{:S(2)}) async-start(bf16[4,192,256]{2,1,0:T(8,128)(2,1)} %shard_map.140), calls=%async_computation.5 | async-start | bytes 786432 | tf_op jit(solution)/shard_map/all_to_all | solution.py:451
  121.7 10.7 %collective-permute-start.5 = (bf16[576,768]{1,0:T(8,128)(2,1)S(1)}, bf16[576,768]{1,0:T(8,128)(2,1)S(1)}, u32[]{:S(2)}, u32[]{:S(2)}) collective-permute-start(bf16[576,768]{1,0:T(8,128)(2,1)S(1)} %all_gather.3.mine), channel_id=1, source_target_pairs={{0,8},{8,0},{1,9},{9,1},{2,10},{10,2},{3,11},{11,3},{4,12},{12,4},... | collective-permute-start | bytes 2654216 | tf_op jit(solution)/shard_map/ppermute | solution.py:443

commit v11 on v10

--- a/solution.py
+++ b/solution.py
@@ -29,7 +29,7 @@
     return lax.broadcasted_iota(jnp.int32, shape, axis)
 
 
-def local_call(body, outs, operands, scratch=(), fetched=0, space=pltpu.VMEM):
+def local_call(body, outs, operands, scratch=(), fetched=0, space=pltpu.VMEM, aliases={}):
     specs = [pl.BlockSpec(memory_space=pltpu.HBM)] * fetched
     specs += [pl.BlockSpec(memory_space=space)] * (operands - fetched)
     shapes = [
@@ -43,6 +43,7 @@
             pl.BlockSpec(memory_space=pltpu.HBM if len(out) > 2 else space) for out in outs
         ),
         scratch_shapes=list(scratch),
+        input_output_aliases=dict(aliases),
         compiler_params=pltpu.CompilerParams(vmem_limit_bytes=VMEM_BYTES),
     )
 
@@ -336,7 +337,7 @@
         value = contract(grad, hidden[...], 0, 0)
         rows = pl.ds(first, value.shape[0])
         left, right = value[:, :cut], value[:, cut:]
-        kept[rows, :] = jnp.where(core == 0, left, right)
+        kept[rows, :] = jnp.where(core == 0, left, right).astype(BF16)
         sent[rows, :] = jnp.where(core == 0, right, left).astype(BF16)
         first += value.shape[0]
 
@@ -374,12 +375,14 @@
     slot_rows = parts[:, tokens:, :PJ].reshape(chips * part, PJ)
     feature_grad = kept_sum[...] + query_got[:, LANES:].astype(F32)
     feature_grad = (feature_grad + contract(donor_hot[...], slot_rows, 0, 0)).astype(BF16)
-    for copy in copies:
-        copy.wait()
-    value = contract(w_query[...], query_grad[...], 0, 1)
+    copies[0].wait()
+    value = contract(w_junction[...], feature_grad, 1, 1)
+    copies[1].wait()
+    value = value + contract(w_query[...], query_grad[...], 0, 1)
+    copies[2].wait()
     value = value + contract(w_key[...], grads[:, :HD], 0, 1)
+    copies[3].wait()
     value = value + contract(w_value[...], grads[:, HD:], 0, 1)
-    value = value + contract(w_junction[...], feature_grad, 1, 1)
     blocks = value.reshape((2 * kept.shape[0],) + kept.shape[1:])
     kept[...], sent[...] = halve(blocks, lax.axis_index("side"))
 
@@ -387,6 +390,20 @@
 def tiles_of(rows, columns, count):
     high, wide = rows * 2 // count, columns // 2
     return [(i, pl.ds(i // 2 * high, high), pl.ds(i % 2 * wide, wide)) for i in range(count)]
+
+
+def pair_body(held, got, out, total, sems):
+    chips, part, _ = total.shape
+    copies = []
+    for chip in range(chips):
+        rows = pl.ds(chip * part, part)
+        value = held[rows, :].astype(F32) + got[rows, :].astype(F32)
+        total[chip] = value.astype(BF16)
+        copy = pltpu.make_async_copy(total.at[chip], out.at[chip], sems.at[chip])
+        copy.start()
+        copies.append(copy)
+    for copy in copies:
+        copy.wait()
 
 
 def sum_body(parts, total):
@@ -420,23 +437,25 @@
     joined[...] = whole[...].astype(BF16)
 
 
-def place_body(mine, theirs, *refs):
-    outs, sems = refs[:-1], refs[-1]
-    core = lax.axis_index("core")
-    cut = mine.shape[1]
-    copies = []
-    for i, out in enumerate(outs):
-        for j, (source, place) in enumerate(((mine, core), (theirs, 1 - core))):
-            columns = pl.ds(pl.multiple_of(place * cut, cut), cut)
-            copies.append(
-                pltpu.make_async_copy(
-                    source.at[pl.ds(i * HD, HD)], out.at[:, columns], sems.at[2 * i + j]
-                )
-            )
+def place(source, outs, sems, core):
+    cut = source.shape[1]
+    columns = pl.ds(pl.multiple_of(core * cut, cut), cut)
+    copies = [
+        pltpu.make_async_copy(source.at[pl.ds(i * HD, HD)], out.at[:, columns], sems.at[i])
+        for i, out in enumerate(outs)
+    ]
     for copy in copies:
         copy.start()
     for copy in copies:
         copy.wait()
+
+
+def own_half_body(mine, *refs):
+    place(mine, refs[:3], refs[3], lax.axis_index("core"))
+
+
+def other_half_body(theirs, *refs):
+    place(theirs, refs[3:6], refs[6], 1 - lax.axis_index("core"))
 
 
 def swap(value, axis="core"):
@@ -542,7 +561,7 @@
     block = (width // heads, tokens)
     grads, query_grad, weight_held, weight_sent = local_call(
         grads_body,
-        [((tokens, KV), BF16), ((tokens, HD), BF16), ((rows, cut), F32), ((rows, cut), BF16)],
+        [((tokens, KV), BF16), ((tokens, HD), BF16), ((rows, cut), BF16), ((rows, cut), BF16)],
         operands=4,
     )(parts, query_held, query_got, hidden)
     held, sent = local_call(
@@ -563,12 +582,17 @@
     )
 
     weight_got, sent = lax.optimization_barrier((swap(weight_sent), sent))
-    (term,) = local_call(total_body, [((rows, cut), BF16)], operands=2)(weight_held, weight_got)
     part = rows // chips
+    (term,) = local_call(
+        pair_body,
+        [((chips, part, cut), BF16, True)],
+        operands=2,
+        scratch=[pltpu.VMEM((chips, part, cut), BF16), pltpu.SemaphoreType.DMA((chips,))],
+    )(weight_held, weight_got)
     tile = (part * 2 // intervals, cut // 2)
     (tiles,) = local_call(
         cut_body, [((intervals,) + tile, BF16)], operands=1, scratch=[pltpu.VMEM((part, cut), F32)]
-    )(exchange(term.reshape(chips, part, cut), "x"))
+    )(exchange(term, "x"))
     tiles, got = lax.optimization_barrier((tiles, swap(sent, "side")))
     (blocks,) = local_call(total_body, [((heads // SIDES,) + block, BF16)], operands=2)(held, got)
     (copies,) = local_call(spread_body, [((intervals,) + tile, BF16)], operands=1)(
@@ -581,13 +605,18 @@
     term = lax.all_gather(term, "x", axis=0, tiled=True)
     term, blocks = lax.optimization_barrier((term, blocks))
     (grad_input,) = local_call(sum_body, [(block, BF16)], operands=1)(blocks)
+    wide = [((HD, width), BF16)] * 3
+    sems = [pltpu.SemaphoreType.DMA((3,))]
+    theirs = swap(term)
+    grads = local_call(own_half_body, wide, operands=1, scratch=sems, space=pl.ANY)(term)
     grads = local_call(
-        place_body,
-        [((HD, width), BF16)] * 3,
-        operands=2,
-        scratch=[pltpu.SemaphoreType.DMA((2 * 3,))],
+        other_half_body,
+        wide,
+        operands=4,
+        scratch=sems,
         space=pl.ANY,
-    )(term, swap(term))
+        aliases={i + 1: i for i in range(3)},
+    )(theirs, *grads)
     return (grad_input.T[None],) + tuple(grads)
 
 

time: 134 us -> 134 us (level)
    pallas_call x2 -> x3, Pallas kernels: 2.32 us -> 2.9 us  [the longest x1 1.03 us: on_device(): local_call(pair_body, [((chips, part, cut), BF16, True)], operands=2, scr...]
  transfers between devices with their start and end apart: 11 -> 11, of which waited for: 7 -> 7; matrix products, arithmetic and copies ran while one was open for 0% -> 0% of each run, Pallas kernels for 4% -> 5%
where the time goes in v11:
time: 134 us
  starting transfers between devices  57.1 us (43%)
  waiting for transfers between devices  31.4 us (23%)
  blocking collectives  26.2 us (20%)
  Pallas kernels  18.1 us (14%)
    ppermute x6, starting transfers between devices, swap(): return lax.ppermute(value, axis, [(0, 1), (1, 0)])  31.8 us
    all_to_all x5, waiting for transfers between devices, exchange(): return lax.all_to_all(value, axis, 0, 0, tiled=True)  28.3 us
    all_to_all x5, starting transfers between devices, exchange(): return lax.all_to_all(value, axis, 0, 0, tiled=True)  25.3 us
    all_to_all x1, blocking collectives, exchange(): return lax.all_to_all(value, axis, 0, 0, tiled=True)  15 us
    all_gather x1, blocking collectives, on_device(): term = lax.all_gather(term, 'x', axis=0, tiled=True)  11.2 us
    pallas_call x1, Pallas kernels, on_device(): local_call(project_body, [((chips, height, KV), BF16, True), ((slots, tok...  3.47 us
    ppermute x6, waiting for transfers between devices, swap(): return lax.ppermute(value, axis, [(0, 1), (1, 0)])  3.14 us
    pallas_call x1, Pallas kernels, on_device(): local_call(input_body, [((heads // 2,) + block, F32), ((heads // 2,) + bl...  3.08 us
  transfers between devices with their start and end apart: 11, of which 7 were waited for; matrix products, arithmetic and copies ran while one was open for 0% of the time, Pallas kernels for 5%

profile of v11, /device:TPU:1, one launch (start us, length us, event | category | flops | bytes accessed | tf_op | source)
XLA Modules:
  0.0 133.7 jit_solution(9478526699676315537)
XLA Ops:
  0.6 0.0 copy-start.1
  0.6 0.0 copy-start
  0.7 0.0 copy-start.2
  0.7 0.0 copy-start.3
  0.7 3.5 %shard_map.130 = (bf16[4,272,384]{2,1,0:T(8,128)(2,1)}, bf16[64,256]{1,0:T(8,128)(2,1)S(1)}) custom-call(bf16[256,1536]{1,0:T(8,128)(2,1)} %bitcast.11, bf16[192,1536]{1,0:T(8,128)(2,1)} %w_key_hbm.3, bf16[192,1536]{1,0:T(8,128)(2,1)} %w_value_hbm.3, bf16[1536,128]{1,0:T(8,128)(2,1)} %w_junction_hbm.3, s32[8,8]{1,0:T(8,128)} %bitcast.16, s32[8,8]{1,0:T(8,128)} %bitcast.17, ...), custom_call_target="tpu_custom_call" | custom-call | tf_op jit(solution)/shard_map/pallas_call | solution.py:495
  4.2 4.9 %all-to-all-start = ((bf16[4,272,384]{2,1,0:T(8,128)(2,1)}), bf16[4,272,384]{2,1,0:T(8,128)(2,1)S(1)}, u32[]{:S(2)}, u32[]{:S(2)}) async-start(bf16[4,272,384]{2,1,0:T(8,128)(2,1)} %get-tuple-element.35), calls=%async_computation | async-start | bytes 1671168 | tf_op jit(solution)/shard_map/all_to_all | solution.py:470
  9.0 0.0 copy-done.1
  9.0 0.0 copy-done
  9.0 0.0 copy-done.2
  9.0 0.0 copy-done.3
  9.0 0.6 shard_map.129.own
  9.6 7.5 %collective-permute-start = (bf16[256,640]{1,0:T(8,128)(2,1)S(1)}, bf16[256,640]{1,0:T(8,128)(2,1)S(1)}, u32[]{:S(2)}, u32[]{:S(2)}) collective-permute-start(bf16[256,640]{1,0:T(8,128)(2,1)S(1)} %shard_map.129.own), channel_id=1, source_target_pairs={{0,8},{8,0},{1,9},{9,1},{2,10},{10,2},{3,11},{11,3},{4,12},{12,4},... | collective-permute-start | bytes 983048 | tf_op jit(solution)/shard_map/ppermute | solution.py:462
  17.1 1.2 collective-permute-done.other
  18.3 0.0 all-to-all-done.mine
  18.3 1.8 %shard_map.131 = (f32[2,256,1024]{2,1,0:T(8,128)S(1)}, f32[2,256,1024]{2,1,0:T(8,128)S(1)}, f32[2,8,256]{2,1,0:T(8,128)S(1)}) custom-call(bf16[256,640]{1,0:T(8,128)(2,1)S(1)} %shard_map.129.own, bf16[256,640]{1,0:T(8,128)(2,1)S(1)} %collective-permute-done.other, bf16[4,272,384]{2,1,0:T(8,128)(2,1)S(1)} %all-to-all-done.mine), custom_call_target="tpu_custom_call" | custom-call | tf_op jit(solution)/shard_map/pallas_call | solution.py:530
  20.1 7.8 %collective-permute-start.1 = (f32[2,8,256]{2,1,0:T(8,128)S(1)}, f32[2,8,256]{2,1,0:T(8,128)S(1)}, u32[]{:S(2)}, u32[]{:S(2)}) collective-permute-start(f32[2,8,256]{2,1,0:T(8,128)S(1)} %get-tuple-element.38.stats), channel_id=1, source_target_pairs={{0,8},{8,0},{1,9},{9,1},{2,10},{10,2},{3,11},{11,3},{4,12},{12,4},... | collective-permute-start | bytes 49160 | tf_op jit(solution)/shard_map/ppermute | solution.py:462
  28.0 0.6 shard_map.132
  28.6 0.2 collective-permute-done.1.got
  28.8 2.5 %shard_map.133 = (bf16[4,272,384]{2,1,0:T(8,128)(2,1)}, bf16[256,384]{1,0:T(8,128)(2,1)}, f32[256,256]{1,0:T(8,128)S(1)}) custom-call(bf16[256,640]{1,0:T(8,128)(2,1)S(1)} %shard_map.129.own, bf16[256,640]{1,0:T(8,128)(2,1)S(1)} %collective-permute-done.other, bf16[4,272,384]{2,1,0:T(8,128)(2,1)S(1)} %all-to-all-done.mine, ...), custom_call_target="tpu_custom_call" | custom-call | tf_op jit(solution)/shard_map/pallas_call | solution.py:541
  31.3 3.5 %all-to-all-start.1 = ((bf16[4,272,384]{2,1,0:T(8,128)(2,1)}), bf16[4,272,384]{2,1,0:T(8,128)(2,1)S(1)}, u32[]{:S(2)}, u32[]{:S(2)}) async-start(bf16[4,272,384]{2,1,0:T(8,128)(2,1)} %get-tuple-element.41), calls=%async_computation.1 | async-start | bytes 1671168 | tf_op jit(solution)/shard_map/all_to_all | solution.py:470
  34.8 2.3 %collective-permute-start.2 = (bf16[256,384]{1,0:T(8,128)(2,1)}, bf16[256,384]{1,0:T(8,128)(2,1)S(1)}, u32[]{:S(2)}, u32[]{:S(2)}) collective-permute-start(bf16[256,384]{1,0:T(8,128)(2,1)} %get-tuple-element.42), channel_id=1, source_target_pairs={{0,8},{8,0},{1,9},{9,1},{2,10},{10,2},{3,11},{11,3},{4,12},{12,4},... | collective-permute-start | bytes 589832 | tf_op jit(solution)/shard_map/ppermute | solution.py:462
  37.1 1.3 collective-permute-done.2.query_got
  38.4 9.0 %all-to-all-done.1.parts = bf16[4,272,384]{2,1,0:T(8,128)(2,1)S(1)} async-done(((bf16[4,272,384]{2,1,0:T(8,128)(2,1)}), bf16[4,272,384]{2,1,0:T(8,128)(2,1)S(1)}, u32[]{:S(2)}, u32[]{:S(2)}) %all-to-all-start.1) | async-done | bytes 835616 | tf_op jit(solution)/shard_map/all_to_all | solution.py:470
  47.4 0.7 shard_map.134
  48.1 3.1 %collective-permute-start.3 = (bf16[576,768]{1,0:T(8,128)(2,1)S(1)}, bf16[576,768]{1,0:T(8,128)(2,1)S(1)}, u32[]{:S(2)}, u32[]{:S(2)}) collective-permute-start(bf16[576,768]{1,0:T(8,128)(2,1)S(1)} %get-tuple-element.47), channel_id=1, source_target_pairs={{0,8},{8,0},{1,9},{9,1},{2,10},{10,2},{3,11},{11,3},{4,12},{12,4},... | collective-permute-start | bytes 2654216 | tf_op jit(solution)/shard_map/ppermute | solution.py:462
  51.2 3.1 %shard_map.135 = (f32[4,192,256]{2,1,0:T(8,128)S(1)}, bf16[4,192,256]{2,1,0:T(8,128)(2,1)S(1)}) custom-call(bf16[192,1536]{1,0:T(8,128)(2,1)} %w_query_hbm.1, bf16[192,1536]{1,0:T(8,128)(2,1)} %w_key_hbm.3, bf16[192,1536]{1,0:T(8,128)(2,1)} %w_value_hbm.3, bf16[1536,128]{1,0:T(8,128)(2,1)} %w_junction_hbm.3, bf16[4,272,384]{2,1,0:T(8,128)(2,1)S(1)} %all-to-all-done.1.parts, ...), custom_call_target="tpu_custom_call" | custom-call | tf_op jit(solution)/shard_map/pallas_call | solution.py:567
  54.2 0.0 collective-permute-done.3.got
  54.3 1.0 shard_map.136
  55.3 3.5 %all-to-all-start.2 = ((bf16[4,144,768]{2,1,0:T(8,128)(2,1)}), bf16[4,144,768]{2,1,0:T(8,128)(2,1)S(1)}, u32[]{:S(2)}, u32[]{:S(2)}) async-start(bf16[4,144,768]{2,1,0:T(8,128)(2,1)} %shard_map.136), calls=%async_computation.2 | async-start | bytes 1769472 | tf_op jit(solution)/shard_map/all_to_all | solution.py:470
  58.8 2.5 %collective-permute-start.4 = (bf16[4,192,256]{2,1,0:T(8,128)(2,1)S(1)}, bf16[4,192,256]{2,1,0:T(8,128)(2,1)S(1)}, u32[]{:S(2)}, u32[]{:S(2)}) collective-permute-start(bf16[4,192,256]{2,1,0:T(8,128)(2,1)S(1)} %get-tuple-element.54), channel_id=1, source_target_pairs={{0,1},{1,0},{2,3},{3,2},{4,5},{5,4},{6,7},{7,6},{8,9},{9,8},{10,11... | collective-permute-start | bytes 1179656 | tf_op jit(solution)/shard_map/ppermute | solution.py:462
  61.3 10.9 %all-to-all-done.2.parts = bf16[4,144,768]{2,1,0:T(8,128)(2,1)S(1)} async-done(((bf16[4,144,768]{2,1,0:T(8,128)(2,1)}), bf16[4,144,768]{2,1,0:T(8,128)(2,1)S(1)}, u32[]{:S(2)}, u32[]{:S(2)}) %all-to-all-start.2) | async-done | bytes 884768 | tf_op jit(solution)/shard_map/all_to_all | solution.py:470
  72.3 0.2 shard_map.137
  72.5 0.0 collective-permute-done.4.refs_1_
  72.5 15.0 %all_to_all.30.parts = bf16[8,36,384]{2,1,0:T(8,128)(2,1)S(1)} all-to-all(bf16[8,36,384]{2,1,0:T(8,128)(2,1)S(1)} %shard_map.137), channel_id=1, replica_groups=mesh['interval'=8,'x'=4,'core'=2,'pair'=4,'side'=2] {'interval'}, dimensions={0} | all-to-all | bytes 442368 | tf_op jit(solution)/shard_map/all_to_all | solution.py:470
  87.5 0.7 shard_map.138
  88.2 3.4 %all-to-all-start.4 = ((bf16[8,36,384]{2,1,0:T(8,128)(2,1)}), bf16[8,36,384]{2,1,0:T(8,128)(2,1)S(1)}, u32[]{:S(2)}, u32[]{:S(2)}) async-start(bf16[8,36,384]{2,1,0:T(8,128)(2,1)} %shard_map.138), calls=%async_computation.4 | async-start | bytes 491520 | tf_op jit(solution)/shard_map/all_to_all | solution.py:470
  91.7 0.8 shard_map.140
  92.5 8.3 %all-to-all-done.4.tiles = bf16[8,36,384]{2,1,0:T(8,128)(2,1)S(1)} async-done(((bf16[8,36,384]{2,1,0:T(8,128)(2,1)}), bf16[8,36,384]{2,1,0:T(8,128)(2,1)S(1)}, u32[]{:S(2)}, u32[]{:S(2)}) %all-to-all-start.4) | async-done | bytes 221216 | tf_op jit(solution)/shard_map/all_to_all | solution.py:470
  100.8 10.0 %all-to-all-start.5 = ((bf16[4,192,256]{2,1,0:T(8,128)(2,1)}), bf16[4,192,256]{2,1,0:T(8,128)(2,1)S(1)}, u32[]{:S(2)}, u32[]{:S(2)}) async-start(bf16[4,192,256]{2,1,0:T(8,128)(2,1)} %shard_map.140), calls=%async_computation.5 | async-start | bytes 786432 | tf_op jit(solution)/shard_map/all_to_all | solution.py:470
  110.9 11.2 %all_gather.3.mine = bf16[576,768]{1,0:T(8,128)(2,1)S(1)} all-gather(bf16[144,768]{1,0:T(8,128)(2,1)S(1)} %shard_map.139), channel_id=1, replica_groups=mesh['interval'=8,'x'=4,'core'=2,'pair'=4,'side'=2] {'x'}, dimensions={0}, use_global_device_ids=true | all-gather | bytes 1105920 | tf_op jit(solution)/shard_map/all_gather | solution.py:605
  122.1 0.0 all-to-all-done.5.parts
  122.1 8.6 %collective-permute-start.5 = (bf16[576,768]{1,0:T(8,128)(2,1)S(1)}, bf16[576,768]{1,0:T(8,128)(2,1)S(1)}, u32[]{:S(2)}, u32[]{:S(2)}) collective-permute-start(bf16[576,768]{1,0:T(8,128)(2,1)S(1)} %all_gather.3.mine), channel_id=1, source_target_pairs={{0,8},{8,0},{1,9},{9,1},{2,10},{10,2},{3,11},{11,3},{4,12},{12,4},... | collective-permute-start | bytes 2654216 | tf_op jit(solution)/shard_map/ppermute | solution.py:462
  130.7 0.9 shard_map.142
  131.7 0.7 shard_map.141
  132.4 0.4 collective-permute-done.5.theirs
  132.7 0.9 shard_map.143
  (1 shorter events, 0.0 us)
Async XLA Ops:
  0.6 8.4 %copy-start.1 = (bf16[1536,128]{1,0:T(8,128)(2,1)S(1)}, bf16[1536,128]{1,0:T(8,128)(2,1)}, u32[]{:S(2)}) copy-start(bf16[1536,128]{1,0:T(8,128)(2,1)} %w_junction_hbm.3) | copy-start | bytes 1179652
  0.6 8.4 %copy-start = (bf16[1,256,1536]{2,1,0:T(8,128)(2,1)S(1)}, bf16[1,256,1536]{2,1,0:T(8,128)(2,1)}, u32[]{:S(2)}) copy-start(bf16[1,256,1536]{2,1,0:T(8,128)(2,1)} %param.10) | copy-start | bytes 2359300
  0.7 8.4 %copy-start.2 = (bf16[192,1536]{1,0:T(8,128)(2,1)S(1)}, bf16[192,1536]{1,0:T(8,128)(2,1)}, u32[]{:S(2)}) copy-start(bf16[192,1536]{1,0:T(8,128)(2,1)} %w_query_hbm.1) | copy-start | bytes 1769476
  0.7 8.4 %copy-start.3 = (bf16[1,256,192]{1,2,0:T(8,128)(2,1)S(1)}, bf16[1,256,192]{1,2,0:T(8,128)(2,1)}, u32[]{:S(2)}) copy-start(bf16[1,256,192]{1,2,0:T(8,128)(2,1)} %param.11) | copy-start | bytes 294916
  4.2 14.2 %all-to-all-start = ((bf16[4,272,384]{2,1,0:T(8,128)(2,1)}), bf16[4,272,384]{2,1,0:T(8,128)(2,1)S(1)}, u32[]{:S(2)}, u32[]{:S(2)}) async-start(bf16[4,272,384]{2,1,0:T(8,128)(2,1)} %get-tuple-element.35), calls=%async_computation | async-start | bytes 1671168 | tf_op jit(solution)/shard_map/all_to_all | solution.py:470
  9.6 8.7 %collective-permute-start = (bf16[256,640]{1,0:T(8,128)(2,1)S(1)}, bf16[256,640]{1,0:T(8,128)(2,1)S(1)}, u32[]{:S(2)}, u32[]{:S(2)}) collective-permute-start(bf16[256,640]{1,0:T(8,128)(2,1)S(1)} %shard_map.129.own), channel_id=1, source_target_pairs={{0,8},{8,0},{1,9},{9,1},{2,10},{10,2},{3,11},{11,3},{4,12},{12,4},... | collective-permute-start | bytes 983048 | tf_op jit(solution)/shard_map/ppermute | solution.py:462
  20.1 8.7 %collective-permute-start.1 = (f32[2,8,256]{2,1,0:T(8,128)S(1)}, f32[2,8,256]{2,1,0:T(8,128)S(1)}, u32[]{:S(2)}, u32[]{:S(2)}) collective-permute-start(f32[2,8,256]{2,1,0:T(8,128)S(1)} %get-tuple-element.38.stats), channel_id=1, source_target_pairs={{0,8},{8,0},{1,9},{9,1},{2,10},{10,2},{3,11},{11,3},{4,12},{12,4},... | collective-permute-start | bytes 49160 | tf_op jit(solution)/shard_map/ppermute | solution.py:462
  31.3 16.1 %all-to-all-start.1 = ((bf16[4,272,384]{2,1,0:T(8,128)(2,1)}), bf16[4,272,384]{2,1,0:T(8,128)(2,1)S(1)}, u32[]{:S(2)}, u32[]{:S(2)}) async-start(bf16[4,272,384]{2,1,0:T(8,128)(2,1)} %get-tuple-element.41), calls=%async_computation.1 | async-start | bytes 1671168 | tf_op jit(solution)/shard_map/all_to_all | solution.py:470
  34.8 3.5 %collective-permute-start.2 = (bf16[256,384]{1,0:T(8,128)(2,1)}, bf16[256,384]{1,0:T(8,128)(2,1)S(1)}, u32[]{:S(2)}, u32[]{:S(2)}) collective-permute-start(bf16[256,384]{1,0:T(8,128)(2,1)} %get-tuple-element.42), channel_id=1, source_target_pairs={{0,8},{8,0},{1,9},{9,1},{2,10},{10,2},{3,11},{11,3},{4,12},{12,4},... | collective-permute-start | bytes 589832 | tf_op jit(solution)/shard_map/ppermute | solution.py:462
  48.1 6.2 %collective-permute-start.3 = (bf16[576,768]{1,0:T(8,128)(2,1)S(1)}, bf16[576,768]{1,0:T(8,128)(2,1)S(1)}, u32[]{:S(2)}, u32[]{:S(2)}) collective-permute-start(bf16[576,768]{1,0:T(8,128)(2,1)S(1)} %get-tuple-element.47), channel_id=1, source_target_pairs={{0,8},{8,0},{1,9},{9,1},{2,10},{10,2},{3,11},{11,3},{4,12},{12,4},... | collective-permute-start | bytes 2654216 | tf_op jit(solution)/shard_map/ppermute | solution.py:462
  55.3 17.0 %all-to-all-start.2 = ((bf16[4,144,768]{2,1,0:T(8,128)(2,1)}), bf16[4,144,768]{2,1,0:T(8,128)(2,1)S(1)}, u32[]{:S(2)}, u32[]{:S(2)}) async-start(bf16[4,144,768]{2,1,0:T(8,128)(2,1)} %shard_map.136), calls=%async_computation.2 | async-start | bytes 1769472 | tf_op jit(solution)/shard_map/all_to_all | solution.py:470
  58.8 13.7 %collective-permute-start.4 = (bf16[4,192,256]{2,1,0:T(8,128)(2,1)S(1)}, bf16[4,192,256]{2,1,0:T(8,128)(2,1)S(1)}, u32[]{:S(2)}, u32[]{:S(2)}) collective-permute-start(bf16[4,192,256]{2,1,0:T(8,128)(2,1)S(1)} %get-tuple-element.54), channel_id=1, source_target_pairs={{0,1},{1,0},{2,3},{3,2},{4,5},{5,4},{6,7},{7,6},{8,9},{9,8},{10,11... | collective-permute-start | bytes 1179656 | tf_op jit(solution)/shard_map/ppermute | solution.py:462
  88.2 12.5 %all-to-all-start.4 = ((bf16[8,36,384]{2,1,0:T(8,128)(2,1)}), bf16[8,36,384]{2,1,0:T(8,128)(2,1)S(1)}, u32[]{:S(2)}, u32[]{:S(2)}) async-start(bf16[8,36,384]{2,1,0:T(8,128)(2,1)} %shard_map.138), calls=%async_computation.4 | async-start | bytes 491520 | tf_op jit(solution)/shard_map/all_to_all | solution.py:470
  100.8 21.3 %all-to-all-start.5 = ((bf16[4,192,256]{2,1,0:T(8,128)(2,1)}), bf16[4,192,256]{2,1,0:T(8,128)(2,1)S(1)}, u32[]{:S(2)}, u32[]{:S(2)}) async-start(bf16[4,192,256]{2,1,0:T(8,128)(2,1)} %shard_map.140), calls=%async_computation.5 | async-start | bytes 786432 | tf_op jit(solution)/shard_map/all_to_all | solution.py:470
  122.1 10.7 %collective-permute-start.5 = (bf16[576,768]{1,0:T(8,128)(2,1)S(1)}, bf16[576,768]{1,0:T(8,128)(2,1)S(1)}, u32[]{:S(2)}, u32[]{:S(2)}) collective-permute-start(bf16[576,768]{1,0:T(8,128)(2,1)S(1)} %all_gather.3.mine), channel_id=1, source_target_pairs={{0,8},{8,0},{1,9},{9,1},{2,10},{10,2},{3,11},{11,3},{4,12},{12,4},... | collective-permute-start | bytes 2654216 | tf_op jit(solution)/shard_map/ppermute | solution.py:462

commit v12 on v11

--- a/solution.py
+++ b/solution.py
@@ -355,34 +355,27 @@
     query_grad,
     kept,
     sent,
-    w_query,
-    w_key,
-    w_value,
+    weights,
     w_junction,
     sems,
 ):
-    sources = (w_junction_hbm, w_query_hbm, w_key_hbm, w_value_hbm)
-    targets = (w_junction, w_query, w_key, w_value)
     copies = [
-        pltpu.make_async_copy(source, target, sems.at[i])
-        for i, (source, target) in enumerate(zip(sources, targets))
+        pltpu.make_async_copy(source, weights.at[pl.ds(i * HD, HD)], sems.at[i])
+        for i, source in enumerate((w_query_hbm, w_key_hbm, w_value_hbm))
     ]
+    copies.append(pltpu.make_async_copy(w_junction_hbm, w_junction, sems.at[3]))
     for copy in copies:
         copy.start()
+    both = jnp.concatenate([query_grad[...], grads[...]], axis=1)
     chips, height, _ = parts.shape
     tokens = grads.shape[0]
     part = height - tokens
     slot_rows = parts[:, tokens:, :PJ].reshape(chips * part, PJ)
     feature_grad = kept_sum[...] + query_got[:, LANES:].astype(F32)
     feature_grad = (feature_grad + contract(donor_hot[...], slot_rows, 0, 0)).astype(BF16)
-    copies[0].wait()
-    value = contract(w_junction[...], feature_grad, 1, 1)
-    copies[1].wait()
-    value = value + contract(w_query[...], query_grad[...], 0, 1)
-    copies[2].wait()
-    value = value + contract(w_key[...], grads[:, :HD], 0, 1)
-    copies[3].wait()
-    value = value + contract(w_value[...], grads[:, HD:], 0, 1)
+    for copy in copies:
+        copy.wait()
+    value = contract(weights[...], both, 0, 1) + contract(w_junction[...], feature_grad, 1, 1)
     blocks = value.reshape((2 * kept.shape[0],) + kept.shape[1:])
     kept[...], sent[...] = halve(blocks, lax.axis_index("side"))
 
@@ -569,8 +562,11 @@
         [((heads // 2,) + block, F32), ((heads // 2,) + block, BF16)],
         operands=10,
         fetched=4,
-        scratch=[pltpu.VMEM((HD, width), BF16)] * 3
-        + [pltpu.VMEM((width, PJ), BF16), pltpu.SemaphoreType.DMA((4,))],
+        scratch=[
+            pltpu.VMEM((rows, width), BF16),
+            pltpu.VMEM((width, PJ), BF16),
+            pltpu.SemaphoreType.DMA((4,)),
+        ],
     )(
         *in_hbm(w_query, w_key, w_value, w_junction),
         parts,

time: 134 us -> 134 us (level)
  no operation moved by 1% of the time
where the time goes in v12:
time: 134 us; the launch traced here: 133 us
  starting transfers between devices  57.1 us (43%)
  waiting for transfers between devices  31.4 us (23%)
  blocking collectives  26.2 us (20%)
  Pallas kernels  17.5 us (13%)
    ppermute x6, starting transfers between devices, swap(): return lax.ppermute(value, axis, [(0, 1), (1, 0)])  31.8 us
    all_to_all x5, waiting for transfers between devices, exchange(): return lax.all_to_all(value, axis, 0, 0, tiled=True)  28.3 us
    all_to_all x5, starting transfers between devices, exchange(): return lax.all_to_all(value, axis, 0, 0, tiled=True)  25.3 us
    all_to_all x1, blocking collectives, exchange(): return lax.all_to_all(value, axis, 0, 0, tiled=True)  15 us
    all_gather x1, blocking collectives, on_device(): term = lax.all_gather(term, 'x', axis=0, tiled=True)  11.2 us
    pallas_call x1, Pallas kernels, on_device(): local_call(project_body, [((chips, height, KV), BF16, True), ((slots, tok...  3.47 us
    ppermute x6, waiting for transfers between devices, swap(): return lax.ppermute(value, axis, [(0, 1), (1, 0)])  3.14 us
  transfers between devices with their start and end apart: 11, of which 7 were waited for; matrix products, arithmetic and copies ran while one was open for 0% of the time, Pallas kernels for 5%

profile of v12, /device:TPU:1, one launch (start us, length us, event | category | flops | bytes accessed | tf_op | source)
XLA Modules:
  0.0 133.2 jit_solution(18137829107415041591)
XLA Ops:
  0.6 0.0 copy-start.1
  0.6 0.0 copy-start
  0.7 0.0 copy-start.2
  0.7 0.0 copy-start.3
  0.7 3.5 %shard_map.130 = (bf16[4,272,384]{2,1,0:T(8,128)(2,1)}, bf16[64,256]{1,0:T(8,128)(2,1)S(1)}) custom-call(bf16[256,1536]{1,0:T(8,128)(2,1)} %bitcast.11, bf16[192,1536]{1,0:T(8,128)(2,1)} %w_key_hbm.3, bf16[192,1536]{1,0:T(8,128)(2,1)} %w_value_hbm.3, bf16[1536,128]{1,0:T(8,128)(2,1)} %w_junction_hbm.3, s32[8,8]{1,0:T(8,128)} %bitcast.16, s32[8,8]{1,0:T(8,128)} %bitcast.17, ...), custom_call_target="tpu_custom_call" | custom-call | tf_op jit(solution)/shard_map/pallas_call | solution.py:488
  4.2 4.9 %all-to-all-start = ((bf16[4,272,384]{2,1,0:T(8,128)(2,1)}), bf16[4,272,384]{2,1,0:T(8,128)(2,1)S(1)}, u32[]{:S(2)}, u32[]{:S(2)}) async-start(bf16[4,272,384]{2,1,0:T(8,128)(2,1)} %get-tuple-element.35), calls=%async_computation | async-start | bytes 1671168 | tf_op jit(solution)/shard_map/all_to_all | solution.py:463
  9.0 0.0 copy-done.1
  9.0 0.0 copy-done
  9.0 0.0 copy-done.2
  9.0 0.0 copy-done.3
  9.0 0.6 shard_map.129.own
  9.6 7.5 %collective-permute-start = (bf16[256,640]{1,0:T(8,128)(2,1)S(1)}, bf16[256,640]{1,0:T(8,128)(2,1)S(1)}, u32[]{:S(2)}, u32[]{:S(2)}) collective-permute-start(bf16[256,640]{1,0:T(8,128)(2,1)S(1)} %shard_map.129.own), channel_id=1, source_target_pairs={{0,8},{8,0},{1,9},{9,1},{2,10},{10,2},{3,11},{11,3},{4,12},{12,4},... | collective-permute-start | bytes 983048 | tf_op jit(solution)/shard_map/ppermute | solution.py:455
  17.1 1.2 collective-permute-done.other
  18.3 0.0 all-to-all-done.mine
  18.3 1.8 %shard_map.131 = (f32[2,256,1024]{2,1,0:T(8,128)S(1)}, f32[2,256,1024]{2,1,0:T(8,128)S(1)}, f32[2,8,256]{2,1,0:T(8,128)S(1)}) custom-call(bf16[256,640]{1,0:T(8,128)(2,1)S(1)} %shard_map.129.own, bf16[256,640]{1,0:T(8,128)(2,1)S(1)} %collective-permute-done.other, bf16[4,272,384]{2,1,0:T(8,128)(2,1)S(1)} %all-to-all-done.mine), custom_call_target="tpu_custom_call" | custom-call | tf_op jit(solution)/shard_map/pallas_call | solution.py:523
  20.1 7.8 %collective-permute-start.1 = (f32[2,8,256]{2,1,0:T(8,128)S(1)}, f32[2,8,256]{2,1,0:T(8,128)S(1)}, u32[]{:S(2)}, u32[]{:S(2)}) collective-permute-start(f32[2,8,256]{2,1,0:T(8,128)S(1)} %get-tuple-element.38.stats), channel_id=1, source_target_pairs={{0,8},{8,0},{1,9},{9,1},{2,10},{10,2},{3,11},{11,3},{4,12},{12,4},... | collective-permute-start | bytes 49160 | tf_op jit(solution)/shard_map/ppermute | solution.py:455
  28.0 0.6 shard_map.132
  28.6 0.2 collective-permute-done.1.got
  28.8 2.5 %shard_map.133 = (bf16[4,272,384]{2,1,0:T(8,128)(2,1)}, bf16[256,384]{1,0:T(8,128)(2,1)}, f32[256,256]{1,0:T(8,128)S(1)}) custom-call(bf16[256,640]{1,0:T(8,128)(2,1)S(1)} %shard_map.129.own, bf16[256,640]{1,0:T(8,128)(2,1)S(1)} %collective-permute-done.other, bf16[4,272,384]{2,1,0:T(8,128)(2,1)S(1)} %all-to-all-done.mine, ...), custom_call_target="tpu_custom_call" | custom-call | tf_op jit(solution)/shard_map/pallas_call | solution.py:534
  31.3 3.5 %all-to-all-start.1 = ((bf16[4,272,384]{2,1,0:T(8,128)(2,1)}), bf16[4,272,384]{2,1,0:T(8,128)(2,1)S(1)}, u32[]{:S(2)}, u32[]{:S(2)}) async-start(bf16[4,272,384]{2,1,0:T(8,128)(2,1)} %get-tuple-element.41), calls=%async_computation.1 | async-start | bytes 1671168 | tf_op jit(solution)/shard_map/all_to_all | solution.py:463
  34.8 2.3 %collective-permute-start.2 = (bf16[256,384]{1,0:T(8,128)(2,1)}, bf16[256,384]{1,0:T(8,128)(2,1)S(1)}, u32[]{:S(2)}, u32[]{:S(2)}) collective-permute-start(bf16[256,384]{1,0:T(8,128)(2,1)} %get-tuple-element.42), channel_id=1, source_target_pairs={{0,8},{8,0},{1,9},{9,1},{2,10},{10,2},{3,11},{11,3},{4,12},{12,4},... | collective-permute-start | bytes 589832 | tf_op jit(solution)/shard_map/ppermute | solution.py:455
  37.1 1.3 collective-permute-done.2.query_got
  38.4 9.0 %all-to-all-done.1.parts = bf16[4,272,384]{2,1,0:T(8,128)(2,1)S(1)} async-done(((bf16[4,272,384]{2,1,0:T(8,128)(2,1)}), bf16[4,272,384]{2,1,0:T(8,128)(2,1)S(1)}, u32[]{:S(2)}, u32[]{:S(2)}) %all-to-all-start.1) | async-done | bytes 835616 | tf_op jit(solution)/shard_map/all_to_all | solution.py:463
  47.4 0.7 shard_map.134
  48.1 3.1 %collective-permute-start.3 = (bf16[576,768]{1,0:T(8,128)(2,1)S(1)}, bf16[576,768]{1,0:T(8,128)(2,1)S(1)}, u32[]{:S(2)}, u32[]{:S(2)}) collective-permute-start(bf16[576,768]{1,0:T(8,128)(2,1)S(1)} %get-tuple-element.47), channel_id=1, source_target_pairs={{0,8},{8,0},{1,9},{9,1},{2,10},{10,2},{3,11},{11,3},{4,12},{12,4},... | collective-permute-start | bytes 2654216 | tf_op jit(solution)/shard_map/ppermute | solution.py:455
  51.2 2.6 %shard_map.135 = (f32[4,192,256]{2,1,0:T(8,128)S(1)}, bf16[4,192,256]{2,1,0:T(8,128)(2,1)S(1)}) custom-call(bf16[192,1536]{1,0:T(8,128)(2,1)} %w_query_hbm.1, bf16[192,1536]{1,0:T(8,128)(2,1)} %w_key_hbm.3, bf16[192,1536]{1,0:T(8,128)(2,1)} %w_value_hbm.3, bf16[1536,128]{1,0:T(8,128)(2,1)} %w_junction_hbm.3, bf16[4,272,384]{2,1,0:T(8,128)(2,1)S(1)} %all-to-all-done.1.parts, ...), custom_call_target="tpu_custom_call" | custom-call | tf_op jit(solution)/shard_map/pallas_call | solution.py:560
  53.7 0.0 collective-permute-done.3.got
  53.7 1.0 shard_map.136
  54.8 3.5 %all-to-all-start.2 = ((bf16[4,144,768]{2,1,0:T(8,128)(2,1)}), bf16[4,144,768]{2,1,0:T(8,128)(2,1)S(1)}, u32[]{:S(2)}, u32[]{:S(2)}) async-start(bf16[4,144,768]{2,1,0:T(8,128)(2,1)} %shard_map.136), calls=%async_computation.2 | async-start | bytes 1769472 | tf_op jit(solution)/shard_map/all_to_all | solution.py:463
  58.3 2.5 %collective-permute-start.4 = (bf16[4,192,256]{2,1,0:T(8,128)(2,1)S(1)}, bf16[4,192,256]{2,1,0:T(8,128)(2,1)S(1)}, u32[]{:S(2)}, u32[]{:S(2)}) collective-permute-start(bf16[4,192,256]{2,1,0:T(8,128)(2,1)S(1)} %get-tuple-element.54), channel_id=1, source_target_pairs={{0,1},{1,0},{2,3},{3,2},{4,5},{5,4},{6,7},{7,6},{8,9},{9,8},{10,11... | collective-permute-start | bytes 1179656 | tf_op jit(solution)/shard_map/ppermute | solution.py:455
  60.8 11.0 %all-to-all-done.2.parts = bf16[4,144,768]{2,1,0:T(8,128)(2,1)S(1)} async-done(((bf16[4,144,768]{2,1,0:T(8,128)(2,1)}), bf16[4,144,768]{2,1,0:T(8,128)(2,1)S(1)}, u32[]{:S(2)}, u32[]{:S(2)}) %all-to-all-start.2) | async-done | bytes 884768 | tf_op jit(solution)/shard_map/all_to_all | solution.py:463
  71.8 0.2 shard_map.137
  72.0 0.0 collective-permute-done.4.refs_1_
  72.0 15.0 %all_to_all.30.parts = bf16[8,36,384]{2,1,0:T(8,128)(2,1)S(1)} all-to-all(bf16[8,36,384]{2,1,0:T(8,128)(2,1)S(1)} %shard_map.137), channel_id=1, replica_groups=mesh['interval'=8,'x'=4,'core'=2,'pair'=4,'side'=2] {'interval'}, dimensions={0} | all-to-all | bytes 442368 | tf_op jit(solution)/shard_map/all_to_all | solution.py:463
  87.0 0.7 shard_map.138
  87.7 3.4 %all-to-all-start.4 = ((bf16[8,36,384]{2,1,0:T(8,128)(2,1)}), bf16[8,36,384]{2,1,0:T(8,128)(2,1)S(1)}, u32[]{:S(2)}, u32[]{:S(2)}) async-start(bf16[8,36,384]{2,1,0:T(8,128)(2,1)} %shard_map.138), calls=%async_computation.4 | async-start | bytes 491520 | tf_op jit(solution)/shard_map/all_to_all | solution.py:463
  91.2 0.8 shard_map.140
  92.0 8.3 %all-to-all-done.4.tiles = bf16[8,36,384]{2,1,0:T(8,128)(2,1)S(1)} async-done(((bf16[8,36,384]{2,1,0:T(8,128)(2,1)}), bf16[8,36,384]{2,1,0:T(8,128)(2,1)S(1)}, u32[]{:S(2)}, u32[]{:S(2)}) %all-to-all-start.4) | async-done | bytes 221216 | tf_op jit(solution)/shard_map/all_to_all | solution.py:463
  100.3 10.0 %all-to-all-start.5 = ((bf16[4,192,256]{2,1,0:T(8,128)(2,1)}), bf16[4,192,256]{2,1,0:T(8,128)(2,1)S(1)}, u32[]{:S(2)}, u32[]{:S(2)}) async-start(bf16[4,192,256]{2,1,0:T(8,128)(2,1)} %shard_map.140), calls=%async_computation.5 | async-start | bytes 786432 | tf_op jit(solution)/shard_map/all_to_all | solution.py:463
  110.3 11.2 %all_gather.3.mine = bf16[576,768]{1,0:T(8,128)(2,1)S(1)} all-gather(bf16[144,768]{1,0:T(8,128)(2,1)S(1)} %shard_map.139), channel_id=1, replica_groups=mesh['interval'=8,'x'=4,'core'=2,'pair'=4,'side'=2] {'x'}, dimensions={0}, use_global_device_ids=true | all-gather | bytes 1105920 | tf_op jit(solution)/shard_map/all_gather | solution.py:601
  121.5 0.0 all-to-all-done.5.parts
  121.5 8.6 %collective-permute-start.5 = (bf16[576,768]{1,0:T(8,128)(2,1)S(1)}, bf16[576,768]{1,0:T(8,128)(2,1)S(1)}, u32[]{:S(2)}, u32[]{:S(2)}) collective-permute-start(bf16[576,768]{1,0:T(8,128)(2,1)S(1)} %all_gather.3.mine), channel_id=1, source_target_pairs={{0,8},{8,0},{1,9},{9,1},{2,10},{10,2},{3,11},{11,3},{4,12},{12,4},... | collective-permute-start | bytes 2654216 | tf_op jit(solution)/shard_map/ppermute | solution.py:455
  130.2 0.9 shard_map.142
  131.2 0.7 shard_map.141
  131.8 0.4 collective-permute-done.5.theirs
  132.2 0.9 shard_map.143
  (1 shorter events, 0.0 us)
Async XLA Ops:
  0.6 8.4 %copy-start.1 = (bf16[1536,128]{1,0:T(8,128)(2,1)S(1)}, bf16[1536,128]{1,0:T(8,128)(2,1)}, u32[]{:S(2)}) copy-start(bf16[1536,128]{1,0:T(8,128)(2,1)} %w_junction_hbm.3) | copy-start | bytes 1179652
  0.6 8.4 %copy-start = (bf16[1,256,1536]{2,1,0:T(8,128)(2,1)S(1)}, bf16[1,256,1536]{2,1,0:T(8,128)(2,1)}, u32[]{:S(2)}) copy-start(bf16[1,256,1536]{2,1,0:T(8,128)(2,1)} %param.10) | copy-start | bytes 2359300
  0.7 8.4 %copy-start.2 = (bf16[192,1536]{1,0:T(8,128)(2,1)S(1)}, bf16[192,1536]{1,0:T(8,128)(2,1)}, u32[]{:S(2)}) copy-start(bf16[192,1536]{1,0:T(8,128)(2,1)} %w_query_hbm.1) | copy-start | bytes 1769476
  0.7 8.4 %copy-start.3 = (bf16[1,256,192]{1,2,0:T(8,128)(2,1)S(1)}, bf16[1,256,192]{1,2,0:T(8,128)(2,1)}, u32[]{:S(2)}) copy-start(bf16[1,256,192]{1,2,0:T(8,128)(2,1)} %param.11) | copy-start | bytes 294916
  4.2 14.2 %all-to-all-start = ((bf16[4,272,384]{2,1,0:T(8,128)(2,1)}), bf16[4,272,384]{2,1,0:T(8,128)(2,1)S(1)}, u32[]{:S(2)}, u32[]{:S(2)}) async-start(bf16[4,272,384]{2,1,0:T(8,128)(2,1)} %get-tuple-element.35), calls=%async_computation | async-start | bytes 1671168 | tf_op jit(solution)/shard_map/all_to_all | solution.py:463
  9.6 8.7 %collective-permute-start = (bf16[256,640]{1,0:T(8,128)(2,1)S(1)}, bf16[256,640]{1,0:T(8,128)(2,1)S(1)}, u32[]{:S(2)}, u32[]{:S(2)}) collective-permute-start(bf16[256,640]{1,0:T(8,128)(2,1)S(1)} %shard_map.129.own), channel_id=1, source_target_pairs={{0,8},{8,0},{1,9},{9,1},{2,10},{10,2},{3,11},{11,3},{4,12},{12,4},... | collective-permute-start | bytes 983048 | tf_op jit(solution)/shard_map/ppermute | solution.py:455
  20.1 8.7 %collective-permute-start.1 = (f32[2,8,256]{2,1,0:T(8,128)S(1)}, f32[2,8,256]{2,1,0:T(8,128)S(1)}, u32[]{:S(2)}, u32[]{:S(2)}) collective-permute-start(f32[2,8,256]{2,1,0:T(8,128)S(1)} %get-tuple-element.38.stats), channel_id=1, source_target_pairs={{0,8},{8,0},{1,9},{9,1},{2,10},{10,2},{3,11},{11,3},{4,12},{12,4},... | collective-permute-start | bytes 49160 | tf_op jit(solution)/shard_map/ppermute | solution.py:455
  31.3 16.1 %all-to-all-start.1 = ((bf16[4,272,384]{2,1,0:T(8,128)(2,1)}), bf16[4,272,384]{2,1,0:T(8,128)(2,1)S(1)}, u32[]{:S(2)}, u32[]{:S(2)}) async-start(bf16[4,272,384]{2,1,0:T(8,128)(2,1)} %get-tuple-element.41), calls=%async_computation.1 | async-start | bytes 1671168 | tf_op jit(solution)/shard_map/all_to_all | solution.py:463
  34.8 3.5 %collective-permute-start.2 = (bf16[256,384]{1,0:T(8,128)(2,1)}, bf16[256,384]{1,0:T(8,128)(2,1)S(1)}, u32[]{:S(2)}, u32[]{:S(2)}) collective-permute-start(bf16[256,384]{1,0:T(8,128)(2,1)} %get-tuple-element.42), channel_id=1, source_target_pairs={{0,8},{8,0},{1,9},{9,1},{2,10},{10,2},{3,11},{11,3},{4,12},{12,4},... | collective-permute-start | bytes 589832 | tf_op jit(solution)/shard_map/ppermute | solution.py:455
  48.1 5.7 %collective-permute-start.3 = (bf16[576,768]{1,0:T(8,128)(2,1)S(1)}, bf16[576,768]{1,0:T(8,128)(2,1)S(1)}, u32[]{:S(2)}, u32[]{:S(2)}) collective-permute-start(bf16[576,768]{1,0:T(8,128)(2,1)S(1)} %get-tuple-element.47), channel_id=1, source_target_pairs={{0,8},{8,0},{1,9},{9,1},{2,10},{10,2},{3,11},{11,3},{4,12},{12,4},... | collective-permute-start | bytes 2654216 | tf_op jit(solution)/shard_map/ppermute | solution.py:455
  54.8 17.0 %all-to-all-start.2 = ((bf16[4,144,768]{2,1,0:T(8,128)(2,1)}), bf16[4,144,768]{2,1,0:T(8,128)(2,1)S(1)}, u32[]{:S(2)}, u32[]{:S(2)}) async-start(bf16[4,144,768]{2,1,0:T(8,128)(2,1)} %shard_map.136), calls=%async_computation.2 | async-start | bytes 1769472 | tf_op jit(solution)/shard_map/all_to_all | solution.py:463
  58.3 13.7 %collective-permute-start.4 = (bf16[4,192,256]{2,1,0:T(8,128)(2,1)S(1)}, bf16[4,192,256]{2,1,0:T(8,128)(2,1)S(1)}, u32[]{:S(2)}, u32[]{:S(2)}) collective-permute-start(bf16[4,192,256]{2,1,0:T(8,128)(2,1)S(1)} %get-tuple-element.54), channel_id=1, source_target_pairs={{0,1},{1,0},{2,3},{3,2},{4,5},{5,4},{6,7},{7,6},{8,9},{9,8},{10,11... | collective-permute-start | bytes 1179656 | tf_op jit(solution)/shard_map/ppermute | solution.py:455
  87.7 12.5 %all-to-all-start.4 = ((bf16[8,36,384]{2,1,0:T(8,128)(2,1)}), bf16[8,36,384]{2,1,0:T(8,128)(2,1)S(1)}, u32[]{:S(2)}, u32[]{:S(2)}) async-start(bf16[8,36,384]{2,1,0:T(8,128)(2,1)} %shard_map.138), calls=%async_computation.4 | async-start | bytes 491520 | tf_op jit(solution)/shard_map/all_to_all | solution.py:463
  100.3 21.3 %all-to-all-start.5 = ((bf16[4,192,256]{2,1,0:T(8,128)(2,1)}), bf16[4,192,256]{2,1,0:T(8,128)(2,1)S(1)}, u32[]{:S(2)}, u32[]{:S(2)}) async-start(bf16[4,192,256]{2,1,0:T(8,128)(2,1)} %shard_map.140), calls=%async_computation.5 | async-start | bytes 786432 | tf_op jit(solution)/shard_map/all_to_all | solution.py:463
  121.5 10.7 %collective-permute-start.5 = (bf16[576,768]{1,0:T(8,128)(2,1)S(1)}, bf16[576,768]{1,0:T(8,128)(2,1)S(1)}, u32[]{:S(2)}, u32[]{:S(2)}) collective-permute-start(bf16[576,768]{1,0:T(8,128)(2,1)S(1)} %all_gather.3.mine), channel_id=1, source_target_pairs={{0,8},{8,0},{1,9},{9,1},{2,10},{10,2},{3,11},{11,3},{4,12},{12,4},... | collective-permute-start | bytes 2654216 | tf_op jit(solution)/shard_map/ppermute | solution.py:455

commit v13 on v12

--- a/solution.py
+++ b/solution.py
@@ -577,7 +577,7 @@
         query_grad,
     )
 
-    weight_got, sent = lax.optimization_barrier((swap(weight_sent), sent))
+    weight_got = swap(weight_sent)
     part = rows // chips
     (term,) = local_call(
         pair_body,
@@ -589,11 +589,12 @@
     (tiles,) = local_call(
         cut_body, [((intervals,) + tile, BF16)], operands=1, scratch=[pltpu.VMEM((part, cut), F32)]
     )(exchange(term, "x"))
-    tiles, got = lax.optimization_barrier((tiles, swap(sent, "side")))
-    (blocks,) = local_call(total_body, [((heads // SIDES,) + block, BF16)], operands=2)(held, got)
+    got = swap(sent, "side")
     (copies,) = local_call(spread_body, [((intervals,) + tile, BF16)], operands=1)(
         exchange(tiles, "interval")
     )
+    copies, got = lax.optimization_barrier((copies, got))
+    (blocks,) = local_call(total_body, [((heads // SIDES,) + block, BF16)], operands=2)(held, got)
     (term,) = local_call(
         join_body, [((part, cut), BF16)], operands=1, scratch=[pltpu.VMEM((part, cut), F32)]
     )(exchange(copies, "interval"))

time: 134 us -> 133 us (level)
  waiting for transfers between devices: 31.4 us -> 29.7 us
    all_to_all x5, waiting for transfers between devices: 28.3 us -> 24.5 us  [exchange(): return lax.all_to_all(value, axis, 0, 0, tiled=True)]
    ppermute x6, waiting for transfers between devices: 3.14 us -> 5.17 us  [swap(): return lax.ppermute(value, axis, [(0, 1), (1, 0)])]
  transfers between devices with their start and end apart: 11 -> 11, of which waited for: 7 -> 8; matrix products, arithmetic and copies ran while one was open for 0% -> 0% of each run, Pallas kernels for 5% -> 6%
where the time goes in v13:
time: 133 us
  starting transfers between devices  57.5 us (43%)
  waiting for transfers between devices  29.7 us (22%)
  blocking collectives  26.2 us (20%)
  Pallas kernels  18.3 us (14%)
    ppermute x6, starting transfers between devices, swap(): return lax.ppermute(value, axis, [(0, 1), (1, 0)])  32.2 us
    all_to_all x5, starting transfers between devices, exchange(): return lax.all_to_all(value, axis, 0, 0, tiled=True)  25.3 us
    all_to_all x5, waiting for transfers between devices, exchange(): return lax.all_to_all(value, axis, 0, 0, tiled=True)  24.5 us
    all_to_all x1, blocking collectives, exchange(): return lax.all_to_all(value, axis, 0, 0, tiled=True)  14.7 us
    all_gather x1, blocking collectives, on_device(): term = lax.all_gather(term, 'x', axis=0, tiled=True)  11.5 us
    ppermute x6, waiting for transfers between devices, swap(): return lax.ppermute(value, axis, [(0, 1), (1, 0)])  5.17 us
    pallas_call x1, Pallas kernels, on_device(): local_call(project_body, [((chips, height, KV), BF16, True), ((slots, tok...  3.47 us
    pallas_call x1, Pallas kernels, on_device(): local_call(input_body, [((heads // 2,) + block, F32), ((heads // 2,) + bl...  3.35 us
  transfers between devices with their start and end apart: 11, of which 8 were waited for; matrix products, arithmetic and copies ran while one was open for 0% of the time, Pallas kernels for 6%

profile of v13, /device:TPU:1, one launch (start us, length us, event | category | flops | bytes accessed | tf_op | source)
XLA Modules:
  0.0 132.6 jit_solution(7789032536020353449)
XLA Ops:
  0.6 0.0 copy-start.1
  0.6 0.0 copy-start
  0.7 0.0 copy-start.2
  0.7 0.0 copy-start.3
  0.7 3.5 %shard_map.130 = (bf16[4,272,384]{2,1,0:T(8,128)(2,1)}, bf16[64,256]{1,0:T(8,128)(2,1)S(1)}) custom-call(bf16[256,1536]{1,0:T(8,128)(2,1)} %bitcast.11, bf16[192,1536]{1,0:T(8,128)(2,1)} %w_key_hbm.3, bf16[192,1536]{1,0:T(8,128)(2,1)} %w_value_hbm.3, bf16[1536,128]{1,0:T(8,128)(2,1)} %w_junction_hbm.3, s32[8,8]{1,0:T(8,128)} %bitcast.16, s32[8,8]{1,0:T(8,128)} %bitcast.17, ...), custom_call_target="tpu_custom_call" | custom-call | tf_op jit(solution)/shard_map/pallas_call | solution.py:488
  4.2 4.9 %all-to-all-start = ((bf16[4,272,384]{2,1,0:T(8,128)(2,1)}), bf16[4,272,384]{2,1,0:T(8,128)(2,1)S(1)}, u32[]{:S(2)}, u32[]{:S(2)}) async-start(bf16[4,272,384]{2,1,0:T(8,128)(2,1)} %get-tuple-element.33), calls=%async_computation | async-start | bytes 1671168 | tf_op jit(solution)/shard_map/all_to_all | solution.py:463
  9.0 0.0 copy-done.1
  9.0 0.0 copy-done
  9.0 0.0 copy-done.2
  9.0 0.0 copy-done.3
  9.0 0.6 shard_map.129.own
  9.6 7.5 %collective-permute-start = (bf16[256,640]{1,0:T(8,128)(2,1)S(1)}, bf16[256,640]{1,0:T(8,128)(2,1)S(1)}, u32[]{:S(2)}, u32[]{:S(2)}) collective-permute-start(bf16[256,640]{1,0:T(8,128)(2,1)S(1)} %shard_map.129.own), channel_id=1, source_target_pairs={{0,8},{8,0},{1,9},{9,1},{2,10},{10,2},{3,11},{11,3},{4,12},{12,4},... | collective-permute-start | bytes 983048 | tf_op jit(solution)/shard_map/ppermute | solution.py:455
  17.1 1.2 collective-permute-done.other
  18.3 0.0 all-to-all-done.mine
  18.3 1.8 %shard_map.131 = (f32[2,256,1024]{2,1,0:T(8,128)S(1)}, f32[2,256,1024]{2,1,0:T(8,128)S(1)}, f32[2,8,256]{2,1,0:T(8,128)S(1)}) custom-call(bf16[256,640]{1,0:T(8,128)(2,1)S(1)} %shard_map.129.own, bf16[256,640]{1,0:T(8,128)(2,1)S(1)} %collective-permute-done.other, bf16[4,272,384]{2,1,0:T(8,128)(2,1)S(1)} %all-to-all-done.mine), custom_call_target="tpu_custom_call" | custom-call | tf_op jit(solution)/shard_map/pallas_call | solution.py:523
  20.1 7.8 %collective-permute-start.1 = (f32[2,8,256]{2,1,0:T(8,128)S(1)}, f32[2,8,256]{2,1,0:T(8,128)S(1)}, u32[]{:S(2)}, u32[]{:S(2)}) collective-permute-start(f32[2,8,256]{2,1,0:T(8,128)S(1)} %get-tuple-element.36.stats), channel_id=1, source_target_pairs={{0,8},{8,0},{1,9},{9,1},{2,10},{10,2},{3,11},{11,3},{4,12},{12,4},... | collective-permute-start | bytes 49160 | tf_op jit(solution)/shard_map/ppermute | solution.py:455
  28.0 0.6 shard_map.132
  28.6 0.2 collective-permute-done.1.got
  28.8 2.5 %shard_map.133 = (bf16[4,272,384]{2,1,0:T(8,128)(2,1)}, bf16[256,384]{1,0:T(8,128)(2,1)}, f32[256,256]{1,0:T(8,128)S(1)}) custom-call(bf16[256,640]{1,0:T(8,128)(2,1)S(1)} %shard_map.129.own, bf16[256,640]{1,0:T(8,128)(2,1)S(1)} %collective-permute-done.other, bf16[4,272,384]{2,1,0:T(8,128)(2,1)S(1)} %all-to-all-done.mine, ...), custom_call_target="tpu_custom_call" | custom-call | tf_op jit(solution)/shard_map/pallas_call | solution.py:534
  31.3 3.5 %all-to-all-start.1 = ((bf16[4,272,384]{2,1,0:T(8,128)(2,1)}), bf16[4,272,384]{2,1,0:T(8,128)(2,1)S(1)}, u32[]{:S(2)}, u32[]{:S(2)}) async-start(bf16[4,272,384]{2,1,0:T(8,128)(2,1)} %get-tuple-element.39), calls=%async_computation.1 | async-start | bytes 1671168 | tf_op jit(solution)/shard_map/all_to_all | solution.py:463
  34.8 2.3 %collective-permute-start.2 = (bf16[256,384]{1,0:T(8,128)(2,1)}, bf16[256,384]{1,0:T(8,128)(2,1)S(1)}, u32[]{:S(2)}, u32[]{:S(2)}) collective-permute-start(bf16[256,384]{1,0:T(8,128)(2,1)} %get-tuple-element.40), channel_id=1, source_target_pairs={{0,8},{8,0},{1,9},{9,1},{2,10},{10,2},{3,11},{11,3},{4,12},{12,4},... | collective-permute-start | bytes 589832 | tf_op jit(solution)/shard_map/ppermute | solution.py:455
  37.1 1.3 collective-permute-done.2.query_got
  38.4 9.0 %all-to-all-done.1.parts = bf16[4,272,384]{2,1,0:T(8,128)(2,1)S(1)} async-done(((bf16[4,272,384]{2,1,0:T(8,128)(2,1)}), bf16[4,272,384]{2,1,0:T(8,128)(2,1)S(1)}, u32[]{:S(2)}, u32[]{:S(2)}) %all-to-all-start.1) | async-done | bytes 835616 | tf_op jit(solution)/shard_map/all_to_all | solution.py:463
  47.4 0.7 shard_map.134
  48.1 3.1 %collective-permute-start.3 = (bf16[576,768]{1,0:T(8,128)(2,1)S(1)}, bf16[576,768]{1,0:T(8,128)(2,1)S(1)}, u32[]{:S(2)}, u32[]{:S(2)}) collective-permute-start(bf16[576,768]{1,0:T(8,128)(2,1)S(1)} %get-tuple-element.45), channel_id=1, source_target_pairs={{0,8},{8,0},{1,9},{9,1},{2,10},{10,2},{3,11},{11,3},{4,12},{12,4},... | collective-permute-start | bytes 2654216 | tf_op jit(solution)/shard_map/ppermute | solution.py:455
  51.2 2.0 %collective-permute-done.3.got = bf16[576,768]{1,0:T(8,128)(2,1)S(1)} collective-permute-done((bf16[576,768]{1,0:T(8,128)(2,1)S(1)}, bf16[576,768]{1,0:T(8,128)(2,1)S(1)}, u32[]{:S(2)}, u32[]{:S(2)}) %collective-permute-start.3) | collective-permute-done | bytes 884768 | tf_op jit(solution)/shard_map/ppermute | solution.py:455
  53.2 1.0 shard_map.135
  54.2 3.5 %all-to-all-start.2 = ((bf16[4,144,768]{2,1,0:T(8,128)(2,1)}), bf16[4,144,768]{2,1,0:T(8,128)(2,1)S(1)}, u32[]{:S(2)}, u32[]{:S(2)}) async-start(bf16[4,144,768]{2,1,0:T(8,128)(2,1)} %shard_map.135), calls=%async_computation.2 | async-start | bytes 1769472 | tf_op jit(solution)/shard_map/all_to_all | solution.py:463
  57.7 3.4 %shard_map.138 = (f32[4,192,256]{2,1,0:T(8,128)S(1)}, bf16[4,192,256]{2,1,0:T(8,128)(2,1)}) custom-call(bf16[192,1536]{1,0:T(8,128)(2,1)} %w_query_hbm.1, bf16[192,1536]{1,0:T(8,128)(2,1)} %w_key_hbm.3, bf16[192,1536]{1,0:T(8,128)(2,1)} %w_value_hbm.3, bf16[1536,128]{1,0:T(8,128)(2,1)} %w_junction_hbm.3, bf16[4,272,384]{2,1,0:T(8,128)(2,1)S(1)} %all-to-all-done.1.parts, ...), custom_call_target="tpu_custom_call" | custom-call | tf_op jit(solution)/shard_map/pallas_call | solution.py:560
  61.1 2.5 %collective-permute-start.4 = (bf16[4,192,256]{2,1,0:T(8,128)(2,1)}, bf16[4,192,256]{2,1,0:T(8,128)(2,1)S(1)}, u32[]{:S(2)}, u32[]{:S(2)}) collective-permute-start(bf16[4,192,256]{2,1,0:T(8,128)(2,1)} %get-tuple-element.50), channel_id=1, source_target_pairs={{0,1},{1,0},{2,3},{3,2},{4,5},{5,4},{6,7},{7,6},{8,9},{9,8},{10,11... | collective-permute-start | bytes 1179656 | tf_op jit(solution)/shard_map/ppermute | solution.py:455
  63.6 7.2 %all-to-all-done.2.parts = bf16[4,144,768]{2,1,0:T(8,128)(2,1)S(1)} async-done(((bf16[4,144,768]{2,1,0:T(8,128)(2,1)}), bf16[4,144,768]{2,1,0:T(8,128)(2,1)S(1)}, u32[]{:S(2)}, u32[]{:S(2)}) %all-to-all-start.2) | async-done | bytes 884768 | tf_op jit(solution)/shard_map/all_to_all | solution.py:463
  70.8 0.2 shard_map.136
  71.0 14.7 %all_to_all.30.parts = bf16[8,36,384]{2,1,0:T(8,128)(2,1)S(1)} all-to-all(bf16[8,36,384]{2,1,0:T(8,128)(2,1)S(1)} %shard_map.136), channel_id=1, replica_groups=mesh['interval'=8,'x'=4,'core'=2,'pair'=4,'side'=2] {'interval'}, dimensions={0} | all-to-all | bytes 442368 | tf_op jit(solution)/shard_map/all_to_all | solution.py:463
  85.7 0.7 shard_map.137
  86.4 0.0 collective-permute-done.4.refs_1_
  86.4 3.4 %all-to-all-start.4 = ((bf16[8,36,384]{2,1,0:T(8,128)(2,1)}), bf16[8,36,384]{2,1,0:T(8,128)(2,1)S(1)}, u32[]{:S(2)}, u32[]{:S(2)}) async-start(bf16[8,36,384]{2,1,0:T(8,128)(2,1)} %shard_map.137), calls=%async_computation.4 | async-start | bytes 491520 | tf_op jit(solution)/shard_map/all_to_all | solution.py:463
  89.8 0.8 shard_map.140
  90.6 8.3 %all-to-all-done.4.tiles = bf16[8,36,384]{2,1,0:T(8,128)(2,1)S(1)} async-done(((bf16[8,36,384]{2,1,0:T(8,128)(2,1)}), bf16[8,36,384]{2,1,0:T(8,128)(2,1)S(1)}, u32[]{:S(2)}, u32[]{:S(2)}) %all-to-all-start.4) | async-done | bytes 221216 | tf_op jit(solution)/shard_map/all_to_all | solution.py:463
  99.0 10.0 %all-to-all-start.5 = ((bf16[4,192,256]{2,1,0:T(8,128)(2,1)}), bf16[4,192,256]{2,1,0:T(8,128)(2,1)S(1)}, u32[]{:S(2)}, u32[]{:S(2)}) async-start(bf16[4,192,256]{2,1,0:T(8,128)(2,1)} %shard_map.140), calls=%async_computation.5 | async-start | bytes 786432 | tf_op jit(solution)/shard_map/all_to_all | solution.py:463
  109.0 11.5 %all_gather.3.mine = bf16[576,768]{1,0:T(8,128)(2,1)S(1)} all-gather(bf16[144,768]{1,0:T(8,128)(2,1)S(1)} %shard_map.139), channel_id=1, replica_groups=mesh['interval'=8,'x'=4,'core'=2,'pair'=4,'side'=2] {'x'}, dimensions={0}, use_global_device_ids=true | all-gather | bytes 1105920 | tf_op jit(solution)/shard_map/all_gather | solution.py:602
  120.6 0.0 all-to-all-done.5.parts
  120.6 9.0 %collective-permute-start.5 = (bf16[576,768]{1,0:T(8,128)(2,1)S(1)}, bf16[576,768]{1,0:T(8,128)(2,1)S(1)}, u32[]{:S(2)}, u32[]{:S(2)}) collective-permute-start(bf16[576,768]{1,0:T(8,128)(2,1)S(1)} %all_gather.3.mine), channel_id=1, source_target_pairs={{0,8},{8,0},{1,9},{9,1},{2,10},{10,2},{3,11},{11,3},{4,12},{12,4},... | collective-permute-start | bytes 2654216 | tf_op jit(solution)/shard_map/ppermute | solution.py:455
  129.6 0.9 shard_map.142
  130.6 0.7 shard_map.141
  131.3 0.4 collective-permute-done.5.theirs
  131.6 0.9 shard_map.143
  (1 shorter events, 0.0 us)
Async XLA Ops:
  0.6 8.4 %copy-start.1 = (bf16[1536,128]{1,0:T(8,128)(2,1)S(1)}, bf16[1536,128]{1,0:T(8,128)(2,1)}, u32[]{:S(2)}) copy-start(bf16[1536,128]{1,0:T(8,128)(2,1)} %w_junction_hbm.3) | copy-start | bytes 1179652
  0.6 8.4 %copy-start = (bf16[1,256,1536]{2,1,0:T(8,128)(2,1)S(1)}, bf16[1,256,1536]{2,1,0:T(8,128)(2,1)}, u32[]{:S(2)}) copy-start(bf16[1,256,1536]{2,1,0:T(8,128)(2,1)} %param.10) | copy-start | bytes 2359300
  0.7 8.4 %copy-start.2 = (bf16[192,1536]{1,0:T(8,128)(2,1)S(1)}, bf16[192,1536]{1,0:T(8,128)(2,1)}, u32[]{:S(2)}) copy-start(bf16[192,1536]{1,0:T(8,128)(2,1)} %w_query_hbm.1) | copy-start | bytes 1769476
  0.7 8.4 %copy-start.3 = (bf16[1,256,192]{1,2,0:T(8,128)(2,1)S(1)}, bf16[1,256,192]{1,2,0:T(8,128)(2,1)}, u32[]{:S(2)}) copy-start(bf16[1,256,192]{1,2,0:T(8,128)(2,1)} %param.11) | copy-start | bytes 294916
  4.2 14.2 %all-to-all-start = ((bf16[4,272,384]{2,1,0:T(8,128)(2,1)}), bf16[4,272,384]{2,1,0:T(8,128)(2,1)S(1)}, u32[]{:S(2)}, u32[]{:S(2)}) async-start(bf16[4,272,384]{2,1,0:T(8,128)(2,1)} %get-tuple-element.33), calls=%async_computation | async-start | bytes 1671168 | tf_op jit(solution)/shard_map/all_to_all | solution.py:463
  9.6 8.7 %collective-permute-start = (bf16[256,640]{1,0:T(8,128)(2,1)S(1)}, bf16[256,640]{1,0:T(8,128)(2,1)S(1)}, u32[]{:S(2)}, u32[]{:S(2)}) collective-permute-start(bf16[256,640]{1,0:T(8,128)(2,1)S(1)} %shard_map.129.own), channel_id=1, source_target_pairs={{0,8},{8,0},{1,9},{9,1},{2,10},{10,2},{3,11},{11,3},{4,12},{12,4},... | collective-permute-start | bytes 983048 | tf_op jit(solution)/shard_map/ppermute | solution.py:455
  20.1 8.7 %collective-permute-start.1 = (f32[2,8,256]{2,1,0:T(8,128)S(1)}, f32[2,8,256]{2,1,0:T(8,128)S(1)}, u32[]{:S(2)}, u32[]{:S(2)}) collective-permute-start(f32[2,8,256]{2,1,0:T(8,128)S(1)} %get-tuple-element.36.stats), channel_id=1, source_target_pairs={{0,8},{8,0},{1,9},{9,1},{2,10},{10,2},{3,11},{11,3},{4,12},{12,4},... | collective-permute-start | bytes 49160 | tf_op jit(solution)/shard_map/ppermute | solution.py:455
  31.3 16.1 %all-to-all-start.1 = ((bf16[4,272,384]{2,1,0:T(8,128)(2,1)}), bf16[4,272,384]{2,1,0:T(8,128)(2,1)S(1)}, u32[]{:S(2)}, u32[]{:S(2)}) async-start(bf16[4,272,384]{2,1,0:T(8,128)(2,1)} %get-tuple-element.39), calls=%async_computation.1 | async-start | bytes 1671168 | tf_op jit(solution)/shard_map/all_to_all | solution.py:463
  34.8 3.5 %collective-permute-start.2 = (bf16[256,384]{1,0:T(8,128)(2,1)}, bf16[256,384]{1,0:T(8,128)(2,1)S(1)}, u32[]{:S(2)}, u32[]{:S(2)}) collective-permute-start(bf16[256,384]{1,0:T(8,128)(2,1)} %get-tuple-element.40), channel_id=1, source_target_pairs={{0,8},{8,0},{1,9},{9,1},{2,10},{10,2},{3,11},{11,3},{4,12},{12,4},... | collective-permute-start | bytes 589832 | tf_op jit(solution)/shard_map/ppermute | solution.py:455
  48.1 5.1 %collective-permute-start.3 = (bf16[576,768]{1,0:T(8,128)(2,1)S(1)}, bf16[576,768]{1,0:T(8,128)(2,1)S(1)}, u32[]{:S(2)}, u32[]{:S(2)}) collective-permute-start(bf16[576,768]{1,0:T(8,128)(2,1)S(1)} %get-tuple-element.45), channel_id=1, source_target_pairs={{0,8},{8,0},{1,9},{9,1},{2,10},{10,2},{3,11},{11,3},{4,12},{12,4},... | collective-permute-start | bytes 2654216 | tf_op jit(solution)/shard_map/ppermute | solution.py:455
  54.2 16.6 %all-to-all-start.2 = ((bf16[4,144,768]{2,1,0:T(8,128)(2,1)}), bf16[4,144,768]{2,1,0:T(8,128)(2,1)S(1)}, u32[]{:S(2)}, u32[]{:S(2)}) async-start(bf16[4,144,768]{2,1,0:T(8,128)(2,1)} %shard_map.135), calls=%async_computation.2 | async-start | bytes 1769472 | tf_op jit(solution)/shard_map/all_to_all | solution.py:463
  61.1 25.3 %collective-permute-start.4 = (bf16[4,192,256]{2,1,0:T(8,128)(2,1)}, bf16[4,192,256]{2,1,0:T(8,128)(2,1)S(1)}, u32[]{:S(2)}, u32[]{:S(2)}) collective-permute-start(bf16[4,192,256]{2,1,0:T(8,128)(2,1)} %get-tuple-element.50), channel_id=1, source_target_pairs={{0,1},{1,0},{2,3},{3,2},{4,5},{5,4},{6,7},{7,6},{8,9},{9,8},{10,11... | collective-permute-start | bytes 1179656 | tf_op jit(solution)/shard_map/ppermute | solution.py:455
  86.4 12.5 %all-to-all-start.4 = ((bf16[8,36,384]{2,1,0:T(8,128)(2,1)}), bf16[8,36,384]{2,1,0:T(8,128)(2,1)S(1)}, u32[]{:S(2)}, u32[]{:S(2)}) async-start(bf16[8,36,384]{2,1,0:T(8,128)(2,1)} %shard_map.137), calls=%async_computation.4 | async-start | bytes 491520 | tf_op jit(solution)/shard_map/all_to_all | solution.py:463
  99.0 21.6 %all-to-all-start.5 = ((bf16[4,192,256]{2,1,0:T(8,128)(2,1)}), bf16[4,192,256]{2,1,0:T(8,128)(2,1)S(1)}, u32[]{:S(2)}, u32[]{:S(2)}) async-start(bf16[4,192,256]{2,1,0:T(8,128)(2,1)} %shard_map.140), calls=%async_computation.5 | async-start | bytes 786432 | tf_op jit(solution)/shard_map/all_to_all | solution.py:463
  120.6 11.1 %collective-permute-start.5 = (bf16[576,768]{1,0:T(8,128)(2,1)S(1)}, bf16[576,768]{1,0:T(8,128)(2,1)S(1)}, u32[]{:S(2)}, u32[]{:S(2)}) collective-permute-start(bf16[576,768]{1,0:T(8,128)(2,1)S(1)} %all_gather.3.mine), channel_id=1, source_target_pairs={{0,8},{8,0},{1,9},{9,1},{2,10},{10,2},{3,11},{11,3},{4,12},{12,4},... | collective-permute-start | bytes 2654216 | tf_op jit(solution)/shard_map/ppermute | solution.py:455

commit v14 on v13

--- a/solution.py
+++ b/solution.py
@@ -135,7 +135,7 @@
     extra = jnp.zeros((slots, PJ), F32)
     for i, column in enumerate(scalars):
         extra = jnp.where(lane == i, column, extra)
-    for copy in copies[4:]:
+    for copy in copies[4:7]:
         copy.wait()
     x = hidden[...]
     rows[...] = contract(x, weights[...], 1, 1).astype(BF16)
@@ -146,6 +146,7 @@
     ]
     for copy in leaving:
         copy.start()
+    copies[7].wait()
     feats = contract(x, w_junction[...], 1, 0).astype(BF16)
     slot_rows[...] = jnp.concatenate(
         [

time: 133 us -> 133 us (level)
  no operation moved by 1% of the time
where the time goes in v14:
time: 133 us
  starting transfers between devices  57.5 us (43%)
  waiting for transfers between devices  29.7 us (22%)
  blocking collectives  26.2 us (20%)
  Pallas kernels  18.4 us (14%)
    ppermute x6, starting transfers between devices, swap(): return lax.ppermute(value, axis, [(0, 1), (1, 0)])  32.2 us
    all_to_all x5, starting transfers between devices, exchange(): return lax.all_to_all(value, axis, 0, 0, tiled=True)  25.3 us
    all_to_all x5, waiting for transfers between devices, exchange(): return lax.all_to_all(value, axis, 0, 0, tiled=True)  24.5 us
    all_to_all x1, blocking collectives, exchange(): return lax.all_to_all(value, axis, 0, 0, tiled=True)  14.7 us
    all_gather x1, blocking collectives, on_device(): term = lax.all_gather(term, 'x', axis=0, tiled=True)  11.5 us
    ppermute x6, waiting for transfers between devices, swap(): return lax.ppermute(value, axis, [(0, 1), (1, 0)])  5.17 us
    pallas_call x1, Pallas kernels, on_device(): local_call(project_body, [((chips, height, KV), BF16, True), ((slots, tok...  3.51 us
    pallas_call x1, Pallas kernels, on_device(): local_call(input_body, [((heads // 2,) + block, F32), ((heads // 2,) + bl...  3.35 us
  transfers between devices with their start and end apart: 11, of which 8 were waited for; matrix products, arithmetic and copies ran while one was open for 0% of the time, Pallas kernels for 6%

profile of v14, /device:TPU:1, one launch (start us, length us, event | category | flops | bytes accessed | tf_op | source)
XLA Modules:
  0.0 132.6 jit_solution(2971871151923283832)
XLA Ops:
  0.6 0.0 copy-start.1
  0.6 0.0 copy-start
  0.7 0.0 copy-start.2
  0.7 0.0 copy-start.3
  0.7 3.5 %shard_map.130 = (bf16[4,272,384]{2,1,0:T(8,128)(2,1)}, bf16[64,256]{1,0:T(8,128)(2,1)S(1)}) custom-call(bf16[256,1536]{1,0:T(8,128)(2,1)} %bitcast.11, bf16[192,1536]{1,0:T(8,128)(2,1)} %w_key_hbm.3, bf16[192,1536]{1,0:T(8,128)(2,1)} %w_value_hbm.3, bf16[1536,128]{1,0:T(8,128)(2,1)} %w_junction_hbm.3, s32[8,8]{1,0:T(8,128)} %bitcast.16, s32[8,8]{1,0:T(8,128)} %bitcast.17, ...), custom_call_target="tpu_custom_call" | custom-call | tf_op jit(solution)/shard_map/pallas_call | solution.py:489
  4.2 4.9 %all-to-all-start = ((bf16[4,272,384]{2,1,0:T(8,128)(2,1)}), bf16[4,272,384]{2,1,0:T(8,128)(2,1)S(1)}, u32[]{:S(2)}, u32[]{:S(2)}) async-start(bf16[4,272,384]{2,1,0:T(8,128)(2,1)} %get-tuple-element.33), calls=%async_computation | async-start | bytes 1671168 | tf_op jit(solution)/shard_map/all_to_all | solution.py:464
  9.1 0.0 copy-done.1
  9.1 0.0 copy-done
  9.1 0.0 copy-done.2
  9.1 0.0 copy-done.3
  9.1 0.6 shard_map.129.own
  9.7 7.5 %collective-permute-start = (bf16[256,640]{1,0:T(8,128)(2,1)S(1)}, bf16[256,640]{1,0:T(8,128)(2,1)S(1)}, u32[]{:S(2)}, u32[]{:S(2)}) collective-permute-start(bf16[256,640]{1,0:T(8,128)(2,1)S(1)} %shard_map.129.own), channel_id=1, source_target_pairs={{0,8},{8,0},{1,9},{9,1},{2,10},{10,2},{3,11},{11,3},{4,12},{12,4},... | collective-permute-start | bytes 983048 | tf_op jit(solution)/shard_map/ppermute | solution.py:456
  17.1 1.2 collective-permute-done.other
  18.4 0.0 all-to-all-done.mine
  18.4 1.8 %shard_map.131 = (f32[2,256,1024]{2,1,0:T(8,128)S(1)}, f32[2,256,1024]{2,1,0:T(8,128)S(1)}, f32[2,8,256]{2,1,0:T(8,128)S(1)}) custom-call(bf16[256,640]{1,0:T(8,128)(2,1)S(1)} %shard_map.129.own, bf16[256,640]{1,0:T(8,128)(2,1)S(1)} %collective-permute-done.other, bf16[4,272,384]{2,1,0:T(8,128)(2,1)S(1)} %all-to-all-done.mine), custom_call_target="tpu_custom_call" | custom-call | tf_op jit(solution)/shard_map/pallas_call | solution.py:524
  20.2 7.8 %collective-permute-start.1 = (f32[2,8,256]{2,1,0:T(8,128)S(1)}, f32[2,8,256]{2,1,0:T(8,128)S(1)}, u32[]{:S(2)}, u32[]{:S(2)}) collective-permute-start(f32[2,8,256]{2,1,0:T(8,128)S(1)} %get-tuple-element.36.stats), channel_id=1, source_target_pairs={{0,8},{8,0},{1,9},{9,1},{2,10},{10,2},{3,11},{11,3},{4,12},{12,4},... | collective-permute-start | bytes 49160 | tf_op jit(solution)/shard_map/ppermute | solution.py:456
  28.0 0.6 shard_map.132
  28.6 0.2 collective-permute-done.1.got
  28.8 2.5 %shard_map.133 = (bf16[4,272,384]{2,1,0:T(8,128)(2,1)}, bf16[256,384]{1,0:T(8,128)(2,1)}, f32[256,256]{1,0:T(8,128)S(1)}) custom-call(bf16[256,640]{1,0:T(8,128)(2,1)S(1)} %shard_map.129.own, bf16[256,640]{1,0:T(8,128)(2,1)S(1)} %collective-permute-done.other, bf16[4,272,384]{2,1,0:T(8,128)(2,1)S(1)} %all-to-all-done.mine, ...), custom_call_target="tpu_custom_call" | custom-call | tf_op jit(solution)/shard_map/pallas_call | solution.py:535
  31.3 3.5 %all-to-all-start.1 = ((bf16[4,272,384]{2,1,0:T(8,128)(2,1)}), bf16[4,272,384]{2,1,0:T(8,128)(2,1)S(1)}, u32[]{:S(2)}, u32[]{:S(2)}) async-start(bf16[4,272,384]{2,1,0:T(8,128)(2,1)} %get-tuple-element.39), calls=%async_computation.1 | async-start | bytes 1671168 | tf_op jit(solution)/shard_map/all_to_all | solution.py:464
  34.9 2.3 %collective-permute-start.2 = (bf16[256,384]{1,0:T(8,128)(2,1)}, bf16[256,384]{1,0:T(8,128)(2,1)S(1)}, u32[]{:S(2)}, u32[]{:S(2)}) collective-permute-start(bf16[256,384]{1,0:T(8,128)(2,1)} %get-tuple-element.40), channel_id=1, source_target_pairs={{0,8},{8,0},{1,9},{9,1},{2,10},{10,2},{3,11},{11,3},{4,12},{12,4},... | collective-permute-start | bytes 589832 | tf_op jit(solution)/shard_map/ppermute | solution.py:456
  37.1 1.3 collective-permute-done.2.query_got
  38.4 9.0 %all-to-all-done.1.parts = bf16[4,272,384]{2,1,0:T(8,128)(2,1)S(1)} async-done(((bf16[4,272,384]{2,1,0:T(8,128)(2,1)}), bf16[4,272,384]{2,1,0:T(8,128)(2,1)S(1)}, u32[]{:S(2)}, u32[]{:S(2)}) %all-to-all-start.1) | async-done | bytes 835616 | tf_op jit(solution)/shard_map/all_to_all | solution.py:464
  47.4 0.7 shard_map.134
  48.1 3.1 %collective-permute-start.3 = (bf16[576,768]{1,0:T(8,128)(2,1)S(1)}, bf16[576,768]{1,0:T(8,128)(2,1)S(1)}, u32[]{:S(2)}, u32[]{:S(2)}) collective-permute-start(bf16[576,768]{1,0:T(8,128)(2,1)S(1)} %get-tuple-element.45), channel_id=1, source_target_pairs={{0,8},{8,0},{1,9},{9,1},{2,10},{10,2},{3,11},{11,3},{4,12},{12,4},... | collective-permute-start | bytes 2654216 | tf_op jit(solution)/shard_map/ppermute | solution.py:456
  51.2 2.0 %collective-permute-done.3.got = bf16[576,768]{1,0:T(8,128)(2,1)S(1)} collective-permute-done((bf16[576,768]{1,0:T(8,128)(2,1)S(1)}, bf16[576,768]{1,0:T(8,128)(2,1)S(1)}, u32[]{:S(2)}, u32[]{:S(2)}) %collective-permute-start.3) | collective-permute-done | bytes 884768 | tf_op jit(solution)/shard_map/ppermute | solution.py:456
  53.2 1.0 shard_map.135
  54.3 3.5 %all-to-all-start.2 = ((bf16[4,144,768]{2,1,0:T(8,128)(2,1)}), bf16[4,144,768]{2,1,0:T(8,128)(2,1)S(1)}, u32[]{:S(2)}, u32[]{:S(2)}) async-start(bf16[4,144,768]{2,1,0:T(8,128)(2,1)} %shard_map.135), calls=%async_computation.2 | async-start | bytes 1769472 | tf_op jit(solution)/shard_map/all_to_all | solution.py:464
  57.8 3.4 %shard_map.138 = (f32[4,192,256]{2,1,0:T(8,128)S(1)}, bf16[4,192,256]{2,1,0:T(8,128)(2,1)}) custom-call(bf16[192,1536]{1,0:T(8,128)(2,1)} %w_query_hbm.1, bf16[192,1536]{1,0:T(8,128)(2,1)} %w_key_hbm.3, bf16[192,1536]{1,0:T(8,128)(2,1)} %w_value_hbm.3, bf16[1536,128]{1,0:T(8,128)(2,1)} %w_junction_hbm.3, bf16[4,272,384]{2,1,0:T(8,128)(2,1)S(1)} %all-to-all-done.1.parts, ...), custom_call_target="tpu_custom_call" | custom-call | tf_op jit(solution)/shard_map/pallas_call | solution.py:561
  61.1 2.5 %collective-permute-start.4 = (bf16[4,192,256]{2,1,0:T(8,128)(2,1)}, bf16[4,192,256]{2,1,0:T(8,128)(2,1)S(1)}, u32[]{:S(2)}, u32[]{:S(2)}) collective-permute-start(bf16[4,192,256]{2,1,0:T(8,128)(2,1)} %get-tuple-element.50), channel_id=1, source_target_pairs={{0,1},{1,0},{2,3},{3,2},{4,5},{5,4},{6,7},{7,6},{8,9},{9,8},{10,11... | collective-permute-start | bytes 1179656 | tf_op jit(solution)/shard_map/ppermute | solution.py:456
  63.7 7.2 %all-to-all-done.2.parts = bf16[4,144,768]{2,1,0:T(8,128)(2,1)S(1)} async-done(((bf16[4,144,768]{2,1,0:T(8,128)(2,1)}), bf16[4,144,768]{2,1,0:T(8,128)(2,1)S(1)}, u32[]{:S(2)}, u32[]{:S(2)}) %all-to-all-start.2) | async-done | bytes 884768 | tf_op jit(solution)/shard_map/all_to_all | solution.py:464
  70.8 0.2 shard_map.136
  71.0 14.7 %all_to_all.30.parts = bf16[8,36,384]{2,1,0:T(8,128)(2,1)S(1)} all-to-all(bf16[8,36,384]{2,1,0:T(8,128)(2,1)S(1)} %shard_map.136), channel_id=1, replica_groups=mesh['interval'=8,'x'=4,'core'=2,'pair'=4,'side'=2] {'interval'}, dimensions={0} | all-to-all | bytes 442368 | tf_op jit(solution)/shard_map/all_to_all | solution.py:464
  85.7 0.7 shard_map.137
  86.5 0.0 collective-permute-done.4.refs_1_
  86.5 3.4 %all-to-all-start.4 = ((bf16[8,36,384]{2,1,0:T(8,128)(2,1)}), bf16[8,36,384]{2,1,0:T(8,128)(2,1)S(1)}, u32[]{:S(2)}, u32[]{:S(2)}) async-start(bf16[8,36,384]{2,1,0:T(8,128)(2,1)} %shard_map.137), calls=%async_computation.4 | async-start | bytes 491520 | tf_op jit(solution)/shard_map/all_to_all | solution.py:464
  89.9 0.8 shard_map.140
  90.7 8.3 %all-to-all-done.4.tiles = bf16[8,36,384]{2,1,0:T(8,128)(2,1)S(1)} async-done(((bf16[8,36,384]{2,1,0:T(8,128)(2,1)}), bf16[8,36,384]{2,1,0:T(8,128)(2,1)S(1)}, u32[]{:S(2)}, u32[]{:S(2)}) %all-to-all-start.4) | async-done | bytes 221216 | tf_op jit(solution)/shard_map/all_to_all | solution.py:464
  99.0 10.0 %all-to-all-start.5 = ((bf16[4,192,256]{2,1,0:T(8,128)(2,1)}), bf16[4,192,256]{2,1,0:T(8,128)(2,1)S(1)}, u32[]{:S(2)}, u32[]{:S(2)}) async-start(bf16[4,192,256]{2,1,0:T(8,128)(2,1)} %shard_map.140), calls=%async_computation.5 | async-start | bytes 786432 | tf_op jit(solution)/shard_map/all_to_all | solution.py:464
  109.1 11.5 %all_gather.3.mine = bf16[576,768]{1,0:T(8,128)(2,1)S(1)} all-gather(bf16[144,768]{1,0:T(8,128)(2,1)S(1)} %shard_map.139), channel_id=1, replica_groups=mesh['interval'=8,'x'=4,'core'=2,'pair'=4,'side'=2] {'x'}, dimensions={0}, use_global_device_ids=true | all-gather | bytes 1105920 | tf_op jit(solution)/shard_map/all_gather | solution.py:603
  120.6 0.0 all-to-all-done.5.parts
  120.6 9.0 %collective-permute-start.5 = (bf16[576,768]{1,0:T(8,128)(2,1)S(1)}, bf16[576,768]{1,0:T(8,128)(2,1)S(1)}, u32[]{:S(2)}, u32[]{:S(2)}) collective-permute-start(bf16[576,768]{1,0:T(8,128)(2,1)S(1)} %all_gather.3.mine), channel_id=1, source_target_pairs={{0,8},{8,0},{1,9},{9,1},{2,10},{10,2},{3,11},{11,3},{4,12},{12,4},... | collective-permute-start | bytes 2654216 | tf_op jit(solution)/shard_map/ppermute | solution.py:456
  129.6 0.9 shard_map.142
  130.6 0.7 shard_map.141
  131.3 0.4 collective-permute-done.5.theirs
  131.7 0.9 shard_map.143
  (1 shorter events, 0.0 us)
Async XLA Ops:
  0.6 8.4 %copy-start.1 = (bf16[1536,128]{1,0:T(8,128)(2,1)S(1)}, bf16[1536,128]{1,0:T(8,128)(2,1)}, u32[]{:S(2)}) copy-start(bf16[1536,128]{1,0:T(8,128)(2,1)} %w_junction_hbm.3) | copy-start | bytes 1179652
  0.6 8.4 %copy-start = (bf16[1,256,1536]{2,1,0:T(8,128)(2,1)S(1)}, bf16[1,256,1536]{2,1,0:T(8,128)(2,1)}, u32[]{:S(2)}) copy-start(bf16[1,256,1536]{2,1,0:T(8,128)(2,1)} %param.10) | copy-start | bytes 2359300
  0.7 8.4 %copy-start.2 = (bf16[192,1536]{1,0:T(8,128)(2,1)S(1)}, bf16[192,1536]{1,0:T(8,128)(2,1)}, u32[]{:S(2)}) copy-start(bf16[192,1536]{1,0:T(8,128)(2,1)} %w_query_hbm.1) | copy-start | bytes 1769476
  0.7 8.4 %copy-start.3 = (bf16[1,256,192]{1,2,0:T(8,128)(2,1)S(1)}, bf16[1,256,192]{1,2,0:T(8,128)(2,1)}, u32[]{:S(2)}) copy-start(bf16[1,256,192]{1,2,0:T(8,128)(2,1)} %param.11) | copy-start | bytes 294916
  4.2 14.2 %all-to-all-start = ((bf16[4,272,384]{2,1,0:T(8,128)(2,1)}), bf16[4,272,384]{2,1,0:T(8,128)(2,1)S(1)}, u32[]{:S(2)}, u32[]{:S(2)}) async-start(bf16[4,272,384]{2,1,0:T(8,128)(2,1)} %get-tuple-element.33), calls=%async_computation | async-start | bytes 1671168 | tf_op jit(solution)/shard_map/all_to_all | solution.py:464
  9.7 8.7 %collective-permute-start = (bf16[256,640]{1,0:T(8,128)(2,1)S(1)}, bf16[256,640]{1,0:T(8,128)(2,1)S(1)}, u32[]{:S(2)}, u32[]{:S(2)}) collective-permute-start(bf16[256,640]{1,0:T(8,128)(2,1)S(1)} %shard_map.129.own), channel_id=1, source_target_pairs={{0,8},{8,0},{1,9},{9,1},{2,10},{10,2},{3,11},{11,3},{4,12},{12,4},... | collective-permute-start | bytes 983048 | tf_op jit(solution)/shard_map/ppermute | solution.py:456
  20.2 8.7 %collective-permute-start.1 = (f32[2,8,256]{2,1,0:T(8,128)S(1)}, f32[2,8,256]{2,1,0:T(8,128)S(1)}, u32[]{:S(2)}, u32[]{:S(2)}) collective-permute-start(f32[2,8,256]{2,1,0:T(8,128)S(1)} %get-tuple-element.36.stats), channel_id=1, source_target_pairs={{0,8},{8,0},{1,9},{9,1},{2,10},{10,2},{3,11},{11,3},{4,12},{12,4},... | collective-permute-start | bytes 49160 | tf_op jit(solution)/shard_map/ppermute | solution.py:456
  31.3 16.1 %all-to-all-start.1 = ((bf16[4,272,384]{2,1,0:T(8,128)(2,1)}), bf16[4,272,384]{2,1,0:T(8,128)(2,1)S(1)}, u32[]{:S(2)}, u32[]{:S(2)}) async-start(bf16[4,272,384]{2,1,0:T(8,128)(2,1)} %get-tuple-element.39), calls=%async_computation.1 | async-start | bytes 1671168 | tf_op jit(solution)/shard_map/all_to_all | solution.py:464
  34.9 3.5 %collective-permute-start.2 = (bf16[256,384]{1,0:T(8,128)(2,1)}, bf16[256,384]{1,0:T(8,128)(2,1)S(1)}, u32[]{:S(2)}, u32[]{:S(2)}) collective-permute-start(bf16[256,384]{1,0:T(8,128)(2,1)} %get-tuple-element.40), channel_id=1, source_target_pairs={{0,8},{8,0},{1,9},{9,1},{2,10},{10,2},{3,11},{11,3},{4,12},{12,4},... | collective-permute-start | bytes 589832 | tf_op jit(solution)/shard_map/ppermute | solution.py:456
  48.1 5.1 %collective-permute-start.3 = (bf16[576,768]{1,0:T(8,128)(2,1)S(1)}, bf16[576,768]{1,0:T(8,128)(2,1)S(1)}, u32[]{:S(2)}, u32[]{:S(2)}) collective-permute-start(bf16[576,768]{1,0:T(8,128)(2,1)S(1)} %get-tuple-element.45), channel_id=1, source_target_pairs={{0,8},{8,0},{1,9},{9,1},{2,10},{10,2},{3,11},{11,3},{4,12},{12,4},... | collective-permute-start | bytes 2654216 | tf_op jit(solution)/shard_map/ppermute | solution.py:456
  54.3 16.6 %all-to-all-start.2 = ((bf16[4,144,768]{2,1,0:T(8,128)(2,1)}), bf16[4,144,768]{2,1,0:T(8,128)(2,1)S(1)}, u32[]{:S(2)}, u32[]{:S(2)}) async-start(bf16[4,144,768]{2,1,0:T(8,128)(2,1)} %shard_map.135), calls=%async_computation.2 | async-start | bytes 1769472 | tf_op jit(solution)/shard_map/all_to_all | solution.py:464
  61.1 25.3 %collective-permute-start.4 = (bf16[4,192,256]{2,1,0:T(8,128)(2,1)}, bf16[4,192,256]{2,1,0:T(8,128)(2,1)S(1)}, u32[]{:S(2)}, u32[]{:S(2)}) collective-permute-start(bf16[4,192,256]{2,1,0:T(8,128)(2,1)} %get-tuple-element.50), channel_id=1, source_target_pairs={{0,1},{1,0},{2,3},{3,2},{4,5},{5,4},{6,7},{7,6},{8,9},{9,8},{10,11... | collective-permute-start | bytes 1179656 | tf_op jit(solution)/shard_map/ppermute | solution.py:456
  86.5 12.5 %all-to-all-start.4 = ((bf16[8,36,384]{2,1,0:T(8,128)(2,1)}), bf16[8,36,384]{2,1,0:T(8,128)(2,1)S(1)}, u32[]{:S(2)}, u32[]{:S(2)}) async-start(bf16[8,36,384]{2,1,0:T(8,128)(2,1)} %shard_map.137), calls=%async_computation.4 | async-start | bytes 491520 | tf_op jit(solution)/shard_map/all_to_all | solution.py:464
  99.0 21.6 %all-to-all-start.5 = ((bf16[4,192,256]{2,1,0:T(8,128)(2,1)}), bf16[4,192,256]{2,1,0:T(8,128)(2,1)S(1)}, u32[]{:S(2)}, u32[]{:S(2)}) async-start(bf16[4,192,256]{2,1,0:T(8,128)(2,1)} %shard_map.140), calls=%async_computation.5 | async-start | bytes 786432 | tf_op jit(solution)/shard_map/all_to_all | solution.py:464
  120.6 11.1 %collective-permute-start.5 = (bf16[576,768]{1,0:T(8,128)(2,1)S(1)}, bf16[576,768]{1,0:T(8,128)(2,1)S(1)}, u32[]{:S(2)}, u32[]{:S(2)}) collective-permute-start(bf16[576,768]{1,0:T(8,128)(2,1)S(1)} %all_gather.3.mine), channel_id=1, source_target_pairs={{0,8},{8,0},{1,9},{9,1},{2,10},{10,2},{3,11},{11,3},{4,12},{12,4},... | collective-permute-start | bytes 2654216 | tf_op jit(solution)/shard_map/ppermute | solution.py:456
